TPU v7x, 128 devices: a whole 4x4x4 slice. The times are simulated.
128 devices in a mesh: cuts: 8 (over x, core), tile: 16 (over z, y).
Axes of the slice: x: 4, y: 4, z: 4, core: 2. Of those that a mesh axis runs over, the one named last changes fastest.
Arguments:
- acquired: bfloat16 [2097152, 256], P(('cuts', 'tile')), may hold values from -6 to 6
- stencil: bfloat16 [4096, 1024], P('tile'), may hold values from -0.03125 to 0.03125
- send_slots: int32 [128, 16, 1280], P(('cuts', 'tile')), may hold values from 0 to 16383
- send_lines: int32 [128, 16, 1280], P(('cuts', 'tile')), may hold values from 0 to 2047
- send_counts: int32 [128, 16], P(('cuts', 'tile')), may hold values from 1 to 1280, as said below
- return_slots: int32 [128, 16, 128], P(('cuts', 'tile')), may hold values from 0 to 255
- return_counts: int32 [128, 16], P(('cuts', 'tile')), may hold values from 1 to 128, as said below
Outputs:
- field_out: bfloat16 [128, 256, 256], P(('cuts', 'tile'))
- returned: bfloat16 [2048, 128, 256], P(('cuts', 'tile'))
Inputs may be any that keep to these rules, and one draw needn't show every extreme that they name: `send_counts`: some tile receives 1280 rows from every device. `return_counts`: some reader tile receives 128 lines from every owner.
All inputs are finite; a program needn't handle non-finite values.
Results may differ from a plain program's by a relative error of at most 0.00075.
Values may be sent and summed in bfloat16 or wider, within the bound.
No kernel may reach another device: no remote copies, remote signals or barrier semaphores. Data moves between devices by JAX's collectives and lax.ppermute only.
A program may use at most 192 MiB of HBM per device.

v0:
```python
import jax
import jax.numpy as jnp
from jax import lax
from jax.sharding import PartitionSpec as P

NX = 256
NY = 256
TAPS = 4
ITERS = 2
ZDEV = 1


def with_halo(cells, sides, width):
    for axis, dim in sides:
        count = lax.axis_size(axis)
        ends = count - 1
        head = lax.slice_in_dim(cells, 0, width, axis=dim)
        tail = lax.slice_in_dim(cells, cells.shape[dim] - width, cells.shape[dim], axis=dim)
        cells = jnp.concatenate(
            [
                lax.ppermute(tail, axis, [(i, (i + 1) % count) for i in range(ends)]),
                cells,
                lax.ppermute(head, axis, [((i + 1) % count, i) for i in range(ends)]),
            ],
            axis=dim,
        )
    return cells


def local_sum(padded, inner):
    ypad = jnp.pad(inner, ((0, 0), (1, 1), (0, 0)))
    xpad = jnp.pad(inner, ((0, 0), (0, 0), (1, 1)))
    return padded[2:] + padded[:-2] + ypad[:, 2:] + ypad[:, :-2] + xpad[:, :, 2:] + xpad[:, :, :-2]


def line_sums(rows_block, lines_block, line_total):
    line_range = jnp.arange(line_total, dtype=jnp.int32)
    onehot = (line_range[:, None] == lines_block[None, :]).astype(jnp.bfloat16)
    return jnp.dot(onehot, rows_block, preferred_element_type=jnp.float32)


def apply_stencil(line_field, stencil):
    plane_total = line_field.shape[0] // NY
    product = jnp.dot(line_field, stencil.astype(jnp.float32), precision=lax.Precision.HIGHEST)
    product = product.reshape(plane_total, NY, TAPS, NX)
    accum_planes = product[:, :, 0, :]
    for shift_k in range(1, TAPS):
        accum_planes = accum_planes + jnp.roll(product[:, :, shift_k, :], shift_k, axis=1)
    return accum_planes


def local(acquired, stencil, send_slots, send_lines, send_counts, return_slots, return_counts):
    tile_count = lax.axis_size("tile")
    cut_count = lax.axis_size("cuts")
    slots = send_slots[0]
    line_ids = send_lines[0]
    counts = send_counts[0]
    slot_total = slots.shape[1]
    slot_index = jnp.arange(slot_total, dtype=jnp.int32)
    usable = slot_index[None, :] < counts[:, None]
    picked = jnp.take(acquired, slots.reshape(-1), axis=0).reshape(tile_count, slot_total, NX)
    picked = jnp.where(usable[:, :, None], picked, jnp.zeros_like(picked))
    line_ids = jnp.where(usable, line_ids, 0)
    group_lines = cut_count * ZDEV * NY
    arrived, arrived_lines = (
        lax.all_to_all(picked, "tile", split_axis=0, concat_axis=0, tiled=True),
        lax.all_to_all(line_ids, "tile", split_axis=0, concat_axis=0, tiled=True),
    )

    def add_source(carry_lines, source_item):
        rows_block, lines_block = source_item
        return (carry_lines + line_sums(rows_block, lines_block, group_lines), None)

    line_buffer = jnp.zeros((group_lines, NX), jnp.float32)
    line_buffer, _ = lax.scan(add_source, line_buffer, (arrived, arrived_lines))
    line_planes = line_buffer.reshape(cut_count * ZDEV, NY, NX)
    own_lines = lax.psum_scatter(line_planes, "cuts", scatter_dimension=0, tiled=True)
    smooth_field = apply_stencil(own_lines.reshape(ZDEV * NY, NX), stencil)
    for sweep in range(ITERS):
        padded = with_halo(smooth_field, ((("cuts", "tile"), 0),), 1)
        smooth_field = smooth_field + 0.15 * (local_sum(padded, smooth_field) - 6.0 * smooth_field)
    field_out = smooth_field.astype(jnp.bfloat16)
    read_ids = return_slots[0]
    read_counts = return_counts[0]
    read_total = read_ids.shape[1]
    flat_field = field_out.reshape(ZDEV * NY, NX)
    read_index = jnp.arange(read_total, dtype=jnp.int32)
    usable_back = read_index[None, :] < read_counts[:, None]
    own_range = jnp.arange(ZDEV * NY, dtype=jnp.int32)
    selector = (read_ids.reshape(-1)[:, None] == own_range[None, :]) & usable_back.reshape(-1)[
        :, None
    ]
    outgoing = jnp.dot(
        selector.astype(jnp.bfloat16), flat_field, preferred_element_type=jnp.float32
    )
    outgoing = outgoing.astype(jnp.bfloat16).reshape(tile_count, read_total, NX)
    returned = lax.all_to_all(outgoing, "tile", split_axis=0, concat_axis=0, tiled=True)
    return (field_out, returned)


def solution(mesh):
    in_specs = (
        P(("cuts", "tile"), None),
        P("tile", None),
        P(("cuts", "tile"), None, None),
        P(("cuts", "tile"), None, None),
        P(("cuts", "tile"), None),
        P(("cuts", "tile"), None, None),
        P(("cuts", "tile"), None),
    )
    out_specs = (P(("cuts", "tile"), None, None), P(("cuts", "tile"), None, None))
    return jax.shard_map(local, mesh=mesh, in_specs=in_specs, out_specs=out_specs, check_vma=False)
```

profile of v0, /device:TPU:1, one launch (start us, length us, event | category | flops | bytes accessed | tf_op | source)
XLA Modules:
  0.0 430.5 jit_solution(4103234589685691059)
XLA Ops:
  7.2 1.7 compare_select_fusion.1
  8.8 8.6 %all-to-all-start = ((s32[16,1,1280]{2,1,0:T(1,128)}), s32[16,1,1280]{2,1,0:T(1,128)S(1)}, u32[]{:S(2)}, u32[]{:S(2)}) async-start(s32[16,1,1280]{2,1,0:T(1,128)} %compare_select_fusion.1), calls=%async_computation | async-start | bytes 163840 | tf_op jit(solution)/shard_map/all_to_all | solution.py:67
  17.4 0.7 iota_compare_fusion.5
  18.2 0.9 compare_and_fusion
  19.1 1.0 copy.13
  20.1 0.1 compare_select_fusion
  20.2 80.7 %gather_fusion = bf16[20480,256]{1,0:T(8,128)(2,1)} fusion(bf16[16384,256]{1,0:T(8,128)(2,1)} %param.9, s32[20480]{0:T(1024)S(1)} %broadcast_clamp_fusion), kind=kCustom, calls=%fused_computation | custom fusion | bytes 21053440 | tf_op jit(solution)/shard_map/jit(_take)/gather | solution.py:61
  100.9 9.3 %select_select_fusion = bf16[16,1280,256]{2,1,0:T(8,128)(2,1)} fusion(bf16[16,1280,256]{2,1,0:T(8,128)(2,1)} %bitcast.53, pred[16,1280]{1,0:T(8,128)(4,1)S(1)} %compare_and_fusion, pred[16,1280]{1,0:T(8,128)(4,1)S(1)} %iota_compare_fusion.5), kind=kLoop, calls=%fused_computation.9 | loop fusion | flops 10485760 | bytes 21012480 | tf_op jit(solution)/shard_map/jit(_where)/select_n | solution.py:62
  110.2 6.7 %all-to-all-start.1 = ((bf16[16,1280,256]{2,1,0:T(8,128)(2,1)}), bf16[16,1280,256]{2,1,0:T(8,128)(2,1)}, u32[]{:S(2)}, u32[]{:S(2)}) async-start(bf16[16,1280,256]{2,1,0:T(8,128)(2,1)} %select_select_fusion), calls=%async_computation.1 | async-start | bytes 20971520 | tf_op jit(solution)/shard_map/all_to_all | solution.py:66
  116.9 0.0 reduce-scatter.2.cloned.1.call-start
  117.0 152.3 %all-to-all-done.1 = bf16[16,1280,256]{2,1,0:T(8,128)(2,1)} async-done(((bf16[16,1280,256]{2,1,0:T(8,128)(2,1)}), bf16[16,1280,256]{2,1,0:T(8,128)(2,1)}, u32[]{:S(2)}, u32[]{:S(2)}) %all-to-all-start.1) | async-done | bytes 10485792 | tf_op jit(solution)/shard_map/all_to_all | solution.py:66
  269.3 61.4 %while.11 = (s32[]{:T(128)}, f32[2048,256]{1,0:T(8,128)S(1)}, s32[16,1280]{1,0:T(8,128)S(1)}, bf16[16,1280,256]{2,1,0:T(8,128)(2,1)}, s32[]{:T(128)}, /*index=5*/s32[]{:T(128)}) while((s32[]{:T(128)}, f32[2048,256]{1,0:T(8,128)S(1)}, s32[16,1280]{1,0:T(8,128)S(1)}, bf16[16,1280,256]{2,1,0:T(8,128)(2,1)}, s32[]{:T(128)}, ...), condition=%wide.region_1.2_spmd.clone, body=%wide.region_0.1_spmd.clone.sunk | while | flops 1345847296 | bytes 4865619 | solution.py:75
  269.3 3.8 fusion.31
  273.2 3.8 fusion.31
  277.1 3.8 fusion.31
  280.9 3.8 fusion.31
  284.7 3.8 fusion.31
  288.5 3.8 fusion.31
  292.4 3.8 fusion.31
  296.2 3.8 fusion.31
  300.1 3.8 fusion.31
  303.9 3.8 fusion.31
  307.7 3.8 fusion.31
  311.6 3.8 fusion.31
  315.4 3.8 fusion.31
  319.2 3.8 fusion.31
  323.1 3.8 fusion.31
  326.9 3.8 fusion.31
  330.7 1.3 copy-done
  332.0 0.2 copy.11
  332.3 32.7 %reduce-scatter.2.cloned.1.call-done = f32[1,256,256]{2,1,0:T(8,128)} async-done(((f32[8,256,256]{2,1,0:T(8,128)}), f32[1,256,256]{2,1,0:T(8,128)}) %reduce-scatter.2.cloned.1.call-update) | async-done | bytes 262160 | tf_op jit(solution)/shard_map/reduce_scatter | solution.py:77
  364.9 1.6 convolution_bitcast_fusion
  366.5 0.1 slice_bitcast_fusion
  366.6 0.1 fusion.23
  366.7 10.3 %collective-permute-start = (f32[1,256,256]{2,1,0:T(8,128)S(1)}, f32[1,256,256]{2,1,0:T(8,128)S(1)}, u32[]{:S(2)}, u32[]{:S(2)}) collective-permute-start(f32[1,256,256]{2,1,0:T(8,128)S(1)} %fusion.23), channel_id=1, source_target_pairs={{1,0},{2,1},{3,2},{4,3},{5,4},{6,5},{7,6},{8,7},{9,8},{10,9},{11,1... | collective-permute-start | bytes 786440 | tf_op jit(solution)/shard_map/ppermute | solution.py:23
  377.0 1.9 collective-permute-start.1
  378.9 2.3 collective-permute-done
  381.2 6.8 %collective-permute-done.1 = f32[1,256,256]{2,1,0:T(8,128)S(1)} collective-permute-done((f32[1,256,256]{2,1,0:T(8,128)S(1)}, f32[1,256,256]{2,1,0:T(8,128)S(1)}, u32[]{:S(2)}, u32[]{:S(2)}) %collective-permute-start.1) | collective-permute-done | bytes 262176 | tf_op jit(solution)/shard_map/ppermute | solution.py:21
  388.0 0.2 fusion.14
  388.2 1.9 collective-permute-start.2
  390.1 3.4 collective-permute-start.3
  393.5 0.1 fusion.26
  393.6 1.8 collective-permute-done.2
  395.4 5.8 %collective-permute-done.3 = f32[1,256,256]{2,1,0:T(8,128)S(1)} collective-permute-done((f32[1,256,256]{2,1,0:T(8,128)S(1)}, f32[1,256,256]{2,1,0:T(8,128)S(1)}, u32[]{:S(2)}, u32[]{:S(2)}) %collective-permute-start.3) | collective-permute-done | bytes 262176 | tf_op jit(solution)/shard_map/ppermute | solution.py:21
  401.1 0.2 fusion.20
  401.4 1.8 convolution_convert_fusion
  403.2 19.5 %all_to_all.19 = bf16[16,128,256]{2,1,0:T(8,128)(2,1)S(1)} all-to-all(bf16[16,128,256]{2,1,0:T(8,128)(2,1)S(1)} %bitcast.59), channel_id=1, replica_groups=mesh['cuts'=8,'tile'=16] {'tile'}, dimensions={0} | all-to-all | bytes 2097152 | tf_op jit(solution)/shard_map/all_to_all | solution.py:97
  422.7 1.0 copy.23
  (33 shorter events, 0.5 us)
Async XLA Ops:
  8.8 101.4 %all-to-all-start = ((s32[16,1,1280]{2,1,0:T(1,128)}), s32[16,1,1280]{2,1,0:T(1,128)S(1)}, u32[]{:S(2)}, u32[]{:S(2)}) async-start(s32[16,1,1280]{2,1,0:T(1,128)} %compare_select_fusion.1), calls=%async_computation | async-start | bytes 163840 | tf_op jit(solution)/shard_map/all_to_all | solution.py:67
  110.2 159.1 %all-to-all-start.1 = ((bf16[16,1280,256]{2,1,0:T(8,128)(2,1)}), bf16[16,1280,256]{2,1,0:T(8,128)(2,1)}, u32[]{:S(2)}, u32[]{:S(2)}) async-start(bf16[16,1280,256]{2,1,0:T(8,128)(2,1)} %select_select_fusion), calls=%async_computation.1 | async-start | bytes 20971520 | tf_op jit(solution)/shard_map/all_to_all | solution.py:66
  116.9 248.0 %reduce-scatter.2.cloned.1.call-start = ((), (), s32[]{:S(2)}) async-start(), calls=%async_computation.4 | async-start | bytes 2359296 | tf_op jit(solution)/shard_map/reduce_scatter | solution.py:77
  269.3 62.7 %copy-start.1 = (bf16[256,1024]{1,0:T(8,128)(2,1)S(1)}, bf16[256,1024]{1,0:T(8,128)(2,1)}, u32[]{:S(2)}) copy-start(bf16[256,1024]{1,0:T(8,128)(2,1)} %param.10) | copy-start | bytes 1572868
  330.7 1.3 copy-start
  330.7 62.8 %copy-start.3 = (s32[1,16]{1,0:T(1,128)S(1)}, s32[1,16]{1,0:T(1,128)}, u32[]{:S(2)}) copy-start(s32[1,16]{1,0:T(1,128)} %param.15) | copy-start | bytes 196
  330.7 70.7 %copy-start.4 = (s32[1,16,128]{2,1,0:T(8,128)S(1)}, s32[1,16,128]{2,1,0:T(8,128)}, u32[]{:S(2)}) copy-start(s32[1,16,128]{2,1,0:T(8,128)} %param.14) | copy-start | bytes 24580
  366.7 14.5 %collective-permute-start = (f32[1,256,256]{2,1,0:T(8,128)S(1)}, f32[1,256,256]{2,1,0:T(8,128)S(1)}, u32[]{:S(2)}, u32[]{:S(2)}) collective-permute-start(f32[1,256,256]{2,1,0:T(8,128)S(1)} %fusion.23), channel_id=1, source_target_pairs={{1,0},{2,1},{3,2},{4,3},{5,4},{6,5},{7,6},{8,7},{9,8},{10,9},{11,1... | collective-permute-start | bytes 786440 | tf_op jit(solution)/shard_map/ppermute | solution.py:23
  377.0 11.0 %collective-permute-start.1 = (f32[1,256,256]{2,1,0:T(8,128)S(1)}, f32[1,256,256]{2,1,0:T(8,128)S(1)}, u32[]{:S(2)}, u32[]{:S(2)}) collective-permute-start(f32[1,256,256]{2,1,0:T(8,128)S(1)} %fusion.23), channel_id=1, source_target_pairs={{0,1},{1,2},{2,3},{3,4},{4,5},{5,6},{6,7},{7,8},{8,9},{9,10},{10,1... | collective-permute-start | bytes 786440 | tf_op jit(solution)/shard_map/ppermute | solution.py:21
  388.2 7.2 %collective-permute-start.2 = (f32[1,256,256]{2,1,0:T(8,128)S(1)}, f32[1,256,256]{2,1,0:T(8,128)S(1)}, u32[]{:S(2)}, u32[]{:S(2)}) collective-permute-start(f32[1,256,256]{2,1,0:T(8,128)S(1)} %fusion.14), channel_id=1, source_target_pairs={{1,0},{2,1},{3,2},{4,3},{5,4},{6,5},{7,6},{8,7},{9,8},{10,9},{11,1... | collective-permute-start | bytes 786440 | tf_op jit(solution)/shard_map/ppermute | solution.py:23
  390.1 11.0 %collective-permute-start.3 = (f32[1,256,256]{2,1,0:T(8,128)S(1)}, f32[1,256,256]{2,1,0:T(8,128)S(1)}, u32[]{:S(2)}, u32[]{:S(2)}) collective-permute-start(f32[1,256,256]{2,1,0:T(8,128)S(1)} %fusion.14), channel_id=1, source_target_pairs={{0,1},{1,2},{2,3},{3,4},{4,5},{5,6},{6,7},{7,8},{8,9},{9,10},{10,1... | collective-permute-start | bytes 786440 | tf_op jit(solution)/shard_map/ppermute | solution.py:21
  401.4 22.3 %copy-start.2 = (bf16[1,256,256]{2,1,0:T(8,128)(2,1)}, bf16[1,256,256]{2,1,0:T(8,128)(2,1)S(1)}, u32[]{:S(2)}) copy-start(bf16[1,256,256]{2,1,0:T(8,128)(2,1)S(1)} %fusion.20) | copy-start | bytes 393220
Sparse Core Ops, SparseCore 0:
  332.2 32.7 reduce-scatter.1
where the time goes:
time: 433 us; the launch traced here: 431 us
  waiting for transfers between devices  202 us (47%)
  local copies, waits for them, and re-layouts  84.7 us (20%)
  matrix products  63.8 us (15%)
  starting transfers between devices  32.9 us (8%)
  blocking collectives  19.5 us (5%)
  between operations  14.3 us (3%)
  other arithmetic  13.3 us (3%)
    all_to_all x1, waiting for transfers between devices, local(): lax.all_to_all(picked, 'tile', split_axis=0, concat_axis=0, tiled=True)  152 us
    gather x1, local copies, waits for them, and re-layouts, local(): jnp.take(acquired, slots.reshape(-1), axis=0)  80.7 us
    dot_general x16, matrix products, line_sums(): return jnp.dot(onehot, rows_block, preferred_element_type=jnp.float32)  60.4 us
    reduce_scatter x1, waiting for transfers between devices, local(): lax.psum_scatter(line_planes, 'cuts', scatter_dimension=0, tiled=True)  32.7 us
    all_to_all x1, blocking collectives, local(): lax.all_to_all(outgoing, 'tile', split_axis=0, concat_axis=0, tiled=True)  19.5 us
    ppermute x2, waiting for transfers between devices, with_halo(): lax.ppermute(tail, axis, [(i, (i + 1) % count) for i in range(ends)])  12.6 us
    ppermute x2, starting transfers between devices, with_halo(): lax.ppermute(head, axis, [((i + 1) % count, i) for i in range(ends)])  12.2 us
    select_n x1, other arithmetic, local(): picked = jnp.where(usable[:, :, None], picked, jnp.zeros_like(picked))  9.32 us
  transfers between devices with their start and end apart: 7, of which 6 were waited for; matrix products, arithmetic and copies ran while one was open for 22% of the time, Pallas kernels for 0%

commit v1 on v0

v1 whole, which is shorter than its diff:
```python
import functools
import math

import jax
import jax.numpy as jnp
from jax import lax
from jax.experimental import pallas as pl
from jax.experimental.pallas import tpu as pltpu
from jax.sharding import PartitionSpec as P

NX = 256
NY = 256
TAPS = 4
HALF = 128
ALPHA = math.log(2.0) / 64.0
TOP = 32700.0
CHUNK = 256


def params(mib):
    return pltpu.CompilerParams(
        vmem_limit_bytes=mib * 1024 * 1024, dimension_semantics=("arbitrary",)
    )


def encode(block):
    top = jnp.max(jnp.abs(block), axis=1, keepdims=True)
    code = jnp.ceil(jnp.log(jnp.maximum(top, 1e-33)) * (1.0 / ALPHA))
    values = block * (TOP / jnp.exp(code * ALPHA))
    values = jnp.round(values).astype(jnp.int32).astype(jnp.int16)
    return values, code


def eye(size):
    return lax.broadcasted_iota(jnp.int32, (size, size), 0) == lax.broadcasted_iota(
        jnp.int32, (size, size), 1
    )


def to_row(column):
    return jnp.sum(jnp.where(eye(HALF), column, 0.0), axis=0, keepdims=True)


def to_column(row):
    return jnp.sum(jnp.where(eye(HALF), row, 0.0), axis=1, keepdims=True)


def decode(values, code_row):
    scale = jnp.exp(code_row * ALPHA) * (1.0 / TOP)
    return values.astype(jnp.int32).astype(jnp.float32) * to_column(scale)


def code_block(rows):
    block = jnp.zeros((16, NX), jnp.float32)
    index = lax.broadcasted_iota(jnp.int32, (16, NX), 0)
    for i, row in enumerate(rows):
        block = jnp.where(index == i, row, block)
    return block.astype(jnp.int32).astype(jnp.int16)


def gather_kernel(slots_ref, counts_ref, acq_ref, out_ref, wide_ref, stage_ref):
    step = pl.program_id(0)
    rows = acq_ref.shape[0]

    @pl.when(step == 0)
    def _():
        def widen(i, carry):
            base = pl.multiple_of(i * 64, 64)
            x = acq_ref[pl.ds(base, 64), :].astype(jnp.float32)
            wide_ref[pl.ds(base, 64), 0, :] = x[:, :128]
            wide_ref[pl.ds(base, 64), 1, :] = x[:, 128:]
            return carry

        lax.fori_loop(0, rows // 64, widen, 0)
        stage_ref[...] = jnp.zeros(stage_ref.shape, jnp.float32)

    count = counts_ref[step]

    def pick(i, carry):
        base = i * 16
        for u in range(16):
            stage_ref[base + u] = wide_ref[slots_ref[step, base + u]]
        return carry

    lax.fori_loop(0, (count + 15) // 16, pick, 0)

    def narrow(i, carry):
        base = pl.multiple_of(i * CHUNK, CHUNK)
        out_ref[0, pl.ds(base, CHUNK), 0:128] = stage_ref[pl.ds(base, CHUNK), 0, :].astype(jnp.bfloat16)
        out_ref[0, pl.ds(base, CHUNK), 128:256] = stage_ref[pl.ds(base, CHUNK), 1, :].astype(jnp.bfloat16)
        return carry

    lax.fori_loop(0, (count + CHUNK - 1) // CHUNK, narrow, 0)


def gather_rows(acquired, slots, counts):
    tiles, cap = slots.shape
    return pl.pallas_call(
        gather_kernel,
        grid_spec=pltpu.PrefetchScalarGridSpec(
            num_scalar_prefetch=2,
            grid=(tiles,),
            in_specs=[pl.BlockSpec(acquired.shape, lambda t, s, c: (0, 0))],
            out_specs=pl.BlockSpec((1, cap, NX), lambda t, s, c: (t, 0, 0)),
            scratch_shapes=[
                pltpu.VMEM((acquired.shape[0], 2, 128), jnp.float32),
                pltpu.VMEM((cap, 2, 128), jnp.float32),
            ],
        ),
        out_shape=jax.ShapeDtypeStruct((tiles, cap, NX), jnp.bfloat16),
        compiler_params=params(48),
        name="gather_rows",
    )(slots, counts, acquired)


def lines_kernel(
    own_n, peer_n, own_ref, peer_ref, own_lines, peer_lines, alias_ref,
    a0_ref, a1_ref, a2_ref, a3_ref, b_ref, acc_ref, code_ref,
):
    step = pl.program_id(0)
    last = pl.num_programs(0) - 1
    acc_ref[...] = jnp.zeros(acc_ref.shape, jnp.float32)
    position = lax.broadcasted_iota(jnp.int32, (CHUNK, CHUNK), 0)

    def add(rows_ref, lines_ref):
        def body(i, carry):
            base = pl.multiple_of(i * CHUNK, CHUNK)
            rows = rows_ref[0, pl.ds(base, CHUNK), :]
            ids = lines_ref[0, pl.ds(i, 1), :]
            for m in range(acc_ref.shape[0] // CHUNK):
                hot = jnp.where(position + m * CHUNK == ids, 1.0, 0.0).astype(jnp.bfloat16)
                span = pl.ds(m * CHUNK, CHUNK)
                acc_ref[span, :] += jnp.dot(hot, rows, preferred_element_type=jnp.float32)
            return carry

        return body

    lax.fori_loop(0, (own_n[step] + CHUNK - 1) // CHUNK, add(own_ref, own_lines), 0)
    lax.fori_loop(0, (peer_n[step] + CHUNK - 1) // CHUNK, add(peer_ref, peer_lines), 0)

    outs = (a0_ref, a1_ref, a2_ref, a3_ref)
    tiles = a0_ref.shape[0] // HALF
    for k in range(4):
        values, code = encode(acc_ref[pl.ds(k * HALF, HALF), :])
        outs[k][pl.ds(pl.multiple_of(step * HALF, HALF), HALF), :] = values
        row = to_row(code)
        code_ref[k, pl.ds(step, 1), :] = row

    codes = []
    for k in range(4):
        values, code = encode(acc_ref[pl.ds(512 + k * HALF, HALF), :])
        b_ref[0, pl.ds(k * HALF, HALF), :] = values
        codes.append(to_row(code))
    b_ref[0, pl.ds(512, 16), :] = code_block(
        [jnp.concatenate(codes[0:2], axis=1), jnp.concatenate(codes[2:4], axis=1)]
    )

    @pl.when(step == last)
    def _():
        for k in range(4):
            first = code_ref[k]
            both = jnp.concatenate([first, jnp.zeros_like(first)], axis=1)
            both = jnp.concatenate([both, jnp.zeros_like(both)], axis=0)
            outs[k][pl.ds(last * HALF + HALF, 16), :] = both.astype(jnp.int32).astype(jnp.int16)


def line_blocks(own_rows, peer_rows, own_lines, peer_lines, own_n, peer_n, b_old, first, tiles_all):
    tiles, cap, _ = own_rows.shape
    span = cap // CHUNK
    row_spec = pl.BlockSpec((1, cap, NX), lambda t, *_: (t, 0, 0))
    line_spec = pl.BlockSpec((1, span, CHUNK), lambda t, *_: (t, 0, 0))
    a_shape = (tiles * HALF + 16, NX)
    args = [own_n, peer_n, own_rows, peer_rows, own_lines, peer_lines]
    aliases = {}
    if b_old is None:
        b_old = jnp.zeros((16, NX), jnp.int16)
    else:
        aliases = {6: 4}
    args.append(b_old)
    return pl.pallas_call(
        lines_kernel,
        grid_spec=pltpu.PrefetchScalarGridSpec(
            num_scalar_prefetch=2,
            grid=(tiles,),
            in_specs=[row_spec, row_spec, line_spec, line_spec, pl.BlockSpec(memory_space=pl.ANY)],
            out_specs=[pl.BlockSpec(a_shape, lambda t, *_: (0, 0))] * 4
            + [pl.BlockSpec((1, 4 * HALF + 16, NX), lambda t, *_: (t + first, 0, 0))],
            scratch_shapes=[
                pltpu.VMEM((8 * HALF, NX), jnp.float32),
                pltpu.VMEM((4, 8, HALF), jnp.float32),
            ],
        ),
        out_shape=[jax.ShapeDtypeStruct(a_shape, jnp.int16)] * 4
        + [jax.ShapeDtypeStruct((tiles_all, 4 * HALF + 16, NX), jnp.int16)],
        input_output_aliases=aliases,
        compiler_params=params(48),
        name="line_blocks",
    )(*args)


def sum_x_kernel(p0, p1, p2, p3, c0, c1, c2, c3, alias_ref, out_ref):
    step = pl.program_id(0)
    total = jnp.zeros((HALF, NX), jnp.float32)
    index = lax.broadcasted_iota(jnp.int32, (16, HALF), 0)
    for values, codes in ((p0, c0), (p1, c1), (p2, c2), (p3, c3)):
        table = codes[:, 0:HALF].astype(jnp.int32).astype(jnp.float32)
        row = jnp.sum(jnp.where(index == step, table, 0.0), axis=0, keepdims=True)
        total = total + decode(values[...], row)
    values, code = encode(total)
    out_ref[0, pl.ds(0, HALF), :] = values
    row = to_row(code)
    out_ref[0, pl.ds(HALF, 16), :] = code_block([jnp.concatenate([row, row], axis=1)])


def sum_x(parts, old, first, tiles_all):
    tiles = (parts[0].shape[0] - 16) // HALF
    aliases = {}
    if old is None:
        old = jnp.zeros((16, NX), jnp.int16)
    else:
        aliases = {8: 0}
    return pl.pallas_call(
        sum_x_kernel,
        grid=(tiles,),
        in_specs=[pl.BlockSpec((HALF, NX), lambda t: (t, 0))] * 4
        + [pl.BlockSpec((16, NX), lambda t: (tiles * HALF // 16, 0))] * 4
        + [pl.BlockSpec(memory_space=pl.ANY)],
        out_specs=pl.BlockSpec((1, HALF + 16, NX), lambda t: (t + first, 0, 0)),
        out_shape=jax.ShapeDtypeStruct((tiles_all, HALF + 16, NX), jnp.int16),
        input_output_aliases=aliases,
        compiler_params=params(32),
        name="sum_x",
    )(*parts, *parts, old)


def sum_tile_kernel(in_ref, o0, o1, o2, o3, acc_ref):
    step = pl.program_id(0)
    table = in_ref[0, pl.ds(4 * HALF, 16), :].astype(jnp.int32).astype(jnp.float32)
    for k in range(4):
        row = table[k // 2 : k // 2 + 1, (k % 2) * HALF : (k % 2) * HALF + HALF]
        part = decode(in_ref[0, pl.ds(k * HALF, HALF), :], row)
        old = jnp.where(step == 0, jnp.zeros_like(part), acc_ref[pl.ds(k * HALF, HALF), :])
        acc_ref[pl.ds(k * HALF, HALF), :] = old + part

    @pl.when(step == pl.num_programs(0) - 1)
    def _():
        for k, out in enumerate((o0, o1, o2, o3)):
            values, code = encode(acc_ref[pl.ds(k * HALF, HALF), :])
            out[pl.ds(0, HALF), :] = values
            row = to_row(code)
            out[pl.ds(HALF, 16), :] = code_block([jnp.concatenate([row, row], axis=1)])


def sum_tile(arrived):
    tiles, rows, _ = arrived.shape
    out_shape = (HALF + 16, NX)
    return pl.pallas_call(
        sum_tile_kernel,
        grid=(tiles,),
        in_specs=[pl.BlockSpec((1, rows, NX), lambda t: (t, 0, 0))],
        out_specs=[pl.BlockSpec(out_shape, lambda t: (0, 0))] * 4,
        out_shape=[jax.ShapeDtypeStruct(out_shape, jnp.int16)] * 4,
        scratch_shapes=[pltpu.VMEM((4 * HALF, NX), jnp.float32)],
        compiler_params=params(32),
        name="sum_tile",
    )(arrived)


def first_code(block):
    return block[0:1, 0:HALF].astype(jnp.int32).astype(jnp.float32)


def plane_kernel(a_ref, b0, b1, b2, b3, stencil_ref, plane_ref, send_ref, lines_ref):
    def body(i, carry):
        return carry + decode(a_ref[i, pl.ds(0, HALF), :], first_code(a_ref[i, pl.ds(HALF, 16), :]))

    lines_ref[pl.ds(0, HALF), :] = lax.fori_loop(
        0, a_ref.shape[0], body, jnp.zeros((HALF, NX), jnp.float32)
    )
    total = jnp.zeros((HALF, NX), jnp.float32)
    for b in (b0, b1, b2, b3):
        total = total + decode(b[pl.ds(0, HALF), :], first_code(b[pl.ds(HALF, 16), :]))
    lines_ref[pl.ds(HALF, HALF), :] = total

    lines = lines_ref[...]
    high = lines.astype(jnp.bfloat16)
    rest = lines - high.astype(jnp.float32)
    mid = rest.astype(jnp.bfloat16)
    low = (rest - mid.astype(jnp.float32)).astype(jnp.bfloat16)
    plane = jnp.zeros((NY, NX), jnp.float32)
    for k in range(TAPS):
        weights = stencil_ref[:, k * NX : (k + 1) * NX]
        product = jnp.dot(high, weights, preferred_element_type=jnp.float32)
        product += jnp.dot(mid, weights, preferred_element_type=jnp.float32)
        product += jnp.dot(low, weights, preferred_element_type=jnp.float32)
        if k:
            product = pltpu.roll(product, k, 0)
        plane = plane + product
    plane_ref[...] = plane
    rows = []
    for h in range(2):
        values, code = encode(plane[h * HALF : (h + 1) * HALF])
        send_ref[pl.ds(h * HALF, HALF), :] = values
        rows.append(to_row(code))
    send_ref[pl.ds(NY, 16), :] = code_block([jnp.concatenate(rows, axis=1)])


def own_plane(a, bs, stencil):
    return pl.pallas_call(
        plane_kernel,
        out_shape=[
            jax.ShapeDtypeStruct((NY, NX), jnp.float32),
            jax.ShapeDtypeStruct((NY + 16, NX), jnp.int16),
        ],
        scratch_shapes=[pltpu.VMEM((NY, NX), jnp.float32)],
        compiler_params=pltpu.CompilerParams(vmem_limit_bytes=32 * 1024 * 1024),
        name="own_plane",
    )(a, *bs, stencil)


def smooth_kernel(edge_ref, plane_ref, l1, l2, r1, r2, out_ref):
    def halo(ref):
        table = ref[pl.ds(NY, 16), :].astype(jnp.int32).astype(jnp.float32)
        parts = [
            decode(ref[pl.ds(h * HALF, HALF), :], table[0:1, h * HALF : (h + 1) * HALF])
            for h in range(2)
        ]
        return jnp.concatenate(parts, axis=0)

    row = lax.broadcasted_iota(jnp.int32, (NY, NX), 0)
    col = lax.broadcasted_iota(jnp.int32, (NY, NX), 1)

    def step(below, mid, above):
        near = jnp.where(row == 0, 0.0, pltpu.roll(mid, 1, 0))
        near += jnp.where(row == NY - 1, 0.0, pltpu.roll(mid, NY - 1, 0))
        near += jnp.where(col == 0, 0.0, pltpu.roll(mid, 1, 1))
        near += jnp.where(col == NX - 1, 0.0, pltpu.roll(mid, NX - 1, 1))
        return mid + 0.15 * (near + below + above - 6.0 * mid)

    plane = plane_ref[...]
    left, right = halo(l1), halo(r1)
    lower = step(halo(l2), left, plane)
    upper = step(plane, right, halo(r2))
    lower = jnp.where(edge_ref[0] > 0, lower, 0.0)
    upper = jnp.where(edge_ref[1] > 0, upper, 0.0)
    out_ref[...] = step(lower, step(left, plane, right), upper).astype(jnp.bfloat16)


def smooth(edges, plane, halos):
    vmem = pl.BlockSpec(memory_space=pltpu.VMEM)
    return pl.pallas_call(
        smooth_kernel,
        in_specs=[pl.BlockSpec(memory_space=pltpu.SMEM)] + [vmem] * 5,
        out_specs=vmem,
        out_shape=jax.ShapeDtypeStruct((NY, NX), jnp.bfloat16),
        compiler_params=pltpu.CompilerParams(vmem_limit_bytes=32 * 1024 * 1024),
        name="smooth",
    )(edges, plane, *halos)


def local(acquired, stencil, send_slots, send_lines, send_counts, return_slots, return_counts):
    tile_count = lax.axis_size("tile")
    cut_count = lax.axis_size("cuts")
    tile_half = tile_count // 2
    here = lax.axis_index("cuts")
    here_x = here // 2
    here_core = here % 2
    slots = send_slots[0]
    counts = send_counts[0]
    cap = slots.shape[1]
    slot_index = jnp.arange(cap, dtype=jnp.int32)
    usable = slot_index[None, :] < counts[:, None]
    masked = jnp.where(usable, send_lines[0], -1)
    tail = jnp.broadcast_to(counts[:, None], (tile_count, 128))
    sheet = jnp.concatenate([masked, tail], axis=1)
    swap = [(i, i ^ 1) for i in range(cut_count)]
    peer_sheet = lax.ppermute(sheet, "cuts", swap)
    peer_counts = peer_sheet[:, cap]

    def line_codes(ids):
        cut = ids // NY
        y = ids % NY
        mine = (ids >= 0) & (cut % 2 == here_core)
        ahead = (cut // 2 - here_x) % 4
        place = (y // HALF) * (4 * HALF) + ahead * HALF + y % HALF
        return jnp.where(mine, place, -1).reshape(tile_count, cap // CHUNK, CHUNK)

    own_codes = line_codes(masked)
    peer_codes = line_codes(peer_sheet[:, :cap])

    rows, peer_rows = [], []
    for h in range(2):
        part = slice(h * tile_half, (h + 1) * tile_half)
        rows.append(gather_rows(acquired, slots[part], counts[part]))
        peer_rows.append(lax.ppermute(rows[h], "cuts", swap))

    def x_send(block, k):
        return lax.ppermute(block, "cuts", [(i, (i + 2 * k) % cut_count) for i in range(cut_count)])

    b_blocks = None
    a_parts = []
    for h in range(2):
        part = slice(h * tile_half, (h + 1) * tile_half)
        *a_blocks, b_blocks = line_blocks(
            rows[h], peer_rows[h], own_codes[part], peer_codes[part],
            counts[part], peer_counts[part], b_blocks, h * tile_half, tile_count,
        )
        a_parts.append([a_blocks[0]] + [x_send(a_blocks[k], k) for k in (1, 2, 3)])
    b_arrived = lax.all_to_all(b_blocks, "tile", split_axis=0, concat_axis=0, tiled=True)
    a_sums = None
    for h in range(2):
        a_sums = sum_x(a_parts[h], a_sums, h * tile_half, tile_count)
    a_arrived = lax.all_to_all(a_sums, "tile", split_axis=0, concat_axis=0, tiled=True)
    b_sums = sum_tile(b_arrived)
    b_final = [b_sums[0]] + [x_send(b_sums[k], k) for k in (1, 2, 3)]
    plane, coded = own_plane(a_arrived, b_final, stencil)

    total = cut_count * tile_count

    def plane_send(k):
        pairs = [(i, i + k) for i in range(total) if 0 <= i + k < total]
        return lax.ppermute(coded, ("cuts", "tile"), pairs)

    halos = [plane_send(1), plane_send(2), plane_send(-1), plane_send(-2)]
    place = here * tile_count + lax.axis_index("tile")
    edges = jnp.stack([place > 0, place < total - 1]).astype(jnp.int32)
    field = smooth(edges, plane, halos)

    read_ids = return_slots[0]
    read_total = read_ids.shape[1]
    usable_back = jnp.arange(read_total, dtype=jnp.int32)[None, :] < return_counts[0][:, None]
    selector = jnp.where(usable_back, read_ids, -1).reshape(-1)[:, None] == jnp.arange(
        NY, dtype=jnp.int32
    )
    outgoing = jnp.dot(selector.astype(jnp.bfloat16), field, preferred_element_type=jnp.float32)
    outgoing = outgoing.astype(jnp.bfloat16).reshape(tile_count, read_total, NX)
    returned = lax.all_to_all(outgoing, "tile", split_axis=0, concat_axis=0, tiled=True)
    return field[None], returned


def solution(mesh):
    in_specs = (
        P(("cuts", "tile"), None),
        P("tile", None),
        P(("cuts", "tile"), None, None),
        P(("cuts", "tile"), None, None),
        P(("cuts", "tile"), None),
        P(("cuts", "tile"), None, None),
        P(("cuts", "tile"), None),
    )
    out_specs = (P(("cuts", "tile"), None, None), P(("cuts", "tile"), None, None))
    return jax.shard_map(local, mesh=mesh, in_specs=in_specs, out_specs=out_specs, check_vma=False)
```

time: 433 us -> 270 us (0.62)
  waiting for transfers between devices: 202 us -> 61.7 us
  Pallas kernels: 0 us -> 118 us
  local copies, waits for them, and re-layouts: 84.7 us -> 4.51 us
  matrix products: 63.8 us -> 1.64 us
  starting transfers between devices: 32.9 us -> 58.8 us
  between operations: 14.3 us -> 0.8 us
  other arithmetic: 13.3 us -> 0.77 us
    all_to_all x2, waiting for transfers between devices: 152 us -> 9.3 us  [the longest x1 9.3 us: local(): lax.all_to_all(b_blocks, 'tile', split_axis=0, concat_axis=0, tiled=True)]
    pallas_call x0 -> x9, Pallas kernels: none -> 118 us  [the longest x2 62.2 us: gather_rows(): pl.pallas_call(gather_kernel, grid_spec=pltpu.PrefetchScalarGridSpec(num_...]
    gather x1 -> x0, local copies, waits for them, and re-layouts: 80.7 us -> none  [local(): jnp.take(acquired, slots.reshape(-1), axis=0)]
    dot_general x18 -> x1, matrix products: 63.8 us -> 1.64 us  [local(): jnp.dot(selector.astype(jnp.bfloat16), field, preferred_element_type=jnp....]
    ppermute x4 -> x16, waiting for transfers between devices: 16.6 us -> 52.4 us  [the longest x9 41.7 us: x_send(): lax.ppermute(block, 'cuts', [(i, (i + 2 * k) % cut_count) for i in range(...]
    reduce_scatter x1 -> x0, waiting for transfers between devices: 32.7 us -> none  [local(): lax.psum_scatter(line_planes, 'cuts', scatter_dimension=0, tiled=True)]
    ppermute x4 -> x16, starting transfers between devices: 17.5 us -> 40.9 us  [the longest x4 18.7 us: plane_send(): return lax.ppermute(coded, ('cuts', 'tile'), pairs)]
    select_n x3, other arithmetic: 11.1 us -> 0.69 us  [the longest x2 0.61 us: line_codes(): return jnp.where(mine, place, -1).reshape(tile_count, cap // CHUNK, CHUNK)]
  transfers between devices with their start and end apart: 7 -> 18, of which waited for: 6 -> 11; matrix products, arithmetic and copies ran while one was open for 22% -> 0% of each run, Pallas kernels for 0% -> 25%
where the time goes in v1:
time: 270 us; the launch traced here: 268 us
  Pallas kernels  118 us (44%)
  waiting for transfers between devices  61.7 us (23%)
  starting transfers between devices  58.8 us (22%)
  blocking collectives  21.8 us (8%)
  local copies, waits for them, and re-layouts  4.51 us (2%)
    pallas_call x2, Pallas kernels, gather_rows(): pl.pallas_call(gather_kernel, grid_spec=pltpu.PrefetchScalarGridSpec(num_...  62.2 us
    ppermute x9, waiting for transfers between devices, x_send(): lax.ppermute(block, 'cuts', [(i, (i + 2 * k) % cut_count) for i in range(...  41.7 us
    pallas_call x2, Pallas kernels, line_blocks(): pl.pallas_call(lines_kernel, grid_spec=pltpu.PrefetchScalarGridSpec(num_s...  33.5 us
    all_to_all x1, blocking collectives, local(): lax.all_to_all(outgoing, 'tile', split_axis=0, concat_axis=0, tiled=True)  21.8 us
    ppermute x4, starting transfers between devices, plane_send(): return lax.ppermute(coded, ('cuts', 'tile'), pairs)  18.7 us
    ppermute x9, starting transfers between devices, x_send(): lax.ppermute(block, 'cuts', [(i, (i + 2 * k) % cut_count) for i in range(...  17.7 us
    all_to_all x1, starting transfers between devices, local(): lax.all_to_all(b_blocks, 'tile', split_axis=0, concat_axis=0, tiled=True)  13.1 us
    pallas_call x1, Pallas kernels, sum_tile(): pl.pallas_call(sum_tile_kernel, grid=(tiles,), in_specs=[pl.BlockSpec((1,...  9.49 us
  transfers between devices with their start and end apart: 18, of which 11 were waited for; matrix products, arithmetic and copies ran while one was open for 0% of the time, Pallas kernels for 25%

profile of v1, /device:TPU:1, one launch (start us, length us, event | category | flops | bytes accessed | tf_op | source)
XLA Modules:
  0.0 267.9 jit_solution(15120117916969379977)
XLA Ops:
  0.6 0.8 slice_bitcast_fusion.2
  1.4 0.8 slice_bitcast_fusion
  2.2 27.8 %gather_rows.3.own_ref = bf16[8,1280,256]{2,1,0:T(8,128)(2,1)} custom-call(s32[8,1280]{1,0:T(8,128)S(1)} %get-tuple-element.42.slots_ref, s32[8]{0:T(128)S(1)} %get-tuple-element.44.counts_ref.own_n, bf16[16384,256]{1,0:T(8,128)(2,1)} %acq_ref.3), custom_call_target="tpu_custom_call" | custom-call | tf_op jit(solution)/shard_map/gather_rows/pallas_call | solution.py:98
  30.0 3.9 %collective-permute-start.2 = (bf16[8,1280,256]{2,1,0:T(8,128)(2,1)}, bf16[8,1280,256]{2,1,0:T(8,128)(2,1)}, u32[]{:S(2)}, u32[]{:S(2)}) collective-permute-start(bf16[8,1280,256]{2,1,0:T(8,128)(2,1)} %gather_rows.3.own_ref), channel_id=1, source_target_pairs={{0,16},{16,0},{32,48},{48,32},{64,80},{80,64},{96,112},{112,96},{1... | collective-permute-start | bytes 15728648 | tf_op jit(solution)/shard_map/ppermute | solution.py:395
  34.0 34.4 %gather_rows.2.own_ref = bf16[8,1280,256]{2,1,0:T(8,128)(2,1)} custom-call(s32[8,1280]{1,0:T(8,128)S(1)} %get-tuple-element.43.slots_ref, s32[8]{0:T(128)S(1)} %get-tuple-element.45.counts_ref.own_n, bf16[16384,256]{1,0:T(8,128)(2,1)} %acq_ref.3), custom_call_target="tpu_custom_call" | custom-call | tf_op jit(solution)/shard_map/gather_rows/pallas_call | solution.py:98
  68.4 0.3 fusion.5
  68.8 0.1 broadcast_in_dim.22
  68.8 0.6 collective-permute-start
  69.5 7.3 %collective-permute-done = s32[16,1408]{1,0:T(8,128)S(1)} collective-permute-done((s32[16,1408]{1,0:T(8,128)S(1)}, s32[16,1408]{1,0:T(8,128)S(1)}, u32[]{:S(2)}, u32[]{:S(2)}) %collective-permute-start) | collective-permute-done | bytes 90144 | tf_op jit(solution)/shard_map/ppermute | solution.py:377
  76.8 0.3 fusion.13
  77.2 0.1 slice_reduce_fusion
  77.3 15.7 %line_blocks.2 = (s16[1040,256]{1,0:T(8,128)(2,1)S(1)}, s16[1040,256]{1,0:T(8,128)(2,1)S(1)}, s16[1040,256]{1,0:T(8,128)(2,1)S(1)}, s16[1040,256]{1,0:T(8,128)(2,1)S(1)}, s16[16,528,256]{2,1,0:T(8,128)(2,1)}) custom-call(s32[8]{0:T(128)S(1)} %get-tuple-element.44.counts_ref.own_n, s32[8]{0:T(128)S(1)} %get-tuple-element.34.peer_n, ...), custom_call_target="tpu_custom_call" | custom-call | tf_op jit(solution)/shard_map/line_blocks/pallas_call | solution.py:180
  93.0 0.8 copy-done.1
  93.9 0.8 copy-done.2
  94.7 17.8 %line_blocks.3 = (s16[1040,256]{1,0:T(8,128)(2,1)S(1)}, s16[1040,256]{1,0:T(8,128)(2,1)S(1)}, s16[1040,256]{1,0:T(8,128)(2,1)S(1)}, s16[1040,256]{1,0:T(8,128)(2,1)S(1)}, s16[16,528,256]{2,1,0:T(8,128)(2,1)}) custom-call(s32[8]{0:T(128)S(1)} %get-tuple-element.45.counts_ref.own_n, s32[8]{0:T(128)S(1)} %get-tuple-element.35.peer_n, ...), custom_call_target="tpu_custom_call", output_to_operand_aliasing={{4}: (6, {})} | custom-call | tf_op jit(solution)/shard_map/line_blocks/pallas_call | solution.py:180
  112.5 13.1 %all-to-all-start.1 = ((s16[16,528,256]{2,1,0:T(8,128)(2,1)}), s16[16,528,256]{2,1,0:T(8,128)(2,1)}, u32[]{:S(2)}, u32[]{:S(2)}) async-start(s16[16,528,256]{2,1,0:T(8,128)(2,1)} %get-tuple-element.27), calls=%async_computation.1 | async-start | bytes 8650752 | tf_op jit(solution)/shard_map/all_to_all | solution.py:409
  125.6 4.7 %collective-permute-start.6 = (s16[1040,256]{1,0:T(8,128)(2,1)}, s16[1040,256]{1,0:T(8,128)(2,1)S(1)}, u32[]{:S(2)}, u32[]{:S(2)}) collective-permute-start(s16[1040,256]{1,0:T(8,128)(2,1)} %copy-done.2), channel_id=1, source_target_pairs={{0,32},{16,48},{32,64},{48,80},{64,96},{80,112},{96,0},{112,16},{1... | collective-permute-start | bytes 1597448 | tf_op jit(solution)/shard_map/ppermute | solution.py:398
  130.3 0.3 collective-permute-start.7
  130.6 2.2 collective-permute-start.8
  132.8 1.9 collective-permute-start.4
  134.7 6.9 %collective-permute-done.6.p1.c1 = s16[1040,256]{1,0:T(8,128)(2,1)S(1)} collective-permute-done((s16[1040,256]{1,0:T(8,128)(2,1)}, s16[1040,256]{1,0:T(8,128)(2,1)S(1)}, u32[]{:S(2)}, u32[]{:S(2)}) %collective-permute-start.6) | collective-permute-done | bytes 532512 | tf_op jit(solution)/shard_map/ppermute | solution.py:398
  141.6 1.0 collective-permute-start.5
  142.7 11.2 %collective-permute-done.7.p2.c2 = s16[1040,256]{1,0:T(8,128)(2,1)S(1)} collective-permute-done((s16[1040,256]{1,0:T(8,128)(2,1)}, s16[1040,256]{1,0:T(8,128)(2,1)S(1)}, u32[]{:S(2)}, u32[]{:S(2)}) %collective-permute-start.7) | collective-permute-done | bytes 532512 | tf_op jit(solution)/shard_map/ppermute | solution.py:398
  153.9 0.2 collective-permute-done.8.p3.c3
  154.1 3.9 %sum_x.2.alias_ref = s16[16,144,256]{2,1,0:T(8,128)(2,1)} custom-call(s16[1040,256]{1,0:T(8,128)(2,1)S(1)} %get-tuple-element.23.p0.c0, s16[1040,256]{1,0:T(8,128)(2,1)S(1)} %collective-permute-done.6.p1.c1, s16[1040,256]{1,0:T(8,128)(2,1)S(1)} %collective-permute-done.7.p2.c2, s16[1040,256]{1,0:T(8,128)(2,1)S(1)} %collective-permute-done.8.p3.c3, ...), custom_call_target="tpu_custom_call" | custom-call | tf_op jit(solution)/shard_map/sum_x/pallas_call | solution.py:222
  157.9 6.5 %collective-permute-done.3.p1.c1 = s16[1040,256]{1,0:T(8,128)(2,1)S(1)} collective-permute-done((s16[1040,256]{1,0:T(8,128)(2,1)S(1)}, s16[1040,256]{1,0:T(8,128)(2,1)S(1)}, u32[]{:S(2)}, u32[]{:S(2)}) %collective-permute-start.3) | collective-permute-done | bytes 532512 | tf_op jit(solution)/shard_map/ppermute | solution.py:398
  164.4 12.2 %collective-permute-done.4.p2.c2 = s16[1040,256]{1,0:T(8,128)(2,1)S(1)} collective-permute-done((s16[1040,256]{1,0:T(8,128)(2,1)S(1)}, s16[1040,256]{1,0:T(8,128)(2,1)S(1)}, u32[]{:S(2)}, u32[]{:S(2)}) %collective-permute-start.4) | collective-permute-done | bytes 532512 | tf_op jit(solution)/shard_map/ppermute | solution.py:398
  176.6 0.4 collective-permute-done.5.p3.c3
  176.9 3.9 %sum_x.3 = s16[16,144,256]{2,1,0:T(8,128)(2,1)} custom-call(s16[1040,256]{1,0:T(8,128)(2,1)S(1)} %get-tuple-element.19.p0.c0, s16[1040,256]{1,0:T(8,128)(2,1)S(1)} %collective-permute-done.3.p1.c1, s16[1040,256]{1,0:T(8,128)(2,1)S(1)} %collective-permute-done.4.p2.c2, ...), custom_call_target="tpu_custom_call", output_to_operand_aliasing={{}: (8, {})} | custom-call | tf_op jit(solution)/shard_map/sum_x/pallas_call | solution.py:222
  180.8 9.3 %all-to-all-done.1.in_ref = s16[16,528,256]{2,1,0:T(8,128)(2,1)} async-done(((s16[16,528,256]{2,1,0:T(8,128)(2,1)}), s16[16,528,256]{2,1,0:T(8,128)(2,1)}, u32[]{:S(2)}, u32[]{:S(2)}) %all-to-all-start.1) | async-done | bytes 4325408 | tf_op jit(solution)/shard_map/all_to_all | solution.py:409
  190.1 4.8 %all-to-all-start = ((s16[16,144,256]{2,1,0:T(8,128)(2,1)}), s16[16,144,256]{2,1,0:T(8,128)(2,1)S(1)}, u32[]{:S(2)}, u32[]{:S(2)}) async-start(s16[16,144,256]{2,1,0:T(8,128)(2,1)} %sum_x.3), calls=%async_computation | async-start | bytes 2359296 | tf_op jit(solution)/shard_map/all_to_all | solution.py:413
  195.0 9.5 %sum_tile.1 = (s16[144,256]{1,0:T(8,128)(2,1)S(1)}, s16[144,256]{1,0:T(8,128)(2,1)S(1)}, s16[144,256]{1,0:T(8,128)(2,1)S(1)}, s16[144,256]{1,0:T(8,128)(2,1)S(1)}) custom-call(s16[16,528,256]{2,1,0:T(8,128)(2,1)} %all-to-all-done.1.in_ref), custom_call_target="tpu_custom_call" | custom-call | tf_op jit(solution)/shard_map/sum_tile/pallas_call | solution.py:257
  204.5 4.6 %collective-permute-start.10 = (s16[144,256]{1,0:T(8,128)(2,1)S(1)}, s16[144,256]{1,0:T(8,128)(2,1)S(1)}, u32[]{:S(2)}, u32[]{:S(2)}) collective-permute-start(s16[144,256]{1,0:T(8,128)(2,1)S(1)} %get-tuple-element.30), channel_id=1, source_target_pairs={{0,64},{16,80},{32,96},{48,112},{64,0},{80,16},{96,32},{112,48},{1... | collective-permute-start | bytes 221192 | tf_op jit(solution)/shard_map/ppermute | solution.py:398
  209.1 2.9 %collective-permute-start.11 = (s16[144,256]{1,0:T(8,128)(2,1)S(1)}, s16[144,256]{1,0:T(8,128)(2,1)S(1)}, u32[]{:S(2)}, u32[]{:S(2)}) collective-permute-start(s16[144,256]{1,0:T(8,128)(2,1)S(1)} %get-tuple-element.31), channel_id=1, source_target_pairs={{0,96},{16,112},{32,0},{48,16},{64,32},{80,48},{96,64},{112,80},{1... | collective-permute-start | bytes 221192 | tf_op jit(solution)/shard_map/ppermute | solution.py:398
  212.0 1.4 collective-permute-done.11.b3
  213.4 3.0 %collective-permute-done.9.b1 = s16[144,256]{1,0:T(8,128)(2,1)S(1)} collective-permute-done((s16[144,256]{1,0:T(8,128)(2,1)S(1)}, s16[144,256]{1,0:T(8,128)(2,1)S(1)}, u32[]{:S(2)}, u32[]{:S(2)}) %collective-permute-start.9) | collective-permute-done | bytes 73760 | tf_op jit(solution)/shard_map/ppermute | solution.py:398
  216.4 2.6 own_plane.1
  219.0 3.3 %collective-permute-start.12 = (s16[272,256]{1,0:T(8,128)(2,1)S(1)}, s16[272,256]{1,0:T(8,128)(2,1)S(1)}, u32[]{:S(2)}, u32[]{:S(2)}) collective-permute-start(s16[272,256]{1,0:T(8,128)(2,1)S(1)} %get-tuple-element.33), channel_id=1, source_target_pairs={{0,1},{1,2},{2,3},{3,4},{4,5},{5,6},{6,7},{7,8},{8,9},{9,10},{10,1... | collective-permute-start | bytes 417800 | tf_op jit(solution)/shard_map/ppermute | solution.py:422
  222.2 4.3 %collective-permute-start.13 = (s16[272,256]{1,0:T(8,128)(2,1)S(1)}, s16[272,256]{1,0:T(8,128)(2,1)S(1)}, u32[]{:S(2)}, u32[]{:S(2)}) collective-permute-start(s16[272,256]{1,0:T(8,128)(2,1)S(1)} %get-tuple-element.33), channel_id=1, source_target_pairs={{0,2},{1,3},{2,4},{3,5},{4,6},{5,7},{6,8},{7,9},{8,10},{9,11},{10,... | collective-permute-start | bytes 417800 | tf_op jit(solution)/shard_map/ppermute | solution.py:422
  226.6 6.3 %collective-permute-start.14 = (s16[272,256]{1,0:T(8,128)(2,1)S(1)}, s16[272,256]{1,0:T(8,128)(2,1)S(1)}, u32[]{:S(2)}, u32[]{:S(2)}) collective-permute-start(s16[272,256]{1,0:T(8,128)(2,1)S(1)} %get-tuple-element.33), channel_id=1, source_target_pairs={{1,0},{2,1},{3,2},{4,3},{5,4},{6,5},{7,6},{8,7},{9,8},{10,9},{11,1... | collective-permute-start | bytes 417800 | tf_op jit(solution)/shard_map/ppermute | solution.py:422
  232.9 4.8 %collective-permute-start.15 = (s16[272,256]{1,0:T(8,128)(2,1)S(1)}, s16[272,256]{1,0:T(8,128)(2,1)S(1)}, u32[]{:S(2)}, u32[]{:S(2)}) collective-permute-start(s16[272,256]{1,0:T(8,128)(2,1)S(1)} %get-tuple-element.33), channel_id=1, source_target_pairs={{2,0},{3,1},{4,2},{5,3},{6,4},{7,5},{8,6},{9,7},{10,8},{11,9},{12,... | collective-permute-start | bytes 417800 | tf_op jit(solution)/shard_map/ppermute | solution.py:422
  237.7 0.1 bitcast_select_fusion.1
  237.8 0.1 add_convert_fusion.edge_ref
  237.9 3.4 %collective-permute-done.15.r2 = s16[272,256]{1,0:T(8,128)(2,1)S(1)} collective-permute-done((s16[272,256]{1,0:T(8,128)(2,1)S(1)}, s16[272,256]{1,0:T(8,128)(2,1)S(1)}, u32[]{:S(2)}, u32[]{:S(2)}) %collective-permute-start.15) | collective-permute-done | bytes 139296 | tf_op jit(solution)/shard_map/ppermute | solution.py:422
  241.2 2.2 smooth.1
  243.5 1.6 convolution_convert_fusion
  245.1 21.8 %all_to_all.15 = bf16[16,128,256]{2,1,0:T(8,128)(2,1)S(1)} all-to-all(bf16[16,128,256]{2,1,0:T(8,128)(2,1)S(1)} %bitcast.28), channel_id=1, replica_groups=mesh['cuts'=8,'tile'=16] {'tile'}, dimensions={0} | all-to-all | bytes 2097152 | tf_op jit(solution)/shard_map/all_to_all | solution.py:437
  266.9 1.0 copy.18
  (30 shorter events, 0.2 us)
Async XLA Ops:
  30.0 47.3 %collective-permute-start.2 = (bf16[8,1280,256]{2,1,0:T(8,128)(2,1)}, bf16[8,1280,256]{2,1,0:T(8,128)(2,1)}, u32[]{:S(2)}, u32[]{:S(2)}) collective-permute-start(bf16[8,1280,256]{2,1,0:T(8,128)(2,1)} %gather_rows.3.own_ref), channel_id=1, source_target_pairs={{0,16},{16,0},{32,48},{48,32},{64,80},{80,64},{96,112},{112,96},{1... | collective-permute-start | bytes 15728648 | tf_op jit(solution)/shard_map/ppermute | solution.py:395
  34.0 34.4 %copy-start.3 = (s32[1,16,1280]{2,1,0:T(8,128)S(1)}, s32[1,16,1280]{2,1,0:T(8,128)}, u32[]{:S(2)}) copy-start(s32[1,16,1280]{2,1,0:T(8,128)} %param.10) | copy-start | bytes 245764
  34.0 34.4 %copy-start.4 = (s32[1,16]{1,0:T(1,128)S(1)}, s32[1,16]{1,0:T(1,128)}, u32[]{:S(2)}) copy-start(s32[1,16]{1,0:T(1,128)} %param.11) | copy-start | bytes 196
  68.4 26.2 %collective-permute-start.1 = (bf16[8,1280,256]{2,1,0:T(8,128)(2,1)}, bf16[8,1280,256]{2,1,0:T(8,128)(2,1)}, u32[]{:S(2)}, u32[]{:S(2)}) collective-permute-start(bf16[8,1280,256]{2,1,0:T(8,128)(2,1)} %gather_rows.2.own_ref), channel_id=1, source_target_pairs={{0,16},{16,0},{32,48},{48,32},{64,80},{80,64},{96,112},{112,96},{1... | collective-permute-start | bytes 15728648 | tf_op jit(solution)/shard_map/ppermute | solution.py:395
  68.8 8.0 %collective-permute-start = (s32[16,1408]{1,0:T(8,128)S(1)}, s32[16,1408]{1,0:T(8,128)S(1)}, u32[]{:S(2)}, u32[]{:S(2)}) collective-permute-start(s32[16,1408]{1,0:T(8,128)S(1)} %pad_add_fusion), channel_id=1, source_target_pairs={{0,16},{16,0},{32,48},{48,32},{64,80},{80,64},{96,112},{112,96},{1... | collective-permute-start | bytes 270344 | tf_op jit(solution)/shard_map/ppermute | solution.py:377
  93.0 0.8 copy-start.1
  93.9 0.8 copy-start.2
  112.5 77.7 %all-to-all-start.1 = ((s16[16,528,256]{2,1,0:T(8,128)(2,1)}), s16[16,528,256]{2,1,0:T(8,128)(2,1)}, u32[]{:S(2)}, u32[]{:S(2)}) async-start(s16[16,528,256]{2,1,0:T(8,128)(2,1)} %get-tuple-element.27), calls=%async_computation.1 | async-start | bytes 8650752 | tf_op jit(solution)/shard_map/all_to_all | solution.py:409
  125.6 16.1 %collective-permute-start.6 = (s16[1040,256]{1,0:T(8,128)(2,1)}, s16[1040,256]{1,0:T(8,128)(2,1)S(1)}, u32[]{:S(2)}, u32[]{:S(2)}) collective-permute-start(s16[1040,256]{1,0:T(8,128)(2,1)} %copy-done.2), channel_id=1, source_target_pairs={{0,32},{16,48},{32,64},{48,80},{64,96},{80,112},{96,0},{112,16},{1... | collective-permute-start | bytes 1597448 | tf_op jit(solution)/shard_map/ppermute | solution.py:398
  130.3 23.6 %collective-permute-start.7 = (s16[1040,256]{1,0:T(8,128)(2,1)}, s16[1040,256]{1,0:T(8,128)(2,1)S(1)}, u32[]{:S(2)}, u32[]{:S(2)}) collective-permute-start(s16[1040,256]{1,0:T(8,128)(2,1)} %copy-done.1), channel_id=1, source_target_pairs={{0,64},{16,80},{32,96},{48,112},{64,0},{80,16},{96,32},{112,48},{1... | collective-permute-start | bytes 1597448 | tf_op jit(solution)/shard_map/ppermute | solution.py:398
  130.6 23.5 %collective-permute-start.8 = (s16[1040,256]{1,0:T(8,128)(2,1)S(1)}, s16[1040,256]{1,0:T(8,128)(2,1)S(1)}, u32[]{:S(2)}, u32[]{:S(2)}) collective-permute-start(s16[1040,256]{1,0:T(8,128)(2,1)S(1)} %get-tuple-element.26), channel_id=1, source_target_pairs={{0,96},{16,112},{32,0},{48,16},{64,32},{80,48},{96,64},{112,80},{1... | collective-permute-start | bytes 1597448 | tf_op jit(solution)/shard_map/ppermute | solution.py:398
  132.8 31.6 %collective-permute-start.3 = (s16[1040,256]{1,0:T(8,128)(2,1)S(1)}, s16[1040,256]{1,0:T(8,128)(2,1)S(1)}, u32[]{:S(2)}, u32[]{:S(2)}) collective-permute-start(s16[1040,256]{1,0:T(8,128)(2,1)S(1)} %get-tuple-element.20), channel_id=1, source_target_pairs={{0,32},{16,48},{32,64},{48,80},{64,96},{80,112},{96,0},{112,16},{1... | collective-permute-start | bytes 1597448 | tf_op jit(solution)/shard_map/ppermute | solution.py:398
  132.8 43.8 %collective-permute-start.4 = (s16[1040,256]{1,0:T(8,128)(2,1)S(1)}, s16[1040,256]{1,0:T(8,128)(2,1)S(1)}, u32[]{:S(2)}, u32[]{:S(2)}) collective-permute-start(s16[1040,256]{1,0:T(8,128)(2,1)S(1)} %get-tuple-element.21), channel_id=1, source_target_pairs={{0,64},{16,80},{32,96},{48,112},{64,0},{80,16},{96,32},{112,48},{1... | collective-permute-start | bytes 1597448 | tf_op jit(solution)/shard_map/ppermute | solution.py:398
  141.6 35.3 %collective-permute-start.5 = (s16[1040,256]{1,0:T(8,128)(2,1)S(1)}, s16[1040,256]{1,0:T(8,128)(2,1)S(1)}, u32[]{:S(2)}, u32[]{:S(2)}) collective-permute-start(s16[1040,256]{1,0:T(8,128)(2,1)S(1)} %get-tuple-element.22), channel_id=1, source_target_pairs={{0,96},{16,112},{32,0},{48,16},{64,32},{80,48},{96,64},{112,80},{1... | collective-permute-start | bytes 1597448 | tf_op jit(solution)/shard_map/ppermute | solution.py:398
  180.8 35.6 %copy-start = (bf16[256,1024]{1,0:T(8,128)(2,1)S(1)}, bf16[256,1024]{1,0:T(8,128)(2,1)}, u32[]{:S(2)}) copy-start(bf16[256,1024]{1,0:T(8,128)(2,1)} %stencil_ref.1) | copy-start | bytes 1572868
  180.8 56.9 %copy-start.5 = (s32[1,16,128]{2,1,0:T(8,128)S(1)}, s32[1,16,128]{2,1,0:T(8,128)}, u32[]{:S(2)}) copy-start(s32[1,16,128]{2,1,0:T(8,128)} %param.12) | copy-start | bytes 24580
  180.8 56.9 %copy-start.6 = (s32[1,16]{1,0:T(1,128)S(1)}, s32[1,16]{1,0:T(1,128)}, u32[]{:S(2)}) copy-start(s32[1,16]{1,0:T(1,128)} %param.13) | copy-start | bytes 196
  190.1 21.9 %all-to-all-start = ((s16[16,144,256]{2,1,0:T(8,128)(2,1)}), s16[16,144,256]{2,1,0:T(8,128)(2,1)S(1)}, u32[]{:S(2)}, u32[]{:S(2)}) async-start(s16[16,144,256]{2,1,0:T(8,128)(2,1)} %sum_x.3), calls=%async_computation | async-start | bytes 2359296 | tf_op jit(solution)/shard_map/all_to_all | solution.py:413
  204.5 7.5 %collective-permute-start.10 = (s16[144,256]{1,0:T(8,128)(2,1)S(1)}, s16[144,256]{1,0:T(8,128)(2,1)S(1)}, u32[]{:S(2)}, u32[]{:S(2)}) collective-permute-start(s16[144,256]{1,0:T(8,128)(2,1)S(1)} %get-tuple-element.30), channel_id=1, source_target_pairs={{0,64},{16,80},{32,96},{48,112},{64,0},{80,16},{96,32},{112,48},{1... | collective-permute-start | bytes 221192 | tf_op jit(solution)/shard_map/ppermute | solution.py:398
  209.1 4.3 %collective-permute-start.11 = (s16[144,256]{1,0:T(8,128)(2,1)S(1)}, s16[144,256]{1,0:T(8,128)(2,1)S(1)}, u32[]{:S(2)}, u32[]{:S(2)}) collective-permute-start(s16[144,256]{1,0:T(8,128)(2,1)S(1)} %get-tuple-element.31), channel_id=1, source_target_pairs={{0,96},{16,112},{32,0},{48,16},{64,32},{80,48},{96,64},{112,80},{1... | collective-permute-start | bytes 221192 | tf_op jit(solution)/shard_map/ppermute | solution.py:398
  212.0 4.4 %collective-permute-start.9 = (s16[144,256]{1,0:T(8,128)(2,1)S(1)}, s16[144,256]{1,0:T(8,128)(2,1)S(1)}, u32[]{:S(2)}, u32[]{:S(2)}) collective-permute-start(s16[144,256]{1,0:T(8,128)(2,1)S(1)} %get-tuple-element.29), channel_id=1, source_target_pairs={{0,32},{16,48},{32,64},{48,80},{64,96},{80,112},{96,0},{112,16},{1... | collective-permute-start | bytes 221192 | tf_op jit(solution)/shard_map/ppermute | solution.py:398
  219.0 18.9 %collective-permute-start.12 = (s16[272,256]{1,0:T(8,128)(2,1)S(1)}, s16[272,256]{1,0:T(8,128)(2,1)S(1)}, u32[]{:S(2)}, u32[]{:S(2)}) collective-permute-start(s16[272,256]{1,0:T(8,128)(2,1)S(1)} %get-tuple-element.33), channel_id=1, source_target_pairs={{0,1},{1,2},{2,3},{3,4},{4,5},{5,6},{6,7},{7,8},{8,9},{9,10},{10,1... | collective-permute-start | bytes 417800 | tf_op jit(solution)/shard_map/ppermute | solution.py:422
  222.2 15.6 %collective-permute-start.13 = (s16[272,256]{1,0:T(8,128)(2,1)S(1)}, s16[272,256]{1,0:T(8,128)(2,1)S(1)}, u32[]{:S(2)}, u32[]{:S(2)}) collective-permute-start(s16[272,256]{1,0:T(8,128)(2,1)S(1)} %get-tuple-element.33), channel_id=1, source_target_pairs={{0,2},{1,3},{2,4},{3,5},{4,6},{5,7},{6,8},{7,9},{8,10},{9,11},{10,... | collective-permute-start | bytes 417800 | tf_op jit(solution)/shard_map/ppermute | solution.py:422
  226.6 11.3 %collective-permute-start.14 = (s16[272,256]{1,0:T(8,128)(2,1)S(1)}, s16[272,256]{1,0:T(8,128)(2,1)S(1)}, u32[]{:S(2)}, u32[]{:S(2)}) collective-permute-start(s16[272,256]{1,0:T(8,128)(2,1)S(1)} %get-tuple-element.33), channel_id=1, source_target_pairs={{1,0},{2,1},{3,2},{4,3},{5,4},{6,5},{7,6},{8,7},{9,8},{10,9},{11,1... | collective-permute-start | bytes 417800 | tf_op jit(solution)/shard_map/ppermute | solution.py:422
  232.9 8.4 %collective-permute-start.15 = (s16[272,256]{1,0:T(8,128)(2,1)S(1)}, s16[272,256]{1,0:T(8,128)(2,1)S(1)}, u32[]{:S(2)}, u32[]{:S(2)}) collective-permute-start(s16[272,256]{1,0:T(8,128)(2,1)S(1)} %get-tuple-element.33), channel_id=1, source_target_pairs={{2,0},{3,1},{4,2},{5,3},{6,4},{7,5},{8,6},{9,7},{10,8},{11,9},{12,... | collective-permute-start | bytes 417800 | tf_op jit(solution)/shard_map/ppermute | solution.py:422

commit v2 on v1

v2 whole, which is shorter than its diff:
```python
import functools
import math

import jax
import jax.numpy as jnp
from jax import lax
from jax.experimental import pallas as pl
from jax.experimental.pallas import tpu as pltpu
from jax.sharding import PartitionSpec as P

NX = 256
NY = 256
TAPS = 4
LA = 160
LB = NY - LA
ALPHA = math.log(2.0) / 64.0
TOP = 32700.0
CHUNK = 256
PICK = 32


def params(mib):
    return pltpu.CompilerParams(
        vmem_limit_bytes=mib * 1024 * 1024, dimension_semantics=("arbitrary",)
    )


def hbm(shape, dtype):
    return pltpu.HBM(shape, dtype)


def encode(block):
    top = to_row(jnp.max(jnp.abs(block), axis=1, keepdims=True))
    code = jnp.ceil(jnp.log(jnp.maximum(top, 1e-33)) * (1.0 / ALPHA))
    factor = to_column(TOP / jnp.exp(code * ALPHA))
    values = (block * factor + 12582912.0) - 12582912.0
    return values.astype(jnp.int32).astype(jnp.int16), code


def eye(size):
    return lax.broadcasted_iota(jnp.int32, (size, size), 0) == lax.broadcasted_iota(
        jnp.int32, (size, size), 1
    )


def to_row(column):
    return jnp.sum(jnp.where(eye(column.shape[0]), column, 0.0), axis=0, keepdims=True)


def to_column(row):
    return jnp.sum(jnp.where(eye(row.shape[1]), row, 0.0), axis=1, keepdims=True)


def decode(values, code_row):
    scale = jnp.exp(code_row * ALPHA) * (1.0 / TOP)
    return values.astype(jnp.int32).astype(jnp.float32) * to_column(scale)


def code_block(rows):
    block = jnp.zeros((16, NX), jnp.float32)
    index = lax.broadcasted_iota(jnp.int32, (16, NX), 0)
    for i, row in enumerate(rows):
        block = jnp.where(index == i, row, block)
    return block.astype(jnp.int32).astype(jnp.int16)


def gather_kernel(slots_ref, counts_ref, acq_ref, out_ref, wide_ref, half_ref, sem, *, first, cap):
    step = pl.program_id(0)
    pieces = sem.shape[0]
    piece = half_ref.shape[0] // pieces

    @pl.when(step == 0)
    def _():
        copies = []
        for k in range(pieces):
            span = pl.ds(k * piece, piece)
            copies.append(
                pltpu.make_async_copy(acq_ref.at[span, :], half_ref.at[span, :], sem.at[k])
            )
            copies[k].start()
        for k in range(pieces):
            copies[k].wait()

            def widen(i, carry):
                span = pl.ds(pl.multiple_of(k * piece + i * CHUNK, CHUNK), CHUNK)
                wide_ref[span, :] = half_ref[span, :].astype(jnp.float32)
                return carry

            lax.fori_loop(0, piece // CHUNK, widen, 0)

    count = counts_ref[first + step]
    start = (first + step) * cap

    def pick(i, carry):
        base = pl.multiple_of(i * PICK, PICK)
        rows = [wide_ref[pl.ds(slots_ref[start + base + u], 1), :] for u in range(PICK)]
        out_ref[0, pl.ds(base, PICK), :] = jnp.concatenate(rows, axis=0).astype(jnp.bfloat16)
        return carry

    def clear(i, carry):
        base = pl.multiple_of(i * PICK, PICK)
        out_ref[0, pl.ds(base, PICK), :] = jnp.zeros((PICK, NX), jnp.bfloat16)
        return carry

    picks = (count + PICK - 1) // PICK
    lax.fori_loop(0, picks, pick, 0)
    lax.fori_loop(picks, (count + CHUNK - 1) // CHUNK * (CHUNK // PICK), clear, 0)


def gather_rows(acquired, slots, counts, first, tiles, cap):
    body = functools.partial(gather_kernel, first=first, cap=cap)
    return pl.pallas_call(
        body,
        grid_spec=pltpu.PrefetchScalarGridSpec(
            num_scalar_prefetch=2,
            grid=(tiles,),
            in_specs=[pl.BlockSpec(memory_space=pl.ANY)],
            out_specs=pl.BlockSpec((1, cap, NX), lambda t, s, c: (t, 0, 0)),
            scratch_shapes=[
                pltpu.VMEM(acquired.shape, jnp.float32),
                pltpu.VMEM(acquired.shape, jnp.bfloat16),
                pltpu.SemaphoreType.DMA((8,)),
            ],
        ),
        out_shape=jax.ShapeDtypeStruct((tiles, cap, NX), jnp.bfloat16),
        compiler_params=params(48),
        cost_estimate=pl.CostEstimate(flops=0, transcendentals=0, bytes_accessed=40_000_000),
        name="gather_rows",
    )(slots, counts, acquired)


def lines_kernel(
    own_n, peer_n, own_ref, peer_ref, own_lines, peer_lines, alias_ref,
    a0_ref, a1_ref, a2_ref, a3_ref, b_ref, acc_ref, code_ref, *, first,
):
    step = pl.program_id(0)
    last = pl.num_programs(0) - 1
    acc_ref[...] = jnp.zeros(acc_ref.shape, jnp.float32)
    position = lax.broadcasted_iota(jnp.int32, (CHUNK, CHUNK), 0)

    def add(rows_ref, lines_ref):
        def body(i, carry):
            base = pl.multiple_of(i * CHUNK, CHUNK)
            rows = rows_ref[0, pl.ds(base, CHUNK), :]
            ids = lines_ref[0, pl.ds(i, 1), :]
            for m in range(acc_ref.shape[0] // CHUNK):
                hot = jnp.where(position + m * CHUNK == ids, 1.0, 0.0).astype(jnp.bfloat16)
                span = pl.ds(m * CHUNK, CHUNK)
                acc_ref[span, :] += jnp.dot(hot, rows, preferred_element_type=jnp.float32)
            return carry

        return body

    own_steps = (own_n[first + step] + CHUNK - 1) // CHUNK
    peer_steps = (peer_n[first + step] + CHUNK - 1) // CHUNK
    lax.fori_loop(0, own_steps, add(own_ref, own_lines), 0)
    lax.fori_loop(0, peer_steps, add(peer_ref, peer_lines), 0)

    outs = (a0_ref, a1_ref, a2_ref, a3_ref)
    for k in range(4):
        values, code = encode(acc_ref[pl.ds(k * LA, LA), :])
        outs[k][pl.ds(pl.multiple_of(step * LA, LA), LA), :] = values
        code_ref[k, pl.ds(step, 1), :] = pad_row(code)

    codes = []
    for k in range(4):
        values, code = encode(acc_ref[pl.ds(4 * LA + k * LB, LB), :])
        b_ref[0, pl.ds(k * LB, LB), :] = values
        codes.append(pad_row(code))
    b_ref[0, pl.ds(4 * LB, 16), :] = code_block(codes)

    @pl.when(step == last)
    def _():
        for k in range(4):
            table = code_ref[k]
            both = jnp.concatenate([table, jnp.zeros_like(table)], axis=0)
            outs[k][pl.ds((last + 1) * LA, 16), :] = both.astype(jnp.int32).astype(jnp.int16)


def pad_row(row):
    return jnp.concatenate([row, jnp.zeros((1, NX - row.shape[1]), jnp.float32)], axis=1)


def line_blocks(own_rows, peer_rows, own_lines, peer_lines, own_n, peer_n, b_old, first, tiles_all):
    tiles, cap, _ = own_rows.shape
    span = cap // CHUNK
    row_spec = pl.BlockSpec((1, cap, NX), lambda t, *_: (t, 0, 0))
    line_spec = pl.BlockSpec((1, span, CHUNK), lambda t, *_: (t + first, 0, 0))
    a_shape = (tiles * LA + 16, NX)
    args = [own_n, peer_n, own_rows, peer_rows, own_lines, peer_lines]
    aliases = {}
    if b_old is None:
        b_old = jnp.zeros((16, NX), jnp.int16)
    else:
        aliases = {6: 4}
    args.append(b_old)
    return pl.pallas_call(
        functools.partial(lines_kernel, first=first),
        grid_spec=pltpu.PrefetchScalarGridSpec(
            num_scalar_prefetch=2,
            grid=(tiles,),
            in_specs=[row_spec, row_spec, line_spec, line_spec, pl.BlockSpec(memory_space=pl.ANY)],
            out_specs=[pl.BlockSpec(a_shape, lambda t, *_: (0, 0))] * 4
            + [pl.BlockSpec((1, 4 * LB + 16, NX), lambda t, *_: (t + first, 0, 0))],
            scratch_shapes=[
                pltpu.VMEM((4 * NY, NX), jnp.float32),
                pltpu.VMEM((4, tiles, NX), jnp.float32),
            ],
        ),
        out_shape=[hbm(a_shape, jnp.int16)] * 4
        + [hbm((tiles_all, 4 * LB + 16, NX), jnp.int16)],
        input_output_aliases=aliases,
        compiler_params=params(48),
        cost_estimate=pl.CostEstimate(
            flops=2 * 1024 * 256 * 20480, transcendentals=0, bytes_accessed=40_000_000
        ),
        name="line_blocks",
    )(*args)


def code_row(block, index, length):
    table = block.astype(jnp.int32).astype(jnp.float32)
    rows = lax.broadcasted_iota(jnp.int32, table.shape, 0)
    row = jnp.sum(jnp.where(rows == index, table, 0.0), axis=0, keepdims=True)
    return row[:, 0:length]


def sum_x_kernel(p0, p1, p2, p3, c0, c1, c2, c3, alias_ref, out_ref):
    step = pl.program_id(0)
    total = jnp.zeros((LA, NX), jnp.float32)
    for values, codes in ((p0, c0), (p1, c1), (p2, c2), (p3, c3)):
        total = total + decode(values[...], code_row(codes[...], step, LA))
    values, code = encode(total)
    out_ref[0, pl.ds(0, LA), :] = values
    out_ref[0, pl.ds(LA, 16), :] = code_block([pad_row(code)])


def sum_x(parts, old, first, tiles_all):
    tiles = (parts[0].shape[0] - 16) // LA
    aliases = {}
    if old is None:
        old = jnp.zeros((16, NX), jnp.int16)
    else:
        aliases = {8: 0}
    return pl.pallas_call(
        sum_x_kernel,
        grid=(tiles,),
        in_specs=[pl.BlockSpec((LA, NX), lambda t: (t, 0))] * 4
        + [pl.BlockSpec((16, NX), lambda t: (tiles * LA // 16, 0))] * 4
        + [pl.BlockSpec(memory_space=pl.ANY)],
        out_specs=pl.BlockSpec((1, LA + 16, NX), lambda t: (t + first, 0, 0)),
        out_shape=hbm((tiles_all, LA + 16, NX), jnp.int16),
        input_output_aliases=aliases,
        compiler_params=params(32),
        name="sum_x",
    )(*parts, *parts, old)


def sum_tile_kernel(in_ref, o0, o1, o2, o3, acc_ref):
    step = pl.program_id(0)

    @pl.when(step == 0)
    def _():
        acc_ref[...] = jnp.zeros(acc_ref.shape, jnp.float32)

    table = in_ref[0, pl.ds(4 * LB, 16), :].astype(jnp.int32).astype(jnp.float32)
    for k in range(4):
        acc_ref[pl.ds(k * LB, LB), :] += decode(
            in_ref[0, pl.ds(k * LB, LB), :], table[k : k + 1, 0:LB]
        )

    @pl.when(step == pl.num_programs(0) - 1)
    def _():
        for k, out in enumerate((o0, o1, o2, o3)):
            values, code = encode(acc_ref[pl.ds(k * LB, LB), :])
            out[pl.ds(0, LB), :] = values
            out[pl.ds(LB, 16), :] = code_block([pad_row(code)])


def sum_tile(arrived):
    tiles, rows, _ = arrived.shape
    out_shape = (LB + 16, NX)
    return pl.pallas_call(
        sum_tile_kernel,
        grid=(tiles,),
        in_specs=[pl.BlockSpec((1, rows, NX), lambda t: (t, 0, 0))],
        out_specs=[pl.BlockSpec(out_shape, lambda t: (0, 0))] * 4,
        out_shape=[jax.ShapeDtypeStruct(out_shape, jnp.int16)] * 4,
        scratch_shapes=[pltpu.VMEM((4 * LB, NX), jnp.float32)],
        compiler_params=params(32),
        name="sum_tile",
    )(arrived)


def plane_kernel(a_ref, b0, b1, b2, b3, stencil_ref, plane_ref, send_ref, lines_ref):
    def body(i, carry):
        codes = code_row(a_ref[i, pl.ds(LA, 16), :], 0, LA)
        lines_ref[pl.ds(0, LA), :] += decode(a_ref[i, pl.ds(0, LA), :], codes)
        return carry

    lines_ref[pl.ds(0, LA), :] = jnp.zeros((LA, NX), jnp.float32)
    lax.fori_loop(0, a_ref.shape[0], body, 0)
    total = jnp.zeros((LB, NX), jnp.float32)
    for b in (b0, b1, b2, b3):
        total = total + decode(b[pl.ds(0, LB), :], code_row(b[pl.ds(LB, 16), :], 0, LB))
    lines_ref[pl.ds(LA, LB), :] = total

    lines = lines_ref[...]
    high = lines.astype(jnp.bfloat16)
    rest = lines - high.astype(jnp.float32)
    mid = rest.astype(jnp.bfloat16)
    low = (rest - mid.astype(jnp.float32)).astype(jnp.bfloat16)
    plane = jnp.zeros((NY, NX), jnp.float32)
    for k in range(TAPS):
        weights = stencil_ref[:, k * NX : (k + 1) * NX]
        product = jnp.dot(high, weights, preferred_element_type=jnp.float32)
        product += jnp.dot(mid, weights, preferred_element_type=jnp.float32)
        product += jnp.dot(low, weights, preferred_element_type=jnp.float32)
        if k:
            product = pltpu.roll(product, k, 0)
        plane = plane + product
    plane_ref[...] = plane
    rows = []
    for h in range(2):
        values, code = encode(plane[h * 128 : (h + 1) * 128])
        send_ref[pl.ds(h * 128, 128), :] = values
        rows.append(code)
    send_ref[pl.ds(NY, 16), :] = code_block([jnp.concatenate(rows, axis=1)])


def own_plane(a, bs, stencil):
    return pl.pallas_call(
        plane_kernel,
        out_shape=[
            jax.ShapeDtypeStruct((NY, NX), jnp.float32),
            jax.ShapeDtypeStruct((NY + 16, NX), jnp.int16),
        ],
        scratch_shapes=[pltpu.VMEM((NY, NX), jnp.float32)],
        compiler_params=pltpu.CompilerParams(vmem_limit_bytes=32 * 1024 * 1024),
        name="own_plane",
    )(a, *bs, stencil)


def smooth_kernel(edge_ref, plane_ref, l1, l2, r1, r2, out_ref):
    def halo(ref):
        table = ref[pl.ds(NY, 16), :].astype(jnp.int32).astype(jnp.float32)
        parts = [
            decode(ref[pl.ds(h * 128, 128), :], table[0:1, h * 128 : (h + 1) * 128])
            for h in range(2)
        ]
        return jnp.concatenate(parts, axis=0)

    row = lax.broadcasted_iota(jnp.int32, (NY, NX), 0)
    col = lax.broadcasted_iota(jnp.int32, (NY, NX), 1)

    def step(below, mid, above):
        near = jnp.where(row == 0, 0.0, pltpu.roll(mid, 1, 0))
        near += jnp.where(row == NY - 1, 0.0, pltpu.roll(mid, NY - 1, 0))
        near += jnp.where(col == 0, 0.0, pltpu.roll(mid, 1, 1))
        near += jnp.where(col == NX - 1, 0.0, pltpu.roll(mid, NX - 1, 1))
        return mid + 0.15 * (near + below + above - 6.0 * mid)

    plane = plane_ref[...]
    left, right = halo(l1), halo(r1)
    lower = step(halo(l2), left, plane)
    upper = step(plane, right, halo(r2))
    lower = jnp.where(edge_ref[0] > 0, lower, 0.0)
    upper = jnp.where(edge_ref[1] > 0, upper, 0.0)
    out_ref[...] = step(lower, step(left, plane, right), upper).astype(jnp.bfloat16)


def smooth(edges, plane, halos):
    vmem = pl.BlockSpec(memory_space=pltpu.VMEM)
    return pl.pallas_call(
        smooth_kernel,
        in_specs=[pl.BlockSpec(memory_space=pltpu.SMEM)] + [vmem] * 5,
        out_specs=vmem,
        out_shape=jax.ShapeDtypeStruct((NY, NX), jnp.bfloat16),
        compiler_params=pltpu.CompilerParams(vmem_limit_bytes=32 * 1024 * 1024),
        name="smooth",
    )(edges, plane, *halos)


def after_kernel(x_ref, *refs):
    del x_ref, refs


def after(x, others):
    anywhere = pl.BlockSpec(memory_space=pl.ANY)
    return pl.pallas_call(
        after_kernel,
        in_specs=[anywhere] * (1 + len(others)),
        out_specs=anywhere,
        out_shape=hbm(x.shape, x.dtype),
        input_output_aliases={0: 0},
        name="after",
    )(x, *others)


def local(acquired, stencil, send_slots, send_lines, send_counts, return_slots, return_counts):
    tile_count = lax.axis_size("tile")
    cut_count = lax.axis_size("cuts")
    tile_half = tile_count // 2
    here = lax.axis_index("cuts")
    here_x = here // 2
    here_core = here % 2
    slots = send_slots[0]
    counts = send_counts[0]
    cap = slots.shape[1]
    slot_index = jnp.arange(cap, dtype=jnp.int32)
    usable = slot_index[None, :] < counts[:, None]
    masked = jnp.where(usable, send_lines[0], -1)
    tail = jnp.broadcast_to(counts[:, None], (tile_count, 128))
    sheet = jnp.concatenate([masked, tail], axis=1)
    swap = [(i, i ^ 1) for i in range(cut_count)]
    flat_slots = slots.reshape(-1)

    def line_codes(ids):
        cut = ids // NY
        y = ids % NY
        mine = (ids >= 0) & (cut % 2 == here_core)
        ahead = (cut // 2 - here_x) % 4
        place = jnp.where(y < LA, ahead * LA + y, 4 * LA + ahead * LB + y - LA)
        return jnp.where(mine, place, -1).reshape(tile_count, cap // CHUNK, CHUNK)

    own_codes = line_codes(masked)

    counts, sheet = lax.optimization_barrier((counts, sheet))
    peer_sheet = lax.ppermute(sheet, "cuts", swap)
    rows, peer_rows = [], []
    for h in range(2):
        if h:
            counts, peer_sheet = lax.optimization_barrier((counts, peer_sheet))
        rows.append(gather_rows(acquired, flat_slots, counts, h * tile_half, tile_half, cap))
        peer_rows.append(lax.ppermute(rows[h], "cuts", swap))
    peer_counts = peer_sheet[:, cap]
    peer_codes = line_codes(peer_sheet[:, :cap])

    def x_send(block, k):
        return lax.ppermute(block, "cuts", [(i, (i + 2 * k) % cut_count) for i in range(cut_count)])

    b_blocks = None
    a_parts = []
    for h in range(2):
        *a_blocks, b_blocks = line_blocks(
            rows[h], peer_rows[h], own_codes, peer_codes,
            counts, peer_counts, b_blocks, h * tile_half, tile_count,
        )
        a_parts.append([a_blocks[0]] + [x_send(a_blocks[k], k) for k in (1, 2, 3)])
    near = (a_parts[0][1], a_parts[0][3])
    b_blocks = after(b_blocks, near)
    b_arrived = lax.all_to_all(b_blocks, "tile", split_axis=0, concat_axis=0, tiled=True)
    a_sums = None
    for h in range(2):
        a_sums = sum_x(a_parts[h], a_sums, h * tile_half, tile_count)
    a_arrived = lax.all_to_all(a_sums, "tile", split_axis=0, concat_axis=0, tiled=True)
    b_sums = sum_tile(b_arrived)
    b_final = [b_sums[0]] + [x_send(b_sums[k], k) for k in (1, 2, 3)]
    plane, coded = own_plane(a_arrived, b_final, stencil)

    total = cut_count * tile_count

    def plane_send(k):
        pairs = [(i, i + k) for i in range(total) if 0 <= i + k < total]
        return lax.ppermute(coded, ("cuts", "tile"), pairs)

    halos = [plane_send(1), plane_send(2), plane_send(-1), plane_send(-2)]
    place = here * tile_count + lax.axis_index("tile")
    edges = jnp.stack([place > 0, place < total - 1]).astype(jnp.int32)
    field = smooth(edges, plane, halos)

    read_ids = return_slots[0]
    read_total = read_ids.shape[1]
    usable_back = jnp.arange(read_total, dtype=jnp.int32)[None, :] < return_counts[0][:, None]
    selector = jnp.where(usable_back, read_ids, -1).reshape(-1)[:, None] == jnp.arange(
        NY, dtype=jnp.int32
    )
    outgoing = jnp.dot(selector.astype(jnp.bfloat16), field, preferred_element_type=jnp.float32)
    outgoing = outgoing.astype(jnp.bfloat16).reshape(tile_count, read_total, NX)
    returned = lax.all_to_all(outgoing, "tile", split_axis=0, concat_axis=0, tiled=True)
    return field[None], returned


def solution(mesh):
    in_specs = (
        P(("cuts", "tile"), None),
        P("tile", None),
        P(("cuts", "tile"), None, None),
        P(("cuts", "tile"), None, None),
        P(("cuts", "tile"), None),
        P(("cuts", "tile"), None, None),
        P(("cuts", "tile"), None),
    )
    out_specs = (P(("cuts", "tile"), None, None), P(("cuts", "tile"), None, None))
    return jax.shard_map(local, mesh=mesh, in_specs=in_specs, out_specs=out_specs, check_vma=False)
```

time: 270 us -> 230 us (0.85)
  Pallas kernels: 118 us -> 85 us
  starting transfers between devices: 58.8 us -> 50.9 us
  waiting for transfers between devices: 61.7 us -> 54.2 us
  local copies, waits for them, and re-layouts: 4.51 us -> 8.81 us
  blocking collectives: 21.8 us -> 24.9 us
    pallas_call x6 -> x7, Pallas kernels: 104 us -> 75.8 us  [the longest x2 38 us: line_blocks(): pl.pallas_call(functools.partial(lines_kernel, first=first), grid_spec=pl...]
    all_to_all x1, waiting for transfers between devices: 0.01 us -> 11.2 us  [local(): lax.all_to_all(a_sums, 'tile', split_axis=0, concat_axis=0, tiled=True)]
    all_to_all x1, waiting for transfers between devices: 9.3 us -> 0.01 us  [local(): lax.all_to_all(b_blocks, 'tile', split_axis=0, concat_axis=0, tiled=True)]
    ppermute x9, waiting for transfers between devices: 41.7 us -> 32.7 us  [x_send(): lax.ppermute(block, 'cuts', [(i, (i + 2 * k) % cut_count) for i in range(...]
    pallas_call x1, Pallas kernels: 9.49 us -> 2.79 us  [sum_tile(): pl.pallas_call(sum_tile_kernel, grid=(tiles,), in_specs=[pl.BlockSpec((1,...]
    unnamed x15 -> x25, local copies, waits for them, and re-layouts: 2.59 us -> 7.02 us
    ppermute x9, starting transfers between devices: 17.7 us -> 14 us  [x_send(): lax.ppermute(block, 'cuts', [(i, (i + 2 * k) % cut_count) for i in range(...]
    all_to_all x1, blocking collectives: 21.8 us -> 24.9 us  [local(): lax.all_to_all(outgoing, 'tile', split_axis=0, concat_axis=0, tiled=True)]
  transfers between devices with their start and end apart: 18 -> 18, of which waited for: 11 -> 7; matrix products, arithmetic and copies ran while one was open for 0% -> 0% of each run, Pallas kernels for 25% -> 28%
where the time goes in v2:
time: 230 us; the launch traced here: 228 us
  Pallas kernels  85 us (37%)
  waiting for transfers between devices  54.2 us (24%)
  starting transfers between devices  50.9 us (22%)
  blocking collectives  24.9 us (11%)
  local copies, waits for them, and re-layouts  8.81 us (4%)
    pallas_call x2, Pallas kernels, line_blocks(): pl.pallas_call(functools.partial(lines_kernel, first=first), grid_spec=pl...  38 us
    ppermute x9, waiting for transfers between devices, x_send(): lax.ppermute(block, 'cuts', [(i, (i + 2 * k) % cut_count) for i in range(...  32.7 us
    pallas_call x2, Pallas kernels, gather_rows(): pl.pallas_call(body, grid_spec=pltpu.PrefetchScalarGridSpec(num_scalar_pr...  28.7 us
    all_to_all x1, blocking collectives, local(): lax.all_to_all(outgoing, 'tile', split_axis=0, concat_axis=0, tiled=True)  24.9 us
    ppermute x4, starting transfers between devices, plane_send(): return lax.ppermute(coded, ('cuts', 'tile'), pairs)  15.6 us
    ppermute x9, starting transfers between devices, x_send(): lax.ppermute(block, 'cuts', [(i, (i + 2 * k) % cut_count) for i in range(...  14 us
    all_to_all x1, starting transfers between devices, local(): lax.all_to_all(b_blocks, 'tile', split_axis=0, concat_axis=0, tiled=True)  12.2 us
    all_to_all x1, waiting for transfers between devices, local(): lax.all_to_all(a_sums, 'tile', split_axis=0, concat_axis=0, tiled=True)  11.2 us
  transfers between devices with their start and end apart: 18, of which 7 were waited for; matrix products, arithmetic and copies ran while one was open for 0% of the time, Pallas kernels for 28%

profile of v2, /device:TPU:1, one launch (start us, length us, event | category | flops | bytes accessed | tf_op | source)
XLA Modules:
  0.0 228.1 jit_solution(16662460060869620131)
XLA Ops:
  0.6 1.0 bitcast_select_fusion
  1.6 0.7 broadcast_in_dim.24
  2.3 0.9 reshape_squeeze.3.slots_ref
  3.2 0.7 copy-done.7
  3.9 14.5 %gather_rows.3.own_ref = bf16[8,1280,256]{2,1,0:T(8,128)(2,1)} custom-call(s32[20480]{0:T(1024)S(1)} %reshape_squeeze.3.slots_ref, s32[16]{0:T(128)S(1)} %bitcast.17, bf16[16384,256]{1,0:T(8,128)(2,1)} %acq_ref.3), custom_call_target="tpu_custom_call" | custom-call | bytes 40000000 | tf_op jit(solution)/shard_map/gather_rows/pallas_call | solution.py:112
  18.4 1.7 collective-permute-start.2
  20.2 0.1 collective-permute-start
  20.3 5.9 %collective-permute-done = s32[16,1408]{1,0:T(8,128)S(1)} collective-permute-done((s32[16,1408]{1,0:T(8,128)S(1)}, s32[16,1408]{1,0:T(8,128)S(1)}, u32[]{:S(2)}, u32[]{:S(2)}) %collective-permute-start) | collective-permute-done | bytes 90144 | tf_op jit(solution)/shard_map/ppermute | solution.py:429
  26.1 14.2 %gather_rows.2.own_ref = bf16[8,1280,256]{2,1,0:T(8,128)(2,1)} custom-call(s32[20480]{0:T(1024)S(1)} %reshape_squeeze.3.slots_ref, s32[16]{0:T(128)S(1)} %bitcast.18, bf16[16384,256]{1,0:T(8,128)(2,1)} %acq_ref.3), custom_call_target="tpu_custom_call" | custom-call | bytes 40000000 | tf_op jit(solution)/shard_map/gather_rows/pallas_call | solution.py:112
  40.3 0.6 collective-permute-start.1
  41.0 0.4 select_select_fusion.own_lines
  41.4 0.2 select_select_fusion.1
  41.6 0.1 slice_reduce_fusion.peer_n
  41.8 18.7 %line_blocks.2 = (s16[1296,256]{1,0:T(8,128)(2,1)}, s16[1296,256]{1,0:T(8,128)(2,1)}, s16[1296,256]{1,0:T(8,128)(2,1)}, s16[1296,256]{1,0:T(8,128)(2,1)}, s16[16,400,256]{2,1,0:T(8,128)(2,1)}) custom-call(s32[16]{0:T(128)S(1)} %bitcast.20, s32[16]{0:T(128)S(1)} %slice_reduce_fusion.peer_n, bf16[8,1280,256]{2,1,0:T(8,128)(2,1)} %gather_rows.3.own_ref, ...), custom_call_target="tpu_custom_call" | custom-call | flops 10737418240 | bytes 40000000 | tf_op jit(solution)/shard_map/line_blocks/pallas_call | solution.py:197
  60.5 2.9 %collective-permute-start.6 = (s16[1296,256]{1,0:T(8,128)(2,1)}, s16[1296,256]{1,0:T(8,128)(2,1)S(1)}, u32[]{:S(2)}, u32[]{:S(2)}) collective-permute-start(s16[1296,256]{1,0:T(8,128)(2,1)} %get-tuple-element.32), channel_id=1, source_target_pairs={{0,32},{16,48},{32,64},{48,80},{64,96},{80,112},{96,0},{112,16},{1... | collective-permute-start | bytes 1990664 | tf_op jit(solution)/shard_map/ppermute | solution.py:440
  63.4 19.3 %line_blocks.3 = (s16[1296,256]{1,0:T(8,128)(2,1)}, s16[1296,256]{1,0:T(8,128)(2,1)}, s16[1296,256]{1,0:T(8,128)(2,1)}, s16[1296,256]{1,0:T(8,128)(2,1)}, s16[16,400,256]{2,1,0:T(8,128)(2,1)}) custom-call(s32[16]{0:T(128)S(1)} %bitcast.21, s32[16]{0:T(128)S(1)} %slice_reduce_fusion.peer_n, ...), custom_call_target="tpu_custom_call", output_to_operand_aliasing={{4}: (6, {})} | custom-call | flops 10737418240 | bytes 40000000 | tf_op jit(solution)/shard_map/line_blocks/pallas_call | solution.py:197
  82.7 0.8 copy-done
  83.5 0.2 copy-done.2
  83.8 12.2 %all-to-all-start.1 = ((s16[16,400,256]{2,1,0:T(8,128)(2,1)}), s16[16,400,256]{2,1,0:T(8,128)(2,1)S(1)}, u32[]{:S(2)}, u32[]{:S(2)}) async-start(s16[16,400,256]{2,1,0:T(8,128)(2,1)} %after.1), calls=%async_computation.1 | async-start | bytes 6553600 | tf_op jit(solution)/shard_map/all_to_all | solution.py:452
  96.0 1.4 collective-permute-start.7
  97.4 1.6 collective-permute-start.3
  99.0 2.6 %collective-permute-start.4 = (s16[1296,256]{1,0:T(8,128)(2,1)}, s16[1296,256]{1,0:T(8,128)(2,1)S(1)}, u32[]{:S(2)}, u32[]{:S(2)}) collective-permute-start(s16[1296,256]{1,0:T(8,128)(2,1)} %get-tuple-element.29), channel_id=1, source_target_pairs={{0,64},{16,80},{32,96},{48,112},{64,0},{80,16},{96,32},{112,48},{1... | collective-permute-start | bytes 1990664 | tf_op jit(solution)/shard_map/ppermute | solution.py:440
  101.6 11.8 %collective-permute-done.7.p2.c2 = s16[1296,256]{1,0:T(8,128)(2,1)S(1)} collective-permute-done((s16[1296,256]{1,0:T(8,128)(2,1)}, s16[1296,256]{1,0:T(8,128)(2,1)S(1)}, u32[]{:S(2)}, u32[]{:S(2)}) %collective-permute-start.7) | collective-permute-done | bytes 663584 | tf_op jit(solution)/shard_map/ppermute | solution.py:440
  113.4 1.1 copy-done.1
  114.5 1.1 copy-done.3
  115.6 1.1 copy-done.4
  116.6 4.5 %sum_x.2.alias_ref = s16[16,176,256]{2,1,0:T(8,128)(2,1)} custom-call(s16[1296,256]{1,0:T(8,128)(2,1)S(1)} %copy-done.4, s16[1296,256]{1,0:T(8,128)(2,1)S(1)} %copy-done.1, s16[1296,256]{1,0:T(8,128)(2,1)S(1)} %collective-permute-done.7.p2.c2, s16[1296,256]{1,0:T(8,128)(2,1)S(1)} %copy-done.3, s16[1296,256]{1,0:T(8,128)(2,1)S(1)} %copy-done.4, ...), custom_call_target="tpu_custom_call" | custom-call | tf_op jit(solution)/shard_map/sum_x/pallas_call | solution.py:245
  121.2 8.9 %collective-permute-done.3.p1.c1 = s16[1296,256]{1,0:T(8,128)(2,1)S(1)} collective-permute-done((s16[1296,256]{1,0:T(8,128)(2,1)}, s16[1296,256]{1,0:T(8,128)(2,1)S(1)}, u32[]{:S(2)}, u32[]{:S(2)}) %collective-permute-start.3) | collective-permute-done | bytes 663584 | tf_op jit(solution)/shard_map/ppermute | solution.py:440
  130.1 11.7 %collective-permute-done.4.p2.c2 = s16[1296,256]{1,0:T(8,128)(2,1)S(1)} collective-permute-done((s16[1296,256]{1,0:T(8,128)(2,1)}, s16[1296,256]{1,0:T(8,128)(2,1)S(1)}, u32[]{:S(2)}, u32[]{:S(2)}) %collective-permute-start.4) | collective-permute-done | bytes 663584 | tf_op jit(solution)/shard_map/ppermute | solution.py:440
  141.8 0.3 collective-permute-done.5.p3.c3
  142.1 4.6 %sum_x.3 = s16[16,176,256]{2,1,0:T(8,128)(2,1)} custom-call(s16[1296,256]{1,0:T(8,128)(2,1)S(1)} %copy-done.5, s16[1296,256]{1,0:T(8,128)(2,1)S(1)} %collective-permute-done.3.p1.c1, s16[1296,256]{1,0:T(8,128)(2,1)S(1)} %collective-permute-done.4.p2.c2, s16[1296,256]{1,0:T(8,128)(2,1)S(1)} %collective-permute-done.5.p3.c3, ...), custom_call_target="tpu_custom_call", output_to_operand_aliasing={{}: (8, {})} | custom-call | tf_op jit(solution)/shard_map/sum_x/pallas_call | solution.py:245
  146.7 6.6 %all-to-all-start = ((s16[16,176,256]{2,1,0:T(8,128)(2,1)}), s16[16,176,256]{2,1,0:T(8,128)(2,1)}, u32[]{:S(2)}, u32[]{:S(2)}) async-start(s16[16,176,256]{2,1,0:T(8,128)(2,1)} %sum_x.3), calls=%async_computation | async-start | bytes 2883584 | tf_op jit(solution)/shard_map/all_to_all | solution.py:456
  153.3 2.8 %sum_tile.1 = (s16[112,256]{1,0:T(8,128)(2,1)S(1)}, s16[112,256]{1,0:T(8,128)(2,1)S(1)}, s16[112,256]{1,0:T(8,128)(2,1)S(1)}, s16[112,256]{1,0:T(8,128)(2,1)S(1)}) custom-call(s16[16,400,256]{2,1,0:T(8,128)(2,1)S(1)} %all-to-all-done.1.in_ref), custom_call_target="tpu_custom_call" | custom-call | tf_op jit(solution)/shard_map/sum_tile/pallas_call | solution.py:283
  156.1 2.7 %collective-permute-start.10 = (s16[112,256]{1,0:T(8,128)(2,1)S(1)}, s16[112,256]{1,0:T(8,128)(2,1)S(1)}, u32[]{:S(2)}, u32[]{:S(2)}) collective-permute-start(s16[112,256]{1,0:T(8,128)(2,1)S(1)} %get-tuple-element.38), channel_id=1, source_target_pairs={{0,64},{16,80},{32,96},{48,112},{64,0},{80,16},{96,32},{112,48},{1... | collective-permute-start | bytes 172040 | tf_op jit(solution)/shard_map/ppermute | solution.py:440
  158.8 2.7 %collective-permute-start.11 = (s16[112,256]{1,0:T(8,128)(2,1)S(1)}, s16[112,256]{1,0:T(8,128)(2,1)S(1)}, u32[]{:S(2)}, u32[]{:S(2)}) collective-permute-start(s16[112,256]{1,0:T(8,128)(2,1)S(1)} %get-tuple-element.39), channel_id=1, source_target_pairs={{0,96},{16,112},{32,0},{48,16},{64,32},{80,48},{96,64},{112,80},{1... | collective-permute-start | bytes 172040 | tf_op jit(solution)/shard_map/ppermute | solution.py:440
  161.5 11.2 %all-to-all-done.a_ref = s16[16,176,256]{2,1,0:T(8,128)(2,1)} async-done(((s16[16,176,256]{2,1,0:T(8,128)(2,1)}), s16[16,176,256]{2,1,0:T(8,128)(2,1)}, u32[]{:S(2)}, u32[]{:S(2)}) %all-to-all-start) | async-done | bytes 1441824 | tf_op jit(solution)/shard_map/all_to_all | solution.py:456
  172.8 1.0 copy-done.6
  173.8 4.2 %own_plane.1 = (f32[256,256]{1,0:T(8,128)S(1)}, s16[272,256]{1,0:T(8,128)(2,1)S(1)}) custom-call(s16[16,176,256]{2,1,0:T(8,128)(2,1)} %all-to-all-done.a_ref, s16[112,256]{1,0:T(8,128)(2,1)S(1)} %get-tuple-element.36.b0, s16[112,256]{1,0:T(8,128)(2,1)S(1)} %collective-permute-done.9.b1, s16[112,256]{1,0:T(8,128)(2,1)S(1)} %collective-permute-done.10.b2, ...), custom_call_target="tpu_custom_call" | custom-call | tf_op jit(solution)/shard_map/own_plane/pallas_call | solution.py:332
  178.0 2.2 collective-permute-start.12
  180.2 4.5 %collective-permute-start.13 = (s16[272,256]{1,0:T(8,128)(2,1)S(1)}, s16[272,256]{1,0:T(8,128)(2,1)S(1)}, u32[]{:S(2)}, u32[]{:S(2)}) collective-permute-start(s16[272,256]{1,0:T(8,128)(2,1)S(1)} %get-tuple-element.41), channel_id=1, source_target_pairs={{0,2},{1,3},{2,4},{3,5},{4,6},{5,7},{6,8},{7,9},{8,10},{9,11},{10,... | collective-permute-start | bytes 417800 | tf_op jit(solution)/shard_map/ppermute | solution.py:465
  184.7 6.3 %collective-permute-start.14 = (s16[272,256]{1,0:T(8,128)(2,1)S(1)}, s16[272,256]{1,0:T(8,128)(2,1)S(1)}, u32[]{:S(2)}, u32[]{:S(2)}) collective-permute-start(s16[272,256]{1,0:T(8,128)(2,1)S(1)} %get-tuple-element.41), channel_id=1, source_target_pairs={{1,0},{2,1},{3,2},{4,3},{5,4},{6,5},{7,6},{8,7},{9,8},{10,9},{11,1... | collective-permute-start | bytes 417800 | tf_op jit(solution)/shard_map/ppermute | solution.py:465
  191.0 2.7 %collective-permute-start.15 = (s16[272,256]{1,0:T(8,128)(2,1)S(1)}, s16[272,256]{1,0:T(8,128)(2,1)S(1)}, u32[]{:S(2)}, u32[]{:S(2)}) collective-permute-start(s16[272,256]{1,0:T(8,128)(2,1)S(1)} %get-tuple-element.41), channel_id=1, source_target_pairs={{2,0},{3,1},{4,2},{5,3},{6,4},{7,5},{8,6},{9,7},{10,8},{11,9},{12,... | collective-permute-start | bytes 417800 | tf_op jit(solution)/shard_map/ppermute | solution.py:465
  193.7 0.1 add_convert_fusion.edge_ref
  193.8 4.5 %collective-permute-done.15.r2 = s16[272,256]{1,0:T(8,128)(2,1)S(1)} collective-permute-done((s16[272,256]{1,0:T(8,128)(2,1)S(1)}, s16[272,256]{1,0:T(8,128)(2,1)S(1)}, u32[]{:S(2)}, u32[]{:S(2)}) %collective-permute-start.15) | collective-permute-done | bytes 139296 | tf_op jit(solution)/shard_map/ppermute | solution.py:465
  198.3 2.2 smooth.1
  200.5 1.6 convolution_convert_fusion
  202.2 24.9 %all_to_all.15 = bf16[16,128,256]{2,1,0:T(8,128)(2,1)S(1)} all-to-all(bf16[16,128,256]{2,1,0:T(8,128)(2,1)S(1)} %bitcast.22), channel_id=1, replica_groups=mesh['cuts'=8,'tile'=16] {'tile'}, dimensions={0} | all-to-all | bytes 2097152 | tf_op jit(solution)/shard_map/all_to_all | solution.py:480
  227.1 1.0 copy.16
  (38 shorter events, 0.2 us)
Async XLA Ops:
  3.2 0.7 copy-start.7
  18.4 22.5 %copy-start.9 = (s32[1,16,1280]{2,1,0:T(8,128)S(1)}, s32[1,16,1280]{2,1,0:T(8,128)}, u32[]{:S(2)}) copy-start(s32[1,16,1280]{2,1,0:T(8,128)} %param.10) | copy-start | bytes 245764
  18.4 22.5 %copy-start.8 = (s32[1,16]{1,0:T(1,128)S(1)}, s32[1,16]{1,0:T(1,128)}, u32[]{:S(2)}) copy-start(s32[1,16]{1,0:T(1,128)} %param.11) | copy-start | bytes 196
  18.4 23.3 %collective-permute-start.2 = (bf16[8,1280,256]{2,1,0:T(8,128)(2,1)}, bf16[8,1280,256]{2,1,0:T(8,128)(2,1)}, u32[]{:S(2)}, u32[]{:S(2)}) collective-permute-start(bf16[8,1280,256]{2,1,0:T(8,128)(2,1)} %gather_rows.3.own_ref), channel_id=1, source_target_pairs={{0,16},{16,0},{32,48},{48,32},{64,80},{80,64},{96,112},{112,96},{1... | collective-permute-start | bytes 15728648 | tf_op jit(solution)/shard_map/ppermute | solution.py:435
  20.2 6.0 %collective-permute-start = (s32[16,1408]{1,0:T(8,128)S(1)}, s32[16,1408]{1,0:T(8,128)S(1)}, u32[]{:S(2)}, u32[]{:S(2)}) collective-permute-start(s32[16,1408]{1,0:T(8,128)S(1)} %pad_add_fusion), channel_id=1, source_target_pairs={{0,16},{16,0},{32,48},{48,32},{64,80},{80,64},{96,112},{112,96},{1... | collective-permute-start | bytes 270344 | tf_op jit(solution)/shard_map/ppermute | solution.py:429
  40.3 23.1 %collective-permute-start.1 = (bf16[8,1280,256]{2,1,0:T(8,128)(2,1)}, bf16[8,1280,256]{2,1,0:T(8,128)(2,1)}, u32[]{:S(2)}, u32[]{:S(2)}) collective-permute-start(bf16[8,1280,256]{2,1,0:T(8,128)(2,1)} %gather_rows.2.own_ref), channel_id=1, source_target_pairs={{0,16},{16,0},{32,48},{48,32},{64,80},{80,64},{96,112},{112,96},{1... | collective-permute-start | bytes 15728648 | tf_op jit(solution)/shard_map/ppermute | solution.py:435
  60.5 22.2 %collective-permute-start.6 = (s16[1296,256]{1,0:T(8,128)(2,1)}, s16[1296,256]{1,0:T(8,128)(2,1)S(1)}, u32[]{:S(2)}, u32[]{:S(2)}) collective-permute-start(s16[1296,256]{1,0:T(8,128)(2,1)} %get-tuple-element.32), channel_id=1, source_target_pairs={{0,32},{16,48},{32,64},{48,80},{64,96},{80,112},{96,0},{112,16},{1... | collective-permute-start | bytes 1990664 | tf_op jit(solution)/shard_map/ppermute | solution.py:440
  63.4 19.3 %collective-permute-start.8 = (s16[1296,256]{1,0:T(8,128)(2,1)}, s16[1296,256]{1,0:T(8,128)(2,1)S(1)}, u32[]{:S(2)}, u32[]{:S(2)}) collective-permute-start(s16[1296,256]{1,0:T(8,128)(2,1)} %get-tuple-element.34), channel_id=1, source_target_pairs={{0,96},{16,112},{32,0},{48,16},{64,32},{80,48},{96,64},{112,80},{1... | collective-permute-start | bytes 1990664 | tf_op jit(solution)/shard_map/ppermute | solution.py:440
  82.7 0.9 copy-start
  82.7 1.1 copy-start.2
  83.8 62.9 %all-to-all-start.1 = ((s16[16,400,256]{2,1,0:T(8,128)(2,1)}), s16[16,400,256]{2,1,0:T(8,128)(2,1)S(1)}, u32[]{:S(2)}, u32[]{:S(2)}) async-start(s16[16,400,256]{2,1,0:T(8,128)(2,1)} %after.1), calls=%async_computation.1 | async-start | bytes 6553600 | tf_op jit(solution)/shard_map/all_to_all | solution.py:452
  96.0 17.4 %collective-permute-start.7 = (s16[1296,256]{1,0:T(8,128)(2,1)}, s16[1296,256]{1,0:T(8,128)(2,1)S(1)}, u32[]{:S(2)}, u32[]{:S(2)}) collective-permute-start(s16[1296,256]{1,0:T(8,128)(2,1)} %get-tuple-element.33), channel_id=1, source_target_pairs={{0,64},{16,80},{32,96},{48,112},{64,0},{80,16},{96,32},{112,48},{1... | collective-permute-start | bytes 1990664 | tf_op jit(solution)/shard_map/ppermute | solution.py:440
  97.4 32.6 %collective-permute-start.3 = (s16[1296,256]{1,0:T(8,128)(2,1)}, s16[1296,256]{1,0:T(8,128)(2,1)S(1)}, u32[]{:S(2)}, u32[]{:S(2)}) collective-permute-start(s16[1296,256]{1,0:T(8,128)(2,1)} %get-tuple-element.28), channel_id=1, source_target_pairs={{0,32},{16,48},{32,64},{48,80},{64,96},{80,112},{96,0},{112,16},{1... | collective-permute-start | bytes 1990664 | tf_op jit(solution)/shard_map/ppermute | solution.py:440
  99.0 42.8 %collective-permute-start.4 = (s16[1296,256]{1,0:T(8,128)(2,1)}, s16[1296,256]{1,0:T(8,128)(2,1)S(1)}, u32[]{:S(2)}, u32[]{:S(2)}) collective-permute-start(s16[1296,256]{1,0:T(8,128)(2,1)} %get-tuple-element.29), channel_id=1, source_target_pairs={{0,64},{16,80},{32,96},{48,112},{64,0},{80,16},{96,32},{112,48},{1... | collective-permute-start | bytes 1990664 | tf_op jit(solution)/shard_map/ppermute | solution.py:440
  101.6 40.5 %collective-permute-start.5 = (s16[1296,256]{1,0:T(8,128)(2,1)}, s16[1296,256]{1,0:T(8,128)(2,1)S(1)}, u32[]{:S(2)}, u32[]{:S(2)}) collective-permute-start(s16[1296,256]{1,0:T(8,128)(2,1)} %get-tuple-element.30), channel_id=1, source_target_pairs={{0,96},{16,112},{32,0},{48,16},{64,32},{80,48},{96,64},{112,80},{1... | collective-permute-start | bytes 1990664 | tf_op jit(solution)/shard_map/ppermute | solution.py:440
  113.4 1.1 copy-start.1
  114.5 1.1 copy-start.3
  115.6 1.1 copy-start.4
  116.6 25.5 %copy-start.5 = (s16[1296,256]{1,0:T(8,128)(2,1)S(1)}, s16[1296,256]{1,0:T(8,128)(2,1)}, u32[]{:S(2)}) copy-start(s16[1296,256]{1,0:T(8,128)(2,1)} %get-tuple-element.27.p0.c0) | copy-start | bytes 1990660
  146.7 26.1 %all-to-all-start = ((s16[16,176,256]{2,1,0:T(8,128)(2,1)}), s16[16,176,256]{2,1,0:T(8,128)(2,1)}, u32[]{:S(2)}, u32[]{:S(2)}) async-start(s16[16,176,256]{2,1,0:T(8,128)(2,1)} %sum_x.3), calls=%async_computation | async-start | bytes 2883584 | tf_op jit(solution)/shard_map/all_to_all | solution.py:456
  153.3 40.3 %copy-start.10 = (s32[1,16,128]{2,1,0:T(8,128)S(1)}, s32[1,16,128]{2,1,0:T(8,128)}, u32[]{:S(2)}) copy-start(s32[1,16,128]{2,1,0:T(8,128)} %param.12) | copy-start | bytes 24580
  153.3 40.3 %copy-start.11 = (s32[1,16]{1,0:T(1,128)S(1)}, s32[1,16]{1,0:T(1,128)}, u32[]{:S(2)}) copy-start(s32[1,16]{1,0:T(1,128)} %param.13) | copy-start | bytes 196
  156.1 16.6 %collective-permute-start.10 = (s16[112,256]{1,0:T(8,128)(2,1)S(1)}, s16[112,256]{1,0:T(8,128)(2,1)S(1)}, u32[]{:S(2)}, u32[]{:S(2)}) collective-permute-start(s16[112,256]{1,0:T(8,128)(2,1)S(1)} %get-tuple-element.38), channel_id=1, source_target_pairs={{0,64},{16,80},{32,96},{48,112},{64,0},{80,16},{96,32},{112,48},{1... | collective-permute-start | bytes 172040 | tf_op jit(solution)/shard_map/ppermute | solution.py:440
  158.8 13.9 %collective-permute-start.11 = (s16[112,256]{1,0:T(8,128)(2,1)S(1)}, s16[112,256]{1,0:T(8,128)(2,1)S(1)}, u32[]{:S(2)}, u32[]{:S(2)}) collective-permute-start(s16[112,256]{1,0:T(8,128)(2,1)S(1)} %get-tuple-element.39), channel_id=1, source_target_pairs={{0,96},{16,112},{32,0},{48,16},{64,32},{80,48},{96,64},{112,80},{1... | collective-permute-start | bytes 172040 | tf_op jit(solution)/shard_map/ppermute | solution.py:440
  161.5 11.2 %collective-permute-start.9 = (s16[112,256]{1,0:T(8,128)(2,1)S(1)}, s16[112,256]{1,0:T(8,128)(2,1)S(1)}, u32[]{:S(2)}, u32[]{:S(2)}) collective-permute-start(s16[112,256]{1,0:T(8,128)(2,1)S(1)} %get-tuple-element.37), channel_id=1, source_target_pairs={{0,32},{16,48},{32,64},{48,80},{64,96},{80,112},{96,0},{112,16},{1... | collective-permute-start | bytes 172040 | tf_op jit(solution)/shard_map/ppermute | solution.py:440
  172.8 1.0 copy-start.6
  178.0 15.8 %collective-permute-start.12 = (s16[272,256]{1,0:T(8,128)(2,1)S(1)}, s16[272,256]{1,0:T(8,128)(2,1)S(1)}, u32[]{:S(2)}, u32[]{:S(2)}) collective-permute-start(s16[272,256]{1,0:T(8,128)(2,1)S(1)} %get-tuple-element.41), channel_id=1, source_target_pairs={{0,1},{1,2},{2,3},{3,4},{4,5},{5,6},{6,7},{7,8},{8,9},{9,10},{10,1... | collective-permute-start | bytes 417800 | tf_op jit(solution)/shard_map/ppermute | solution.py:465
  180.2 13.6 %collective-permute-start.13 = (s16[272,256]{1,0:T(8,128)(2,1)S(1)}, s16[272,256]{1,0:T(8,128)(2,1)S(1)}, u32[]{:S(2)}, u32[]{:S(2)}) collective-permute-start(s16[272,256]{1,0:T(8,128)(2,1)S(1)} %get-tuple-element.41), channel_id=1, source_target_pairs={{0,2},{1,3},{2,4},{3,5},{4,6},{5,7},{6,8},{7,9},{8,10},{9,11},{10,... | collective-permute-start | bytes 417800 | tf_op jit(solution)/shard_map/ppermute | solution.py:465
  184.7 9.1 %collective-permute-start.14 = (s16[272,256]{1,0:T(8,128)(2,1)S(1)}, s16[272,256]{1,0:T(8,128)(2,1)S(1)}, u32[]{:S(2)}, u32[]{:S(2)}) collective-permute-start(s16[272,256]{1,0:T(8,128)(2,1)S(1)} %get-tuple-element.41), channel_id=1, source_target_pairs={{1,0},{2,1},{3,2},{4,3},{5,4},{6,5},{7,6},{8,7},{9,8},{10,9},{11,1... | collective-permute-start | bytes 417800 | tf_op jit(solution)/shard_map/ppermute | solution.py:465
  191.0 7.3 %collective-permute-start.15 = (s16[272,256]{1,0:T(8,128)(2,1)S(1)}, s16[272,256]{1,0:T(8,128)(2,1)S(1)}, u32[]{:S(2)}, u32[]{:S(2)}) collective-permute-start(s16[272,256]{1,0:T(8,128)(2,1)S(1)} %get-tuple-element.41), channel_id=1, source_target_pairs={{2,0},{3,1},{4,2},{5,3},{6,4},{7,5},{8,6},{9,7},{10,8},{11,9},{12,... | collective-permute-start | bytes 417800 | tf_op jit(solution)/shard_map/ppermute | solution.py:465

commit v3 on v2

--- a/solution.py
+++ b/solution.py
@@ -11,7 +11,7 @@
 NX = 256
 NY = 256
 TAPS = 4
-LA = 160
+LA = 144
 LB = NY - LA
 ALPHA = math.log(2.0) / 64.0
 TOP = 32700.0
@@ -64,7 +64,9 @@
     return block.astype(jnp.int32).astype(jnp.int16)
 
 
-def gather_kernel(slots_ref, counts_ref, acq_ref, out_ref, wide_ref, half_ref, sem, *, first, cap):
+def gather_kernel(
+    slots_ref, counts_ref, acq_ref, lines_ref, out_ref, wide_ref, half_ref, sem, *, first, cap
+):
     step = pl.program_id(0)
     pieces = sem.shape[0]
     piece = half_ref.shape[0] // pieces
@@ -106,55 +108,130 @@
     lax.fori_loop(0, picks, pick, 0)
     lax.fori_loop(picks, (count + CHUNK - 1) // CHUNK * (CHUNK // PICK), clear, 0)
 
-
-def gather_rows(acquired, slots, counts, first, tiles, cap):
+    ids = lines_ref[pl.ds(first + step, 1), :]
+    position = lax.broadcasted_iota(jnp.int32, ids.shape, 1)
+    ids = jnp.where(position < count, ids + 1, 0)
+    index = lax.broadcasted_iota(jnp.int32, (8, NX), 0)
+    table = jnp.where(index == 7, count, 0)
+    for i in range(cap // CHUNK):
+        table = jnp.where(index == i, ids[:, i * CHUNK : (i + 1) * CHUNK], table)
+    both = jnp.concatenate([table >> 6, table & 63], axis=0)
+    out_ref[0, pl.ds(cap, 16), :] = both.astype(jnp.float32).astype(jnp.bfloat16)
+
+
+def gather_rows(acquired, slots, counts, lines, first, tiles):
+    cap = lines.shape[1]
     body = functools.partial(gather_kernel, first=first, cap=cap)
     return pl.pallas_call(
         body,
         grid_spec=pltpu.PrefetchScalarGridSpec(
             num_scalar_prefetch=2,
             grid=(tiles,),
-            in_specs=[pl.BlockSpec(memory_space=pl.ANY)],
-            out_specs=pl.BlockSpec((1, cap, NX), lambda t, s, c: (t, 0, 0)),
+            in_specs=[
+                pl.BlockSpec(memory_space=pl.ANY),
+                pl.BlockSpec(lines.shape, lambda t, s, c: (0, 0)),
+            ],
+            out_specs=pl.BlockSpec((1, cap + 16, NX), lambda t, s, c: (t, 0, 0)),
             scratch_shapes=[
                 pltpu.VMEM(acquired.shape, jnp.float32),
                 pltpu.VMEM(acquired.shape, jnp.bfloat16),
                 pltpu.SemaphoreType.DMA((8,)),
             ],
         ),
-        out_shape=jax.ShapeDtypeStruct((tiles, cap, NX), jnp.bfloat16),
+        out_shape=hbm((tiles, cap + 16, NX), jnp.bfloat16),
         compiler_params=params(48),
         cost_estimate=pl.CostEstimate(flops=0, transcendentals=0, bytes_accessed=40_000_000),
         name="gather_rows",
-    )(slots, counts, acquired)
+    )(slots, counts, acquired, lines)
 
 
 def lines_kernel(
-    own_n, peer_n, own_ref, peer_ref, own_lines, peer_lines, alias_ref,
-    a0_ref, a1_ref, a2_ref, a3_ref, b_ref, acc_ref, code_ref, *, first,
+    own_n, peer_n, place_ref, own_hbm, peer_hbm, alias_ref,
+    a0_ref, a1_ref, a2_ref, a3_ref, b_ref,
+    acc_ref, code_ref, rows_ref, ids_ref, sem, *, first, cap,
 ):
     step = pl.program_id(0)
     last = pl.num_programs(0) - 1
+    most = cap // CHUNK
+
+    def chunks(tile):
+        return (own_n[first + tile] + CHUNK - 1) // CHUNK, (peer_n[tile] + CHUNK - 1) // CHUNK
+
+    def for_copies(tile, act):
+        slot = lax.rem(tile, 2)
+        own, peer = chunks(tile)
+        for j, (source, base, count) in enumerate(((own_hbm, 0, own), (peer_hbm, own, peer))):
+            for i in range(most):
+                copy = pltpu.make_async_copy(
+                    source.at[tile, pl.ds(i * CHUNK, CHUNK), :],
+                    rows_ref.at[slot, pl.ds(pl.multiple_of((base + i) * CHUNK, CHUNK), CHUNK), :],
+                    sem.at[slot, j * (most + 1) + i],
+                )
+
+                @pl.when(i < count)
+                def _():
+                    act(copy)
+
+            act(
+                pltpu.make_async_copy(
+                    source.at[tile, pl.ds(cap, 16), :],
+                    ids_ref.at[slot, j],
+                    sem.at[slot, j * (most + 1) + most],
+                )
+            )
+
+    @pl.when(step == 0)
+    def _():
+        for_copies(0, lambda copy: copy.start())
+
+    @pl.when(step < last)
+    def _():
+        for_copies(step + 1, lambda copy: copy.start())
+
+    for_copies(step, lambda copy: copy.wait())
+
+    slot = lax.rem(step, 2)
+    own, peer = chunks(step)
+    here_core, here_x = place_ref[0], place_ref[1]
+    for j in range(2):
+        pair = ids_ref[slot, j].astype(jnp.float32).astype(jnp.int32)
+        line = pair[0:8] * 64 + pair[8:16] - 1
+        cut = line >> 8
+        y = line & (NY - 1)
+        mine = (line >= 0) & ((cut & 1) == here_core)
+        ahead = ((cut >> 1) - here_x) & 3
+        target = jnp.where(y < LA, ahead * LA + y, 4 * LA + ahead * LB + y - LA)
+        target = jnp.where(mine, target, -1)
+        for i in range(most):
+            spot = i if j == 0 else own + i
+            code_ref[4, pl.ds(spot, 1), :] = target[i : i + 1].astype(jnp.float32)
+
     acc_ref[...] = jnp.zeros(acc_ref.shape, jnp.float32)
-    position = lax.broadcasted_iota(jnp.int32, (CHUNK, CHUNK), 0)
-
-    def add(rows_ref, lines_ref):
-        def body(i, carry):
-            base = pl.multiple_of(i * CHUNK, CHUNK)
-            rows = rows_ref[0, pl.ds(base, CHUNK), :]
-            ids = lines_ref[0, pl.ds(i, 1), :]
-            for m in range(acc_ref.shape[0] // CHUNK):
-                hot = jnp.where(position + m * CHUNK == ids, 1.0, 0.0).astype(jnp.bfloat16)
-                span = pl.ds(m * CHUNK, CHUNK)
-                acc_ref[span, :] += jnp.dot(hot, rows, preferred_element_type=jnp.float32)
-            return carry
-
-        return body
-
-    own_steps = (own_n[first + step] + CHUNK - 1) // CHUNK
-    peer_steps = (peer_n[first + step] + CHUNK - 1) // CHUNK
-    lax.fori_loop(0, own_steps, add(own_ref, own_lines), 0)
-    lax.fori_loop(0, peer_steps, add(peer_ref, peer_lines), 0)
+    position = lax.broadcasted_iota(jnp.int32, (CHUNK, CHUNK), 0).astype(jnp.float32)
+
+    def add(start, width):
+        rows = rows_ref[slot, pl.ds(pl.multiple_of(start * CHUNK, CHUNK), width * CHUNK), :]
+        ids = [code_ref[4, pl.ds(start + i, 1), :] for i in range(width)]
+        for m in range(acc_ref.shape[0] // CHUNK):
+            hot = [
+                jnp.where(position == row - m * CHUNK, 1.0, 0.0).astype(jnp.bfloat16) for row in ids
+            ]
+            hot = jnp.concatenate(hot, axis=1) if width > 1 else hot[0]
+            span = pl.ds(m * CHUNK, CHUNK)
+            acc_ref[span, :] += jnp.dot(hot, rows, preferred_element_type=jnp.float32)
+
+    total = own + peer
+
+    def four(i, carry):
+        add(i * 4, 4)
+        return carry
+
+    lax.fori_loop(0, total // 4, four, 0)
+    for width in (1, 2, 3):
+
+        @pl.when(total % 4 == width)
+        def _():
+            add(total // 4 * 4, width)
 
     outs = (a0_ref, a1_ref, a2_ref, a3_ref)
     for k in range(4):
@@ -172,39 +249,41 @@
     @pl.when(step == last)
     def _():
         for k in range(4):
-            table = code_ref[k]
-            both = jnp.concatenate([table, jnp.zeros_like(table)], axis=0)
-            outs[k][pl.ds((last + 1) * LA, 16), :] = both.astype(jnp.int32).astype(jnp.int16)
+            outs[k][pl.ds((last + 1) * LA, 16), :] = code_ref[k].astype(jnp.int32).astype(jnp.int16)
 
 
 def pad_row(row):
     return jnp.concatenate([row, jnp.zeros((1, NX - row.shape[1]), jnp.float32)], axis=1)
 
 
-def line_blocks(own_rows, peer_rows, own_lines, peer_lines, own_n, peer_n, b_old, first, tiles_all):
+def line_blocks(own_rows, peer_rows, own_n, peer_n, place, b_old, first, tiles_all):
     tiles, cap, _ = own_rows.shape
-    span = cap // CHUNK
-    row_spec = pl.BlockSpec((1, cap, NX), lambda t, *_: (t, 0, 0))
-    line_spec = pl.BlockSpec((1, span, CHUNK), lambda t, *_: (t + first, 0, 0))
+    cap -= 16
     a_shape = (tiles * LA + 16, NX)
-    args = [own_n, peer_n, own_rows, peer_rows, own_lines, peer_lines]
+    own_rows = pltpu.with_memory_space_constraint(own_rows, pltpu.HBM)
+    peer_rows = pltpu.with_memory_space_constraint(peer_rows, pltpu.HBM)
+    args = [own_n, peer_n, place, own_rows, peer_rows]
     aliases = {}
     if b_old is None:
         b_old = jnp.zeros((16, NX), jnp.int16)
     else:
-        aliases = {6: 4}
+        aliases = {5: 4}
     args.append(b_old)
     return pl.pallas_call(
-        functools.partial(lines_kernel, first=first),
+        functools.partial(lines_kernel, first=first, cap=cap),
         grid_spec=pltpu.PrefetchScalarGridSpec(
-            num_scalar_prefetch=2,
+            num_scalar_prefetch=3,
             grid=(tiles,),
-            in_specs=[row_spec, row_spec, line_spec, line_spec, pl.BlockSpec(memory_space=pl.ANY)],
+            in_specs=[pl.BlockSpec(memory_space=pltpu.HBM)] * 2
+            + [pl.BlockSpec(memory_space=pl.ANY)],
             out_specs=[pl.BlockSpec(a_shape, lambda t, *_: (0, 0))] * 4
             + [pl.BlockSpec((1, 4 * LB + 16, NX), lambda t, *_: (t + first, 0, 0))],
             scratch_shapes=[
                 pltpu.VMEM((4 * NY, NX), jnp.float32),
-                pltpu.VMEM((4, tiles, NX), jnp.float32),
+                pltpu.VMEM((5, 16, NX), jnp.float32),
+                pltpu.VMEM((2, 2 * cap, NX), jnp.bfloat16),
+                pltpu.VMEM((2, 2, 16, NX), jnp.bfloat16),
+                pltpu.SemaphoreType.DMA((2, 2 * (cap // CHUNK + 1))),
             ],
         ),
         out_shape=[hbm(a_shape, jnp.int16)] * 4
@@ -225,14 +304,23 @@
     return row[:, 0:length]
 
 
-def sum_x_kernel(p0, p1, p2, p3, c0, c1, c2, c3, alias_ref, out_ref):
-    step = pl.program_id(0)
-    total = jnp.zeros((LA, NX), jnp.float32)
-    for values, codes in ((p0, c0), (p1, c1), (p2, c2), (p3, c3)):
-        total = total + decode(values[...], code_row(codes[...], step, LA))
-    values, code = encode(total)
-    out_ref[0, pl.ds(0, LA), :] = values
-    out_ref[0, pl.ds(LA, 16), :] = code_block([pad_row(code)])
+def sum_x_kernel(p0, p1, p2, p3, alias_ref, out_ref, sum_ref, sem, *, first):
+    tiles = sum_ref.shape[0]
+
+    def copy_out(i):
+        return pltpu.make_async_copy(sum_ref.at[i], out_ref.at[first + i], sem.at[i])
+
+    for i in range(tiles):
+        total = jnp.zeros((LA, NX), jnp.float32)
+        for part in (p0, p1, p2, p3):
+            codes = code_row(part[pl.ds(tiles * LA, 16), :], i, LA)
+            total = total + decode(part[pl.ds(i * LA, LA), :], codes)
+        values, code = encode(total)
+        sum_ref[i, pl.ds(0, LA), :] = values
+        sum_ref[i, pl.ds(LA, 16), :] = code_block([pad_row(code)])
+        copy_out(i).start()
+    for i in range(tiles):
+        copy_out(i).wait()
 
 
 def sum_x(parts, old, first, tiles_all):
@@ -241,19 +329,20 @@
     if old is None:
         old = jnp.zeros((16, NX), jnp.int16)
     else:
-        aliases = {8: 0}
-    return pl.pallas_call(
-        sum_x_kernel,
-        grid=(tiles,),
-        in_specs=[pl.BlockSpec((LA, NX), lambda t: (t, 0))] * 4
-        + [pl.BlockSpec((16, NX), lambda t: (tiles * LA // 16, 0))] * 4
-        + [pl.BlockSpec(memory_space=pl.ANY)],
-        out_specs=pl.BlockSpec((1, LA + 16, NX), lambda t: (t + first, 0, 0)),
+        aliases = {4: 0}
+    return pl.pallas_call(
+        functools.partial(sum_x_kernel, first=first),
+        in_specs=[pl.BlockSpec(memory_space=pltpu.VMEM)] * 4 + [pl.BlockSpec(memory_space=pl.ANY)],
+        out_specs=pl.BlockSpec(memory_space=pltpu.HBM),
         out_shape=hbm((tiles_all, LA + 16, NX), jnp.int16),
+        scratch_shapes=[
+            pltpu.VMEM((tiles, LA + 16, NX), jnp.int16),
+            pltpu.SemaphoreType.DMA((tiles,)),
+        ],
         input_output_aliases=aliases,
-        compiler_params=params(32),
+        compiler_params=pltpu.CompilerParams(vmem_limit_bytes=32 * 1024 * 1024),
         name="sum_x",
-    )(*parts, *parts, old)
+    )(*parts, old)
 
 
 def sum_tile_kernel(in_ref, o0, o1, o2, o3, acc_ref):
@@ -341,7 +430,7 @@
     )(a, *bs, stencil)
 
 
-def smooth_kernel(edge_ref, plane_ref, l1, l2, r1, r2, out_ref):
+def smooth_kernel(edge_ref, counts_ref, plane_ref, l1, l2, r1, r2, reads_ref, out_ref, back_ref):
     def halo(ref):
         table = ref[pl.ds(NY, 16), :].astype(jnp.int32).astype(jnp.float32)
         parts = [
@@ -366,19 +455,34 @@
     upper = step(plane, right, halo(r2))
     lower = jnp.where(edge_ref[0] > 0, lower, 0.0)
     upper = jnp.where(edge_ref[1] > 0, upper, 0.0)
-    out_ref[...] = step(lower, step(left, plane, right), upper).astype(jnp.bfloat16)
-
-
-def smooth(edges, plane, halos):
+    field = step(lower, step(left, plane, right), upper).astype(jnp.bfloat16)
+    out_ref[...] = field
+
+    readers, most = reads_ref.shape
+    lane = lax.broadcasted_iota(jnp.int32, (1, most), 1)
+    columns = lax.broadcasted_iota(jnp.int32, (most, NY), 1).astype(jnp.float32)
+    for t in range(readers):
+        ids = jnp.where(lane < counts_ref[t], reads_ref[pl.ds(t, 1), :], -1)
+        hot = jnp.where(columns == to_column(ids.astype(jnp.float32)), 1.0, 0.0)
+        lines = jnp.dot(hot.astype(jnp.bfloat16), field, preferred_element_type=jnp.float32)
+        back_ref[t] = lines.astype(jnp.bfloat16)
+
+
+def smooth(edges, counts, plane, halos, reads):
     vmem = pl.BlockSpec(memory_space=pltpu.VMEM)
+    smem = pl.BlockSpec(memory_space=pltpu.SMEM)
+    readers, most = reads.shape
     return pl.pallas_call(
         smooth_kernel,
-        in_specs=[pl.BlockSpec(memory_space=pltpu.SMEM)] + [vmem] * 5,
-        out_specs=vmem,
-        out_shape=jax.ShapeDtypeStruct((NY, NX), jnp.bfloat16),
+        in_specs=[smem, smem] + [vmem] * 6,
+        out_specs=[vmem, vmem],
+        out_shape=[
+            jax.ShapeDtypeStruct((NY, NX), jnp.bfloat16),
+            jax.ShapeDtypeStruct((readers, most, NX), jnp.bfloat16),
+        ],
         compiler_params=pltpu.CompilerParams(vmem_limit_bytes=32 * 1024 * 1024),
         name="smooth",
-    )(edges, plane, *halos)
+    )(edges, counts, plane, *halos, reads)
 
 
 def after_kernel(x_ref, *refs):
@@ -404,37 +508,23 @@
     here = lax.axis_index("cuts")
     here_x = here // 2
     here_core = here % 2
-    slots = send_slots[0]
+    place = jnp.stack([here_core, here_x]).astype(jnp.int32)
     counts = send_counts[0]
-    cap = slots.shape[1]
-    slot_index = jnp.arange(cap, dtype=jnp.int32)
-    usable = slot_index[None, :] < counts[:, None]
-    masked = jnp.where(usable, send_lines[0], -1)
-    tail = jnp.broadcast_to(counts[:, None], (tile_count, 128))
-    sheet = jnp.concatenate([masked, tail], axis=1)
+    flat_slots = send_slots.reshape(-1)
     swap = [(i, i ^ 1) for i in range(cut_count)]
-    flat_slots = slots.reshape(-1)
-
-    def line_codes(ids):
-        cut = ids // NY
-        y = ids % NY
-        mine = (ids >= 0) & (cut % 2 == here_core)
-        ahead = (cut // 2 - here_x) % 4
-        place = jnp.where(y < LA, ahead * LA + y, 4 * LA + ahead * LB + y - LA)
-        return jnp.where(mine, place, -1).reshape(tile_count, cap // CHUNK, CHUNK)
-
-    own_codes = line_codes(masked)
-
-    counts, sheet = lax.optimization_barrier((counts, sheet))
-    peer_sheet = lax.ppermute(sheet, "cuts", swap)
+
     rows, peer_rows = [], []
     for h in range(2):
-        if h:
-            counts, peer_sheet = lax.optimization_barrier((counts, peer_sheet))
-        rows.append(gather_rows(acquired, flat_slots, counts, h * tile_half, tile_half, cap))
+        rows.append(
+            gather_rows(acquired, flat_slots, counts, send_lines[0], h * tile_half, tile_half)
+        )
         peer_rows.append(lax.ppermute(rows[h], "cuts", swap))
-    peer_counts = peer_sheet[:, cap]
-    peer_codes = line_codes(peer_sheet[:, :cap])
+    cap = send_slots.shape[2]
+    peer_counts = [
+        (part[:, cap + 7, 0].astype(jnp.float32) * 64 + part[:, cap + 15, 0].astype(jnp.float32))
+        .astype(jnp.int32)
+        for part in peer_rows
+    ]
 
     def x_send(block, k):
         return lax.ppermute(block, "cuts", [(i, (i + 2 * k) % cut_count) for i in range(cut_count)])
@@ -443,11 +533,11 @@
     a_parts = []
     for h in range(2):
         *a_blocks, b_blocks = line_blocks(
-            rows[h], peer_rows[h], own_codes, peer_codes,
-            counts, peer_counts, b_blocks, h * tile_half, tile_count,
+            rows[h], peer_rows[h], counts, peer_counts[h], place,
+            b_blocks, h * tile_half, tile_count,
         )
         a_parts.append([a_blocks[0]] + [x_send(a_blocks[k], k) for k in (1, 2, 3)])
-    near = (a_parts[0][1], a_parts[0][3])
+    near = (a_parts[0][1][:16], a_parts[0][3][:16])
     b_blocks = after(b_blocks, near)
     b_arrived = lax.all_to_all(b_blocks, "tile", split_axis=0, concat_axis=0, tiled=True)
     a_sums = None
@@ -465,18 +555,9 @@
         return lax.ppermute(coded, ("cuts", "tile"), pairs)
 
     halos = [plane_send(1), plane_send(2), plane_send(-1), plane_send(-2)]
-    place = here * tile_count + lax.axis_index("tile")
-    edges = jnp.stack([place > 0, place < total - 1]).astype(jnp.int32)
-    field = smooth(edges, plane, halos)
-
-    read_ids = return_slots[0]
-    read_total = read_ids.shape[1]
-    usable_back = jnp.arange(read_total, dtype=jnp.int32)[None, :] < return_counts[0][:, None]
-    selector = jnp.where(usable_back, read_ids, -1).reshape(-1)[:, None] == jnp.arange(
-        NY, dtype=jnp.int32
-    )
-    outgoing = jnp.dot(selector.astype(jnp.bfloat16), field, preferred_element_type=jnp.float32)
-    outgoing = outgoing.astype(jnp.bfloat16).reshape(tile_count, read_total, NX)
+    spot = here * tile_count + lax.axis_index("tile")
+    edges = jnp.stack([spot > 0, spot < total - 1]).astype(jnp.int32)
+    field, outgoing = smooth(edges, return_counts[0], plane, halos, return_slots[0])
     returned = lax.all_to_all(outgoing, "tile", split_axis=0, concat_axis=0, tiled=True)
     return field[None], returned
 

time: 230 us -> 215 us (0.935)
  local copies, waits for them, and re-layouts: 8.81 us -> 4.64 us
  starting transfers between devices: 50.9 us -> 47.4 us
  waiting for transfers between devices: 54.2 us -> 50.8 us
    all_to_all x1, waiting for transfers between devices: 0.01 us -> 10.1 us  [local(): lax.all_to_all(b_blocks, 'tile', split_axis=0, concat_axis=0, tiled=True)]
    all_to_all x1, waiting for transfers between devices: 11.2 us -> 3.01 us  [local(): lax.all_to_all(a_sums, 'tile', split_axis=0, concat_axis=0, tiled=True)]
    pallas_call x5, Pallas kernels: 49.3 us -> 41.5 us  [the longest x2 33.6 us: line_blocks(): pl.pallas_call(functools.partial(lines_kernel, first=first, cap=cap), gri...]
    pallas_call x1, Pallas kernels: 2.79 us -> 9.5 us  [sum_tile(): pl.pallas_call(sum_tile_kernel, grid=(tiles,), in_specs=[pl.BlockSpec((1,...]
    ppermute x1 -> x0, waiting for transfers between devices: 5.86 us -> none  [local(): peer_sheet = lax.ppermute(sheet, 'cuts', swap)]
    all_to_all x1, starting transfers between devices: 12.2 us -> 6.91 us  [local(): lax.all_to_all(b_blocks, 'tile', split_axis=0, concat_axis=0, tiled=True)]
    unnamed x25 -> x19, local copies, waits for them, and re-layouts: 7.02 us -> 2.54 us
    ppermute x4, starting transfers between devices: 15.6 us -> 19.1 us  [plane_send(): return lax.ppermute(coded, ('cuts', 'tile'), pairs)]
  transfers between devices with their start and end apart: 18 -> 17, of which waited for: 7 -> 8; matrix products, arithmetic and copies ran while one was open for 0% -> 1% of each run, Pallas kernels for 28% -> 31%
where the time goes in v3:
time: 215 us; the launch traced here: 214 us
  Pallas kernels  85.3 us (40%)
  waiting for transfers between devices  50.8 us (24%)
  starting transfers between devices  47.4 us (22%)
  blocking collectives  22.8 us (11%)
  local copies, waits for them, and re-layouts  4.64 us (2%)
    ppermute x9, waiting for transfers between devices, x_send(): lax.ppermute(block, 'cuts', [(i, (i + 2 * k) % cut_count) for i in range(...  34.3 us
    pallas_call x2, Pallas kernels, line_blocks(): pl.pallas_call(functools.partial(lines_kernel, first=first, cap=cap), gri...  33.6 us
    pallas_call x2, Pallas kernels, gather_rows(): pl.pallas_call(body, grid_spec=pltpu.PrefetchScalarGridSpec(num_scalar_pr...  31.5 us
    all_to_all x1, blocking collectives, local(): lax.all_to_all(outgoing, 'tile', split_axis=0, concat_axis=0, tiled=True)  22.8 us
    ppermute x4, starting transfers between devices, plane_send(): return lax.ppermute(coded, ('cuts', 'tile'), pairs)  19.1 us
    ppermute x9, starting transfers between devices, x_send(): lax.ppermute(block, 'cuts', [(i, (i + 2 * k) % cut_count) for i in range(...  13.8 us
    all_to_all x1, waiting for transfers between devices, local(): lax.all_to_all(b_blocks, 'tile', split_axis=0, concat_axis=0, tiled=True)  10.1 us
    pallas_call x1, Pallas kernels, sum_tile(): pl.pallas_call(sum_tile_kernel, grid=(tiles,), in_specs=[pl.BlockSpec((1,...  9.5 us
  transfers between devices with their start and end apart: 17, of which 8 were waited for; matrix products, arithmetic and copies ran while one was open for 1% of the time, Pallas kernels for 31%

profile of v3, /device:TPU:1, one launch (start us, length us, event | category | flops | bytes accessed | tf_op | source)
XLA Modules:
  0.0 213.9 jit_solution(4304772925911589542)
XLA Ops:
  0.6 0.9 reshape.19.slots_ref
  1.5 0.9 copy-done.3
  2.4 0.7 copy-done.5
  3.1 13.9 %gather_rows.3.own_hbm = bf16[8,1296,256]{2,1,0:T(8,128)(2,1)} custom-call(s32[20480]{0:T(1024)S(1)} %reshape.19.slots_ref, s32[16]{0:T(128)S(1)} %bitcast.12, bf16[16384,256]{1,0:T(8,128)(2,1)} %acq_ref.3, s32[16,1280]{1,0:T(8,128)S(1)} %bitcast.9), custom_call_target="tpu_custom_call" | custom-call | bytes 40000000 | tf_op jit(solution)/shard_map/gather_rows/pallas_call | solution.py:125
  17.0 0.0 copy-start.6
  17.0 1.6 collective-permute-start.1
  18.6 17.6 %gather_rows.2.own_hbm = bf16[8,1296,256]{2,1,0:T(8,128)(2,1)} custom-call(s32[20480]{0:T(1024)S(1)} %reshape.19.slots_ref, s32[16]{0:T(128)S(1)} %bitcast.13, bf16[16384,256]{1,0:T(8,128)(2,1)} %acq_ref.3, s32[16,1280]{1,0:T(8,128)S(1)} %bitcast.10), custom_call_target="tpu_custom_call" | custom-call | bytes 40000000 | tf_op jit(solution)/shard_map/gather_rows/pallas_call | solution.py:125
  36.2 1.5 collective-permute-start
  37.7 0.1 pad_add_fusion.place_ref
  37.8 0.0 collective-permute-done.1.peer_hbm
  37.8 1.0 fusion.7.peer_n
  38.8 14.9 %line_blocks.2 = (s16[1168,256]{1,0:T(8,128)(2,1)}, s16[1168,256]{1,0:T(8,128)(2,1)}, s16[1168,256]{1,0:T(8,128)(2,1)}, s16[1168,256]{1,0:T(8,128)(2,1)}, s16[16,464,256]{2,1,0:T(8,128)(2,1)}) custom-call(s32[16]{0:T(128)S(1)} %bitcast.14, s32[8]{0:T(128)S(1)} %fusion.7.peer_n, s32[2]{0:T(128)S(1)} %pad_add_fusion.place_ref, ...), custom_call_target="tpu_custom_call" | custom-call | flops 10737418240 | bytes 40000000 | tf_op jit(solution)/shard_map/line_blocks/pallas_call | solution.py:272
  53.7 0.1 collective-permute-start.5
  53.8 2.7 %collective-permute-start.7 = (s16[1168,256]{1,0:T(8,128)(2,1)}, s16[1168,256]{1,0:T(8,128)(2,1)S(1)}, u32[]{:S(2)}, u32[]{:S(2)}) collective-permute-start(s16[1168,256]{1,0:T(8,128)(2,1)} %get-tuple-element.28), channel_id=1, source_target_pairs={{0,96},{16,112},{32,0},{48,16},{64,32},{80,48},{96,64},{112,80},{1... | collective-permute-start | bytes 1794056 | tf_op jit(solution)/shard_map/ppermute | solution.py:530
  56.4 1.0 fusion.6.peer_n
  57.4 18.7 %line_blocks.3 = (s16[1168,256]{1,0:T(8,128)(2,1)}, s16[1168,256]{1,0:T(8,128)(2,1)}, s16[1168,256]{1,0:T(8,128)(2,1)}, s16[1168,256]{1,0:T(8,128)(2,1)}, s16[16,464,256]{2,1,0:T(8,128)(2,1)}) custom-call(s32[16]{0:T(128)S(1)} %bitcast.15, s32[8]{0:T(128)S(1)} %fusion.6.peer_n, s32[2]{0:T(128)S(1)} %pad_add_fusion.place_ref, ...), custom_call_target="tpu_custom_call", output_to_operand_aliasing={{4}: (5, {})} | custom-call | flops 10737418240 | bytes 40000000 | tf_op jit(solution)/shard_map/line_blocks/pallas_call | solution.py:272
  76.1 0.6 slice.28.refs_0_
  76.7 0.6 slice.29.refs_1_
  77.3 6.9 %all-to-all-start.1 = ((s16[16,464,256]{2,1,0:T(8,128)(2,1)}), s16[16,464,256]{2,1,0:T(8,128)(2,1)}, u32[]{:S(2)}, u32[]{:S(2)}) async-start(s16[16,464,256]{2,1,0:T(8,128)(2,1)} %after.1), calls=%async_computation.1 | async-start | bytes 7602176 | tf_op jit(solution)/shard_map/all_to_all | solution.py:542
  84.2 1.1 collective-permute-start.6
  85.3 2.7 %collective-permute-start.2 = (s16[1168,256]{1,0:T(8,128)(2,1)}, s16[1168,256]{1,0:T(8,128)(2,1)S(1)}, u32[]{:S(2)}, u32[]{:S(2)}) collective-permute-start(s16[1168,256]{1,0:T(8,128)(2,1)} %get-tuple-element.22), channel_id=1, source_target_pairs={{0,32},{16,48},{32,64},{48,80},{64,96},{80,112},{96,0},{112,16},{1... | collective-permute-start | bytes 1794056 | tf_op jit(solution)/shard_map/ppermute | solution.py:530
  88.0 0.7 collective-permute-start.3
  88.7 1.7 collective-permute-start.4
  90.4 9.2 %collective-permute-done.6.p2 = s16[1168,256]{1,0:T(8,128)(2,1)S(1)} collective-permute-done((s16[1168,256]{1,0:T(8,128)(2,1)S(1)}, s16[1168,256]{1,0:T(8,128)(2,1)S(1)}, u32[]{:S(2)}, u32[]{:S(2)}) %collective-permute-start.6) | collective-permute-done | bytes 598048 | tf_op jit(solution)/shard_map/ppermute | solution.py:530
  99.6 2.8 %sum_x.2.alias_ref = s16[16,160,256]{2,1,0:T(8,128)(2,1)} custom-call(s16[1168,256]{1,0:T(8,128)(2,1)S(1)} %copy-done.1, s16[1168,256]{1,0:T(8,128)(2,1)S(1)} %collective-permute-done.5.p1, s16[1168,256]{1,0:T(8,128)(2,1)S(1)} %collective-permute-done.6.p2, s16[1168,256]{1,0:T(8,128)(2,1)S(1)} %collective-permute-done.7.p3, ...), custom_call_target="tpu_custom_call" | custom-call | tf_op jit(solution)/shard_map/sum_x/pallas_call | solution.py:333
  102.4 13.4 %collective-permute-done.2.p1 = s16[1168,256]{1,0:T(8,128)(2,1)S(1)} collective-permute-done((s16[1168,256]{1,0:T(8,128)(2,1)}, s16[1168,256]{1,0:T(8,128)(2,1)S(1)}, u32[]{:S(2)}, u32[]{:S(2)}) %collective-permute-start.2) | collective-permute-done | bytes 598048 | tf_op jit(solution)/shard_map/ppermute | solution.py:530
  115.9 9.4 %collective-permute-done.3.p2 = s16[1168,256]{1,0:T(8,128)(2,1)S(1)} collective-permute-done((s16[1168,256]{1,0:T(8,128)(2,1)}, s16[1168,256]{1,0:T(8,128)(2,1)S(1)}, u32[]{:S(2)}, u32[]{:S(2)}) %collective-permute-start.3) | collective-permute-done | bytes 598048 | tf_op jit(solution)/shard_map/ppermute | solution.py:530
  125.3 1.4 collective-permute-done.4.p3
  126.7 2.8 %sum_x.3 = s16[16,160,256]{2,1,0:T(8,128)(2,1)} custom-call(s16[1168,256]{1,0:T(8,128)(2,1)S(1)} %copy-done, s16[1168,256]{1,0:T(8,128)(2,1)S(1)} %collective-permute-done.2.p1, s16[1168,256]{1,0:T(8,128)(2,1)S(1)} %collective-permute-done.3.p2, s16[1168,256]{1,0:T(8,128)(2,1)S(1)} %collective-permute-done.4.p3, ...), custom_call_target="tpu_custom_call", output_to_operand_aliasing={{}: (4, {})} | custom-call | tf_op jit(solution)/shard_map/sum_x/pallas_call | solution.py:333
  129.5 0.0 copy-start.4
  129.5 0.0 copy-start.7
  129.5 10.1 %all-to-all-done.1.in_ref = s16[16,464,256]{2,1,0:T(8,128)(2,1)} async-done(((s16[16,464,256]{2,1,0:T(8,128)(2,1)}), s16[16,464,256]{2,1,0:T(8,128)(2,1)}, u32[]{:S(2)}, u32[]{:S(2)}) %all-to-all-start.1) | async-done | bytes 3801120 | tf_op jit(solution)/shard_map/all_to_all | solution.py:542
  139.6 4.5 %all-to-all-start = ((s16[16,160,256]{2,1,0:T(8,128)(2,1)}), s16[16,160,256]{2,1,0:T(8,128)(2,1)S(1)}, u32[]{:S(2)}, u32[]{:S(2)}) async-start(s16[16,160,256]{2,1,0:T(8,128)(2,1)} %sum_x.3), calls=%async_computation | async-start | bytes 2621440 | tf_op jit(solution)/shard_map/all_to_all | solution.py:546
  144.1 9.5 %sum_tile.1 = (s16[128,256]{1,0:T(8,128)(2,1)S(1)}, s16[128,256]{1,0:T(8,128)(2,1)S(1)}, s16[128,256]{1,0:T(8,128)(2,1)S(1)}, s16[128,256]{1,0:T(8,128)(2,1)S(1)}) custom-call(s16[16,464,256]{2,1,0:T(8,128)(2,1)} %all-to-all-done.1.in_ref), custom_call_target="tpu_custom_call" | custom-call | tf_op jit(solution)/shard_map/sum_tile/pallas_call | solution.py:372
  153.6 3.6 %collective-permute-start.10 = (s16[128,256]{1,0:T(8,128)(2,1)S(1)}, s16[128,256]{1,0:T(8,128)(2,1)S(1)}, u32[]{:S(2)}, u32[]{:S(2)}) collective-permute-start(s16[128,256]{1,0:T(8,128)(2,1)S(1)} %get-tuple-element.33), channel_id=1, source_target_pairs={{0,96},{16,112},{32,0},{48,16},{64,32},{80,48},{96,64},{112,80},{1... | collective-permute-start | bytes 196616 | tf_op jit(solution)/shard_map/ppermute | solution.py:530
  157.2 1.3 collective-permute-start.9
  158.5 3.0 %all-to-all-done.a_ref = s16[16,160,256]{2,1,0:T(8,128)(2,1)S(1)} async-done(((s16[16,160,256]{2,1,0:T(8,128)(2,1)}), s16[16,160,256]{2,1,0:T(8,128)(2,1)S(1)}, u32[]{:S(2)}, u32[]{:S(2)}) %all-to-all-start) | async-done | bytes 1310752 | tf_op jit(solution)/shard_map/all_to_all | solution.py:546
  161.5 0.7 collective-permute-done.8.b1
  162.2 2.8 %own_plane.1 = (f32[256,256]{1,0:T(8,128)S(1)}, s16[272,256]{1,0:T(8,128)(2,1)S(1)}) custom-call(s16[16,160,256]{2,1,0:T(8,128)(2,1)S(1)} %all-to-all-done.a_ref, s16[128,256]{1,0:T(8,128)(2,1)S(1)} %get-tuple-element.30.b0, s16[128,256]{1,0:T(8,128)(2,1)S(1)} %collective-permute-done.8.b1, s16[128,256]{1,0:T(8,128)(2,1)S(1)} %collective-permute-done.9.b2, ...), custom_call_target="tpu_custom_call" | custom-call | tf_op jit(solution)/shard_map/own_plane/pallas_call | solution.py:421
  165.0 3.3 %collective-permute-start.11 = (s16[272,256]{1,0:T(8,128)(2,1)S(1)}, s16[272,256]{1,0:T(8,128)(2,1)S(1)}, u32[]{:S(2)}, u32[]{:S(2)}) collective-permute-start(s16[272,256]{1,0:T(8,128)(2,1)S(1)} %get-tuple-element.35), channel_id=1, source_target_pairs={{0,1},{1,2},{2,3},{3,4},{4,5},{5,6},{6,7},{7,8},{8,9},{9,10},{10,1... | collective-permute-start | bytes 417800 | tf_op jit(solution)/shard_map/ppermute | solution.py:555
  168.3 4.3 %collective-permute-start.12 = (s16[272,256]{1,0:T(8,128)(2,1)S(1)}, s16[272,256]{1,0:T(8,128)(2,1)S(1)}, u32[]{:S(2)}, u32[]{:S(2)}) collective-permute-start(s16[272,256]{1,0:T(8,128)(2,1)S(1)} %get-tuple-element.35), channel_id=1, source_target_pairs={{0,2},{1,3},{2,4},{3,5},{4,6},{5,7},{6,8},{7,9},{8,10},{9,11},{10,... | collective-permute-start | bytes 417800 | tf_op jit(solution)/shard_map/ppermute | solution.py:555
  172.6 6.7 %collective-permute-start.13 = (s16[272,256]{1,0:T(8,128)(2,1)S(1)}, s16[272,256]{1,0:T(8,128)(2,1)S(1)}, u32[]{:S(2)}, u32[]{:S(2)}) collective-permute-start(s16[272,256]{1,0:T(8,128)(2,1)S(1)} %get-tuple-element.35), channel_id=1, source_target_pairs={{1,0},{2,1},{3,2},{4,3},{5,4},{6,5},{7,6},{8,7},{9,8},{10,9},{11,1... | collective-permute-start | bytes 417800 | tf_op jit(solution)/shard_map/ppermute | solution.py:555
  179.4 4.8 %collective-permute-start.14 = (s16[272,256]{1,0:T(8,128)(2,1)S(1)}, s16[272,256]{1,0:T(8,128)(2,1)S(1)}, u32[]{:S(2)}, u32[]{:S(2)}) collective-permute-start(s16[272,256]{1,0:T(8,128)(2,1)S(1)} %get-tuple-element.35), channel_id=1, source_target_pairs={{2,0},{3,1},{4,2},{5,3},{6,4},{7,5},{8,6},{9,7},{10,8},{11,9},{12,... | collective-permute-start | bytes 417800 | tf_op jit(solution)/shard_map/ppermute | solution.py:555
  184.2 0.1 add_convert_fusion.edge_ref
  184.3 3.5 %collective-permute-done.14.r2 = s16[272,256]{1,0:T(8,128)(2,1)S(1)} collective-permute-done((s16[272,256]{1,0:T(8,128)(2,1)S(1)}, s16[272,256]{1,0:T(8,128)(2,1)S(1)}, u32[]{:S(2)}, u32[]{:S(2)}) %collective-permute-start.14) | collective-permute-done | bytes 139296 | tf_op jit(solution)/shard_map/ppermute | solution.py:555
  187.7 2.4 %smooth.1 = (bf16[256,256]{1,0:T(8,128)(2,1)}, bf16[16,128,256]{2,1,0:T(8,128)(2,1)S(1)}) custom-call(s32[2]{0:T(128)S(1)} %add_convert_fusion.edge_ref, s32[16]{0:T(128)S(1)} %bitcast.16, f32[256,256]{1,0:T(8,128)S(1)} %get-tuple-element.34.plane_ref, s16[272,256]{1,0:T(8,128)(2,1)S(1)} %collective-permute-done.11.l1, ...), custom_call_target="tpu_custom_call" | custom-call | tf_op jit(solution)/shard_map/smooth/pallas_call | solution.py:475
  190.1 22.8 %all_to_all.15 = bf16[16,128,256]{2,1,0:T(8,128)(2,1)S(1)} all-to-all(bf16[16,128,256]{2,1,0:T(8,128)(2,1)S(1)} %get-tuple-element.37), channel_id=1, replica_groups=mesh['cuts'=8,'tile'=16] {'tile'}, dimensions={0} | all-to-all | bytes 2097152 | tf_op jit(solution)/shard_map/all_to_all | solution.py:561
  212.9 1.0 copy.16
  (24 shorter events, 0.1 us)
Async XLA Ops:
  1.5 0.9 copy-start.3
  2.4 0.7 copy-start.5
  17.0 21.7 %copy-start.6 = (s32[1,16]{1,0:T(1,128)S(1)}, s32[1,16]{1,0:T(1,128)}, u32[]{:S(2)}) copy-start(s32[1,16]{1,0:T(1,128)} %param.11) | copy-start | bytes 196
  17.0 20.7 %collective-permute-start.1 = (bf16[8,1296,256]{2,1,0:T(8,128)(2,1)}, bf16[8,1296,256]{2,1,0:T(8,128)(2,1)}, u32[]{:S(2)}, u32[]{:S(2)}) collective-permute-start(bf16[8,1296,256]{2,1,0:T(8,128)(2,1)} %gather_rows.3.own_hbm), channel_id=1, source_target_pairs={{0,16},{16,0},{32,48},{48,32},{64,80},{80,64},{96,112},{112,96},{1... | collective-permute-start | bytes 15925256 | tf_op jit(solution)/shard_map/ppermute | solution.py:521
  36.2 20.2 %collective-permute-start = (bf16[8,1296,256]{2,1,0:T(8,128)(2,1)}, bf16[8,1296,256]{2,1,0:T(8,128)(2,1)}, u32[]{:S(2)}, u32[]{:S(2)}) collective-permute-start(bf16[8,1296,256]{2,1,0:T(8,128)(2,1)} %gather_rows.2.own_hbm), channel_id=1, source_target_pairs={{0,16},{16,0},{32,48},{48,32},{64,80},{80,64},{96,112},{112,96},{1... | collective-permute-start | bytes 15925256 | tf_op jit(solution)/shard_map/ppermute | solution.py:521
  53.7 22.4 %collective-permute-start.5 = (s16[1168,256]{1,0:T(8,128)(2,1)}, s16[1168,256]{1,0:T(8,128)(2,1)S(1)}, u32[]{:S(2)}, u32[]{:S(2)}) collective-permute-start(s16[1168,256]{1,0:T(8,128)(2,1)} %get-tuple-element.26), channel_id=1, source_target_pairs={{0,32},{16,48},{32,64},{48,80},{64,96},{80,112},{96,0},{112,16},{1... | collective-permute-start | bytes 1794056 | tf_op jit(solution)/shard_map/ppermute | solution.py:530
  53.8 22.9 %collective-permute-start.7 = (s16[1168,256]{1,0:T(8,128)(2,1)}, s16[1168,256]{1,0:T(8,128)(2,1)S(1)}, u32[]{:S(2)}, u32[]{:S(2)}) collective-permute-start(s16[1168,256]{1,0:T(8,128)(2,1)} %get-tuple-element.28), channel_id=1, source_target_pairs={{0,96},{16,112},{32,0},{48,16},{64,32},{80,48},{96,64},{112,80},{1... | collective-permute-start | bytes 1794056 | tf_op jit(solution)/shard_map/ppermute | solution.py:530
  77.3 6.9 %copy-start.8 = (s16[1168,256]{1,0:T(8,128)(2,1)S(1)}, s16[1168,256]{1,0:T(8,128)(2,1)}, u32[]{:S(2)}) copy-start(s16[1168,256]{1,0:T(8,128)(2,1)} %get-tuple-element.27) | copy-start | bytes 1794052
  77.3 22.3 %copy-start.1 = (s16[1168,256]{1,0:T(8,128)(2,1)S(1)}, s16[1168,256]{1,0:T(8,128)(2,1)}, u32[]{:S(2)}) copy-start(s16[1168,256]{1,0:T(8,128)(2,1)} %get-tuple-element.25.p0) | copy-start | bytes 1794052
  77.3 49.4 %copy-start = (s16[1168,256]{1,0:T(8,128)(2,1)S(1)}, s16[1168,256]{1,0:T(8,128)(2,1)}, u32[]{:S(2)}) copy-start(s16[1168,256]{1,0:T(8,128)(2,1)} %get-tuple-element.21.p0) | copy-start | bytes 1794052
  77.3 62.3 %all-to-all-start.1 = ((s16[16,464,256]{2,1,0:T(8,128)(2,1)}), s16[16,464,256]{2,1,0:T(8,128)(2,1)}, u32[]{:S(2)}, u32[]{:S(2)}) async-start(s16[16,464,256]{2,1,0:T(8,128)(2,1)} %after.1), calls=%async_computation.1 | async-start | bytes 7602176 | tf_op jit(solution)/shard_map/all_to_all | solution.py:542
  84.2 15.4 %collective-permute-start.6 = (s16[1168,256]{1,0:T(8,128)(2,1)S(1)}, s16[1168,256]{1,0:T(8,128)(2,1)S(1)}, u32[]{:S(2)}, u32[]{:S(2)}) collective-permute-start(s16[1168,256]{1,0:T(8,128)(2,1)S(1)} %copy-done.8), channel_id=1, source_target_pairs={{0,64},{16,80},{32,96},{48,112},{64,0},{80,16},{96,32},{112,48},{1... | collective-permute-start | bytes 1794056 | tf_op jit(solution)/shard_map/ppermute | solution.py:530
  85.3 30.5 %collective-permute-start.2 = (s16[1168,256]{1,0:T(8,128)(2,1)}, s16[1168,256]{1,0:T(8,128)(2,1)S(1)}, u32[]{:S(2)}, u32[]{:S(2)}) collective-permute-start(s16[1168,256]{1,0:T(8,128)(2,1)} %get-tuple-element.22), channel_id=1, source_target_pairs={{0,32},{16,48},{32,64},{48,80},{64,96},{80,112},{96,0},{112,16},{1... | collective-permute-start | bytes 1794056 | tf_op jit(solution)/shard_map/ppermute | solution.py:530
  88.0 37.3 %collective-permute-start.3 = (s16[1168,256]{1,0:T(8,128)(2,1)}, s16[1168,256]{1,0:T(8,128)(2,1)S(1)}, u32[]{:S(2)}, u32[]{:S(2)}) collective-permute-start(s16[1168,256]{1,0:T(8,128)(2,1)} %get-tuple-element.23), channel_id=1, source_target_pairs={{0,64},{16,80},{32,96},{48,112},{64,0},{80,16},{96,32},{112,48},{1... | collective-permute-start | bytes 1794056 | tf_op jit(solution)/shard_map/ppermute | solution.py:530
  88.7 38.0 %collective-permute-start.4 = (s16[1168,256]{1,0:T(8,128)(2,1)}, s16[1168,256]{1,0:T(8,128)(2,1)S(1)}, u32[]{:S(2)}, u32[]{:S(2)}) collective-permute-start(s16[1168,256]{1,0:T(8,128)(2,1)} %get-tuple-element.24), channel_id=1, source_target_pairs={{0,96},{16,112},{32,0},{48,16},{64,32},{80,48},{96,64},{112,80},{1... | collective-permute-start | bytes 1794056 | tf_op jit(solution)/shard_map/ppermute | solution.py:530
  126.7 35.5 %copy-start.2 = (bf16[256,1024]{1,0:T(8,128)(2,1)S(1)}, bf16[256,1024]{1,0:T(8,128)(2,1)}, u32[]{:S(2)}) copy-start(bf16[256,1024]{1,0:T(8,128)(2,1)} %stencil_ref.1) | copy-start | bytes 1572868
  129.5 58.3 %copy-start.4 = (s32[1,16,128]{2,1,0:T(8,128)S(1)}, s32[1,16,128]{2,1,0:T(8,128)}, u32[]{:S(2)}) copy-start(s32[1,16,128]{2,1,0:T(8,128)} %param.12) | copy-start | bytes 24580
  129.5 58.3 %copy-start.7 = (s32[1,16]{1,0:T(1,128)S(1)}, s32[1,16]{1,0:T(1,128)}, u32[]{:S(2)}) copy-start(s32[1,16]{1,0:T(1,128)} %param.13) | copy-start | bytes 196
  139.6 21.9 %all-to-all-start = ((s16[16,160,256]{2,1,0:T(8,128)(2,1)}), s16[16,160,256]{2,1,0:T(8,128)(2,1)S(1)}, u32[]{:S(2)}, u32[]{:S(2)}) async-start(s16[16,160,256]{2,1,0:T(8,128)(2,1)} %sum_x.3), calls=%async_computation | async-start | bytes 2621440 | tf_op jit(solution)/shard_map/all_to_all | solution.py:546
  153.6 7.9 %collective-permute-start.10 = (s16[128,256]{1,0:T(8,128)(2,1)S(1)}, s16[128,256]{1,0:T(8,128)(2,1)S(1)}, u32[]{:S(2)}, u32[]{:S(2)}) collective-permute-start(s16[128,256]{1,0:T(8,128)(2,1)S(1)} %get-tuple-element.33), channel_id=1, source_target_pairs={{0,96},{16,112},{32,0},{48,16},{64,32},{80,48},{96,64},{112,80},{1... | collective-permute-start | bytes 196616 | tf_op jit(solution)/shard_map/ppermute | solution.py:530
  157.2 5.0 %collective-permute-start.8 = (s16[128,256]{1,0:T(8,128)(2,1)S(1)}, s16[128,256]{1,0:T(8,128)(2,1)S(1)}, u32[]{:S(2)}, u32[]{:S(2)}) collective-permute-start(s16[128,256]{1,0:T(8,128)(2,1)S(1)} %get-tuple-element.31), channel_id=1, source_target_pairs={{0,32},{16,48},{32,64},{48,80},{64,96},{80,112},{96,0},{112,16},{1... | collective-permute-start | bytes 196616 | tf_op jit(solution)/shard_map/ppermute | solution.py:530
  157.2 5.0 %collective-permute-start.9 = (s16[128,256]{1,0:T(8,128)(2,1)S(1)}, s16[128,256]{1,0:T(8,128)(2,1)S(1)}, u32[]{:S(2)}, u32[]{:S(2)}) collective-permute-start(s16[128,256]{1,0:T(8,128)(2,1)S(1)} %get-tuple-element.32), channel_id=1, source_target_pairs={{0,64},{16,80},{32,96},{48,112},{64,0},{80,16},{96,32},{112,48},{1... | collective-permute-start | bytes 196616 | tf_op jit(solution)/shard_map/ppermute | solution.py:530
  165.0 19.3 %collective-permute-start.11 = (s16[272,256]{1,0:T(8,128)(2,1)S(1)}, s16[272,256]{1,0:T(8,128)(2,1)S(1)}, u32[]{:S(2)}, u32[]{:S(2)}) collective-permute-start(s16[272,256]{1,0:T(8,128)(2,1)S(1)} %get-tuple-element.35), channel_id=1, source_target_pairs={{0,1},{1,2},{2,3},{3,4},{4,5},{5,6},{6,7},{7,8},{8,9},{9,10},{10,1... | collective-permute-start | bytes 417800 | tf_op jit(solution)/shard_map/ppermute | solution.py:555
  168.3 16.0 %collective-permute-start.12 = (s16[272,256]{1,0:T(8,128)(2,1)S(1)}, s16[272,256]{1,0:T(8,128)(2,1)S(1)}, u32[]{:S(2)}, u32[]{:S(2)}) collective-permute-start(s16[272,256]{1,0:T(8,128)(2,1)S(1)} %get-tuple-element.35), channel_id=1, source_target_pairs={{0,2},{1,3},{2,4},{3,5},{4,6},{5,7},{6,8},{7,9},{8,10},{9,11},{10,... | collective-permute-start | bytes 417800 | tf_op jit(solution)/shard_map/ppermute | solution.py:555
  172.6 11.7 %collective-permute-start.13 = (s16[272,256]{1,0:T(8,128)(2,1)S(1)}, s16[272,256]{1,0:T(8,128)(2,1)S(1)}, u32[]{:S(2)}, u32[]{:S(2)}) collective-permute-start(s16[272,256]{1,0:T(8,128)(2,1)S(1)} %get-tuple-element.35), channel_id=1, source_target_pairs={{1,0},{2,1},{3,2},{4,3},{5,4},{6,5},{7,6},{8,7},{9,8},{10,9},{11,1... | collective-permute-start | bytes 417800 | tf_op jit(solution)/shard_map/ppermute | solution.py:555
  179.4 8.4 %collective-permute-start.14 = (s16[272,256]{1,0:T(8,128)(2,1)S(1)}, s16[272,256]{1,0:T(8,128)(2,1)S(1)}, u32[]{:S(2)}, u32[]{:S(2)}) collective-permute-start(s16[272,256]{1,0:T(8,128)(2,1)S(1)} %get-tuple-element.35), channel_id=1, source_target_pairs={{2,0},{3,1},{4,2},{5,3},{6,4},{7,5},{8,6},{9,7},{10,8},{11,9},{12,... | collective-permute-start | bytes 417800 | tf_op jit(solution)/shard_map/ppermute | solution.py:555

commit v4 on v3

--- a/solution.py
+++ b/solution.py
@@ -11,7 +11,7 @@
 NX = 256
 NY = 256
 TAPS = 4
-LA = 144
+LA = 112
 LB = NY - LA
 ALPHA = math.log(2.0) / 64.0
 TOP = 32700.0
@@ -145,10 +145,9 @@
     )(slots, counts, acquired, lines)
 
 
-def lines_kernel(
-    own_n, peer_n, place_ref, own_hbm, peer_hbm, alias_ref,
-    a0_ref, a1_ref, a2_ref, a3_ref, b_ref,
-    acc_ref, code_ref, rows_ref, ids_ref, sem, *, first, cap,
+def sum_lines(
+    own_n, peer_n, place_ref, own_hbm, peer_hbm, acc_ref, spot_ref, rows_ref, ids_ref, sem,
+    *, first, cap, low, length,
 ):
     step = pl.program_id(0)
     last = pl.num_programs(0) - 1
@@ -197,27 +196,27 @@
         pair = ids_ref[slot, j].astype(jnp.float32).astype(jnp.int32)
         line = pair[0:8] * 64 + pair[8:16] - 1
         cut = line >> 8
-        y = line & (NY - 1)
-        mine = (line >= 0) & ((cut & 1) == here_core)
+        y = (line & (NY - 1)) - low
+        mine = (line >= 0) & ((cut & 1) == here_core) & (y >= 0) & (y < length)
         ahead = ((cut >> 1) - here_x) & 3
-        target = jnp.where(y < LA, ahead * LA + y, 4 * LA + ahead * LB + y - LA)
-        target = jnp.where(mine, target, -1)
+        target = jnp.where(mine, ahead * length + y, -1)
         for i in range(most):
             spot = i if j == 0 else own + i
-            code_ref[4, pl.ds(spot, 1), :] = target[i : i + 1].astype(jnp.float32)
+            spot_ref[pl.ds(spot, 1), :] = target[i : i + 1].astype(jnp.float32)
 
     acc_ref[...] = jnp.zeros(acc_ref.shape, jnp.float32)
-    position = lax.broadcasted_iota(jnp.int32, (CHUNK, CHUNK), 0).astype(jnp.float32)
+    block = 2 * length
+    position = lax.broadcasted_iota(jnp.int32, (block, CHUNK), 0).astype(jnp.float32)
 
     def add(start, width):
         rows = rows_ref[slot, pl.ds(pl.multiple_of(start * CHUNK, CHUNK), width * CHUNK), :]
-        ids = [code_ref[4, pl.ds(start + i, 1), :] for i in range(width)]
-        for m in range(acc_ref.shape[0] // CHUNK):
+        ids = [spot_ref[pl.ds(start + i, 1), :] for i in range(width)]
+        for m in range(2):
             hot = [
-                jnp.where(position == row - m * CHUNK, 1.0, 0.0).astype(jnp.bfloat16) for row in ids
+                jnp.where(position == row - m * block, 1.0, 0.0).astype(jnp.bfloat16) for row in ids
             ]
             hot = jnp.concatenate(hot, axis=1) if width > 1 else hot[0]
-            span = pl.ds(m * CHUNK, CHUNK)
+            span = pl.ds(m * block, block)
             acc_ref[span, :] += jnp.dot(hot, rows, preferred_element_type=jnp.float32)
 
     total = own + peer
@@ -233,18 +232,26 @@
         def _():
             add(total // 4 * 4, width)
 
-    outs = (a0_ref, a1_ref, a2_ref, a3_ref)
-    for k in range(4):
-        values, code = encode(acc_ref[pl.ds(k * LA, LA), :])
+    return [encode(acc_ref[pl.ds(k * length, length), :]) for k in range(4)]
+
+
+def tile_kernel(own_n, peer_n, place_ref, own_hbm, peer_hbm, alias_ref, b_ref, *scratch, **sizes):
+    blocks = sum_lines(own_n, peer_n, place_ref, own_hbm, peer_hbm, *scratch, **sizes)
+    for k, (values, _) in enumerate(blocks):
+        b_ref[0, pl.ds(k * LB, LB), :] = values
+    b_ref[0, pl.ds(4 * LB, 16), :] = code_block([pad_row(code) for _, code in blocks])
+
+
+def x_kernel(
+    own_n, peer_n, place_ref, own_hbm, peer_hbm, a0, a1, a2, a3, code_ref, *scratch, **sizes
+):
+    step = pl.program_id(0)
+    last = pl.num_programs(0) - 1
+    blocks = sum_lines(own_n, peer_n, place_ref, own_hbm, peer_hbm, *scratch, **sizes)
+    outs = (a0, a1, a2, a3)
+    for k, (values, code) in enumerate(blocks):
         outs[k][pl.ds(pl.multiple_of(step * LA, LA), LA), :] = values
         code_ref[k, pl.ds(step, 1), :] = pad_row(code)
-
-    codes = []
-    for k in range(4):
-        values, code = encode(acc_ref[pl.ds(4 * LA + k * LB, LB), :])
-        b_ref[0, pl.ds(k * LB, LB), :] = values
-        codes.append(pad_row(code))
-    b_ref[0, pl.ds(4 * LB, 16), :] = code_block(codes)
 
     @pl.when(step == last)
     def _():
@@ -256,45 +263,69 @@
     return jnp.concatenate([row, jnp.zeros((1, NX - row.shape[1]), jnp.float32)], axis=1)
 
 
-def line_blocks(own_rows, peer_rows, own_n, peer_n, place, b_old, first, tiles_all):
-    tiles, cap, _ = own_rows.shape
-    cap -= 16
-    a_shape = (tiles * LA + 16, NX)
-    own_rows = pltpu.with_memory_space_constraint(own_rows, pltpu.HBM)
-    peer_rows = pltpu.with_memory_space_constraint(peer_rows, pltpu.HBM)
-    args = [own_n, peer_n, place, own_rows, peer_rows]
-    aliases = {}
-    if b_old is None:
-        b_old = jnp.zeros((16, NX), jnp.int16)
-    else:
-        aliases = {5: 4}
-    args.append(b_old)
+def lines_call(body, name, ins, grid_tiles, cap, length, out_specs, out_shape, scratch, aliases):
     return pl.pallas_call(
-        functools.partial(lines_kernel, first=first, cap=cap),
+        body,
         grid_spec=pltpu.PrefetchScalarGridSpec(
             num_scalar_prefetch=3,
-            grid=(tiles,),
+            grid=(grid_tiles,),
             in_specs=[pl.BlockSpec(memory_space=pltpu.HBM)] * 2
-            + [pl.BlockSpec(memory_space=pl.ANY)],
-            out_specs=[pl.BlockSpec(a_shape, lambda t, *_: (0, 0))] * 4
-            + [pl.BlockSpec((1, 4 * LB + 16, NX), lambda t, *_: (t + first, 0, 0))],
-            scratch_shapes=[
-                pltpu.VMEM((4 * NY, NX), jnp.float32),
-                pltpu.VMEM((5, 16, NX), jnp.float32),
+            + [pl.BlockSpec(memory_space=pl.ANY)] * (len(ins) - 5),
+            out_specs=out_specs,
+            scratch_shapes=scratch
+            + [
+                pltpu.VMEM((4 * length, NX), jnp.float32),
+                pltpu.VMEM((16, NX), jnp.float32),
                 pltpu.VMEM((2, 2 * cap, NX), jnp.bfloat16),
                 pltpu.VMEM((2, 2, 16, NX), jnp.bfloat16),
                 pltpu.SemaphoreType.DMA((2, 2 * (cap // CHUNK + 1))),
             ],
         ),
-        out_shape=[hbm(a_shape, jnp.int16)] * 4
-        + [hbm((tiles_all, 4 * LB + 16, NX), jnp.int16)],
+        out_shape=out_shape,
         input_output_aliases=aliases,
         compiler_params=params(48),
         cost_estimate=pl.CostEstimate(
-            flops=2 * 1024 * 256 * 20480, transcendentals=0, bytes_accessed=40_000_000
+            flops=2 * 4 * length * 256 * 20480, transcendentals=0, bytes_accessed=20_000_000
         ),
-        name="line_blocks",
-    )(*args)
+        name=name,
+    )(*ins)
+
+
+def in_hbm(x):
+    return pltpu.with_memory_space_constraint(x, pltpu.HBM)
+
+
+def tile_blocks(own_rows, peer_rows, own_n, peer_n, place, b_old, first, tiles_all):
+    tiles, cap, _ = own_rows.shape
+    cap -= 16
+    if b_old is None:
+        b_old, aliases = jnp.zeros((16, NX), jnp.int16), {}
+    else:
+        aliases = {5: 0}
+    return lines_call(
+        functools.partial(tile_kernel, first=first, cap=cap, low=LA, length=LB),
+        "tile_blocks",
+        [own_n, peer_n, place, in_hbm(own_rows), in_hbm(peer_rows), b_old],
+        tiles, cap, LB,
+        pl.BlockSpec((1, 4 * LB + 16, NX), lambda t, *_: (t + first, 0, 0)),
+        hbm((tiles_all, 4 * LB + 16, NX), jnp.int16),
+        [], aliases,
+    )
+
+
+def x_blocks(own_rows, peer_rows, own_n, peer_n, place, first):
+    tiles, cap, _ = own_rows.shape
+    cap -= 16
+    shape = (tiles * LA + 16, NX)
+    return lines_call(
+        functools.partial(x_kernel, first=first, cap=cap, low=0, length=LA),
+        "x_blocks",
+        [own_n, peer_n, place, in_hbm(own_rows), in_hbm(peer_rows)],
+        tiles, cap, LA,
+        [pl.BlockSpec(shape, lambda t, *_: (0, 0))] * 4,
+        [hbm(shape, jnp.int16)] * 4,
+        [pltpu.VMEM((4, 16, NX), jnp.float32)], {},
+    )
 
 
 def code_row(block, index, length):
@@ -346,37 +377,30 @@
 
 
 def sum_tile_kernel(in_ref, o0, o1, o2, o3, acc_ref):
-    step = pl.program_id(0)
-
-    @pl.when(step == 0)
-    def _():
-        acc_ref[...] = jnp.zeros(acc_ref.shape, jnp.float32)
-
-    table = in_ref[0, pl.ds(4 * LB, 16), :].astype(jnp.int32).astype(jnp.float32)
-    for k in range(4):
-        acc_ref[pl.ds(k * LB, LB), :] += decode(
-            in_ref[0, pl.ds(k * LB, LB), :], table[k : k + 1, 0:LB]
-        )
-
-    @pl.when(step == pl.num_programs(0) - 1)
-    def _():
-        for k, out in enumerate((o0, o1, o2, o3)):
-            values, code = encode(acc_ref[pl.ds(k * LB, LB), :])
-            out[pl.ds(0, LB), :] = values
-            out[pl.ds(LB, 16), :] = code_block([pad_row(code)])
+    acc_ref[...] = jnp.zeros(acc_ref.shape, jnp.float32)
+
+    def body(t, carry):
+        table = in_ref[t, pl.ds(4 * LB, 16), :].astype(jnp.int32).astype(jnp.float32)
+        for k in range(4):
+            acc_ref[pl.ds(k * LB, LB), :] += decode(
+                in_ref[t, pl.ds(k * LB, LB), :], table[k : k + 1, 0:LB]
+            )
+        return carry
+
+    lax.fori_loop(0, in_ref.shape[0], body, 0)
+    for k, out in enumerate((o0, o1, o2, o3)):
+        values, code = encode(acc_ref[pl.ds(k * LB, LB), :])
+        out[pl.ds(0, LB), :] = values
+        out[pl.ds(LB, 16), :] = code_block([pad_row(code)])
 
 
 def sum_tile(arrived):
-    tiles, rows, _ = arrived.shape
     out_shape = (LB + 16, NX)
     return pl.pallas_call(
         sum_tile_kernel,
-        grid=(tiles,),
-        in_specs=[pl.BlockSpec((1, rows, NX), lambda t: (t, 0, 0))],
-        out_specs=[pl.BlockSpec(out_shape, lambda t: (0, 0))] * 4,
         out_shape=[jax.ShapeDtypeStruct(out_shape, jnp.int16)] * 4,
         scratch_shapes=[pltpu.VMEM((4 * LB, NX), jnp.float32)],
-        compiler_params=params(32),
+        compiler_params=pltpu.CompilerParams(vmem_limit_bytes=32 * 1024 * 1024),
         name="sum_tile",
     )(arrived)
 
@@ -485,22 +509,6 @@
     )(edges, counts, plane, *halos, reads)
 
 
-def after_kernel(x_ref, *refs):
-    del x_ref, refs
-
-
-def after(x, others):
-    anywhere = pl.BlockSpec(memory_space=pl.ANY)
-    return pl.pallas_call(
-        after_kernel,
-        in_specs=[anywhere] * (1 + len(others)),
-        out_specs=anywhere,
-        out_shape=hbm(x.shape, x.dtype),
-        input_output_aliases={0: 0},
-        name="after",
-    )(x, *others)
-
-
 def local(acquired, stencil, send_slots, send_lines, send_counts, return_slots, return_counts):
     tile_count = lax.axis_size("tile")
     cut_count = lax.axis_size("cuts")
@@ -530,19 +538,16 @@
         return lax.ppermute(block, "cuts", [(i, (i + 2 * k) % cut_count) for i in range(cut_count)])
 
     b_blocks = None
-    a_parts = []
     for h in range(2):
-        *a_blocks, b_blocks = line_blocks(
-            rows[h], peer_rows[h], counts, peer_counts[h], place,
-            b_blocks, h * tile_half, tile_count,
+        b_blocks = tile_blocks(
+            rows[h], peer_rows[h], counts, peer_counts[h], place, b_blocks, h * tile_half, tile_count
         )
-        a_parts.append([a_blocks[0]] + [x_send(a_blocks[k], k) for k in (1, 2, 3)])
-    near = (a_parts[0][1][:16], a_parts[0][3][:16])
-    b_blocks = after(b_blocks, near)
     b_arrived = lax.all_to_all(b_blocks, "tile", split_axis=0, concat_axis=0, tiled=True)
     a_sums = None
     for h in range(2):
-        a_sums = sum_x(a_parts[h], a_sums, h * tile_half, tile_count)
+        a_blocks = x_blocks(rows[h], peer_rows[h], counts, peer_counts[h], place, h * tile_half)
+        parts = [a_blocks[0]] + [x_send(a_blocks[k], k) for k in (1, 2, 3)]
+        a_sums = sum_x(parts, a_sums, h * tile_half, tile_count)
     a_arrived = lax.all_to_all(a_sums, "tile", split_axis=0, concat_axis=0, tiled=True)
     b_sums = sum_tile(b_arrived)
     b_final = [b_sums[0]] + [x_send(b_sums[k], k) for k in (1, 2, 3)]

time: 215 us -> 225 us (1.047)
  Pallas kernels: 85.3 us -> 91.2 us
  blocking collectives: 22.8 us -> 25.5 us
    all_to_all x1, waiting for transfers between devices: 10.1 us -> 0.01 us  [local(): lax.all_to_all(b_blocks, 'tile', split_axis=0, concat_axis=0, tiled=True)]
    pallas_call x4 -> x5, Pallas kernels: 43.1 us -> 51.3 us  [the longest x4 45.9 us: lines_call(): pl.pallas_call(body, grid_spec=pltpu.PrefetchScalarGridSpec(num_scalar_pr...]
    ppermute x2, waiting for transfers between devices: 0.01 us -> 8.01 us  [local(): peer_rows.append(lax.ppermute(rows[h], 'cuts', swap))]
    ppermute x4, starting transfers between devices: 19.1 us -> 15.9 us  [plane_send(): return lax.ppermute(coded, ('cuts', 'tile'), pairs)]
    all_to_all x1, blocking collectives: 22.8 us -> 25.5 us  [local(): lax.all_to_all(outgoing, 'tile', split_axis=0, concat_axis=0, tiled=True)]
  transfers between devices with their start and end apart: 17 -> 17, of which waited for: 8 -> 7; matrix products, arithmetic and copies ran while one was open for 1% -> 1% of each run, Pallas kernels for 31% -> 23%
where the time goes in v4:
time: 225 us; the launch traced here: 222 us
  Pallas kernels  91.2 us (41%)
  waiting for transfers between devices  51 us (23%)
  starting transfers between devices  47.1 us (21%)
  blocking collectives  25.5 us (11%)
  local copies, waits for them, and re-layouts  4.47 us (2%)
    pallas_call x4, Pallas kernels, lines_call(): pl.pallas_call(body, grid_spec=pltpu.PrefetchScalarGridSpec(num_scalar_pr...  45.9 us
    ppermute x9, waiting for transfers between devices, x_send(): lax.ppermute(block, 'cuts', [(i, (i + 2 * k) % cut_count) for i in range(...  34.4 us
    pallas_call x2, Pallas kernels, gather_rows(): pl.pallas_call(body, grid_spec=pltpu.PrefetchScalarGridSpec(num_scalar_pr...  29.7 us
    all_to_all x1, blocking collectives, local(): lax.all_to_all(outgoing, 'tile', split_axis=0, concat_axis=0, tiled=True)  25.5 us
    ppermute x4, starting transfers between devices, plane_send(): return lax.ppermute(coded, ('cuts', 'tile'), pairs)  15.9 us
    ppermute x9, starting transfers between devices, x_send(): lax.ppermute(block, 'cuts', [(i, (i + 2 * k) % cut_count) for i in range(...  14.2 us
    ppermute x2, waiting for transfers between devices, local(): peer_rows.append(lax.ppermute(rows[h], 'cuts', swap))  8.01 us
    all_to_all x1, starting transfers between devices, local(): lax.all_to_all(b_blocks, 'tile', split_axis=0, concat_axis=0, tiled=True)  7.93 us
  transfers between devices with their start and end apart: 17, of which 7 were waited for; matrix products, arithmetic and copies ran while one was open for 1% of the time, Pallas kernels for 23%

profile of v4, /device:TPU:1, one launch (start us, length us, event | category | flops | bytes accessed | tf_op | source)
XLA Modules:
  0.0 222.2 jit_solution(15305262203153802080)
XLA Ops:
  0.6 0.9 reshape.19.slots_ref
  1.5 0.9 copy-done.3
  2.4 0.7 copy-done.5
  3.1 12.7 %gather_rows.2.own_hbm = bf16[8,1296,256]{2,1,0:T(8,128)(2,1)} custom-call(s32[20480]{0:T(1024)S(1)} %reshape.19.slots_ref, s32[16]{0:T(128)S(1)} %bitcast.12, bf16[16384,256]{1,0:T(8,128)(2,1)} %acq_ref.3, s32[16,1280]{1,0:T(8,128)S(1)} %bitcast.9), custom_call_target="tpu_custom_call" | custom-call | bytes 40000000 | tf_op jit(solution)/shard_map/gather_rows/pallas_call | solution.py:125
  15.8 2.3 %collective-permute-start = (bf16[8,1296,256]{2,1,0:T(8,128)(2,1)}, bf16[8,1296,256]{2,1,0:T(8,128)(2,1)}, u32[]{:S(2)}, u32[]{:S(2)}) collective-permute-start(bf16[8,1296,256]{2,1,0:T(8,128)(2,1)} %gather_rows.2.own_hbm), channel_id=1, source_target_pairs={{0,16},{16,0},{32,48},{48,32},{64,80},{80,64},{96,112},{112,96},{1... | collective-permute-start | bytes 15925256 | tf_op jit(solution)/shard_map/ppermute | solution.py:529
  18.1 17.0 %gather_rows.3.own_hbm = bf16[8,1296,256]{2,1,0:T(8,128)(2,1)} custom-call(s32[20480]{0:T(1024)S(1)} %reshape.19.slots_ref, s32[16]{0:T(128)S(1)} %bitcast.13, bf16[16384,256]{1,0:T(8,128)(2,1)} %acq_ref.3, s32[16,1280]{1,0:T(8,128)S(1)} %bitcast.10), custom_call_target="tpu_custom_call" | custom-call | bytes 40000000 | tf_op jit(solution)/shard_map/gather_rows/pallas_call | solution.py:125
  35.0 0.1 collective-permute-start.4
  35.1 0.1 pad_add_fusion.place_ref
  35.2 1.0 fusion.6.peer_n
  36.2 8.0 %collective-permute-done.4.peer_hbm = bf16[8,1296,256]{2,1,0:T(8,128)(2,1)} collective-permute-done((bf16[8,1296,256]{2,1,0:T(8,128)(2,1)}, bf16[8,1296,256]{2,1,0:T(8,128)(2,1)}, u32[]{:S(2)}, u32[]{:S(2)}) %collective-permute-start.4) | collective-permute-done | bytes 5308448 | tf_op jit(solution)/shard_map/ppermute | solution.py:529
  44.2 1.0 fusion.7.peer_n
  45.2 12.6 %tile_blocks.2.alias_ref = s16[16,592,256]{2,1,0:T(8,128)(2,1)} custom-call(s32[16]{0:T(128)S(1)} %bitcast.14, s32[8]{0:T(128)S(1)} %fusion.7.peer_n, s32[2]{0:T(128)S(1)} %pad_add_fusion.place_ref, bf16[8,1296,256]{2,1,0:T(8,128)(2,1)} %gather_rows.3.own_hbm, bf16[8,1296,256]{2,1,0:T(8,128)(2,1)} %collective-permute-done.4.peer_hbm, ...), custom_call_target="tpu_custom_call" | custom-call | flops 6039797760 | bytes 20000000 | tf_op jit(solution)/shard_map/tile_blocks/pallas_call | solution.py:267
  57.8 10.6 %tile_blocks.3 = s16[16,592,256]{2,1,0:T(8,128)(2,1)} custom-call(s32[16]{0:T(128)S(1)} %bitcast.15, s32[8]{0:T(128)S(1)} %fusion.6.peer_n, s32[2]{0:T(128)S(1)} %pad_add_fusion.place_ref, bf16[8,1296,256]{2,1,0:T(8,128)(2,1)} %gather_rows.2.own_hbm, bf16[8,1296,256]{2,1,0:T(8,128)(2,1)} %collective-permute-done.peer_hbm, ...), custom_call_target="tpu_custom_call", output_to_operand_aliasing={{}: (5, {})} | custom-call | flops 6039797760 | bytes 20000000 | tf_op jit(solution)/shard_map/tile_blocks/pallas_call | solution.py:267
  68.5 7.9 %all-to-all-start.1 = ((s16[16,592,256]{2,1,0:T(8,128)(2,1)}), s16[16,592,256]{2,1,0:T(8,128)(2,1)}, u32[]{:S(2)}, u32[]{:S(2)}) async-start(s16[16,592,256]{2,1,0:T(8,128)(2,1)} %tile_blocks.3), calls=%async_computation.1 | async-start | bytes 9699328 | tf_op jit(solution)/shard_map/all_to_all | solution.py:545
  76.4 12.2 %x_blocks.3 = (s16[912,256]{1,0:T(8,128)(2,1)}, s16[912,256]{1,0:T(8,128)(2,1)}, s16[912,256]{1,0:T(8,128)(2,1)}, s16[912,256]{1,0:T(8,128)(2,1)}) custom-call(s32[16]{0:T(128)S(1)} %bitcast.16, s32[8]{0:T(128)S(1)} %fusion.7.peer_n, s32[2]{0:T(128)S(1)} %pad_add_fusion.place_ref, bf16[8,1296,256]{2,1,0:T(8,128)(2,1)} %gather_rows.3.own_hbm, ...), custom_call_target="tpu_custom_call" | custom-call | flops 4697620480 | bytes 20000000 | tf_op jit(solution)/shard_map/x_blocks/pallas_call | solution.py:267
  88.6 0.0 copy-start.2
  88.6 2.7 %collective-permute-start.5 = (s16[912,256]{1,0:T(8,128)(2,1)}, s16[912,256]{1,0:T(8,128)(2,1)S(1)}, u32[]{:S(2)}, u32[]{:S(2)}) collective-permute-start(s16[912,256]{1,0:T(8,128)(2,1)} %get-tuple-element.23), channel_id=1, source_target_pairs={{0,32},{16,48},{32,64},{48,80},{64,96},{80,112},{96,0},{112,16},{1... | collective-permute-start | bytes 1400840 | tf_op jit(solution)/shard_map/ppermute | solution.py:538
  91.3 10.5 %x_blocks.2 = (s16[912,256]{1,0:T(8,128)(2,1)}, s16[912,256]{1,0:T(8,128)(2,1)}, s16[912,256]{1,0:T(8,128)(2,1)}, s16[912,256]{1,0:T(8,128)(2,1)}) custom-call(s32[16]{0:T(128)S(1)} %bitcast.17, s32[8]{0:T(128)S(1)} %fusion.6.peer_n, s32[2]{0:T(128)S(1)} %pad_add_fusion.place_ref, bf16[8,1296,256]{2,1,0:T(8,128)(2,1)} %gather_rows.2.own_hbm, ...), custom_call_target="tpu_custom_call" | custom-call | flops 4697620480 | bytes 20000000 | tf_op jit(solution)/shard_map/x_blocks/pallas_call | solution.py:267
  101.8 1.5 collective-permute-start.1
  103.3 1.3 collective-permute-start.6
  104.7 2.0 collective-permute-start.7
  106.6 0.3 collective-permute-start.2
  106.9 1.6 collective-permute-start.3
  108.5 16.7 %collective-permute-done.6.p2 = s16[912,256]{1,0:T(8,128)(2,1)S(1)} collective-permute-done((s16[912,256]{1,0:T(8,128)(2,1)S(1)}, s16[912,256]{1,0:T(8,128)(2,1)S(1)}, u32[]{:S(2)}, u32[]{:S(2)}) %collective-permute-start.6) | collective-permute-done | bytes 466976 | tf_op jit(solution)/shard_map/ppermute | solution.py:538
  125.2 1.0 collective-permute-done.7.p3
  126.2 2.5 %sum_x.2.alias_ref = s16[16,128,256]{2,1,0:T(8,128)(2,1)} custom-call(s16[912,256]{1,0:T(8,128)(2,1)S(1)} %copy-done.2, s16[912,256]{1,0:T(8,128)(2,1)S(1)} %collective-permute-done.5.p1, s16[912,256]{1,0:T(8,128)(2,1)S(1)} %collective-permute-done.6.p2, s16[912,256]{1,0:T(8,128)(2,1)S(1)} %collective-permute-done.7.p3, ...), custom_call_target="tpu_custom_call" | custom-call | tf_op jit(solution)/shard_map/sum_x/pallas_call | solution.py:364
  128.7 6.4 %collective-permute-done.2.p2 = s16[912,256]{1,0:T(8,128)(2,1)S(1)} collective-permute-done((s16[912,256]{1,0:T(8,128)(2,1)}, s16[912,256]{1,0:T(8,128)(2,1)S(1)}, u32[]{:S(2)}, u32[]{:S(2)}) %collective-permute-start.2) | collective-permute-done | bytes 466976 | tf_op jit(solution)/shard_map/ppermute | solution.py:538
  135.1 10.3 %collective-permute-done.3.p3 = s16[912,256]{1,0:T(8,128)(2,1)S(1)} collective-permute-done((s16[912,256]{1,0:T(8,128)(2,1)}, s16[912,256]{1,0:T(8,128)(2,1)S(1)}, u32[]{:S(2)}, u32[]{:S(2)}) %collective-permute-start.3) | collective-permute-done | bytes 466976 | tf_op jit(solution)/shard_map/ppermute | solution.py:538
  145.4 1.0 copy-done.1
  146.4 2.5 %sum_x.3 = s16[16,128,256]{2,1,0:T(8,128)(2,1)} custom-call(s16[912,256]{1,0:T(8,128)(2,1)S(1)} %copy-done.1, s16[912,256]{1,0:T(8,128)(2,1)S(1)} %collective-permute-done.1.p1, s16[912,256]{1,0:T(8,128)(2,1)S(1)} %collective-permute-done.2.p2, s16[912,256]{1,0:T(8,128)(2,1)S(1)} %collective-permute-done.3.p3, ...), custom_call_target="tpu_custom_call", output_to_operand_aliasing={{}: (4, {})} | custom-call | tf_op jit(solution)/shard_map/sum_x/pallas_call | solution.py:364
  149.0 0.0 copy-start.4
  149.0 0.0 copy-start.7
  149.0 6.7 %all-to-all-start = ((s16[16,128,256]{2,1,0:T(8,128)(2,1)}), s16[16,128,256]{2,1,0:T(8,128)(2,1)S(1)}, u32[]{:S(2)}, u32[]{:S(2)}) async-start(s16[16,128,256]{2,1,0:T(8,128)(2,1)} %sum_x.3), calls=%async_computation | async-start | bytes 2097152 | tf_op jit(solution)/shard_map/all_to_all | solution.py:551
  155.7 5.4 %sum_tile.1 = (s16[160,256]{1,0:T(8,128)(2,1)S(1)}, s16[160,256]{1,0:T(8,128)(2,1)S(1)}, s16[160,256]{1,0:T(8,128)(2,1)S(1)}, s16[160,256]{1,0:T(8,128)(2,1)S(1)}) custom-call(s16[16,592,256]{2,1,0:T(8,128)(2,1)} %all-to-all-done.1.in_ref), custom_call_target="tpu_custom_call" | custom-call | tf_op jit(solution)/shard_map/sum_tile/pallas_call | solution.py:399
  161.2 1.5 collective-permute-start.8
  162.7 3.0 %collective-permute-start.9 = (s16[160,256]{1,0:T(8,128)(2,1)S(1)}, s16[160,256]{1,0:T(8,128)(2,1)S(1)}, u32[]{:S(2)}, u32[]{:S(2)}) collective-permute-start(s16[160,256]{1,0:T(8,128)(2,1)S(1)} %get-tuple-element.28), channel_id=1, source_target_pairs={{0,64},{16,80},{32,96},{48,112},{64,0},{80,16},{96,32},{112,48},{1... | collective-permute-start | bytes 245768 | tf_op jit(solution)/shard_map/ppermute | solution.py:538
  165.7 0.2 collective-permute-start.10
  165.9 5.1 %all-to-all-done.a_ref = s16[16,128,256]{2,1,0:T(8,128)(2,1)S(1)} async-done(((s16[16,128,256]{2,1,0:T(8,128)(2,1)}), s16[16,128,256]{2,1,0:T(8,128)(2,1)S(1)}, u32[]{:S(2)}, u32[]{:S(2)}) %all-to-all-start) | async-done | bytes 1048608 | tf_op jit(solution)/shard_map/all_to_all | solution.py:551
  171.0 2.7 %own_plane.1 = (f32[256,256]{1,0:T(8,128)S(1)}, s16[272,256]{1,0:T(8,128)(2,1)S(1)}) custom-call(s16[16,128,256]{2,1,0:T(8,128)(2,1)S(1)} %all-to-all-done.a_ref, s16[160,256]{1,0:T(8,128)(2,1)S(1)} %get-tuple-element.26.b0, s16[160,256]{1,0:T(8,128)(2,1)S(1)} %collective-permute-done.8.b1, s16[160,256]{1,0:T(8,128)(2,1)S(1)} %collective-permute-done.9.b2, ...), custom_call_target="tpu_custom_call" | custom-call | tf_op jit(solution)/shard_map/own_plane/pallas_call | solution.py:445
  173.8 2.4 %collective-permute-start.11 = (s16[272,256]{1,0:T(8,128)(2,1)S(1)}, s16[272,256]{1,0:T(8,128)(2,1)S(1)}, u32[]{:S(2)}, u32[]{:S(2)}) collective-permute-start(s16[272,256]{1,0:T(8,128)(2,1)S(1)} %get-tuple-element.31), channel_id=1, source_target_pairs={{0,1},{1,2},{2,3},{3,4},{4,5},{5,6},{6,7},{7,8},{8,9},{9,10},{10,1... | collective-permute-start | bytes 417800 | tf_op jit(solution)/shard_map/ppermute | solution.py:560
  176.1 4.3 %collective-permute-start.12 = (s16[272,256]{1,0:T(8,128)(2,1)S(1)}, s16[272,256]{1,0:T(8,128)(2,1)S(1)}, u32[]{:S(2)}, u32[]{:S(2)}) collective-permute-start(s16[272,256]{1,0:T(8,128)(2,1)S(1)} %get-tuple-element.31), channel_id=1, source_target_pairs={{0,2},{1,3},{2,4},{3,5},{4,6},{5,7},{6,8},{7,9},{8,10},{9,11},{10,... | collective-permute-start | bytes 417800 | tf_op jit(solution)/shard_map/ppermute | solution.py:560
  180.4 5.6 %collective-permute-start.13 = (s16[272,256]{1,0:T(8,128)(2,1)S(1)}, s16[272,256]{1,0:T(8,128)(2,1)S(1)}, u32[]{:S(2)}, u32[]{:S(2)}) collective-permute-start(s16[272,256]{1,0:T(8,128)(2,1)S(1)} %get-tuple-element.31), channel_id=1, source_target_pairs={{1,0},{2,1},{3,2},{4,3},{5,4},{6,5},{7,6},{8,7},{9,8},{10,9},{11,1... | collective-permute-start | bytes 417800 | tf_op jit(solution)/shard_map/ppermute | solution.py:560
  186.0 3.6 %collective-permute-start.14 = (s16[272,256]{1,0:T(8,128)(2,1)S(1)}, s16[272,256]{1,0:T(8,128)(2,1)S(1)}, u32[]{:S(2)}, u32[]{:S(2)}) collective-permute-start(s16[272,256]{1,0:T(8,128)(2,1)S(1)} %get-tuple-element.31), channel_id=1, source_target_pairs={{2,0},{3,1},{4,2},{5,3},{6,4},{7,5},{8,6},{9,7},{10,8},{11,9},{12,... | collective-permute-start | bytes 417800 | tf_op jit(solution)/shard_map/ppermute | solution.py:560
  189.7 0.1 add_convert_fusion.edge_ref
  189.8 3.6 %collective-permute-done.14.r2 = s16[272,256]{1,0:T(8,128)(2,1)S(1)} collective-permute-done((s16[272,256]{1,0:T(8,128)(2,1)S(1)}, s16[272,256]{1,0:T(8,128)(2,1)S(1)}, u32[]{:S(2)}, u32[]{:S(2)}) %collective-permute-start.14) | collective-permute-done | bytes 139296 | tf_op jit(solution)/shard_map/ppermute | solution.py:560
  193.4 2.4 %smooth.1 = (bf16[256,256]{1,0:T(8,128)(2,1)}, bf16[16,128,256]{2,1,0:T(8,128)(2,1)S(1)}) custom-call(s32[2]{0:T(128)S(1)} %add_convert_fusion.edge_ref, s32[16]{0:T(128)S(1)} %bitcast.18, f32[256,256]{1,0:T(8,128)S(1)} %get-tuple-element.30.plane_ref, s16[272,256]{1,0:T(8,128)(2,1)S(1)} %collective-permute-done.11.l1, ...), custom_call_target="tpu_custom_call" | custom-call | tf_op jit(solution)/shard_map/smooth/pallas_call | solution.py:499
  195.8 25.5 %all_to_all.15 = bf16[16,128,256]{2,1,0:T(8,128)(2,1)S(1)} all-to-all(bf16[16,128,256]{2,1,0:T(8,128)(2,1)S(1)} %get-tuple-element.33), channel_id=1, replica_groups=mesh['cuts'=8,'tile'=16] {'tile'}, dimensions={0} | all-to-all | bytes 2097152 | tf_op jit(solution)/shard_map/all_to_all | solution.py:566
  221.3 1.0 copy.14
  (25 shorter events, 0.1 us)
Async XLA Ops:
  1.5 0.9 copy-start.3
  2.4 0.7 copy-start.5
  15.8 29.4 %copy-start.6 = (s32[1,16]{1,0:T(1,128)S(1)}, s32[1,16]{1,0:T(1,128)}, u32[]{:S(2)}) copy-start(s32[1,16]{1,0:T(1,128)} %param.11) | copy-start | bytes 196
  15.8 19.5 %collective-permute-start = (bf16[8,1296,256]{2,1,0:T(8,128)(2,1)}, bf16[8,1296,256]{2,1,0:T(8,128)(2,1)}, u32[]{:S(2)}, u32[]{:S(2)}) collective-permute-start(bf16[8,1296,256]{2,1,0:T(8,128)(2,1)} %gather_rows.2.own_hbm), channel_id=1, source_target_pairs={{0,16},{16,0},{32,48},{48,32},{64,80},{80,64},{96,112},{112,96},{1... | collective-permute-start | bytes 15925256 | tf_op jit(solution)/shard_map/ppermute | solution.py:529
  35.0 9.2 %collective-permute-start.4 = (bf16[8,1296,256]{2,1,0:T(8,128)(2,1)}, bf16[8,1296,256]{2,1,0:T(8,128)(2,1)}, u32[]{:S(2)}, u32[]{:S(2)}) collective-permute-start(bf16[8,1296,256]{2,1,0:T(8,128)(2,1)} %gather_rows.3.own_hbm), channel_id=1, source_target_pairs={{0,16},{16,0},{32,48},{48,32},{64,80},{80,64},{96,112},{112,96},{1... | collective-permute-start | bytes 15925256 | tf_op jit(solution)/shard_map/ppermute | solution.py:529
  68.5 80.5 %all-to-all-start.1 = ((s16[16,592,256]{2,1,0:T(8,128)(2,1)}), s16[16,592,256]{2,1,0:T(8,128)(2,1)}, u32[]{:S(2)}, u32[]{:S(2)}) async-start(s16[16,592,256]{2,1,0:T(8,128)(2,1)} %tile_blocks.3), calls=%async_computation.1 | async-start | bytes 9699328 | tf_op jit(solution)/shard_map/all_to_all | solution.py:545
  88.6 14.7 %copy-start.9 = (s16[912,256]{1,0:T(8,128)(2,1)S(1)}, s16[912,256]{1,0:T(8,128)(2,1)}, u32[]{:S(2)}) copy-start(s16[912,256]{1,0:T(8,128)(2,1)} %get-tuple-element.24) | copy-start | bytes 1400836
  88.6 16.1 %copy-start.8 = (s16[912,256]{1,0:T(8,128)(2,1)S(1)}, s16[912,256]{1,0:T(8,128)(2,1)}, u32[]{:S(2)}) copy-start(s16[912,256]{1,0:T(8,128)(2,1)} %get-tuple-element.25) | copy-start | bytes 1400836
  88.6 37.6 %copy-start.2 = (s16[912,256]{1,0:T(8,128)(2,1)S(1)}, s16[912,256]{1,0:T(8,128)(2,1)}, u32[]{:S(2)}) copy-start(s16[912,256]{1,0:T(8,128)(2,1)} %get-tuple-element.22.p0) | copy-start | bytes 1400836
  88.6 18.3 %collective-permute-start.5 = (s16[912,256]{1,0:T(8,128)(2,1)}, s16[912,256]{1,0:T(8,128)(2,1)S(1)}, u32[]{:S(2)}, u32[]{:S(2)}) collective-permute-start(s16[912,256]{1,0:T(8,128)(2,1)} %get-tuple-element.23), channel_id=1, source_target_pairs={{0,32},{16,48},{32,64},{48,80},{64,96},{80,112},{96,0},{112,16},{1... | collective-permute-start | bytes 1400840 | tf_op jit(solution)/shard_map/ppermute | solution.py:538
  101.8 26.9 %collective-permute-start.1 = (s16[912,256]{1,0:T(8,128)(2,1)}, s16[912,256]{1,0:T(8,128)(2,1)S(1)}, u32[]{:S(2)}, u32[]{:S(2)}) collective-permute-start(s16[912,256]{1,0:T(8,128)(2,1)} %get-tuple-element.19), channel_id=1, source_target_pairs={{0,32},{16,48},{32,64},{48,80},{64,96},{80,112},{96,0},{112,16},{1... | collective-permute-start | bytes 1400840 | tf_op jit(solution)/shard_map/ppermute | solution.py:538
  103.3 21.9 %collective-permute-start.6 = (s16[912,256]{1,0:T(8,128)(2,1)S(1)}, s16[912,256]{1,0:T(8,128)(2,1)S(1)}, u32[]{:S(2)}, u32[]{:S(2)}) collective-permute-start(s16[912,256]{1,0:T(8,128)(2,1)S(1)} %copy-done.9), channel_id=1, source_target_pairs={{0,64},{16,80},{32,96},{48,112},{64,0},{80,16},{96,32},{112,48},{1... | collective-permute-start | bytes 1400840 | tf_op jit(solution)/shard_map/ppermute | solution.py:538
  104.7 21.5 %collective-permute-start.7 = (s16[912,256]{1,0:T(8,128)(2,1)S(1)}, s16[912,256]{1,0:T(8,128)(2,1)S(1)}, u32[]{:S(2)}, u32[]{:S(2)}) collective-permute-start(s16[912,256]{1,0:T(8,128)(2,1)S(1)} %copy-done.8), channel_id=1, source_target_pairs={{0,96},{16,112},{32,0},{48,16},{64,32},{80,48},{96,64},{112,80},{1... | collective-permute-start | bytes 1400840 | tf_op jit(solution)/shard_map/ppermute | solution.py:538
  106.6 28.5 %collective-permute-start.2 = (s16[912,256]{1,0:T(8,128)(2,1)}, s16[912,256]{1,0:T(8,128)(2,1)S(1)}, u32[]{:S(2)}, u32[]{:S(2)}) collective-permute-start(s16[912,256]{1,0:T(8,128)(2,1)} %get-tuple-element.20), channel_id=1, source_target_pairs={{0,64},{16,80},{32,96},{48,112},{64,0},{80,16},{96,32},{112,48},{1... | collective-permute-start | bytes 1400840 | tf_op jit(solution)/shard_map/ppermute | solution.py:538
  106.9 38.5 %collective-permute-start.3 = (s16[912,256]{1,0:T(8,128)(2,1)}, s16[912,256]{1,0:T(8,128)(2,1)S(1)}, u32[]{:S(2)}, u32[]{:S(2)}) collective-permute-start(s16[912,256]{1,0:T(8,128)(2,1)} %get-tuple-element.21), channel_id=1, source_target_pairs={{0,96},{16,112},{32,0},{48,16},{64,32},{80,48},{96,64},{112,80},{1... | collective-permute-start | bytes 1400840 | tf_op jit(solution)/shard_map/ppermute | solution.py:538
  145.4 1.0 copy-start.1
  146.4 24.6 %copy-start = (bf16[256,1024]{1,0:T(8,128)(2,1)S(1)}, bf16[256,1024]{1,0:T(8,128)(2,1)}, u32[]{:S(2)}) copy-start(bf16[256,1024]{1,0:T(8,128)(2,1)} %stencil_ref.1) | copy-start | bytes 1572868
  149.0 44.4 %copy-start.4 = (s32[1,16,128]{2,1,0:T(8,128)S(1)}, s32[1,16,128]{2,1,0:T(8,128)}, u32[]{:S(2)}) copy-start(s32[1,16,128]{2,1,0:T(8,128)} %param.12) | copy-start | bytes 24580
  149.0 44.4 %copy-start.7 = (s32[1,16]{1,0:T(1,128)S(1)}, s32[1,16]{1,0:T(1,128)}, u32[]{:S(2)}) copy-start(s32[1,16]{1,0:T(1,128)} %param.13) | copy-start | bytes 196
  149.0 22.0 %all-to-all-start = ((s16[16,128,256]{2,1,0:T(8,128)(2,1)}), s16[16,128,256]{2,1,0:T(8,128)(2,1)S(1)}, u32[]{:S(2)}, u32[]{:S(2)}) async-start(s16[16,128,256]{2,1,0:T(8,128)(2,1)} %sum_x.3), calls=%async_computation | async-start | bytes 2097152 | tf_op jit(solution)/shard_map/all_to_all | solution.py:551
  161.2 9.8 %collective-permute-start.8 = (s16[160,256]{1,0:T(8,128)(2,1)S(1)}, s16[160,256]{1,0:T(8,128)(2,1)S(1)}, u32[]{:S(2)}, u32[]{:S(2)}) collective-permute-start(s16[160,256]{1,0:T(8,128)(2,1)S(1)} %get-tuple-element.27), channel_id=1, source_target_pairs={{0,32},{16,48},{32,64},{48,80},{64,96},{80,112},{96,0},{112,16},{1... | collective-permute-start | bytes 245768 | tf_op jit(solution)/shard_map/ppermute | solution.py:538
  162.7 8.3 %collective-permute-start.9 = (s16[160,256]{1,0:T(8,128)(2,1)S(1)}, s16[160,256]{1,0:T(8,128)(2,1)S(1)}, u32[]{:S(2)}, u32[]{:S(2)}) collective-permute-start(s16[160,256]{1,0:T(8,128)(2,1)S(1)} %get-tuple-element.28), channel_id=1, source_target_pairs={{0,64},{16,80},{32,96},{48,112},{64,0},{80,16},{96,32},{112,48},{1... | collective-permute-start | bytes 245768 | tf_op jit(solution)/shard_map/ppermute | solution.py:538
  165.7 5.3 %collective-permute-start.10 = (s16[160,256]{1,0:T(8,128)(2,1)S(1)}, s16[160,256]{1,0:T(8,128)(2,1)S(1)}, u32[]{:S(2)}, u32[]{:S(2)}) collective-permute-start(s16[160,256]{1,0:T(8,128)(2,1)S(1)} %get-tuple-element.29), channel_id=1, source_target_pairs={{0,96},{16,112},{32,0},{48,16},{64,32},{80,48},{96,64},{112,80},{1... | collective-permute-start | bytes 245768 | tf_op jit(solution)/shard_map/ppermute | solution.py:538
  173.8 16.0 %collective-permute-start.11 = (s16[272,256]{1,0:T(8,128)(2,1)S(1)}, s16[272,256]{1,0:T(8,128)(2,1)S(1)}, u32[]{:S(2)}, u32[]{:S(2)}) collective-permute-start(s16[272,256]{1,0:T(8,128)(2,1)S(1)} %get-tuple-element.31), channel_id=1, source_target_pairs={{0,1},{1,2},{2,3},{3,4},{4,5},{5,6},{6,7},{7,8},{8,9},{9,10},{10,1... | collective-permute-start | bytes 417800 | tf_op jit(solution)/shard_map/ppermute | solution.py:560
  176.1 13.6 %collective-permute-start.12 = (s16[272,256]{1,0:T(8,128)(2,1)S(1)}, s16[272,256]{1,0:T(8,128)(2,1)S(1)}, u32[]{:S(2)}, u32[]{:S(2)}) collective-permute-start(s16[272,256]{1,0:T(8,128)(2,1)S(1)} %get-tuple-element.31), channel_id=1, source_target_pairs={{0,2},{1,3},{2,4},{3,5},{4,6},{5,7},{6,8},{7,9},{8,10},{9,11},{10,... | collective-permute-start | bytes 417800 | tf_op jit(solution)/shard_map/ppermute | solution.py:560
  180.4 9.4 %collective-permute-start.13 = (s16[272,256]{1,0:T(8,128)(2,1)S(1)}, s16[272,256]{1,0:T(8,128)(2,1)S(1)}, u32[]{:S(2)}, u32[]{:S(2)}) collective-permute-start(s16[272,256]{1,0:T(8,128)(2,1)S(1)} %get-tuple-element.31), channel_id=1, source_target_pairs={{1,0},{2,1},{3,2},{4,3},{5,4},{6,5},{7,6},{8,7},{9,8},{10,9},{11,1... | collective-permute-start | bytes 417800 | tf_op jit(solution)/shard_map/ppermute | solution.py:560
  186.0 7.3 %collective-permute-start.14 = (s16[272,256]{1,0:T(8,128)(2,1)S(1)}, s16[272,256]{1,0:T(8,128)(2,1)S(1)}, u32[]{:S(2)}, u32[]{:S(2)}) collective-permute-start(s16[272,256]{1,0:T(8,128)(2,1)S(1)} %get-tuple-element.31), channel_id=1, source_target_pairs={{2,0},{3,1},{4,2},{5,3},{6,4},{7,5},{8,6},{9,7},{10,8},{11,9},{12,... | collective-permute-start | bytes 417800 | tf_op jit(solution)/shard_map/ppermute | solution.py:560

commit v5 on v3

--- a/solution.py
+++ b/solution.py
@@ -11,7 +11,7 @@
 NX = 256
 NY = 256
 TAPS = 4
-LA = 144
+LA = 160
 LB = NY - LA
 ALPHA = math.log(2.0) / 64.0
 TOP = 32700.0
@@ -27,6 +27,10 @@
 
 def hbm(shape, dtype):
     return pltpu.HBM(shape, dtype)
+
+
+def in_hbm(x):
+    return pltpu.with_memory_space_constraint(x, pltpu.HBM)
 
 
 def encode(block):
@@ -64,32 +68,55 @@
     return block.astype(jnp.int32).astype(jnp.int16)
 
 
-def gather_kernel(
-    slots_ref, counts_ref, acq_ref, lines_ref, out_ref, wide_ref, half_ref, sem, *, first, cap
-):
-    step = pl.program_id(0)
+def widen_kernel(acq_ref, wide_ref, half_ref, sem):
     pieces = sem.shape[0]
     piece = half_ref.shape[0] // pieces
-
-    @pl.when(step == 0)
+    copies = []
+    for k in range(pieces):
+        span = pl.ds(k * piece, piece)
+        copies.append(pltpu.make_async_copy(acq_ref.at[span, :], half_ref.at[span, :], sem.at[k]))
+        copies[k].start()
+    for k in range(pieces):
+        copies[k].wait()
+
+        def widen(i, carry):
+            span = pl.ds(pl.multiple_of(k * piece + i * CHUNK, CHUNK), CHUNK)
+            wide_ref[span, :] = half_ref[span, :].astype(jnp.float32)
+            return carry
+
+        lax.fori_loop(0, piece // CHUNK, widen, 0)
+
+
+def first_gather_kernel(
+    slots_ref, counts_ref, acq_ref, lines_hbm, out_ref, wide_ref, lines_ref, half_ref, sem, line_sem,
+    **sizes,
+):
+    fetch = pltpu.make_async_copy(lines_hbm, lines_ref, line_sem)
+
+    @pl.when(pl.program_id(0) == 0)
     def _():
-        copies = []
-        for k in range(pieces):
-            span = pl.ds(k * piece, piece)
-            copies.append(
-                pltpu.make_async_copy(acq_ref.at[span, :], half_ref.at[span, :], sem.at[k])
-            )
-            copies[k].start()
-        for k in range(pieces):
-            copies[k].wait()
-
-            def widen(i, carry):
-                span = pl.ds(pl.multiple_of(k * piece + i * CHUNK, CHUNK), CHUNK)
-                wide_ref[span, :] = half_ref[span, :].astype(jnp.float32)
-                return carry
-
-            lax.fori_loop(0, piece // CHUNK, widen, 0)
-
+        fetch.start()
+        widen_kernel(acq_ref, wide_ref, half_ref, sem)
+        fetch.wait()
+
+    gather_tile(slots_ref, counts_ref, lines_ref, out_ref, wide_ref, **sizes)
+
+
+def next_gather_kernel(
+    slots_ref, counts_ref, wide_ref, lines_hbm, out_ref, lines_ref, line_sem, **sizes
+):
+    fetch = pltpu.make_async_copy(lines_hbm, lines_ref, line_sem)
+
+    @pl.when(pl.program_id(0) == 0)
+    def _():
+        fetch.start()
+        fetch.wait()
+
+    gather_tile(slots_ref, counts_ref, lines_ref, out_ref, wide_ref, **sizes)
+
+
+def gather_tile(slots_ref, counts_ref, lines_ref, out_ref, wide_ref, *, first, cap):
+    step = pl.program_id(0)
     count = counts_ref[first + step]
     start = (first + step) * cap
 
@@ -119,30 +146,44 @@
     out_ref[0, pl.ds(cap, 16), :] = both.astype(jnp.float32).astype(jnp.bfloat16)
 
 
-def gather_rows(acquired, slots, counts, lines, first, tiles):
+def gather_rows(source, slots, counts, lines, first, tiles):
     cap = lines.shape[1]
-    body = functools.partial(gather_kernel, first=first, cap=cap)
+    rows_spec = pl.BlockSpec((1, cap + 16, NX), lambda t, s, c: (t, 0, 0))
+    rows_shape = hbm((tiles, cap + 16, NX), jnp.bfloat16)
+    line_scratch = [pltpu.VMEM(lines.shape, jnp.int32)]
+    line_sem = [pltpu.SemaphoreType.DMA]
+    whole = pl.BlockSpec(memory_space=pltpu.VMEM)
+    if first:
+        body = next_gather_kernel
+        source = pltpu.with_memory_space_constraint(source, pltpu.VMEM)
+        source_spec = whole
+        out_specs, out_shape = rows_spec, rows_shape
+        scratch = line_scratch + line_sem
+    else:
+        body = first_gather_kernel
+        source = pltpu.with_memory_space_constraint(source, pltpu.HBM)
+        source_spec = pl.BlockSpec(memory_space=pltpu.HBM)
+        out_specs = [rows_spec, whole]
+        out_shape = [rows_shape, pltpu.VMEM(source.shape, jnp.float32)]
+        scratch = (
+            line_scratch
+            + [pltpu.VMEM(source.shape, jnp.bfloat16), pltpu.SemaphoreType.DMA((8,))]
+            + line_sem
+        )
     return pl.pallas_call(
-        body,
+        functools.partial(body, first=first, cap=cap),
         grid_spec=pltpu.PrefetchScalarGridSpec(
             num_scalar_prefetch=2,
             grid=(tiles,),
-            in_specs=[
-                pl.BlockSpec(memory_space=pl.ANY),
-                pl.BlockSpec(lines.shape, lambda t, s, c: (0, 0)),
-            ],
-            out_specs=pl.BlockSpec((1, cap + 16, NX), lambda t, s, c: (t, 0, 0)),
-            scratch_shapes=[
-                pltpu.VMEM(acquired.shape, jnp.float32),
-                pltpu.VMEM(acquired.shape, jnp.bfloat16),
-                pltpu.SemaphoreType.DMA((8,)),
-            ],
+            in_specs=[source_spec, pl.BlockSpec(memory_space=pltpu.HBM)],
+            out_specs=out_specs,
+            scratch_shapes=scratch,
         ),
-        out_shape=hbm((tiles, cap + 16, NX), jnp.bfloat16),
-        compiler_params=params(48),
+        out_shape=out_shape,
+        compiler_params=params(14),
         cost_estimate=pl.CostEstimate(flops=0, transcendentals=0, bytes_accessed=40_000_000),
         name="gather_rows",
-    )(slots, counts, acquired, lines)
+    )(slots, counts, source, pltpu.with_memory_space_constraint(lines, pltpu.HBM))
 
 
 def lines_kernel(
@@ -289,7 +330,7 @@
         out_shape=[hbm(a_shape, jnp.int16)] * 4
         + [hbm((tiles_all, 4 * LB + 16, NX), jnp.int16)],
         input_output_aliases=aliases,
-        compiler_params=params(48),
+        compiler_params=params(16),
         cost_estimate=pl.CostEstimate(
             flops=2 * 1024 * 256 * 20480, transcendentals=0, bytes_accessed=40_000_000
         ),
@@ -340,45 +381,51 @@
             pltpu.SemaphoreType.DMA((tiles,)),
         ],
         input_output_aliases=aliases,
-        compiler_params=pltpu.CompilerParams(vmem_limit_bytes=32 * 1024 * 1024),
+        compiler_params=pltpu.CompilerParams(vmem_limit_bytes=12 * 1024 * 1024),
         name="sum_x",
     )(*parts, old)
 
 
-def sum_tile_kernel(in_ref, o0, o1, o2, o3, acc_ref):
-    step = pl.program_id(0)
-
-    @pl.when(step == 0)
-    def _():
-        acc_ref[...] = jnp.zeros(acc_ref.shape, jnp.float32)
-
-    table = in_ref[0, pl.ds(4 * LB, 16), :].astype(jnp.int32).astype(jnp.float32)
-    for k in range(4):
-        acc_ref[pl.ds(k * LB, LB), :] += decode(
-            in_ref[0, pl.ds(k * LB, LB), :], table[k : k + 1, 0:LB]
-        )
-
-    @pl.when(step == pl.num_programs(0) - 1)
-    def _():
-        for k, out in enumerate((o0, o1, o2, o3)):
-            values, code = encode(acc_ref[pl.ds(k * LB, LB), :])
-            out[pl.ds(0, LB), :] = values
-            out[pl.ds(LB, 16), :] = code_block([pad_row(code)])
+def sum_tile_kernel(in_hbm_ref, o0, o1, o2, o3, acc_ref, in_ref, sem):
+    tiles = in_ref.shape[0]
+
+    def fetch(t):
+        return pltpu.make_async_copy(in_hbm_ref.at[t], in_ref.at[t], sem.at[t])
+
+    for t in range(tiles):
+        fetch(t).start()
+    acc_ref[...] = jnp.zeros(acc_ref.shape, jnp.float32)
+
+    def body(t, carry):
+        fetch(t).wait()
+        table = in_ref[t, pl.ds(4 * LB, 16), :].astype(jnp.int32).astype(jnp.float32)
+        for k in range(4):
+            acc_ref[pl.ds(k * LB, LB), :] += decode(
+                in_ref[t, pl.ds(k * LB, LB), :], table[k : k + 1, 0:LB]
+            )
+        return carry
+
+    lax.fori_loop(0, tiles, body, 0)
+    for k, out in enumerate((o0, o1, o2, o3)):
+        values, code = encode(acc_ref[pl.ds(k * LB, LB), :])
+        out[pl.ds(0, LB), :] = values
+        out[pl.ds(LB, 16), :] = code_block([pad_row(code)])
 
 
 def sum_tile(arrived):
-    tiles, rows, _ = arrived.shape
     out_shape = (LB + 16, NX)
     return pl.pallas_call(
         sum_tile_kernel,
-        grid=(tiles,),
-        in_specs=[pl.BlockSpec((1, rows, NX), lambda t: (t, 0, 0))],
-        out_specs=[pl.BlockSpec(out_shape, lambda t: (0, 0))] * 4,
+        in_specs=[pl.BlockSpec(memory_space=pltpu.HBM)],
         out_shape=[jax.ShapeDtypeStruct(out_shape, jnp.int16)] * 4,
-        scratch_shapes=[pltpu.VMEM((4 * LB, NX), jnp.float32)],
-        compiler_params=params(32),
+        scratch_shapes=[
+            pltpu.VMEM((4 * LB, NX), jnp.float32),
+            pltpu.VMEM(arrived.shape, jnp.int16),
+            pltpu.SemaphoreType.DMA(arrived.shape[:1]),
+        ],
+        compiler_params=pltpu.CompilerParams(vmem_limit_bytes=12 * 1024 * 1024),
         name="sum_tile",
-    )(arrived)
+    )(in_hbm(arrived))
 
 
 def plane_kernel(a_ref, b0, b1, b2, b3, stencil_ref, plane_ref, send_ref, lines_ref):
@@ -425,7 +472,7 @@
             jax.ShapeDtypeStruct((NY + 16, NX), jnp.int16),
         ],
         scratch_shapes=[pltpu.VMEM((NY, NX), jnp.float32)],
-        compiler_params=pltpu.CompilerParams(vmem_limit_bytes=32 * 1024 * 1024),
+        compiler_params=pltpu.CompilerParams(vmem_limit_bytes=12 * 1024 * 1024),
         name="own_plane",
     )(a, *bs, stencil)
 
@@ -480,7 +527,7 @@
             jax.ShapeDtypeStruct((NY, NX), jnp.bfloat16),
             jax.ShapeDtypeStruct((readers, most, NX), jnp.bfloat16),
         ],
-        compiler_params=pltpu.CompilerParams(vmem_limit_bytes=32 * 1024 * 1024),
+        compiler_params=pltpu.CompilerParams(vmem_limit_bytes=12 * 1024 * 1024),
         name="smooth",
     )(edges, counts, plane, *halos, reads)
 
@@ -515,9 +562,11 @@
 
     rows, peer_rows = [], []
     for h in range(2):
-        rows.append(
-            gather_rows(acquired, flat_slots, counts, send_lines[0], h * tile_half, tile_half)
-        )
+        source = wide if h else acquired
+        made = gather_rows(source, flat_slots, counts, send_lines[0], h * tile_half, tile_half)
+        if not h:
+            made, wide = made
+        rows.append(made)
         peer_rows.append(lax.ppermute(rows[h], "cuts", swap))
     cap = send_slots.shape[2]
     peer_counts = [
@@ -559,7 +608,7 @@
     edges = jnp.stack([spot > 0, spot < total - 1]).astype(jnp.int32)
     field, outgoing = smooth(edges, return_counts[0], plane, halos, return_slots[0])
     returned = lax.all_to_all(outgoing, "tile", split_axis=0, concat_axis=0, tiled=True)
-    return field[None], returned
+    return field[None], pltpu.with_memory_space_constraint(returned, pltpu.HBM)
 
 
 def solution(mesh):

time: 215 us -> 207 us (0.963)
  Pallas kernels: 85.3 us -> 74.1 us
    pallas_call x3, Pallas kernels: 41 us -> 31.2 us  [the longest x2 27.5 us: gather_rows(): pl.pallas_call(functools.partial(body, first=first, cap=cap), grid_spec=p...]
    all_to_all x1, waiting for transfers between devices: 10.1 us -> 0.86 us  [local(): lax.all_to_all(b_blocks, 'tile', split_axis=0, concat_axis=0, tiled=True)]
    all_to_all x1, waiting for transfers between devices: 3.01 us -> 9.73 us  [local(): lax.all_to_all(a_sums, 'tile', split_axis=0, concat_axis=0, tiled=True)]
    ppermute x4, starting transfers between devices: 19.1 us -> 15.6 us  [plane_send(): return lax.ppermute(coded, ('cuts', 'tile'), pairs)]
    ppermute x9, waiting for transfers between devices: 34.3 us -> 36.9 us  [x_send(): lax.ppermute(block, 'cuts', [(i, (i + 2 * k) % cut_count) for i in range(...]
    all_to_all x1, starting transfers between devices: 6.91 us -> 9.1 us  [local(): lax.all_to_all(b_blocks, 'tile', split_axis=0, concat_axis=0, tiled=True)]
  transfers between devices with their start and end apart: 17 -> 17, of which waited for: 8 -> 7; matrix products, arithmetic and copies ran while one was open for 1% -> 1% of each run, Pallas kernels for 31% -> 27%
where the time goes in v5:
time: 207 us; the launch traced here: 205 us
  Pallas kernels  74.1 us (36%)
  waiting for transfers between devices  52 us (25%)
  starting transfers between devices  47.1 us (23%)
  blocking collectives  24.9 us (12%)
  local copies, waits for them, and re-layouts  3.75 us (2%)
  other arithmetic  2.1 us (1%)
    ppermute x9, waiting for transfers between devices, x_send(): lax.ppermute(block, 'cuts', [(i, (i + 2 * k) % cut_count) for i in range(...  36.9 us
    pallas_call x2, Pallas kernels, line_blocks(): pl.pallas_call(functools.partial(lines_kernel, first=first, cap=cap), gri...  31.9 us
    pallas_call x2, Pallas kernels, gather_rows(): pl.pallas_call(functools.partial(body, first=first, cap=cap), grid_spec=p...  27.5 us
    all_to_all x1, blocking collectives, local(): lax.all_to_all(outgoing, 'tile', split_axis=0, concat_axis=0, tiled=True)  24.9 us
    ppermute x4, starting transfers between devices, plane_send(): return lax.ppermute(coded, ('cuts', 'tile'), pairs)  15.6 us
    ppermute x9, starting transfers between devices, x_send(): lax.ppermute(block, 'cuts', [(i, (i + 2 * k) % cut_count) for i in range(...  14.8 us
    all_to_all x1, waiting for transfers between devices, local(): lax.all_to_all(a_sums, 'tile', split_axis=0, concat_axis=0, tiled=True)  9.73 us
    all_to_all x1, starting transfers between devices, local(): lax.all_to_all(b_blocks, 'tile', split_axis=0, concat_axis=0, tiled=True)  9.1 us
  transfers between devices with their start and end apart: 17, of which 7 were waited for; matrix products, arithmetic and copies ran while one was open for 1% of the time, Pallas kernels for 27%

profile of v5, /device:TPU:1, one launch (start us, length us, event | category | flops | bytes accessed | tf_op | source)
XLA Modules:
  0.0 204.9 jit_solution(9535119316207368918)
XLA Ops:
  0.6 0.9 reshape.19.slots_ref
  1.5 0.7 copy-done.4
  2.2 13.0 %gather_rows.2 = (bf16[8,1296,256]{2,1,0:T(8,128)(2,1)}, f32[16384,256]{1,0:T(8,128)S(1)}) custom-call(s32[20480]{0:T(1024)S(1)} %reshape.19.slots_ref, s32[16]{0:T(128)S(1)} %bitcast.10, bf16[16384,256]{1,0:T(8,128)(2,1)} %acq_ref.1, s32[16,1280]{1,0:T(8,128)} %bitcast.15), custom_call_target="tpu_custom_call" | custom-call | bytes 40000000 | tf_op jit(solution)/shard_map/gather_rows/pallas_call | solution.py:173
  15.2 1.1 collective-permute-start.1
  16.3 14.5 %gather_rows.3.own_hbm = bf16[8,1296,256]{2,1,0:T(8,128)(2,1)} custom-call(s32[20480]{0:T(1024)S(1)} %reshape.19.slots_ref, s32[16]{0:T(128)S(1)} %bitcast.11, f32[16384,256]{1,0:T(8,128)S(1)} %get-tuple-element.22.wide_ref, s32[16,1280]{1,0:T(8,128)} %bitcast.16), custom_call_target="tpu_custom_call" | custom-call | bytes 40000000 | tf_op jit(solution)/shard_map/gather_rows/pallas_call | solution.py:173
  30.8 0.7 collective-permute-start
  31.5 0.1 pad_add_fusion.place_ref
  31.6 0.0 collective-permute-done.1.peer_hbm
  31.6 1.0 fusion.7.peer_n
  32.6 14.2 %line_blocks.2 = (s16[1296,256]{1,0:T(8,128)(2,1)}, s16[1296,256]{1,0:T(8,128)(2,1)}, s16[1296,256]{1,0:T(8,128)(2,1)}, s16[1296,256]{1,0:T(8,128)(2,1)}, s16[16,400,256]{2,1,0:T(8,128)(2,1)}) custom-call(s32[16]{0:T(128)S(1)} %bitcast.12, s32[8]{0:T(128)S(1)} %fusion.7.peer_n, s32[2]{0:T(128)S(1)} %pad_add_fusion.place_ref, ...), custom_call_target="tpu_custom_call" | custom-call | flops 10737418240 | bytes 40000000 | tf_op jit(solution)/shard_map/line_blocks/pallas_call | solution.py:313
  46.8 3.0 %collective-permute-start.5 = (s16[1296,256]{1,0:T(8,128)(2,1)}, s16[1296,256]{1,0:T(8,128)(2,1)S(1)}, u32[]{:S(2)}, u32[]{:S(2)}) collective-permute-start(s16[1296,256]{1,0:T(8,128)(2,1)} %get-tuple-element.30), channel_id=1, source_target_pairs={{0,32},{16,48},{32,64},{48,80},{64,96},{80,112},{96,0},{112,16},{1... | collective-permute-start | bytes 1990664 | tf_op jit(solution)/shard_map/ppermute | solution.py:579
  49.7 1.0 fusion.6.peer_n
  50.7 17.8 %line_blocks.3 = (s16[1296,256]{1,0:T(8,128)(2,1)}, s16[1296,256]{1,0:T(8,128)(2,1)}, s16[1296,256]{1,0:T(8,128)(2,1)}, s16[1296,256]{1,0:T(8,128)(2,1)}, s16[16,400,256]{2,1,0:T(8,128)(2,1)}) custom-call(s32[16]{0:T(128)S(1)} %bitcast.13, s32[8]{0:T(128)S(1)} %fusion.6.peer_n, s32[2]{0:T(128)S(1)} %pad_add_fusion.place_ref, ...), custom_call_target="tpu_custom_call", output_to_operand_aliasing={{4}: (5, {})} | custom-call | flops 10737418240 | bytes 40000000 | tf_op jit(solution)/shard_map/line_blocks/pallas_call | solution.py:313
  68.5 0.0 collective-permute-done.5.p1
  68.5 0.6 slice.28.refs_0_
  69.1 0.6 slice.29.refs_1_
  69.7 9.1 %all-to-all-start.1 = ((s16[16,400,256]{2,1,0:T(8,128)(2,1)}), s16[16,400,256]{2,1,0:T(8,128)(2,1)}, u32[]{:S(2)}, u32[]{:S(2)}) async-start(s16[16,400,256]{2,1,0:T(8,128)(2,1)} %after.1), calls=%async_computation.1 | async-start | bytes 6553600 | tf_op jit(solution)/shard_map/all_to_all | solution.py:591
  78.8 3.0 %collective-permute-start.6 = (s16[1296,256]{1,0:T(8,128)(2,1)S(1)}, s16[1296,256]{1,0:T(8,128)(2,1)S(1)}, u32[]{:S(2)}, u32[]{:S(2)}) collective-permute-start(s16[1296,256]{1,0:T(8,128)(2,1)S(1)} %copy-done.7), channel_id=1, source_target_pairs={{0,64},{16,80},{32,96},{48,112},{64,0},{80,16},{96,32},{112,48},{1... | collective-permute-start | bytes 1990664 | tf_op jit(solution)/shard_map/ppermute | solution.py:579
  81.8 2.9 %collective-permute-start.3 = (s16[1296,256]{1,0:T(8,128)(2,1)}, s16[1296,256]{1,0:T(8,128)(2,1)S(1)}, u32[]{:S(2)}, u32[]{:S(2)}) collective-permute-start(s16[1296,256]{1,0:T(8,128)(2,1)} %get-tuple-element.27), channel_id=1, source_target_pairs={{0,64},{16,80},{32,96},{48,112},{64,0},{80,16},{96,32},{112,48},{1... | collective-permute-start | bytes 1990664 | tf_op jit(solution)/shard_map/ppermute | solution.py:579
  84.8 0.0 collective-permute-start.4
  84.8 11.1 %collective-permute-done.6.p2 = s16[1296,256]{1,0:T(8,128)(2,1)S(1)} collective-permute-done((s16[1296,256]{1,0:T(8,128)(2,1)S(1)}, s16[1296,256]{1,0:T(8,128)(2,1)S(1)}, u32[]{:S(2)}, u32[]{:S(2)}) %collective-permute-start.6) | collective-permute-done | bytes 663584 | tf_op jit(solution)/shard_map/ppermute | solution.py:579
  95.9 2.9 %sum_x.2.alias_ref = s16[16,176,256]{2,1,0:T(8,128)(2,1)} custom-call(s16[1296,256]{1,0:T(8,128)(2,1)S(1)} %copy-done, s16[1296,256]{1,0:T(8,128)(2,1)S(1)} %collective-permute-done.5.p1, s16[1296,256]{1,0:T(8,128)(2,1)S(1)} %collective-permute-done.6.p2, s16[1296,256]{1,0:T(8,128)(2,1)S(1)} %collective-permute-done.7.p3, ...), custom_call_target="tpu_custom_call" | custom-call | tf_op jit(solution)/shard_map/sum_x/pallas_call | solution.py:374
  98.8 14.1 %collective-permute-done.2.p1 = s16[1296,256]{1,0:T(8,128)(2,1)S(1)} collective-permute-done((s16[1296,256]{1,0:T(8,128)(2,1)}, s16[1296,256]{1,0:T(8,128)(2,1)S(1)}, u32[]{:S(2)}, u32[]{:S(2)}) %collective-permute-start.2) | collective-permute-done | bytes 663584 | tf_op jit(solution)/shard_map/ppermute | solution.py:579
  112.9 11.3 %collective-permute-done.3.p2 = s16[1296,256]{1,0:T(8,128)(2,1)S(1)} collective-permute-done((s16[1296,256]{1,0:T(8,128)(2,1)}, s16[1296,256]{1,0:T(8,128)(2,1)S(1)}, u32[]{:S(2)}, u32[]{:S(2)}) %collective-permute-start.3) | collective-permute-done | bytes 663584 | tf_op jit(solution)/shard_map/ppermute | solution.py:579
  124.2 0.4 collective-permute-done.4.p3
  124.6 2.9 %sum_x.3 = s16[16,176,256]{2,1,0:T(8,128)(2,1)} custom-call(s16[1296,256]{1,0:T(8,128)(2,1)S(1)} %copy-done.1, s16[1296,256]{1,0:T(8,128)(2,1)S(1)} %collective-permute-done.2.p1, s16[1296,256]{1,0:T(8,128)(2,1)S(1)} %collective-permute-done.3.p2, s16[1296,256]{1,0:T(8,128)(2,1)S(1)} %collective-permute-done.4.p3, ...), custom_call_target="tpu_custom_call", output_to_operand_aliasing={{}: (4, {})} | custom-call | tf_op jit(solution)/shard_map/sum_x/pallas_call | solution.py:374
  127.6 0.0 copy-start.3
  127.6 0.0 copy-start.6
  127.6 0.9 all-to-all-done.1.in_hbm_ref
  128.5 5.8 %all-to-all-start = ((s16[16,176,256]{2,1,0:T(8,128)(2,1)}), s16[16,176,256]{2,1,0:T(8,128)(2,1)S(1)}, u32[]{:S(2)}, u32[]{:S(2)}) async-start(s16[16,176,256]{2,1,0:T(8,128)(2,1)} %sum_x.3), calls=%async_computation | async-start | bytes 2883584 | tf_op jit(solution)/shard_map/all_to_all | solution.py:595
  134.2 3.7 %sum_tile.1 = (s16[112,256]{1,0:T(8,128)(2,1)S(1)}, s16[112,256]{1,0:T(8,128)(2,1)S(1)}, s16[112,256]{1,0:T(8,128)(2,1)S(1)}, s16[112,256]{1,0:T(8,128)(2,1)S(1)}) custom-call(s16[16,400,256]{2,1,0:T(8,128)(2,1)} %all-to-all-done.1.in_hbm_ref), custom_call_target="tpu_custom_call" | custom-call | tf_op jit(solution)/shard_map/sum_tile/pallas_call | solution.py:417
  137.9 3.4 %collective-permute-start.8 = (s16[112,256]{1,0:T(8,128)(2,1)S(1)}, s16[112,256]{1,0:T(8,128)(2,1)S(1)}, u32[]{:S(2)}, u32[]{:S(2)}) collective-permute-start(s16[112,256]{1,0:T(8,128)(2,1)S(1)} %get-tuple-element.35), channel_id=1, source_target_pairs={{0,32},{16,48},{32,64},{48,80},{64,96},{80,112},{96,0},{112,16},{1... | collective-permute-start | bytes 172040 | tf_op jit(solution)/shard_map/ppermute | solution.py:579
  141.3 1.1 collective-permute-start.9
  142.5 1.3 collective-permute-start.10
  143.8 9.7 %all-to-all-done.a_ref = s16[16,176,256]{2,1,0:T(8,128)(2,1)S(1)} async-done(((s16[16,176,256]{2,1,0:T(8,128)(2,1)}), s16[16,176,256]{2,1,0:T(8,128)(2,1)S(1)}, u32[]{:S(2)}, u32[]{:S(2)}) %all-to-all-start) | async-done | bytes 1441824 | tf_op jit(solution)/shard_map/all_to_all | solution.py:595
  153.6 0.0 collective-permute-done.9.b2
  153.6 0.0 collective-permute-done.10.b3
  153.6 2.8 %own_plane.1 = (f32[256,256]{1,0:T(8,128)S(1)}, s16[272,256]{1,0:T(8,128)(2,1)S(1)}) custom-call(s16[16,176,256]{2,1,0:T(8,128)(2,1)S(1)} %all-to-all-done.a_ref, s16[112,256]{1,0:T(8,128)(2,1)S(1)} %get-tuple-element.34.b0, s16[112,256]{1,0:T(8,128)(2,1)S(1)} %collective-permute-done.8.b1, s16[112,256]{1,0:T(8,128)(2,1)S(1)} %collective-permute-done.9.b2, ...), custom_call_target="tpu_custom_call" | custom-call | tf_op jit(solution)/shard_map/own_plane/pallas_call | solution.py:468
  156.4 2.3 %collective-permute-start.11 = (s16[272,256]{1,0:T(8,128)(2,1)S(1)}, s16[272,256]{1,0:T(8,128)(2,1)S(1)}, u32[]{:S(2)}, u32[]{:S(2)}) collective-permute-start(s16[272,256]{1,0:T(8,128)(2,1)S(1)} %get-tuple-element.39), channel_id=1, source_target_pairs={{0,1},{1,2},{2,3},{3,4},{4,5},{5,6},{6,7},{7,8},{8,9},{9,10},{10,1... | collective-permute-start | bytes 417800 | tf_op jit(solution)/shard_map/ppermute | solution.py:604
  158.7 4.5 %collective-permute-start.12 = (s16[272,256]{1,0:T(8,128)(2,1)S(1)}, s16[272,256]{1,0:T(8,128)(2,1)S(1)}, u32[]{:S(2)}, u32[]{:S(2)}) collective-permute-start(s16[272,256]{1,0:T(8,128)(2,1)S(1)} %get-tuple-element.39), channel_id=1, source_target_pairs={{0,2},{1,3},{2,4},{3,5},{4,6},{5,7},{6,8},{7,9},{8,10},{9,11},{10,... | collective-permute-start | bytes 417800 | tf_op jit(solution)/shard_map/ppermute | solution.py:604
  163.2 6.1 %collective-permute-start.13 = (s16[272,256]{1,0:T(8,128)(2,1)S(1)}, s16[272,256]{1,0:T(8,128)(2,1)S(1)}, u32[]{:S(2)}, u32[]{:S(2)}) collective-permute-start(s16[272,256]{1,0:T(8,128)(2,1)S(1)} %get-tuple-element.39), channel_id=1, source_target_pairs={{1,0},{2,1},{3,2},{4,3},{5,4},{6,5},{7,6},{8,7},{9,8},{10,9},{11,1... | collective-permute-start | bytes 417800 | tf_op jit(solution)/shard_map/ppermute | solution.py:604
  169.3 2.7 %collective-permute-start.14 = (s16[272,256]{1,0:T(8,128)(2,1)S(1)}, s16[272,256]{1,0:T(8,128)(2,1)S(1)}, u32[]{:S(2)}, u32[]{:S(2)}) collective-permute-start(s16[272,256]{1,0:T(8,128)(2,1)S(1)} %get-tuple-element.39), channel_id=1, source_target_pairs={{2,0},{3,1},{4,2},{5,3},{6,4},{7,5},{8,6},{9,7},{10,8},{11,9},{12,... | collective-permute-start | bytes 417800 | tf_op jit(solution)/shard_map/ppermute | solution.py:604
  172.0 0.1 add_convert_fusion.edge_ref
  172.1 0.0 collective-permute-done.11.l1
  172.1 4.5 %collective-permute-done.14.r2 = s16[272,256]{1,0:T(8,128)(2,1)S(1)} collective-permute-done((s16[272,256]{1,0:T(8,128)(2,1)S(1)}, s16[272,256]{1,0:T(8,128)(2,1)S(1)}, u32[]{:S(2)}, u32[]{:S(2)}) %collective-permute-start.14) | collective-permute-done | bytes 139296 | tf_op jit(solution)/shard_map/ppermute | solution.py:604
  176.6 2.4 %smooth.1 = (bf16[256,256]{1,0:T(8,128)(2,1)}, bf16[16,128,256]{2,1,0:T(8,128)(2,1)S(1)}) custom-call(s32[2]{0:T(128)S(1)} %add_convert_fusion.edge_ref, s32[16]{0:T(128)S(1)} %bitcast.14, f32[256,256]{1,0:T(8,128)S(1)} %get-tuple-element.38.plane_ref, s16[272,256]{1,0:T(8,128)(2,1)S(1)} %collective-permute-done.11.l1, ...), custom_call_target="tpu_custom_call" | custom-call | tf_op jit(solution)/shard_map/smooth/pallas_call | solution.py:522
  179.0 24.9 %all_to_all.15 = bf16[16,128,256]{2,1,0:T(8,128)(2,1)S(1)} all-to-all(bf16[16,128,256]{2,1,0:T(8,128)(2,1)S(1)} %get-tuple-element.41), channel_id=1, replica_groups=mesh['cuts'=8,'tile'=16] {'tile'}, dimensions={0} | all-to-all | bytes 2097152 | tf_op jit(solution)/shard_map/all_to_all | solution.py:610
  203.9 1.0 copy.16
  (22 shorter events, 0.0 us)
Async XLA Ops:
  1.5 0.7 copy-start.4
  15.2 16.4 %collective-permute-start.1 = (bf16[8,1296,256]{2,1,0:T(8,128)(2,1)}, bf16[8,1296,256]{2,1,0:T(8,128)(2,1)}, u32[]{:S(2)}, u32[]{:S(2)}) collective-permute-start(bf16[8,1296,256]{2,1,0:T(8,128)(2,1)} %get-tuple-element.23.own_hbm), channel_id=1, source_target_pairs={{0,16},{16,0},{32,48},{48,32},{64,80},{80,64},{96,112},{112,96},{1... | collective-permute-start | bytes 15925256 | tf_op jit(solution)/shard_map/ppermute | solution.py:570
  16.3 16.3 %copy-start.5 = (s32[1,16]{1,0:T(1,128)S(1)}, s32[1,16]{1,0:T(1,128)}, u32[]{:S(2)}) copy-start(s32[1,16]{1,0:T(1,128)} %param.11) | copy-start | bytes 196
  30.8 18.9 %collective-permute-start = (bf16[8,1296,256]{2,1,0:T(8,128)(2,1)}, bf16[8,1296,256]{2,1,0:T(8,128)(2,1)}, u32[]{:S(2)}, u32[]{:S(2)}) collective-permute-start(bf16[8,1296,256]{2,1,0:T(8,128)(2,1)} %gather_rows.3.own_hbm), channel_id=1, source_target_pairs={{0,16},{16,0},{32,48},{48,32},{64,80},{80,64},{96,112},{112,96},{1... | collective-permute-start | bytes 15925256 | tf_op jit(solution)/shard_map/ppermute | solution.py:570
  46.8 21.7 %collective-permute-start.5 = (s16[1296,256]{1,0:T(8,128)(2,1)}, s16[1296,256]{1,0:T(8,128)(2,1)S(1)}, u32[]{:S(2)}, u32[]{:S(2)}) collective-permute-start(s16[1296,256]{1,0:T(8,128)(2,1)} %get-tuple-element.30), channel_id=1, source_target_pairs={{0,32},{16,48},{32,64},{48,80},{64,96},{80,112},{96,0},{112,16},{1... | collective-permute-start | bytes 1990664 | tf_op jit(solution)/shard_map/ppermute | solution.py:579
  49.7 19.4 %collective-permute-start.7 = (s16[1296,256]{1,0:T(8,128)(2,1)}, s16[1296,256]{1,0:T(8,128)(2,1)S(1)}, u32[]{:S(2)}, u32[]{:S(2)}) collective-permute-start(s16[1296,256]{1,0:T(8,128)(2,1)} %get-tuple-element.32), channel_id=1, source_target_pairs={{0,96},{16,112},{32,0},{48,16},{64,32},{80,48},{96,64},{112,80},{1... | collective-permute-start | bytes 1990664 | tf_op jit(solution)/shard_map/ppermute | solution.py:579
  69.7 9.1 %copy-start.7 = (s16[1296,256]{1,0:T(8,128)(2,1)S(1)}, s16[1296,256]{1,0:T(8,128)(2,1)}, u32[]{:S(2)}) copy-start(s16[1296,256]{1,0:T(8,128)(2,1)} %get-tuple-element.31) | copy-start | bytes 1990660
  69.7 26.2 %copy-start = (s16[1296,256]{1,0:T(8,128)(2,1)S(1)}, s16[1296,256]{1,0:T(8,128)(2,1)}, u32[]{:S(2)}) copy-start(s16[1296,256]{1,0:T(8,128)(2,1)} %get-tuple-element.29.p0) | copy-start | bytes 1990660
  69.7 55.0 %copy-start.1 = (s16[1296,256]{1,0:T(8,128)(2,1)S(1)}, s16[1296,256]{1,0:T(8,128)(2,1)}, u32[]{:S(2)}) copy-start(s16[1296,256]{1,0:T(8,128)(2,1)} %get-tuple-element.25.p0) | copy-start | bytes 1990660
  69.7 58.8 %all-to-all-start.1 = ((s16[16,400,256]{2,1,0:T(8,128)(2,1)}), s16[16,400,256]{2,1,0:T(8,128)(2,1)}, u32[]{:S(2)}, u32[]{:S(2)}) async-start(s16[16,400,256]{2,1,0:T(8,128)(2,1)} %after.1), calls=%async_computation.1 | async-start | bytes 6553600 | tf_op jit(solution)/shard_map/all_to_all | solution.py:591
  78.8 17.1 %collective-permute-start.6 = (s16[1296,256]{1,0:T(8,128)(2,1)S(1)}, s16[1296,256]{1,0:T(8,128)(2,1)S(1)}, u32[]{:S(2)}, u32[]{:S(2)}) collective-permute-start(s16[1296,256]{1,0:T(8,128)(2,1)S(1)} %copy-done.7), channel_id=1, source_target_pairs={{0,64},{16,80},{32,96},{48,112},{64,0},{80,16},{96,32},{112,48},{1... | collective-permute-start | bytes 1990664 | tf_op jit(solution)/shard_map/ppermute | solution.py:579
  81.8 31.1 %collective-permute-start.2 = (s16[1296,256]{1,0:T(8,128)(2,1)}, s16[1296,256]{1,0:T(8,128)(2,1)S(1)}, u32[]{:S(2)}, u32[]{:S(2)}) collective-permute-start(s16[1296,256]{1,0:T(8,128)(2,1)} %get-tuple-element.26), channel_id=1, source_target_pairs={{0,32},{16,48},{32,64},{48,80},{64,96},{80,112},{96,0},{112,16},{1... | collective-permute-start | bytes 1990664 | tf_op jit(solution)/shard_map/ppermute | solution.py:579
  81.8 42.4 %collective-permute-start.3 = (s16[1296,256]{1,0:T(8,128)(2,1)}, s16[1296,256]{1,0:T(8,128)(2,1)S(1)}, u32[]{:S(2)}, u32[]{:S(2)}) collective-permute-start(s16[1296,256]{1,0:T(8,128)(2,1)} %get-tuple-element.27), channel_id=1, source_target_pairs={{0,64},{16,80},{32,96},{48,112},{64,0},{80,16},{96,32},{112,48},{1... | collective-permute-start | bytes 1990664 | tf_op jit(solution)/shard_map/ppermute | solution.py:579
  84.8 39.9 %collective-permute-start.4 = (s16[1296,256]{1,0:T(8,128)(2,1)}, s16[1296,256]{1,0:T(8,128)(2,1)S(1)}, u32[]{:S(2)}, u32[]{:S(2)}) collective-permute-start(s16[1296,256]{1,0:T(8,128)(2,1)} %get-tuple-element.28), channel_id=1, source_target_pairs={{0,96},{16,112},{32,0},{48,16},{64,32},{80,48},{96,64},{112,80},{1... | collective-permute-start | bytes 1990664 | tf_op jit(solution)/shard_map/ppermute | solution.py:579
  124.6 28.9 %copy-start.2 = (bf16[256,1024]{1,0:T(8,128)(2,1)S(1)}, bf16[256,1024]{1,0:T(8,128)(2,1)}, u32[]{:S(2)}) copy-start(bf16[256,1024]{1,0:T(8,128)(2,1)} %stencil_ref.1) | copy-start | bytes 1572868
  127.6 49.0 %copy-start.3 = (s32[1,16,128]{2,1,0:T(8,128)S(1)}, s32[1,16,128]{2,1,0:T(8,128)}, u32[]{:S(2)}) copy-start(s32[1,16,128]{2,1,0:T(8,128)} %param.12) | copy-start | bytes 24580
  127.6 49.0 %copy-start.6 = (s32[1,16]{1,0:T(1,128)S(1)}, s32[1,16]{1,0:T(1,128)}, u32[]{:S(2)}) copy-start(s32[1,16]{1,0:T(1,128)} %param.13) | copy-start | bytes 196
  128.5 25.1 %all-to-all-start = ((s16[16,176,256]{2,1,0:T(8,128)(2,1)}), s16[16,176,256]{2,1,0:T(8,128)(2,1)S(1)}, u32[]{:S(2)}, u32[]{:S(2)}) async-start(s16[16,176,256]{2,1,0:T(8,128)(2,1)} %sum_x.3), calls=%async_computation | async-start | bytes 2883584 | tf_op jit(solution)/shard_map/all_to_all | solution.py:595
  137.9 15.6 %collective-permute-start.8 = (s16[112,256]{1,0:T(8,128)(2,1)S(1)}, s16[112,256]{1,0:T(8,128)(2,1)S(1)}, u32[]{:S(2)}, u32[]{:S(2)}) collective-permute-start(s16[112,256]{1,0:T(8,128)(2,1)S(1)} %get-tuple-element.35), channel_id=1, source_target_pairs={{0,32},{16,48},{32,64},{48,80},{64,96},{80,112},{96,0},{112,16},{1... | collective-permute-start | bytes 172040 | tf_op jit(solution)/shard_map/ppermute | solution.py:579
  141.3 12.2 %collective-permute-start.9 = (s16[112,256]{1,0:T(8,128)(2,1)S(1)}, s16[112,256]{1,0:T(8,128)(2,1)S(1)}, u32[]{:S(2)}, u32[]{:S(2)}) collective-permute-start(s16[112,256]{1,0:T(8,128)(2,1)S(1)} %get-tuple-element.36), channel_id=1, source_target_pairs={{0,64},{16,80},{32,96},{48,112},{64,0},{80,16},{96,32},{112,48},{1... | collective-permute-start | bytes 172040 | tf_op jit(solution)/shard_map/ppermute | solution.py:579
  142.5 11.1 %collective-permute-start.10 = (s16[112,256]{1,0:T(8,128)(2,1)S(1)}, s16[112,256]{1,0:T(8,128)(2,1)S(1)}, u32[]{:S(2)}, u32[]{:S(2)}) collective-permute-start(s16[112,256]{1,0:T(8,128)(2,1)S(1)} %get-tuple-element.37), channel_id=1, source_target_pairs={{0,96},{16,112},{32,0},{48,16},{64,32},{80,48},{96,64},{112,80},{1... | collective-permute-start | bytes 172040 | tf_op jit(solution)/shard_map/ppermute | solution.py:579
  156.4 15.7 %collective-permute-start.11 = (s16[272,256]{1,0:T(8,128)(2,1)S(1)}, s16[272,256]{1,0:T(8,128)(2,1)S(1)}, u32[]{:S(2)}, u32[]{:S(2)}) collective-permute-start(s16[272,256]{1,0:T(8,128)(2,1)S(1)} %get-tuple-element.39), channel_id=1, source_target_pairs={{0,1},{1,2},{2,3},{3,4},{4,5},{5,6},{6,7},{7,8},{8,9},{9,10},{10,1... | collective-permute-start | bytes 417800 | tf_op jit(solution)/shard_map/ppermute | solution.py:604
  158.7 13.5 %collective-permute-start.12 = (s16[272,256]{1,0:T(8,128)(2,1)S(1)}, s16[272,256]{1,0:T(8,128)(2,1)S(1)}, u32[]{:S(2)}, u32[]{:S(2)}) collective-permute-start(s16[272,256]{1,0:T(8,128)(2,1)S(1)} %get-tuple-element.39), channel_id=1, source_target_pairs={{0,2},{1,3},{2,4},{3,5},{4,6},{5,7},{6,8},{7,9},{8,10},{9,11},{10,... | collective-permute-start | bytes 417800 | tf_op jit(solution)/shard_map/ppermute | solution.py:604
  163.2 9.0 %collective-permute-start.13 = (s16[272,256]{1,0:T(8,128)(2,1)S(1)}, s16[272,256]{1,0:T(8,128)(2,1)S(1)}, u32[]{:S(2)}, u32[]{:S(2)}) collective-permute-start(s16[272,256]{1,0:T(8,128)(2,1)S(1)} %get-tuple-element.39), channel_id=1, source_target_pairs={{1,0},{2,1},{3,2},{4,3},{5,4},{6,5},{7,6},{8,7},{9,8},{10,9},{11,1... | collective-permute-start | bytes 417800 | tf_op jit(solution)/shard_map/ppermute | solution.py:604
  169.3 7.3 %collective-permute-start.14 = (s16[272,256]{1,0:T(8,128)(2,1)S(1)}, s16[272,256]{1,0:T(8,128)(2,1)S(1)}, u32[]{:S(2)}, u32[]{:S(2)}) collective-permute-start(s16[272,256]{1,0:T(8,128)(2,1)S(1)} %get-tuple-element.39), channel_id=1, source_target_pairs={{2,0},{3,1},{4,2},{5,3},{6,4},{7,5},{8,6},{9,7},{10,8},{11,9},{12,... | collective-permute-start | bytes 417800 | tf_op jit(solution)/shard_map/ppermute | solution.py:604

commit v6 on v5

--- a/solution.py
+++ b/solution.py
@@ -11,6 +11,7 @@
 NX = 256
 NY = 256
 TAPS = 4
+SPLIT = 6
 LA = 160
 LB = NY - LA
 ALPHA = math.log(2.0) / 64.0
@@ -186,50 +187,63 @@
     )(slots, counts, source, pltpu.with_memory_space_constraint(lines, pltpu.HBM))
 
 
-def lines_kernel(
-    own_n, peer_n, place_ref, own_hbm, peer_hbm, alias_ref,
-    a0_ref, a1_ref, a2_ref, a3_ref, b_ref,
-    acc_ref, code_ref, rows_ref, ids_ref, sem, *, first, cap,
-):
+def lines_kernel(own_n, peer_n, place_ref, *refs, first, cap, sources):
+    own_refs, peer_refs = refs[:sources], refs[sources : 2 * sources]
+    a0_ref, a1_ref, a2_ref, a3_ref, b_ref = refs[2 * sources + 1 : 2 * sources + 6]
+    acc_ref, code_ref, rows_ref, ids_ref, sem = refs[2 * sources + 6 :]
+    held = own_refs[0].shape[0]
     step = pl.program_id(0)
     last = pl.num_programs(0) - 1
     most = cap // CHUNK
 
     def chunks(tile):
-        return (own_n[first + tile] + CHUNK - 1) // CHUNK, (peer_n[tile] + CHUNK - 1) // CHUNK
-
-    def for_copies(tile, act):
+        return (own_n[first + tile] + CHUNK - 1) // CHUNK, (
+            peer_n[first + tile] + CHUNK - 1
+        ) // CHUNK
+
+    def for_copies(tile, own_ref, peer_ref, row, act):
         slot = lax.rem(tile, 2)
         own, peer = chunks(tile)
-        for j, (source, base, count) in enumerate(((own_hbm, 0, own), (peer_hbm, own, peer))):
+        for j, (source, base, count) in enumerate(((own_ref, 0, own), (peer_ref, own, peer))):
             for i in range(most):
-                copy = pltpu.make_async_copy(
-                    source.at[tile, pl.ds(i * CHUNK, CHUNK), :],
-                    rows_ref.at[slot, pl.ds(pl.multiple_of((base + i) * CHUNK, CHUNK), CHUNK), :],
-                    sem.at[slot, j * (most + 1) + i],
-                )
 
                 @pl.when(i < count)
                 def _():
-                    act(copy)
+                    act(
+                        pltpu.make_async_copy(
+                            source.at[row, pl.ds(i * CHUNK, CHUNK), :],
+                            rows_ref.at[
+                                slot, pl.ds(pl.multiple_of((base + i) * CHUNK, CHUNK), CHUNK), :
+                            ],
+                            sem.at[slot, j * (most + 1) + i],
+                        )
+                    )
 
             act(
                 pltpu.make_async_copy(
-                    source.at[tile, pl.ds(cap, 16), :],
+                    source.at[row, pl.ds(cap, 16), :],
                     ids_ref.at[slot, j],
                     sem.at[slot, j * (most + 1) + most],
                 )
             )
 
+    def start(tile):
+        for k in range(sources):
+
+            @pl.when((first + tile) // held == k)
+            def _():
+                row = first + tile - k * held
+                for_copies(tile, own_refs[k], peer_refs[k], row, lambda copy: copy.start())
+
     @pl.when(step == 0)
     def _():
-        for_copies(0, lambda copy: copy.start())
+        start(step)
 
     @pl.when(step < last)
     def _():
-        for_copies(step + 1, lambda copy: copy.start())
-
-    for_copies(step, lambda copy: copy.wait())
+        start(step + 1)
+
+    for_copies(step, own_refs[0], peer_refs[0], 0, lambda copy: copy.wait())
 
     slot = lax.rem(step, 2)
     own, peer = chunks(step)
@@ -297,25 +311,23 @@
     return jnp.concatenate([row, jnp.zeros((1, NX - row.shape[1]), jnp.float32)], axis=1)
 
 
-def line_blocks(own_rows, peer_rows, own_n, peer_n, place, b_old, first, tiles_all):
-    tiles, cap, _ = own_rows.shape
-    cap -= 16
+def line_blocks(own_rows, peer_rows, own_n, peer_n, place, b_old, first, tiles, tiles_all):
+    cap = own_rows[0].shape[1] - 16
+    sources = len(own_rows)
     a_shape = (tiles * LA + 16, NX)
-    own_rows = pltpu.with_memory_space_constraint(own_rows, pltpu.HBM)
-    peer_rows = pltpu.with_memory_space_constraint(peer_rows, pltpu.HBM)
-    args = [own_n, peer_n, place, own_rows, peer_rows]
+    args = [own_n, peer_n, place] + [in_hbm(rows) for rows in own_rows + peer_rows]
     aliases = {}
     if b_old is None:
         b_old = jnp.zeros((16, NX), jnp.int16)
     else:
-        aliases = {5: 4}
+        aliases = {len(args): 4}
     args.append(b_old)
     return pl.pallas_call(
-        functools.partial(lines_kernel, first=first, cap=cap),
+        functools.partial(lines_kernel, first=first, cap=cap, sources=sources),
         grid_spec=pltpu.PrefetchScalarGridSpec(
             num_scalar_prefetch=3,
             grid=(tiles,),
-            in_specs=[pl.BlockSpec(memory_space=pltpu.HBM)] * 2
+            in_specs=[pl.BlockSpec(memory_space=pltpu.HBM)] * (2 * sources)
             + [pl.BlockSpec(memory_space=pl.ANY)],
             out_specs=[pl.BlockSpec(a_shape, lambda t, *_: (0, 0))] * 4
             + [pl.BlockSpec((1, 4 * LB + 16, NX), lambda t, *_: (t + first, 0, 0))],
@@ -331,9 +343,6 @@
         + [hbm((tiles_all, 4 * LB + 16, NX), jnp.int16)],
         input_output_aliases=aliases,
         compiler_params=params(16),
-        cost_estimate=pl.CostEstimate(
-            flops=2 * 1024 * 256 * 20480, transcendentals=0, bytes_accessed=40_000_000
-        ),
         name="line_blocks",
     )(*args)
 
@@ -345,7 +354,7 @@
     return row[:, 0:length]
 
 
-def sum_x_kernel(p0, p1, p2, p3, alias_ref, out_ref, sum_ref, sem, *, first):
+def sum_x_kernel(p0, p1, p2, p3, alias_ref, wait_ref, out_ref, token_ref, sum_ref, sem, *, first):
     tiles = sum_ref.shape[0]
 
     def copy_out(i):
@@ -360,22 +369,23 @@
         sum_ref[i, pl.ds(0, LA), :] = values
         sum_ref[i, pl.ds(LA, 16), :] = code_block([pad_row(code)])
         copy_out(i).start()
+    token_ref[...] = jnp.zeros(token_ref.shape, jnp.float32)
     for i in range(tiles):
         copy_out(i).wait()
 
 
-def sum_x(parts, old, first, tiles_all):
+def sum_x(parts, old, later, first, tiles_all):
     tiles = (parts[0].shape[0] - 16) // LA
-    aliases = {}
-    if old is None:
-        old = jnp.zeros((16, NX), jnp.int16)
-    else:
-        aliases = {4: 0}
+    aliases = {4: 0} if first else {}
     return pl.pallas_call(
         functools.partial(sum_x_kernel, first=first),
-        in_specs=[pl.BlockSpec(memory_space=pltpu.VMEM)] * 4 + [pl.BlockSpec(memory_space=pl.ANY)],
-        out_specs=pl.BlockSpec(memory_space=pltpu.HBM),
-        out_shape=hbm((tiles_all, LA + 16, NX), jnp.int16),
+        in_specs=[pl.BlockSpec(memory_space=pltpu.VMEM)] * 4
+        + [pl.BlockSpec(memory_space=pl.ANY)] * 2,
+        out_specs=[pl.BlockSpec(memory_space=pltpu.HBM), pl.BlockSpec(memory_space=pltpu.VMEM)],
+        out_shape=[
+            hbm((tiles_all, LA + 16, NX), jnp.int16),
+            jax.ShapeDtypeStruct((8, 128), jnp.float32),
+        ],
         scratch_shapes=[
             pltpu.VMEM((tiles, LA + 16, NX), jnp.int16),
             pltpu.SemaphoreType.DMA((tiles,)),
@@ -383,7 +393,7 @@
         input_output_aliases=aliases,
         compiler_params=pltpu.CompilerParams(vmem_limit_bytes=12 * 1024 * 1024),
         name="sum_x",
-    )(*parts, old)
+    )(*parts, old, later)
 
 
 def sum_tile_kernel(in_hbm_ref, o0, o1, o2, o3, acc_ref, in_ref, sem):
@@ -540,7 +550,7 @@
     anywhere = pl.BlockSpec(memory_space=pl.ANY)
     return pl.pallas_call(
         after_kernel,
-        in_specs=[anywhere] * (1 + len(others)),
+        in_specs=[anywhere] + [pl.BlockSpec(memory_space=pltpu.VMEM)] * len(others),
         out_specs=anywhere,
         out_shape=hbm(x.shape, x.dtype),
         input_output_aliases={0: 0},
@@ -551,6 +561,7 @@
 def local(acquired, stencil, send_slots, send_lines, send_counts, return_slots, return_counts):
     tile_count = lax.axis_size("tile")
     cut_count = lax.axis_size("cuts")
+    first_tiles = tile_count * SPLIT // 16
     tile_half = tile_count // 2
     here = lax.axis_index("cuts")
     here_x = here // 2
@@ -574,24 +585,26 @@
         .astype(jnp.int32)
         for part in peer_rows
     ]
+    peer_counts[1] = jnp.concatenate(peer_counts)
 
     def x_send(block, k):
         return lax.ppermute(block, "cuts", [(i, (i + 2 * k) % cut_count) for i in range(cut_count)])
 
     b_blocks = None
     a_parts = []
-    for h in range(2):
+    for first, last in ((0, first_tiles), (first_tiles, tile_count)):
+        used = 2 if first else 1
         *a_blocks, b_blocks = line_blocks(
-            rows[h], peer_rows[h], counts, peer_counts[h], place,
-            b_blocks, h * tile_half, tile_count,
+            rows[:used], peer_rows[:used], counts, peer_counts[used - 1], place,
+            b_blocks, first, last - first, tile_count,
         )
         a_parts.append([a_blocks[0]] + [x_send(a_blocks[k], k) for k in (1, 2, 3)])
-    near = (a_parts[0][1][:16], a_parts[0][3][:16])
-    b_blocks = after(b_blocks, near)
+    a_sums, token = sum_x(
+        a_parts[0], jnp.zeros((16, NX), jnp.int16), in_hbm(a_parts[1][0]), 0, tile_count
+    )
+    b_blocks = after(b_blocks, [token])
     b_arrived = lax.all_to_all(b_blocks, "tile", split_axis=0, concat_axis=0, tiled=True)
-    a_sums = None
-    for h in range(2):
-        a_sums = sum_x(a_parts[h], a_sums, h * tile_half, tile_count)
+    a_sums, _ = sum_x(a_parts[1], a_sums, in_hbm(a_parts[1][0]), first_tiles, tile_count)
     a_arrived = lax.all_to_all(a_sums, "tile", split_axis=0, concat_axis=0, tiled=True)
     b_sums = sum_tile(b_arrived)
     b_final = [b_sums[0]] + [x_send(b_sums[k], k) for k in (1, 2, 3)]

time: 207 us -> 208 us (level); the launches traced: 205 us -> 204 us
  blocking collectives: 24.9 us -> 19.1 us
  waiting for transfers between devices: 52 us -> 55.8 us
  Pallas kernels: 74.1 us -> 76.8 us
    all_to_all x1, blocking collectives: 24.9 us -> 19.1 us  [local(): lax.all_to_all(outgoing, 'tile', split_axis=0, concat_axis=0, tiled=True)]
    ppermute x4, waiting for transfers between devices: 4.48 us -> 7.68 us  [plane_send(): return lax.ppermute(coded, ('cuts', 'tile'), pairs)]
    ppermute x9, starting transfers between devices: 14.8 us -> 17.2 us  [x_send(): lax.ppermute(block, 'cuts', [(i, (i + 2 * k) % cut_count) for i in range(...]
    all_to_all x1, waiting for transfers between devices: 0.86 us -> 3.13 us  [local(): lax.all_to_all(b_blocks, 'tile', split_axis=0, concat_axis=0, tiled=True)]
  transfers between devices with their start and end apart: 17 -> 17, of which waited for: 7 -> 8; matrix products, arithmetic and copies ran while one was open for 1% -> 1% of each run, Pallas kernels for 27% -> 27%
where the time goes in v6:
time: 208 us; the launch traced here: 204 us
  Pallas kernels  76.8 us (37%)
  waiting for transfers between devices  55.8 us (27%)
  starting transfers between devices  45.7 us (22%)
  blocking collectives  19.1 us (9%)
  local copies, waits for them, and re-layouts  3.14 us (2%)
  other arithmetic  2.2 us (1%)
    ppermute x9, waiting for transfers between devices, x_send(): lax.ppermute(block, 'cuts', [(i, (i + 2 * k) % cut_count) for i in range(...  35.2 us
    pallas_call x2, Pallas kernels, line_blocks(): pl.pallas_call(functools.partial(lines_kernel, first=first, cap=cap, sour...  31.4 us
    pallas_call x2, Pallas kernels, gather_rows(): pl.pallas_call(functools.partial(body, first=first, cap=cap), grid_spec=p...  28 us
    all_to_all x1, blocking collectives, local(): lax.all_to_all(outgoing, 'tile', split_axis=0, concat_axis=0, tiled=True)  19.1 us
    ppermute x9, starting transfers between devices, x_send(): lax.ppermute(block, 'cuts', [(i, (i + 2 * k) % cut_count) for i in range(...  17.2 us
    ppermute x4, starting transfers between devices, plane_send(): return lax.ppermute(coded, ('cuts', 'tile'), pairs)  15 us
    all_to_all x1, waiting for transfers between devices, local(): lax.all_to_all(a_sums, 'tile', split_axis=0, concat_axis=0, tiled=True)  9.75 us
    all_to_all x1, starting transfers between devices, local(): lax.all_to_all(b_blocks, 'tile', split_axis=0, concat_axis=0, tiled=True)  9.03 us
  transfers between devices with their start and end apart: 17, of which 8 were waited for; matrix products, arithmetic and copies ran while one was open for 1% of the time, Pallas kernels for 27%

profile of v6, /device:TPU:1, one launch (start us, length us, event | category | flops | bytes accessed | tf_op | source)
XLA Modules:
  0.0 203.7 jit_solution(7933953401740925564)
XLA Ops:
  0.6 0.9 reshape.19.slots_ref
  1.5 0.7 copy-done.2
  2.2 13.6 %gather_rows.2 = (bf16[8,1296,256]{2,1,0:T(8,128)(2,1)}, f32[16384,256]{1,0:T(8,128)S(1)}) custom-call(s32[20480]{0:T(1024)S(1)} %reshape.19.slots_ref, s32[16]{0:T(128)S(1)} %bitcast.9, bf16[16384,256]{1,0:T(8,128)(2,1)} %acq_ref.1, s32[16,1280]{1,0:T(8,128)} %bitcast.15), custom_call_target="tpu_custom_call" | custom-call | bytes 40000000 | tf_op jit(solution)/shard_map/gather_rows/pallas_call | solution.py:174
  15.8 0.7 collective-permute-start
  16.5 14.4 %gather_rows.3.refs_1_ = bf16[8,1296,256]{2,1,0:T(8,128)(2,1)} custom-call(s32[20480]{0:T(1024)S(1)} %reshape.19.slots_ref, s32[16]{0:T(128)S(1)} %bitcast.10, f32[16384,256]{1,0:T(8,128)S(1)} %get-tuple-element.26.wide_ref, s32[16,1280]{1,0:T(8,128)} %bitcast.16), custom_call_target="tpu_custom_call" | custom-call | bytes 40000000 | tf_op jit(solution)/shard_map/gather_rows/pallas_call | solution.py:174
  30.9 0.1 collective-permute-start.1
  31.0 0.1 pad_add_fusion.1.place_ref
  31.1 1.0 fusion.6.peer_n
  32.1 11.5 %line_blocks.2 = (s16[976,256]{1,0:T(8,128)(2,1)}, s16[976,256]{1,0:T(8,128)(2,1)}, s16[976,256]{1,0:T(8,128)(2,1)}, s16[976,256]{1,0:T(8,128)(2,1)}, s16[16,400,256]{2,1,0:T(8,128)(2,1)}) custom-call(s32[16]{0:T(128)S(1)} %bitcast.11, s32[8]{0:T(128)S(1)} %fusion.6.peer_n, s32[2]{0:T(128)S(1)} %pad_add_fusion.1.place_ref, ...), custom_call_target="tpu_custom_call" | custom-call | tf_op jit(solution)/shard_map/line_blocks/pallas_call | solution.py:325
  43.7 2.6 %collective-permute-start.5 = (s16[976,256]{1,0:T(8,128)(2,1)}, s16[976,256]{1,0:T(8,128)(2,1)S(1)}, u32[]{:S(2)}, u32[]{:S(2)}) collective-permute-start(s16[976,256]{1,0:T(8,128)(2,1)} %get-tuple-element.33), channel_id=1, source_target_pairs={{0,32},{16,48},{32,64},{48,80},{64,96},{80,112},{96,0},{112,16},{1... | collective-permute-start | bytes 1499144 | tf_op jit(solution)/shard_map/ppermute | solution.py:591
  46.3 3.9 %collective-permute-start.6 = (s16[976,256]{1,0:T(8,128)(2,1)}, s16[976,256]{1,0:T(8,128)(2,1)S(1)}, u32[]{:S(2)}, u32[]{:S(2)}) collective-permute-start(s16[976,256]{1,0:T(8,128)(2,1)} %get-tuple-element.34), channel_id=1, source_target_pairs={{0,64},{16,80},{32,96},{48,112},{64,0},{80,16},{96,32},{112,48},{1... | collective-permute-start | bytes 1499144 | tf_op jit(solution)/shard_map/ppermute | solution.py:591
  50.2 1.5 collective-permute-start.7
  51.7 0.0 collective-permute-done.1.refs_3_
  51.7 1.0 fusion.7
  52.7 0.1 pad_add_fusion.peer_n
  52.8 19.9 %line_blocks.3 = (s16[1616,256]{1,0:T(8,128)(2,1)}, s16[1616,256]{1,0:T(8,128)(2,1)}, s16[1616,256]{1,0:T(8,128)(2,1)}, s16[1616,256]{1,0:T(8,128)(2,1)}, s16[16,400,256]{2,1,0:T(8,128)(2,1)}) custom-call(s32[16]{0:T(128)S(1)} %bitcast.12, s32[16]{0:T(128)S(1)} %pad_add_fusion.peer_n, ...), custom_call_target="tpu_custom_call", output_to_operand_aliasing={{4}: (7, {})} | custom-call | tf_op jit(solution)/shard_map/line_blocks/pallas_call | solution.py:325
  72.8 2.3 %sum_x.2 = (s16[16,176,256]{2,1,0:T(8,128)(2,1)}, f32[8,128]{1,0:T(8,128)S(1)}) custom-call(s16[976,256]{1,0:T(8,128)(2,1)S(1)} %copy-done.1, s16[976,256]{1,0:T(8,128)(2,1)S(1)} %collective-permute-done.5.p1, s16[976,256]{1,0:T(8,128)(2,1)S(1)} %collective-permute-done.6.p2, s16[976,256]{1,0:T(8,128)(2,1)S(1)} %collective-permute-done.7.p3, ...), custom_call_target="tpu_custom_call" | custom-call | tf_op jit(solution)/shard_map/sum_x/pallas_call | solution.py:380
  75.1 0.0 copy-start.5
  75.1 0.6 copy-done.5
  75.7 0.8 after.1
  76.5 9.0 %all-to-all-start.1 = ((s16[16,400,256]{2,1,0:T(8,128)(2,1)}), s16[16,400,256]{2,1,0:T(8,128)(2,1)}, u32[]{:S(2)}, u32[]{:S(2)}) async-start(s16[16,400,256]{2,1,0:T(8,128)(2,1)} %after.1), calls=%async_computation.1 | async-start | bytes 6553600 | tf_op jit(solution)/shard_map/all_to_all | solution.py:606
  85.6 0.7 collective-permute-start.2
  86.3 3.0 %collective-permute-start.3 = (s16[1616,256]{1,0:T(8,128)(2,1)S(1)}, s16[1616,256]{1,0:T(8,128)(2,1)S(1)}, u32[]{:S(2)}, u32[]{:S(2)}) collective-permute-start(s16[1616,256]{1,0:T(8,128)(2,1)S(1)} %copy-done.8), channel_id=1, source_target_pairs={{0,64},{16,80},{32,96},{48,112},{64,0},{80,16},{96,32},{112,48},{1... | collective-permute-start | bytes 2482184 | tf_op jit(solution)/shard_map/ppermute | solution.py:591
  89.3 16.2 %collective-permute-done.2.p1 = s16[1616,256]{1,0:T(8,128)(2,1)S(1)} collective-permute-done((s16[1616,256]{1,0:T(8,128)(2,1)S(1)}, s16[1616,256]{1,0:T(8,128)(2,1)S(1)}, u32[]{:S(2)}, u32[]{:S(2)}) %collective-permute-start.2) | collective-permute-done | bytes 827424 | tf_op jit(solution)/shard_map/ppermute | solution.py:591
  105.5 19.0 %collective-permute-done.3.p2 = s16[1616,256]{1,0:T(8,128)(2,1)S(1)} collective-permute-done((s16[1616,256]{1,0:T(8,128)(2,1)S(1)}, s16[1616,256]{1,0:T(8,128)(2,1)S(1)}, u32[]{:S(2)}, u32[]{:S(2)}) %collective-permute-start.3) | collective-permute-done | bytes 827424 | tf_op jit(solution)/shard_map/ppermute | solution.py:591
  124.4 0.1 collective-permute-done.4.p3
  124.5 5.3 %sum_x.3 = (s16[16,176,256]{2,1,0:T(8,128)(2,1)}, f32[8,128]{1,0:T(8,128)}) custom-call(s16[1616,256]{1,0:T(8,128)(2,1)} %get-tuple-element.28.wait_ref.p0, s16[1616,256]{1,0:T(8,128)(2,1)S(1)} %collective-permute-done.2.p1, s16[1616,256]{1,0:T(8,128)(2,1)S(1)} %collective-permute-done.3.p2, ...), custom_call_target="tpu_custom_call", output_to_operand_aliasing={{0}: (4, {})} | custom-call | tf_op jit(solution)/shard_map/sum_x/pallas_call | solution.py:380
  129.8 0.0 copy-start.4
  129.8 0.0 copy-start.6
  129.8 3.1 %all-to-all-done.1.in_hbm_ref = s16[16,400,256]{2,1,0:T(8,128)(2,1)} async-done(((s16[16,400,256]{2,1,0:T(8,128)(2,1)}), s16[16,400,256]{2,1,0:T(8,128)(2,1)}, u32[]{:S(2)}, u32[]{:S(2)}) %all-to-all-start.1) | async-done | bytes 3276832 | tf_op jit(solution)/shard_map/all_to_all | solution.py:606
  133.0 3.7 %all-to-all-start = ((s16[16,176,256]{2,1,0:T(8,128)(2,1)}), s16[16,176,256]{2,1,0:T(8,128)(2,1)S(1)}, u32[]{:S(2)}, u32[]{:S(2)}) async-start(s16[16,176,256]{2,1,0:T(8,128)(2,1)} %get-tuple-element.37), calls=%async_computation | async-start | bytes 2883584 | tf_op jit(solution)/shard_map/all_to_all | solution.py:608
  136.7 3.7 %sum_tile.1 = (s16[112,256]{1,0:T(8,128)(2,1)S(1)}, s16[112,256]{1,0:T(8,128)(2,1)S(1)}, s16[112,256]{1,0:T(8,128)(2,1)S(1)}, s16[112,256]{1,0:T(8,128)(2,1)S(1)}) custom-call(s16[16,400,256]{2,1,0:T(8,128)(2,1)} %all-to-all-done.1.in_hbm_ref), custom_call_target="tpu_custom_call" | custom-call | tf_op jit(solution)/shard_map/sum_tile/pallas_call | solution.py:427
  140.4 2.9 %collective-permute-start.8 = (s16[112,256]{1,0:T(8,128)(2,1)S(1)}, s16[112,256]{1,0:T(8,128)(2,1)S(1)}, u32[]{:S(2)}, u32[]{:S(2)}) collective-permute-start(s16[112,256]{1,0:T(8,128)(2,1)S(1)} %get-tuple-element.41), channel_id=1, source_target_pairs={{0,32},{16,48},{32,64},{48,80},{64,96},{80,112},{96,0},{112,16},{1... | collective-permute-start | bytes 172040 | tf_op jit(solution)/shard_map/ppermute | solution.py:591
  143.3 2.3 %collective-permute-start.9 = (s16[112,256]{1,0:T(8,128)(2,1)S(1)}, s16[112,256]{1,0:T(8,128)(2,1)S(1)}, u32[]{:S(2)}, u32[]{:S(2)}) collective-permute-start(s16[112,256]{1,0:T(8,128)(2,1)S(1)} %get-tuple-element.42), channel_id=1, source_target_pairs={{0,64},{16,80},{32,96},{48,112},{64,0},{80,16},{96,32},{112,48},{1... | collective-permute-start | bytes 172040 | tf_op jit(solution)/shard_map/ppermute | solution.py:591
  145.6 0.2 collective-permute-start.10
  145.8 9.7 %all-to-all-done.a_ref = s16[16,176,256]{2,1,0:T(8,128)(2,1)S(1)} async-done(((s16[16,176,256]{2,1,0:T(8,128)(2,1)}), s16[16,176,256]{2,1,0:T(8,128)(2,1)S(1)}, u32[]{:S(2)}, u32[]{:S(2)}) %all-to-all-start) | async-done | bytes 1441824 | tf_op jit(solution)/shard_map/all_to_all | solution.py:608
  155.5 2.8 %own_plane.1 = (f32[256,256]{1,0:T(8,128)S(1)}, s16[272,256]{1,0:T(8,128)(2,1)S(1)}) custom-call(s16[16,176,256]{2,1,0:T(8,128)(2,1)S(1)} %all-to-all-done.a_ref, s16[112,256]{1,0:T(8,128)(2,1)S(1)} %get-tuple-element.40.b0, s16[112,256]{1,0:T(8,128)(2,1)S(1)} %collective-permute-done.8.b1, s16[112,256]{1,0:T(8,128)(2,1)S(1)} %collective-permute-done.9.b2, ...), custom_call_target="tpu_custom_call" | custom-call | tf_op jit(solution)/shard_map/own_plane/pallas_call | solution.py:478
  158.4 6.6 %collective-permute-start.14 = (s16[272,256]{1,0:T(8,128)(2,1)S(1)}, s16[272,256]{1,0:T(8,128)(2,1)S(1)}, u32[]{:S(2)}, u32[]{:S(2)}) collective-permute-start(s16[272,256]{1,0:T(8,128)(2,1)S(1)} %get-tuple-element.45), channel_id=1, source_target_pairs={{2,0},{3,1},{4,2},{5,3},{6,4},{7,5},{8,6},{9,7},{10,8},{11,9},{12,... | collective-permute-start | bytes 417800 | tf_op jit(solution)/shard_map/ppermute | solution.py:617
  164.9 4.0 %collective-permute-start.13 = (s16[272,256]{1,0:T(8,128)(2,1)S(1)}, s16[272,256]{1,0:T(8,128)(2,1)S(1)}, u32[]{:S(2)}, u32[]{:S(2)}) collective-permute-start(s16[272,256]{1,0:T(8,128)(2,1)S(1)} %get-tuple-element.45), channel_id=1, source_target_pairs={{1,0},{2,1},{3,2},{4,3},{5,4},{6,5},{7,6},{8,7},{9,8},{10,9},{11,1... | collective-permute-start | bytes 417800 | tf_op jit(solution)/shard_map/ppermute | solution.py:617
  169.0 2.5 %collective-permute-start.12 = (s16[272,256]{1,0:T(8,128)(2,1)S(1)}, s16[272,256]{1,0:T(8,128)(2,1)S(1)}, u32[]{:S(2)}, u32[]{:S(2)}) collective-permute-start(s16[272,256]{1,0:T(8,128)(2,1)S(1)} %get-tuple-element.45), channel_id=1, source_target_pairs={{0,2},{1,3},{2,4},{3,5},{4,6},{5,7},{6,8},{7,9},{8,10},{9,11},{10,... | collective-permute-start | bytes 417800 | tf_op jit(solution)/shard_map/ppermute | solution.py:617
  171.5 1.9 collective-permute-start.11
  173.4 0.1 add_convert_fusion.edge_ref
  173.5 1.9 collective-permute-done.13.r1
  175.4 3.5 %collective-permute-done.12.l2 = s16[272,256]{1,0:T(8,128)(2,1)S(1)} collective-permute-done((s16[272,256]{1,0:T(8,128)(2,1)S(1)}, s16[272,256]{1,0:T(8,128)(2,1)S(1)}, u32[]{:S(2)}, u32[]{:S(2)}) %collective-permute-start.12) | collective-permute-done | bytes 139296 | tf_op jit(solution)/shard_map/ppermute | solution.py:617
  179.0 2.2 %collective-permute-done.11.l1 = s16[272,256]{1,0:T(8,128)(2,1)S(1)} collective-permute-done((s16[272,256]{1,0:T(8,128)(2,1)S(1)}, s16[272,256]{1,0:T(8,128)(2,1)S(1)}, u32[]{:S(2)}, u32[]{:S(2)}) %collective-permute-start.11) | collective-permute-done | bytes 139296 | tf_op jit(solution)/shard_map/ppermute | solution.py:617
  181.2 2.4 %smooth.1 = (bf16[256,256]{1,0:T(8,128)(2,1)}, bf16[16,128,256]{2,1,0:T(8,128)(2,1)S(1)}) custom-call(s32[2]{0:T(128)S(1)} %add_convert_fusion.edge_ref, s32[16]{0:T(128)S(1)} %bitcast.14, f32[256,256]{1,0:T(8,128)S(1)} %get-tuple-element.44.plane_ref, s16[272,256]{1,0:T(8,128)(2,1)S(1)} %collective-permute-done.11.l1, ...), custom_call_target="tpu_custom_call" | custom-call | tf_op jit(solution)/shard_map/smooth/pallas_call | solution.py:532
  183.6 19.1 %all_to_all.15 = bf16[16,128,256]{2,1,0:T(8,128)(2,1)S(1)} all-to-all(bf16[16,128,256]{2,1,0:T(8,128)(2,1)S(1)} %get-tuple-element.47), channel_id=1, replica_groups=mesh['cuts'=8,'tile'=16] {'tile'}, dimensions={0} | all-to-all | bytes 2097152 | tf_op jit(solution)/shard_map/all_to_all | solution.py:623
  202.7 1.0 copy.16
  (25 shorter events, 0.1 us)
Async XLA Ops:
  1.5 0.7 copy-start.2
  15.8 15.3 %collective-permute-start = (bf16[8,1296,256]{2,1,0:T(8,128)(2,1)}, bf16[8,1296,256]{2,1,0:T(8,128)(2,1)}, u32[]{:S(2)}, u32[]{:S(2)}) collective-permute-start(bf16[8,1296,256]{2,1,0:T(8,128)(2,1)} %get-tuple-element.25.refs_0_), channel_id=1, source_target_pairs={{0,16},{16,0},{32,48},{48,32},{64,80},{80,64},{96,112},{112,96},{1... | collective-permute-start | bytes 15925256 | tf_op jit(solution)/shard_map/ppermute | solution.py:581
  16.5 15.6 %copy-start.3 = (s32[1,16]{1,0:T(1,128)S(1)}, s32[1,16]{1,0:T(1,128)}, u32[]{:S(2)}) copy-start(s32[1,16]{1,0:T(1,128)} %param.11) | copy-start | bytes 196
  30.9 20.8 %collective-permute-start.1 = (bf16[8,1296,256]{2,1,0:T(8,128)(2,1)}, bf16[8,1296,256]{2,1,0:T(8,128)(2,1)}, u32[]{:S(2)}, u32[]{:S(2)}) collective-permute-start(bf16[8,1296,256]{2,1,0:T(8,128)(2,1)} %gather_rows.3.refs_1_), channel_id=1, source_target_pairs={{0,16},{16,0},{32,48},{48,32},{64,80},{80,64},{96,112},{112,96},{1... | collective-permute-start | bytes 15925256 | tf_op jit(solution)/shard_map/ppermute | solution.py:581
  43.7 29.1 %collective-permute-start.5 = (s16[976,256]{1,0:T(8,128)(2,1)}, s16[976,256]{1,0:T(8,128)(2,1)S(1)}, u32[]{:S(2)}, u32[]{:S(2)}) collective-permute-start(s16[976,256]{1,0:T(8,128)(2,1)} %get-tuple-element.33), channel_id=1, source_target_pairs={{0,32},{16,48},{32,64},{48,80},{64,96},{80,112},{96,0},{112,16},{1... | collective-permute-start | bytes 1499144 | tf_op jit(solution)/shard_map/ppermute | solution.py:591
  46.3 26.4 %collective-permute-start.6 = (s16[976,256]{1,0:T(8,128)(2,1)}, s16[976,256]{1,0:T(8,128)(2,1)S(1)}, u32[]{:S(2)}, u32[]{:S(2)}) collective-permute-start(s16[976,256]{1,0:T(8,128)(2,1)} %get-tuple-element.34), channel_id=1, source_target_pairs={{0,64},{16,80},{32,96},{48,112},{64,0},{80,16},{96,32},{112,48},{1... | collective-permute-start | bytes 1499144 | tf_op jit(solution)/shard_map/ppermute | solution.py:591
  50.2 22.5 %collective-permute-start.7 = (s16[976,256]{1,0:T(8,128)(2,1)}, s16[976,256]{1,0:T(8,128)(2,1)S(1)}, u32[]{:S(2)}, u32[]{:S(2)}) collective-permute-start(s16[976,256]{1,0:T(8,128)(2,1)} %get-tuple-element.35), channel_id=1, source_target_pairs={{0,96},{16,112},{32,0},{48,16},{64,32},{80,48},{96,64},{112,80},{1... | collective-permute-start | bytes 1499144 | tf_op jit(solution)/shard_map/ppermute | solution.py:591
  52.8 20.0 %copy-start.1 = (s16[976,256]{1,0:T(8,128)(2,1)S(1)}, s16[976,256]{1,0:T(8,128)(2,1)}, u32[]{:S(2)}) copy-start(s16[976,256]{1,0:T(8,128)(2,1)} %get-tuple-element.32.p0) | copy-start | bytes 1499140
  75.1 0.6 copy-start.5
  75.7 9.9 %copy-start.9 = (s16[1616,256]{1,0:T(8,128)(2,1)S(1)}, s16[1616,256]{1,0:T(8,128)(2,1)}, u32[]{:S(2)}) copy-start(s16[1616,256]{1,0:T(8,128)(2,1)} %get-tuple-element.29) | copy-start | bytes 2482180
  75.7 10.6 %copy-start.8 = (s16[1616,256]{1,0:T(8,128)(2,1)S(1)}, s16[1616,256]{1,0:T(8,128)(2,1)}, u32[]{:S(2)}) copy-start(s16[1616,256]{1,0:T(8,128)(2,1)} %get-tuple-element.30) | copy-start | bytes 2482180
  75.7 13.6 %copy-start.7 = (s16[1616,256]{1,0:T(8,128)(2,1)S(1)}, s16[1616,256]{1,0:T(8,128)(2,1)}, u32[]{:S(2)}) copy-start(s16[1616,256]{1,0:T(8,128)(2,1)} %get-tuple-element.31) | copy-start | bytes 2482180
  76.5 56.5 %all-to-all-start.1 = ((s16[16,400,256]{2,1,0:T(8,128)(2,1)}), s16[16,400,256]{2,1,0:T(8,128)(2,1)}, u32[]{:S(2)}, u32[]{:S(2)}) async-start(s16[16,400,256]{2,1,0:T(8,128)(2,1)} %after.1), calls=%async_computation.1 | async-start | bytes 6553600 | tf_op jit(solution)/shard_map/all_to_all | solution.py:606
  85.6 19.9 %collective-permute-start.2 = (s16[1616,256]{1,0:T(8,128)(2,1)S(1)}, s16[1616,256]{1,0:T(8,128)(2,1)S(1)}, u32[]{:S(2)}, u32[]{:S(2)}) collective-permute-start(s16[1616,256]{1,0:T(8,128)(2,1)S(1)} %copy-done.9), channel_id=1, source_target_pairs={{0,32},{16,48},{32,64},{48,80},{64,96},{80,112},{96,0},{112,16},{1... | collective-permute-start | bytes 2482184 | tf_op jit(solution)/shard_map/ppermute | solution.py:591
  86.3 38.2 %collective-permute-start.3 = (s16[1616,256]{1,0:T(8,128)(2,1)S(1)}, s16[1616,256]{1,0:T(8,128)(2,1)S(1)}, u32[]{:S(2)}, u32[]{:S(2)}) collective-permute-start(s16[1616,256]{1,0:T(8,128)(2,1)S(1)} %copy-done.8), channel_id=1, source_target_pairs={{0,64},{16,80},{32,96},{48,112},{64,0},{80,16},{96,32},{112,48},{1... | collective-permute-start | bytes 2482184 | tf_op jit(solution)/shard_map/ppermute | solution.py:591
  89.3 35.2 %collective-permute-start.4 = (s16[1616,256]{1,0:T(8,128)(2,1)S(1)}, s16[1616,256]{1,0:T(8,128)(2,1)S(1)}, u32[]{:S(2)}, u32[]{:S(2)}) collective-permute-start(s16[1616,256]{1,0:T(8,128)(2,1)S(1)} %copy-done.7), channel_id=1, source_target_pairs={{0,96},{16,112},{32,0},{48,16},{64,32},{80,48},{96,64},{112,80},{1... | collective-permute-start | bytes 2482184 | tf_op jit(solution)/shard_map/ppermute | solution.py:591
  124.5 31.0 %copy-start = (bf16[256,1024]{1,0:T(8,128)(2,1)S(1)}, bf16[256,1024]{1,0:T(8,128)(2,1)}, u32[]{:S(2)}) copy-start(bf16[256,1024]{1,0:T(8,128)(2,1)} %stencil_ref.1) | copy-start | bytes 1572868
  129.8 51.3 %copy-start.4 = (s32[1,16,128]{2,1,0:T(8,128)S(1)}, s32[1,16,128]{2,1,0:T(8,128)}, u32[]{:S(2)}) copy-start(s32[1,16,128]{2,1,0:T(8,128)} %param.12) | copy-start | bytes 24580
  129.8 51.3 %copy-start.6 = (s32[1,16]{1,0:T(1,128)S(1)}, s32[1,16]{1,0:T(1,128)}, u32[]{:S(2)}) copy-start(s32[1,16]{1,0:T(1,128)} %param.13) | copy-start | bytes 196
  133.0 22.5 %all-to-all-start = ((s16[16,176,256]{2,1,0:T(8,128)(2,1)}), s16[16,176,256]{2,1,0:T(8,128)(2,1)S(1)}, u32[]{:S(2)}, u32[]{:S(2)}) async-start(s16[16,176,256]{2,1,0:T(8,128)(2,1)} %get-tuple-element.37), calls=%async_computation | async-start | bytes 2883584 | tf_op jit(solution)/shard_map/all_to_all | solution.py:608
  140.4 15.1 %collective-permute-start.8 = (s16[112,256]{1,0:T(8,128)(2,1)S(1)}, s16[112,256]{1,0:T(8,128)(2,1)S(1)}, u32[]{:S(2)}, u32[]{:S(2)}) collective-permute-start(s16[112,256]{1,0:T(8,128)(2,1)S(1)} %get-tuple-element.41), channel_id=1, source_target_pairs={{0,32},{16,48},{32,64},{48,80},{64,96},{80,112},{96,0},{112,16},{1... | collective-permute-start | bytes 172040 | tf_op jit(solution)/shard_map/ppermute | solution.py:591
  143.3 12.2 %collective-permute-start.9 = (s16[112,256]{1,0:T(8,128)(2,1)S(1)}, s16[112,256]{1,0:T(8,128)(2,1)S(1)}, u32[]{:S(2)}, u32[]{:S(2)}) collective-permute-start(s16[112,256]{1,0:T(8,128)(2,1)S(1)} %get-tuple-element.42), channel_id=1, source_target_pairs={{0,64},{16,80},{32,96},{48,112},{64,0},{80,16},{96,32},{112,48},{1... | collective-permute-start | bytes 172040 | tf_op jit(solution)/shard_map/ppermute | solution.py:591
  145.6 10.0 %collective-permute-start.10 = (s16[112,256]{1,0:T(8,128)(2,1)S(1)}, s16[112,256]{1,0:T(8,128)(2,1)S(1)}, u32[]{:S(2)}, u32[]{:S(2)}) collective-permute-start(s16[112,256]{1,0:T(8,128)(2,1)S(1)} %get-tuple-element.43), channel_id=1, source_target_pairs={{0,96},{16,112},{32,0},{48,16},{64,32},{80,48},{96,64},{112,80},{1... | collective-permute-start | bytes 172040 | tf_op jit(solution)/shard_map/ppermute | solution.py:591
  158.4 15.1 %collective-permute-start.14 = (s16[272,256]{1,0:T(8,128)(2,1)S(1)}, s16[272,256]{1,0:T(8,128)(2,1)S(1)}, u32[]{:S(2)}, u32[]{:S(2)}) collective-permute-start(s16[272,256]{1,0:T(8,128)(2,1)S(1)} %get-tuple-element.45), channel_id=1, source_target_pairs={{2,0},{3,1},{4,2},{5,3},{6,4},{7,5},{8,6},{9,7},{10,8},{11,9},{12,... | collective-permute-start | bytes 417800 | tf_op jit(solution)/shard_map/ppermute | solution.py:617
  164.9 10.5 %collective-permute-start.13 = (s16[272,256]{1,0:T(8,128)(2,1)S(1)}, s16[272,256]{1,0:T(8,128)(2,1)S(1)}, u32[]{:S(2)}, u32[]{:S(2)}) collective-permute-start(s16[272,256]{1,0:T(8,128)(2,1)S(1)} %get-tuple-element.45), channel_id=1, source_target_pairs={{1,0},{2,1},{3,2},{4,3},{5,4},{6,5},{7,6},{8,7},{9,8},{10,9},{11,1... | collective-permute-start | bytes 417800 | tf_op jit(solution)/shard_map/ppermute | solution.py:617
  169.0 10.0 %collective-permute-start.12 = (s16[272,256]{1,0:T(8,128)(2,1)S(1)}, s16[272,256]{1,0:T(8,128)(2,1)S(1)}, u32[]{:S(2)}, u32[]{:S(2)}) collective-permute-start(s16[272,256]{1,0:T(8,128)(2,1)S(1)} %get-tuple-element.45), channel_id=1, source_target_pairs={{0,2},{1,3},{2,4},{3,5},{4,6},{5,7},{6,8},{7,9},{8,10},{9,11},{10,... | collective-permute-start | bytes 417800 | tf_op jit(solution)/shard_map/ppermute | solution.py:617
  171.5 9.7 %collective-permute-start.11 = (s16[272,256]{1,0:T(8,128)(2,1)S(1)}, s16[272,256]{1,0:T(8,128)(2,1)S(1)}, u32[]{:S(2)}, u32[]{:S(2)}) collective-permute-start(s16[272,256]{1,0:T(8,128)(2,1)S(1)} %get-tuple-element.45), channel_id=1, source_target_pairs={{0,1},{1,2},{2,3},{3,4},{4,5},{5,6},{6,7},{7,8},{8,9},{9,10},{10,1... | collective-permute-start | bytes 417800 | tf_op jit(solution)/shard_map/ppermute | solution.py:617

commit v7 on v5

--- a/solution.py
+++ b/solution.py
@@ -17,6 +17,7 @@
 TOP = 32700.0
 CHUNK = 256
 PICK = 32
+PAD = 8
 
 
 def params(mib):
@@ -61,8 +62,8 @@
 
 
 def code_block(rows):
-    block = jnp.zeros((16, NX), jnp.float32)
-    index = lax.broadcasted_iota(jnp.int32, (16, NX), 0)
+    block = jnp.zeros((PAD, NX), jnp.float32)
+    index = lax.broadcasted_iota(jnp.int32, (PAD, NX), 0)
     for i, row in enumerate(rows):
         block = jnp.where(index == i, row, block)
     return block.astype(jnp.int32).astype(jnp.int16)
@@ -81,14 +82,34 @@
 
         def widen(i, carry):
             span = pl.ds(pl.multiple_of(k * piece + i * CHUNK, CHUNK), CHUNK)
-            wide_ref[span, :] = half_ref[span, :].astype(jnp.float32)
+            x = half_ref[span, :].astype(jnp.float32)
+            for g in range(CHUNK // 8):
+                for c in range(2):
+                    place = pl.multiple_of((k * piece + i * CHUNK) * 2 + (2 * g + c) * 8, 8)
+                    wide_ref[pl.ds(place, 8), :] = x[g * 8 : g * 8 + 8, c * 128 : c * 128 + 128]
             return carry
 
         lax.fori_loop(0, piece // CHUNK, widen, 0)
 
 
 def first_gather_kernel(
-    slots_ref, counts_ref, acq_ref, lines_hbm, out_ref, wide_ref, lines_ref, half_ref, sem, line_sem,
+    counts_ref, acq_ref, lines_hbm, slots_hbm, out_ref, wide_ref, lines_ref, half_ref, sem, line_sem,
+    slots_ref, slot_sem, **sizes,
+):
+    fetch = pltpu.make_async_copy(lines_hbm, lines_ref, line_sem)
+
+    @pl.when(pl.program_id(0) == 0)
+    def _():
+        fetch.start()
+        slots_of(slots_hbm, slots_ref, slot_sem, 0, **sizes).start()
+        widen_kernel(acq_ref, wide_ref, half_ref, sem)
+        fetch.wait()
+
+    gather_tile(slots_hbm, slots_ref, slot_sem, counts_ref, lines_ref, out_ref, wide_ref, **sizes)
+
+
+def next_gather_kernel(
+    counts_ref, wide_ref, lines_hbm, slots_hbm, out_ref, lines_ref, line_sem, slots_ref, slot_sem,
     **sizes,
 ):
     fetch = pltpu.make_async_copy(lines_hbm, lines_ref, line_sem)
@@ -96,34 +117,39 @@
     @pl.when(pl.program_id(0) == 0)
     def _():
         fetch.start()
-        widen_kernel(acq_ref, wide_ref, half_ref, sem)
+        slots_of(slots_hbm, slots_ref, slot_sem, 0, **sizes).start()
         fetch.wait()
 
-    gather_tile(slots_ref, counts_ref, lines_ref, out_ref, wide_ref, **sizes)
-
-
-def next_gather_kernel(
-    slots_ref, counts_ref, wide_ref, lines_hbm, out_ref, lines_ref, line_sem, **sizes
+    gather_tile(slots_hbm, slots_ref, slot_sem, counts_ref, lines_ref, out_ref, wide_ref, **sizes)
+
+
+def slots_of(slots_hbm, slots_ref, slot_sem, tile, *, first, cap):
+    side = lax.rem(tile, 2)
+    return pltpu.make_async_copy(
+        slots_hbm.at[first + tile], slots_ref.at[pl.ds(side * cap, cap)], slot_sem.at[side]
+    )
+
+
+def gather_tile(
+    slots_hbm, slots_ref, slot_sem, counts_ref, lines_ref, out_ref, wide_ref, *, first, cap
 ):
-    fetch = pltpu.make_async_copy(lines_hbm, lines_ref, line_sem)
-
-    @pl.when(pl.program_id(0) == 0)
+    step = pl.program_id(0)
+
+    @pl.when(step + 1 < pl.num_programs(0))
     def _():
-        fetch.start()
-        fetch.wait()
-
-    gather_tile(slots_ref, counts_ref, lines_ref, out_ref, wide_ref, **sizes)
-
-
-def gather_tile(slots_ref, counts_ref, lines_ref, out_ref, wide_ref, *, first, cap):
-    step = pl.program_id(0)
+        slots_of(slots_hbm, slots_ref, slot_sem, step + 1, first=first, cap=cap).start()
+
+    slots_of(slots_hbm, slots_ref, slot_sem, step, first=first, cap=cap).wait()
     count = counts_ref[first + step]
-    start = (first + step) * cap
+    start = lax.rem(step, 2) * cap
 
     def pick(i, carry):
         base = pl.multiple_of(i * PICK, PICK)
-        rows = [wide_ref[pl.ds(slots_ref[start + base + u], 1), :] for u in range(PICK)]
-        out_ref[0, pl.ds(base, PICK), :] = jnp.concatenate(rows, axis=0).astype(jnp.bfloat16)
+        places = [slots_ref[start + base + u] for u in range(PICK)]
+        for c in range(2):
+            rows = [wide_ref[pl.ds(place + 8 * c, 1), :] for place in places]
+            rows = jnp.concatenate(rows, axis=0).astype(jnp.bfloat16)
+            out_ref[0, pl.ds(base, PICK), c * 128 : c * 128 + 128] = rows
         return carry
 
     def clear(i, carry):
@@ -148,7 +174,7 @@
 
 def gather_rows(source, slots, counts, lines, first, tiles):
     cap = lines.shape[1]
-    rows_spec = pl.BlockSpec((1, cap + 16, NX), lambda t, s, c: (t, 0, 0))
+    rows_spec = pl.BlockSpec((1, cap + 16, NX), lambda t, c: (t, 0, 0))
     rows_shape = hbm((tiles, cap + 16, NX), jnp.bfloat16)
     line_scratch = [pltpu.VMEM(lines.shape, jnp.int32)]
     line_sem = [pltpu.SemaphoreType.DMA]
@@ -164,7 +190,7 @@
         source = pltpu.with_memory_space_constraint(source, pltpu.HBM)
         source_spec = pl.BlockSpec(memory_space=pltpu.HBM)
         out_specs = [rows_spec, whole]
-        out_shape = [rows_shape, pltpu.VMEM(source.shape, jnp.float32)]
+        out_shape = [rows_shape, pltpu.VMEM((source.shape[0] * 2, 128), jnp.float32)]
         scratch = (
             line_scratch
             + [pltpu.VMEM(source.shape, jnp.bfloat16), pltpu.SemaphoreType.DMA((8,))]
@@ -173,17 +199,18 @@
     return pl.pallas_call(
         functools.partial(body, first=first, cap=cap),
         grid_spec=pltpu.PrefetchScalarGridSpec(
-            num_scalar_prefetch=2,
+            num_scalar_prefetch=1,
             grid=(tiles,),
-            in_specs=[source_spec, pl.BlockSpec(memory_space=pltpu.HBM)],
+            in_specs=[source_spec] + [pl.BlockSpec(memory_space=pltpu.HBM)] * 2,
             out_specs=out_specs,
-            scratch_shapes=scratch,
+            scratch_shapes=scratch
+            + [pltpu.SMEM((2 * cap,), jnp.int32), pltpu.SemaphoreType.DMA((2,))],
         ),
         out_shape=out_shape,
         compiler_params=params(14),
         cost_estimate=pl.CostEstimate(flops=0, transcendentals=0, bytes_accessed=40_000_000),
         name="gather_rows",
-    )(slots, counts, source, pltpu.with_memory_space_constraint(lines, pltpu.HBM))
+    )(counts, source, in_hbm(lines), in_hbm(slots))
 
 
 def lines_kernel(
@@ -285,12 +312,12 @@
         values, code = encode(acc_ref[pl.ds(4 * LA + k * LB, LB), :])
         b_ref[0, pl.ds(k * LB, LB), :] = values
         codes.append(pad_row(code))
-    b_ref[0, pl.ds(4 * LB, 16), :] = code_block(codes)
+    b_ref[0, pl.ds(4 * LB, PAD), :] = code_block(codes)
 
     @pl.when(step == last)
     def _():
         for k in range(4):
-            outs[k][pl.ds((last + 1) * LA, 16), :] = code_ref[k].astype(jnp.int32).astype(jnp.int16)
+            outs[k][pl.ds((last + 1) * LA, PAD), :] = code_ref[k, 0:PAD].astype(jnp.int32).astype(jnp.int16)
 
 
 def pad_row(row):
@@ -300,7 +327,7 @@
 def line_blocks(own_rows, peer_rows, own_n, peer_n, place, b_old, first, tiles_all):
     tiles, cap, _ = own_rows.shape
     cap -= 16
-    a_shape = (tiles * LA + 16, NX)
+    a_shape = (tiles * LA + PAD, NX)
     own_rows = pltpu.with_memory_space_constraint(own_rows, pltpu.HBM)
     peer_rows = pltpu.with_memory_space_constraint(peer_rows, pltpu.HBM)
     args = [own_n, peer_n, place, own_rows, peer_rows]
@@ -318,7 +345,7 @@
             in_specs=[pl.BlockSpec(memory_space=pltpu.HBM)] * 2
             + [pl.BlockSpec(memory_space=pl.ANY)],
             out_specs=[pl.BlockSpec(a_shape, lambda t, *_: (0, 0))] * 4
-            + [pl.BlockSpec((1, 4 * LB + 16, NX), lambda t, *_: (t + first, 0, 0))],
+            + [pl.BlockSpec((1, 4 * LB + PAD, NX), lambda t, *_: (t + first, 0, 0))],
             scratch_shapes=[
                 pltpu.VMEM((4 * NY, NX), jnp.float32),
                 pltpu.VMEM((5, 16, NX), jnp.float32),
@@ -328,7 +355,7 @@
             ],
         ),
         out_shape=[hbm(a_shape, jnp.int16)] * 4
-        + [hbm((tiles_all, 4 * LB + 16, NX), jnp.int16)],
+        + [hbm((tiles_all, 4 * LB + PAD, NX), jnp.int16)],
         input_output_aliases=aliases,
         compiler_params=params(16),
         cost_estimate=pl.CostEstimate(
@@ -354,18 +381,18 @@
     for i in range(tiles):
         total = jnp.zeros((LA, NX), jnp.float32)
         for part in (p0, p1, p2, p3):
-            codes = code_row(part[pl.ds(tiles * LA, 16), :], i, LA)
+            codes = code_row(part[pl.ds(tiles * LA, PAD), :], i, LA)
             total = total + decode(part[pl.ds(i * LA, LA), :], codes)
         values, code = encode(total)
         sum_ref[i, pl.ds(0, LA), :] = values
-        sum_ref[i, pl.ds(LA, 16), :] = code_block([pad_row(code)])
+        sum_ref[i, pl.ds(LA, PAD), :] = code_block([pad_row(code)])
         copy_out(i).start()
     for i in range(tiles):
         copy_out(i).wait()
 
 
 def sum_x(parts, old, first, tiles_all):
-    tiles = (parts[0].shape[0] - 16) // LA
+    tiles = (parts[0].shape[0] - PAD) // LA
     aliases = {}
     if old is None:
         old = jnp.zeros((16, NX), jnp.int16)
@@ -375,9 +402,9 @@
         functools.partial(sum_x_kernel, first=first),
         in_specs=[pl.BlockSpec(memory_space=pltpu.VMEM)] * 4 + [pl.BlockSpec(memory_space=pl.ANY)],
         out_specs=pl.BlockSpec(memory_space=pltpu.HBM),
-        out_shape=hbm((tiles_all, LA + 16, NX), jnp.int16),
+        out_shape=hbm((tiles_all, LA + PAD, NX), jnp.int16),
         scratch_shapes=[
-            pltpu.VMEM((tiles, LA + 16, NX), jnp.int16),
+            pltpu.VMEM((tiles, LA + PAD, NX), jnp.int16),
             pltpu.SemaphoreType.DMA((tiles,)),
         ],
         input_output_aliases=aliases,
@@ -398,7 +425,7 @@
 
     def body(t, carry):
         fetch(t).wait()
-        table = in_ref[t, pl.ds(4 * LB, 16), :].astype(jnp.int32).astype(jnp.float32)
+        table = in_ref[t, pl.ds(4 * LB, PAD), :].astype(jnp.int32).astype(jnp.float32)
         for k in range(4):
             acc_ref[pl.ds(k * LB, LB), :] += decode(
                 in_ref[t, pl.ds(k * LB, LB), :], table[k : k + 1, 0:LB]
@@ -409,11 +436,11 @@
     for k, out in enumerate((o0, o1, o2, o3)):
         values, code = encode(acc_ref[pl.ds(k * LB, LB), :])
         out[pl.ds(0, LB), :] = values
-        out[pl.ds(LB, 16), :] = code_block([pad_row(code)])
+        out[pl.ds(LB, PAD), :] = code_block([pad_row(code)])
 
 
 def sum_tile(arrived):
-    out_shape = (LB + 16, NX)
+    out_shape = (LB + PAD, NX)
     return pl.pallas_call(
         sum_tile_kernel,
         in_specs=[pl.BlockSpec(memory_space=pltpu.HBM)],
@@ -430,7 +457,7 @@
 
 def plane_kernel(a_ref, b0, b1, b2, b3, stencil_ref, plane_ref, send_ref, lines_ref):
     def body(i, carry):
-        codes = code_row(a_ref[i, pl.ds(LA, 16), :], 0, LA)
+        codes = code_row(a_ref[i, pl.ds(LA, PAD), :], 0, LA)
         lines_ref[pl.ds(0, LA), :] += decode(a_ref[i, pl.ds(0, LA), :], codes)
         return carry
 
@@ -438,7 +465,7 @@
     lax.fori_loop(0, a_ref.shape[0], body, 0)
     total = jnp.zeros((LB, NX), jnp.float32)
     for b in (b0, b1, b2, b3):
-        total = total + decode(b[pl.ds(0, LB), :], code_row(b[pl.ds(LB, 16), :], 0, LB))
+        total = total + decode(b[pl.ds(0, LB), :], code_row(b[pl.ds(LB, PAD), :], 0, LB))
     lines_ref[pl.ds(LA, LB), :] = total
 
     lines = lines_ref[...]
@@ -461,7 +488,7 @@
         values, code = encode(plane[h * 128 : (h + 1) * 128])
         send_ref[pl.ds(h * 128, 128), :] = values
         rows.append(code)
-    send_ref[pl.ds(NY, 16), :] = code_block([jnp.concatenate(rows, axis=1)])
+    send_ref[pl.ds(NY, PAD), :] = code_block([jnp.concatenate(rows, axis=1)])
 
 
 def own_plane(a, bs, stencil):
@@ -469,7 +496,7 @@
         plane_kernel,
         out_shape=[
             jax.ShapeDtypeStruct((NY, NX), jnp.float32),
-            jax.ShapeDtypeStruct((NY + 16, NX), jnp.int16),
+            jax.ShapeDtypeStruct((NY + PAD, NX), jnp.int16),
         ],
         scratch_shapes=[pltpu.VMEM((NY, NX), jnp.float32)],
         compiler_params=pltpu.CompilerParams(vmem_limit_bytes=12 * 1024 * 1024),
@@ -479,7 +506,7 @@
 
 def smooth_kernel(edge_ref, counts_ref, plane_ref, l1, l2, r1, r2, reads_ref, out_ref, back_ref):
     def halo(ref):
-        table = ref[pl.ds(NY, 16), :].astype(jnp.int32).astype(jnp.float32)
+        table = ref[pl.ds(NY, PAD), :].astype(jnp.int32).astype(jnp.float32)
         parts = [
             decode(ref[pl.ds(h * 128, 128), :], table[0:1, h * 128 : (h + 1) * 128])
             for h in range(2)
@@ -557,13 +584,13 @@
     here_core = here % 2
     place = jnp.stack([here_core, here_x]).astype(jnp.int32)
     counts = send_counts[0]
-    flat_slots = send_slots.reshape(-1)
     swap = [(i, i ^ 1) for i in range(cut_count)]
 
+    places = send_slots[0] + (send_slots[0] & ~7)
     rows, peer_rows = [], []
     for h in range(2):
         source = wide if h else acquired
-        made = gather_rows(source, flat_slots, counts, send_lines[0], h * tile_half, tile_half)
+        made = gather_rows(source, places, counts, send_lines[0], h * tile_half, tile_half)
         if not h:
             made, wide = made
         rows.append(made)
@@ -586,7 +613,7 @@
             b_blocks, h * tile_half, tile_count,
         )
         a_parts.append([a_blocks[0]] + [x_send(a_blocks[k], k) for k in (1, 2, 3)])
-    near = (a_parts[0][1][:16], a_parts[0][3][:16])
+    near = [a_parts[0][1][:16] | a_parts[0][3][:16]]
     b_blocks = after(b_blocks, near)
     b_arrived = lax.all_to_all(b_blocks, "tile", split_axis=0, concat_axis=0, tiled=True)
     a_sums = None

time: 207 us -> 197 us (0.952)
  Pallas kernels: 74.1 us -> 66.4 us
  starting transfers between devices: 47.1 us -> 44.4 us
  other arithmetic: 2.1 us -> 4.23 us
  local copies, waits for them, and re-layouts: 3.75 us -> 1.66 us
    pallas_call x2, Pallas kernels: 27.5 us -> 20 us  [gather_rows(): pl.pallas_call(functools.partial(body, first=first, cap=cap), grid_spec=p...]
    ppermute x9, starting transfers between devices: 14.8 us -> 12.7 us  [x_send(): lax.ppermute(block, 'cuts', [(i, (i + 2 * k) % cut_count) for i in range(...]
  transfers between devices with their start and end apart: 17 -> 17, of which waited for: 7 -> 8; matrix products, arithmetic and copies ran while one was open for 1% -> 1% of each run, Pallas kernels for 27% -> 25%
where the time goes in v7:
time: 197 us; the launch traced here: 195 us
  Pallas kernels  66.4 us (34%)
  waiting for transfers between devices  52.8 us (27%)
  starting transfers between devices  44.4 us (23%)
  blocking collectives  24.8 us (13%)
  other arithmetic  4.23 us (2%)
    ppermute x9, waiting for transfers between devices, x_send(): lax.ppermute(block, 'cuts', [(i, (i + 2 * k) % cut_count) for i in range(...  37.7 us
    pallas_call x2, Pallas kernels, line_blocks(): pl.pallas_call(functools.partial(lines_kernel, first=first, cap=cap), gri...  31.7 us
    all_to_all x1, blocking collectives, local(): lax.all_to_all(outgoing, 'tile', split_axis=0, concat_axis=0, tiled=True)  24.8 us
    pallas_call x2, Pallas kernels, gather_rows(): pl.pallas_call(functools.partial(body, first=first, cap=cap), grid_spec=p...  20 us
    ppermute x4, starting transfers between devices, plane_send(): return lax.ppermute(coded, ('cuts', 'tile'), pairs)  15.6 us
    ppermute x9, starting transfers between devices, x_send(): lax.ppermute(block, 'cuts', [(i, (i + 2 * k) % cut_count) for i in range(...  12.7 us
    all_to_all x1, waiting for transfers between devices, local(): lax.all_to_all(a_sums, 'tile', split_axis=0, concat_axis=0, tiled=True)  10.1 us
    all_to_all x1, starting transfers between devices, local(): lax.all_to_all(b_blocks, 'tile', split_axis=0, concat_axis=0, tiled=True)  8.36 us
  transfers between devices with their start and end apart: 17, of which 8 were waited for; matrix products, arithmetic and copies ran while one was open for 1% of the time, Pallas kernels for 25%

profile of v7, /device:TPU:1, one launch (start us, length us, event | category | flops | bytes accessed | tf_op | source)
XLA Modules:
  0.0 195.2 jit_solution(7802433931914708821)
XLA Ops:
  0.6 1.5 and_add_fusion.slots_hbm
  2.2 0.7 copy-done.4
  2.8 12.7 %gather_rows.2 = (bf16[8,1296,256]{2,1,0:T(8,128)(2,1)}, f32[32768,128]{1,0:T(8,128)S(1)}) custom-call(s32[16]{0:T(128)S(1)} %bitcast.12, bf16[16384,256]{1,0:T(8,128)(2,1)} %acq_ref.1, s32[16,1280]{1,0:T(8,128)} %bitcast.17, s32[16,1280]{1,0:T(8,128)} %and_add_fusion.slots_hbm), custom_call_target="tpu_custom_call" | custom-call | bytes 40000000 | tf_op jit(solution)/shard_map/gather_rows/pallas_call | solution.py:199
  15.5 0.1 collective-permute-start.1
  15.6 0.0 copy-start.5
  15.6 7.4 %gather_rows.3.own_hbm = bf16[8,1296,256]{2,1,0:T(8,128)(2,1)} custom-call(s32[16]{0:T(128)S(1)} %bitcast.13, f32[32768,128]{1,0:T(8,128)S(1)} %get-tuple-element.22.wide_ref, s32[16,1280]{1,0:T(8,128)} %bitcast.18, s32[16,1280]{1,0:T(8,128)} %and_add_fusion.slots_hbm), custom_call_target="tpu_custom_call" | custom-call | bytes 40000000 | tf_op jit(solution)/shard_map/gather_rows/pallas_call | solution.py:199
  23.0 1.0 collective-permute-start
  24.0 0.1 pad_add_fusion.place_ref
  24.0 0.7 collective-permute-done.1.peer_hbm
  24.7 1.0 fusion.7.peer_n
  25.7 17.4 %line_blocks.2 = (s16[1288,256]{1,0:T(8,128)(2,1)}, s16[1288,256]{1,0:T(8,128)(2,1)}, s16[1288,256]{1,0:T(8,128)(2,1)}, s16[1288,256]{1,0:T(8,128)(2,1)}, s16[16,392,256]{2,1,0:T(8,128)(2,1)}) custom-call(s32[16]{0:T(128)S(1)} %bitcast.14, s32[8]{0:T(128)S(1)} %fusion.7.peer_n, s32[2]{0:T(128)S(1)} %pad_add_fusion.place_ref, ...), custom_call_target="tpu_custom_call" | custom-call | flops 10737418240 | bytes 40000000 | tf_op jit(solution)/shard_map/line_blocks/pallas_call | solution.py:340
  43.0 3.0 %collective-permute-start.5 = (s16[1288,256]{1,0:T(8,128)(2,1)}, s16[1288,256]{1,0:T(8,128)(2,1)S(1)}, u32[]{:S(2)}, u32[]{:S(2)}) collective-permute-start(s16[1288,256]{1,0:T(8,128)(2,1)} %get-tuple-element.30), channel_id=1, source_target_pairs={{0,32},{16,48},{32,64},{48,80},{64,96},{80,112},{96,0},{112,16},{1... | collective-permute-start | bytes 1978376 | tf_op jit(solution)/shard_map/ppermute | solution.py:606
  46.0 0.0 collective-permute-start.7
  46.0 0.0 collective-permute-done.peer_hbm
  46.0 1.0 fusion.6.peer_n
  47.0 14.3 %line_blocks.3 = (s16[1288,256]{1,0:T(8,128)(2,1)}, s16[1288,256]{1,0:T(8,128)(2,1)}, s16[1288,256]{1,0:T(8,128)(2,1)}, s16[1288,256]{1,0:T(8,128)(2,1)}, s16[16,392,256]{2,1,0:T(8,128)(2,1)}) custom-call(s32[16]{0:T(128)S(1)} %bitcast.15, s32[8]{0:T(128)S(1)} %fusion.6.peer_n, s32[2]{0:T(128)S(1)} %pad_add_fusion.place_ref, ...), custom_call_target="tpu_custom_call", output_to_operand_aliasing={{4}: (5, {})} | custom-call | flops 10737418240 | bytes 40000000 | tf_op jit(solution)/shard_map/line_blocks/pallas_call | solution.py:340
  61.3 0.6 collective-permute-done.7.p3
  61.9 0.6 slice_or_fusion.refs_0_
  62.5 8.4 %all-to-all-start.1 = ((s16[16,392,256]{2,1,0:T(8,128)(2,1)}), s16[16,392,256]{2,1,0:T(8,128)(2,1)}, u32[]{:S(2)}, u32[]{:S(2)}) async-start(s16[16,392,256]{2,1,0:T(8,128)(2,1)} %after.1), calls=%async_computation.1 | async-start | bytes 6422528 | tf_op jit(solution)/shard_map/all_to_all | solution.py:618
  70.9 2.5 %collective-permute-start.6 = (s16[1288,256]{1,0:T(8,128)(2,1)S(1)}, s16[1288,256]{1,0:T(8,128)(2,1)S(1)}, u32[]{:S(2)}, u32[]{:S(2)}) collective-permute-start(s16[1288,256]{1,0:T(8,128)(2,1)S(1)} %copy-done.7), channel_id=1, source_target_pairs={{0,64},{16,80},{32,96},{48,112},{64,0},{80,16},{96,32},{112,48},{1... | collective-permute-start | bytes 1978376 | tf_op jit(solution)/shard_map/ppermute | solution.py:606
  73.5 0.1 collective-permute-start.2
  73.5 1.5 collective-permute-start.3
  75.0 1.1 collective-permute-start.4
  76.1 11.5 %collective-permute-done.6.p2 = s16[1288,256]{1,0:T(8,128)(2,1)S(1)} collective-permute-done((s16[1288,256]{1,0:T(8,128)(2,1)S(1)}, s16[1288,256]{1,0:T(8,128)(2,1)S(1)}, u32[]{:S(2)}, u32[]{:S(2)}) %collective-permute-start.6) | collective-permute-done | bytes 659488 | tf_op jit(solution)/shard_map/ppermute | solution.py:606
  87.6 2.9 %sum_x.2.alias_ref = s16[16,168,256]{2,1,0:T(8,128)(2,1)} custom-call(s16[1288,256]{1,0:T(8,128)(2,1)S(1)} %copy-done.1, s16[1288,256]{1,0:T(8,128)(2,1)S(1)} %collective-permute-done.5.p1, s16[1288,256]{1,0:T(8,128)(2,1)S(1)} %collective-permute-done.6.p2, s16[1288,256]{1,0:T(8,128)(2,1)S(1)} %collective-permute-done.7.p3, ...), custom_call_target="tpu_custom_call" | custom-call | tf_op jit(solution)/shard_map/sum_x/pallas_call | solution.py:401
  90.6 14.6 %collective-permute-done.2.p1 = s16[1288,256]{1,0:T(8,128)(2,1)S(1)} collective-permute-done((s16[1288,256]{1,0:T(8,128)(2,1)}, s16[1288,256]{1,0:T(8,128)(2,1)S(1)}, u32[]{:S(2)}, u32[]{:S(2)}) %collective-permute-start.2) | collective-permute-done | bytes 659488 | tf_op jit(solution)/shard_map/ppermute | solution.py:606
  105.2 10.6 %collective-permute-done.3.p2 = s16[1288,256]{1,0:T(8,128)(2,1)S(1)} collective-permute-done((s16[1288,256]{1,0:T(8,128)(2,1)}, s16[1288,256]{1,0:T(8,128)(2,1)S(1)}, u32[]{:S(2)}, u32[]{:S(2)}) %collective-permute-start.3) | collective-permute-done | bytes 659488 | tf_op jit(solution)/shard_map/ppermute | solution.py:606
  115.8 0.4 collective-permute-done.4.p3
  116.2 2.9 %sum_x.3 = s16[16,168,256]{2,1,0:T(8,128)(2,1)} custom-call(s16[1288,256]{1,0:T(8,128)(2,1)S(1)} %copy-done, s16[1288,256]{1,0:T(8,128)(2,1)S(1)} %collective-permute-done.2.p1, s16[1288,256]{1,0:T(8,128)(2,1)S(1)} %collective-permute-done.3.p2, s16[1288,256]{1,0:T(8,128)(2,1)S(1)} %collective-permute-done.4.p3, ...), custom_call_target="tpu_custom_call", output_to_operand_aliasing={{}: (4, {})} | custom-call | tf_op jit(solution)/shard_map/sum_x/pallas_call | solution.py:401
  119.1 0.0 copy-start.3
  119.1 0.0 copy-start.6
  119.2 6.6 %all-to-all-start = ((s16[16,168,256]{2,1,0:T(8,128)(2,1)}), s16[16,168,256]{2,1,0:T(8,128)(2,1)S(1)}, u32[]{:S(2)}, u32[]{:S(2)}) async-start(s16[16,168,256]{2,1,0:T(8,128)(2,1)} %sum_x.3), calls=%async_computation | async-start | bytes 2752512 | tf_op jit(solution)/shard_map/all_to_all | solution.py:622
  125.8 3.7 %sum_tile.1 = (s16[104,256]{1,0:T(8,128)(2,1)S(1)}, s16[104,256]{1,0:T(8,128)(2,1)S(1)}, s16[104,256]{1,0:T(8,128)(2,1)S(1)}, s16[104,256]{1,0:T(8,128)(2,1)S(1)}) custom-call(s16[16,392,256]{2,1,0:T(8,128)(2,1)} %all-to-all-done.1.in_hbm_ref), custom_call_target="tpu_custom_call" | custom-call | tf_op jit(solution)/shard_map/sum_tile/pallas_call | solution.py:444
  129.5 1.8 collective-permute-start.8
  131.3 2.7 %collective-permute-start.9 = (s16[104,256]{1,0:T(8,128)(2,1)S(1)}, s16[104,256]{1,0:T(8,128)(2,1)S(1)}, u32[]{:S(2)}, u32[]{:S(2)}) collective-permute-start(s16[104,256]{1,0:T(8,128)(2,1)S(1)} %get-tuple-element.36), channel_id=1, source_target_pairs={{0,64},{16,80},{32,96},{48,112},{64,0},{80,16},{96,32},{112,48},{1... | collective-permute-start | bytes 159752 | tf_op jit(solution)/shard_map/ppermute | solution.py:606
  134.0 0.0 collective-permute-start.10
  134.0 10.1 %all-to-all-done.a_ref = s16[16,168,256]{2,1,0:T(8,128)(2,1)S(1)} async-done(((s16[16,168,256]{2,1,0:T(8,128)(2,1)}), s16[16,168,256]{2,1,0:T(8,128)(2,1)S(1)}, u32[]{:S(2)}, u32[]{:S(2)}) %all-to-all-start) | async-done | bytes 1376288 | tf_op jit(solution)/shard_map/all_to_all | solution.py:622
  144.1 0.0 collective-permute-done.10.b3
  144.1 2.8 %own_plane.1 = (f32[256,256]{1,0:T(8,128)S(1)}, s16[264,256]{1,0:T(8,128)(2,1)S(1)}) custom-call(s16[16,168,256]{2,1,0:T(8,128)(2,1)S(1)} %all-to-all-done.a_ref, s16[104,256]{1,0:T(8,128)(2,1)S(1)} %get-tuple-element.34.b0, s16[104,256]{1,0:T(8,128)(2,1)S(1)} %collective-permute-done.8.b1, s16[104,256]{1,0:T(8,128)(2,1)S(1)} %collective-permute-done.9.b2, ...), custom_call_target="tpu_custom_call" | custom-call | tf_op jit(solution)/shard_map/own_plane/pallas_call | solution.py:495
  146.9 2.5 %collective-permute-start.11 = (s16[264,256]{1,0:T(8,128)(2,1)S(1)}, s16[264,256]{1,0:T(8,128)(2,1)S(1)}, u32[]{:S(2)}, u32[]{:S(2)}) collective-permute-start(s16[264,256]{1,0:T(8,128)(2,1)S(1)} %get-tuple-element.39), channel_id=1, source_target_pairs={{0,1},{1,2},{2,3},{3,4},{4,5},{5,6},{6,7},{7,8},{8,9},{9,10},{10,1... | collective-permute-start | bytes 405512 | tf_op jit(solution)/shard_map/ppermute | solution.py:631
  149.5 4.3 %collective-permute-start.12 = (s16[264,256]{1,0:T(8,128)(2,1)S(1)}, s16[264,256]{1,0:T(8,128)(2,1)S(1)}, u32[]{:S(2)}, u32[]{:S(2)}) collective-permute-start(s16[264,256]{1,0:T(8,128)(2,1)S(1)} %get-tuple-element.39), channel_id=1, source_target_pairs={{0,2},{1,3},{2,4},{3,5},{4,6},{5,7},{6,8},{7,9},{8,10},{9,11},{10,... | collective-permute-start | bytes 405512 | tf_op jit(solution)/shard_map/ppermute | solution.py:631
  153.8 6.0 %collective-permute-start.13 = (s16[264,256]{1,0:T(8,128)(2,1)S(1)}, s16[264,256]{1,0:T(8,128)(2,1)S(1)}, u32[]{:S(2)}, u32[]{:S(2)}) collective-permute-start(s16[264,256]{1,0:T(8,128)(2,1)S(1)} %get-tuple-element.39), channel_id=1, source_target_pairs={{1,0},{2,1},{3,2},{4,3},{5,4},{6,5},{7,6},{8,7},{9,8},{10,9},{11,1... | collective-permute-start | bytes 405512 | tf_op jit(solution)/shard_map/ppermute | solution.py:631
  159.8 2.8 %collective-permute-start.14 = (s16[264,256]{1,0:T(8,128)(2,1)S(1)}, s16[264,256]{1,0:T(8,128)(2,1)S(1)}, u32[]{:S(2)}, u32[]{:S(2)}) collective-permute-start(s16[264,256]{1,0:T(8,128)(2,1)S(1)} %get-tuple-element.39), channel_id=1, source_target_pairs={{2,0},{3,1},{4,2},{5,3},{6,4},{7,5},{8,6},{9,7},{10,8},{11,9},{12,... | collective-permute-start | bytes 405512 | tf_op jit(solution)/shard_map/ppermute | solution.py:631
  162.6 0.1 add_convert_fusion.edge_ref
  162.7 4.3 %collective-permute-done.14.r2 = s16[264,256]{1,0:T(8,128)(2,1)S(1)} collective-permute-done((s16[264,256]{1,0:T(8,128)(2,1)S(1)}, s16[264,256]{1,0:T(8,128)(2,1)S(1)}, u32[]{:S(2)}, u32[]{:S(2)}) %collective-permute-start.14) | collective-permute-done | bytes 135200 | tf_op jit(solution)/shard_map/ppermute | solution.py:631
  167.0 2.4 %smooth.1 = (bf16[256,256]{1,0:T(8,128)(2,1)}, bf16[16,128,256]{2,1,0:T(8,128)(2,1)S(1)}) custom-call(s32[2]{0:T(128)S(1)} %add_convert_fusion.edge_ref, s32[16]{0:T(128)S(1)} %bitcast.16, f32[256,256]{1,0:T(8,128)S(1)} %get-tuple-element.38.plane_ref, s16[264,256]{1,0:T(8,128)(2,1)S(1)} %collective-permute-done.11.l1, ...), custom_call_target="tpu_custom_call" | custom-call | tf_op jit(solution)/shard_map/smooth/pallas_call | solution.py:549
  169.4 24.8 %all_to_all.15 = bf16[16,128,256]{2,1,0:T(8,128)(2,1)S(1)} all-to-all(bf16[16,128,256]{2,1,0:T(8,128)(2,1)S(1)} %get-tuple-element.41), channel_id=1, replica_groups=mesh['cuts'=8,'tile'=16] {'tile'}, dimensions={0} | all-to-all | bytes 2097152 | tf_op jit(solution)/shard_map/all_to_all | solution.py:637
  194.2 1.0 copy.16
  (21 shorter events, 0.0 us)
Async XLA Ops:
  2.2 0.7 copy-start.4
  15.5 9.2 %collective-permute-start.1 = (bf16[8,1296,256]{2,1,0:T(8,128)(2,1)}, bf16[8,1296,256]{2,1,0:T(8,128)(2,1)}, u32[]{:S(2)}, u32[]{:S(2)}) collective-permute-start(bf16[8,1296,256]{2,1,0:T(8,128)(2,1)} %get-tuple-element.23.own_hbm), channel_id=1, source_target_pairs={{0,16},{16,0},{32,48},{48,32},{64,80},{80,64},{96,112},{112,96},{1... | collective-permute-start | bytes 15925256 | tf_op jit(solution)/shard_map/ppermute | solution.py:597
  15.6 10.1 %copy-start.5 = (s32[1,16]{1,0:T(1,128)S(1)}, s32[1,16]{1,0:T(1,128)}, u32[]{:S(2)}) copy-start(s32[1,16]{1,0:T(1,128)} %param.11) | copy-start | bytes 196
  23.0 23.0 %collective-permute-start = (bf16[8,1296,256]{2,1,0:T(8,128)(2,1)}, bf16[8,1296,256]{2,1,0:T(8,128)(2,1)}, u32[]{:S(2)}, u32[]{:S(2)}) collective-permute-start(bf16[8,1296,256]{2,1,0:T(8,128)(2,1)} %gather_rows.3.own_hbm), channel_id=1, source_target_pairs={{0,16},{16,0},{32,48},{48,32},{64,80},{80,64},{96,112},{112,96},{1... | collective-permute-start | bytes 15925256 | tf_op jit(solution)/shard_map/ppermute | solution.py:597
  43.0 18.3 %collective-permute-start.5 = (s16[1288,256]{1,0:T(8,128)(2,1)}, s16[1288,256]{1,0:T(8,128)(2,1)S(1)}, u32[]{:S(2)}, u32[]{:S(2)}) collective-permute-start(s16[1288,256]{1,0:T(8,128)(2,1)} %get-tuple-element.30), channel_id=1, source_target_pairs={{0,32},{16,48},{32,64},{48,80},{64,96},{80,112},{96,0},{112,16},{1... | collective-permute-start | bytes 1978376 | tf_op jit(solution)/shard_map/ppermute | solution.py:606
  46.0 15.9 %collective-permute-start.7 = (s16[1288,256]{1,0:T(8,128)(2,1)}, s16[1288,256]{1,0:T(8,128)(2,1)S(1)}, u32[]{:S(2)}, u32[]{:S(2)}) collective-permute-start(s16[1288,256]{1,0:T(8,128)(2,1)} %get-tuple-element.32), channel_id=1, source_target_pairs={{0,96},{16,112},{32,0},{48,16},{64,32},{80,48},{96,64},{112,80},{1... | collective-permute-start | bytes 1978376 | tf_op jit(solution)/shard_map/ppermute | solution.py:606
  62.5 8.4 %copy-start.7 = (s16[1288,256]{1,0:T(8,128)(2,1)S(1)}, s16[1288,256]{1,0:T(8,128)(2,1)}, u32[]{:S(2)}) copy-start(s16[1288,256]{1,0:T(8,128)(2,1)} %get-tuple-element.31) | copy-start | bytes 1978372
  62.5 25.1 %copy-start.1 = (s16[1288,256]{1,0:T(8,128)(2,1)S(1)}, s16[1288,256]{1,0:T(8,128)(2,1)}, u32[]{:S(2)}) copy-start(s16[1288,256]{1,0:T(8,128)(2,1)} %get-tuple-element.29.p0) | copy-start | bytes 1978372
  62.5 53.6 %copy-start = (s16[1288,256]{1,0:T(8,128)(2,1)S(1)}, s16[1288,256]{1,0:T(8,128)(2,1)}, u32[]{:S(2)}) copy-start(s16[1288,256]{1,0:T(8,128)(2,1)} %get-tuple-element.25.p0) | copy-start | bytes 1978372
  62.5 56.6 %all-to-all-start.1 = ((s16[16,392,256]{2,1,0:T(8,128)(2,1)}), s16[16,392,256]{2,1,0:T(8,128)(2,1)}, u32[]{:S(2)}, u32[]{:S(2)}) async-start(s16[16,392,256]{2,1,0:T(8,128)(2,1)} %after.1), calls=%async_computation.1 | async-start | bytes 6422528 | tf_op jit(solution)/shard_map/all_to_all | solution.py:618
  70.9 16.7 %collective-permute-start.6 = (s16[1288,256]{1,0:T(8,128)(2,1)S(1)}, s16[1288,256]{1,0:T(8,128)(2,1)S(1)}, u32[]{:S(2)}, u32[]{:S(2)}) collective-permute-start(s16[1288,256]{1,0:T(8,128)(2,1)S(1)} %copy-done.7), channel_id=1, source_target_pairs={{0,64},{16,80},{32,96},{48,112},{64,0},{80,16},{96,32},{112,48},{1... | collective-permute-start | bytes 1978376 | tf_op jit(solution)/shard_map/ppermute | solution.py:606
  73.5 31.7 %collective-permute-start.2 = (s16[1288,256]{1,0:T(8,128)(2,1)}, s16[1288,256]{1,0:T(8,128)(2,1)S(1)}, u32[]{:S(2)}, u32[]{:S(2)}) collective-permute-start(s16[1288,256]{1,0:T(8,128)(2,1)} %get-tuple-element.26), channel_id=1, source_target_pairs={{0,32},{16,48},{32,64},{48,80},{64,96},{80,112},{96,0},{112,16},{1... | collective-permute-start | bytes 1978376 | tf_op jit(solution)/shard_map/ppermute | solution.py:606
  73.5 42.3 %collective-permute-start.3 = (s16[1288,256]{1,0:T(8,128)(2,1)}, s16[1288,256]{1,0:T(8,128)(2,1)S(1)}, u32[]{:S(2)}, u32[]{:S(2)}) collective-permute-start(s16[1288,256]{1,0:T(8,128)(2,1)} %get-tuple-element.27), channel_id=1, source_target_pairs={{0,64},{16,80},{32,96},{48,112},{64,0},{80,16},{96,32},{112,48},{1... | collective-permute-start | bytes 1978376 | tf_op jit(solution)/shard_map/ppermute | solution.py:606
  75.0 41.2 %collective-permute-start.4 = (s16[1288,256]{1,0:T(8,128)(2,1)}, s16[1288,256]{1,0:T(8,128)(2,1)S(1)}, u32[]{:S(2)}, u32[]{:S(2)}) collective-permute-start(s16[1288,256]{1,0:T(8,128)(2,1)} %get-tuple-element.28), channel_id=1, source_target_pairs={{0,96},{16,112},{32,0},{48,16},{64,32},{80,48},{96,64},{112,80},{1... | collective-permute-start | bytes 1978376 | tf_op jit(solution)/shard_map/ppermute | solution.py:606
  116.2 27.9 %copy-start.2 = (bf16[256,1024]{1,0:T(8,128)(2,1)S(1)}, bf16[256,1024]{1,0:T(8,128)(2,1)}, u32[]{:S(2)}) copy-start(bf16[256,1024]{1,0:T(8,128)(2,1)} %stencil_ref.1) | copy-start | bytes 1572868
  119.1 47.9 %copy-start.3 = (s32[1,16,128]{2,1,0:T(8,128)S(1)}, s32[1,16,128]{2,1,0:T(8,128)}, u32[]{:S(2)}) copy-start(s32[1,16,128]{2,1,0:T(8,128)} %param.12) | copy-start | bytes 24580
  119.1 47.9 %copy-start.6 = (s32[1,16]{1,0:T(1,128)S(1)}, s32[1,16]{1,0:T(1,128)}, u32[]{:S(2)}) copy-start(s32[1,16]{1,0:T(1,128)} %param.13) | copy-start | bytes 196
  119.2 24.9 %all-to-all-start = ((s16[16,168,256]{2,1,0:T(8,128)(2,1)}), s16[16,168,256]{2,1,0:T(8,128)(2,1)S(1)}, u32[]{:S(2)}, u32[]{:S(2)}) async-start(s16[16,168,256]{2,1,0:T(8,128)(2,1)} %sum_x.3), calls=%async_computation | async-start | bytes 2752512 | tf_op jit(solution)/shard_map/all_to_all | solution.py:622
  129.5 14.6 %collective-permute-start.8 = (s16[104,256]{1,0:T(8,128)(2,1)S(1)}, s16[104,256]{1,0:T(8,128)(2,1)S(1)}, u32[]{:S(2)}, u32[]{:S(2)}) collective-permute-start(s16[104,256]{1,0:T(8,128)(2,1)S(1)} %get-tuple-element.35), channel_id=1, source_target_pairs={{0,32},{16,48},{32,64},{48,80},{64,96},{80,112},{96,0},{112,16},{1... | collective-permute-start | bytes 159752 | tf_op jit(solution)/shard_map/ppermute | solution.py:606
  131.3 12.8 %collective-permute-start.9 = (s16[104,256]{1,0:T(8,128)(2,1)S(1)}, s16[104,256]{1,0:T(8,128)(2,1)S(1)}, u32[]{:S(2)}, u32[]{:S(2)}) collective-permute-start(s16[104,256]{1,0:T(8,128)(2,1)S(1)} %get-tuple-element.36), channel_id=1, source_target_pairs={{0,64},{16,80},{32,96},{48,112},{64,0},{80,16},{96,32},{112,48},{1... | collective-permute-start | bytes 159752 | tf_op jit(solution)/shard_map/ppermute | solution.py:606
  134.0 10.1 %collective-permute-start.10 = (s16[104,256]{1,0:T(8,128)(2,1)S(1)}, s16[104,256]{1,0:T(8,128)(2,1)S(1)}, u32[]{:S(2)}, u32[]{:S(2)}) collective-permute-start(s16[104,256]{1,0:T(8,128)(2,1)S(1)} %get-tuple-element.37), channel_id=1, source_target_pairs={{0,96},{16,112},{32,0},{48,16},{64,32},{80,48},{96,64},{112,80},{1... | collective-permute-start | bytes 159752 | tf_op jit(solution)/shard_map/ppermute | solution.py:606
  146.9 15.7 %collective-permute-start.11 = (s16[264,256]{1,0:T(8,128)(2,1)S(1)}, s16[264,256]{1,0:T(8,128)(2,1)S(1)}, u32[]{:S(2)}, u32[]{:S(2)}) collective-permute-start(s16[264,256]{1,0:T(8,128)(2,1)S(1)} %get-tuple-element.39), channel_id=1, source_target_pairs={{0,1},{1,2},{2,3},{3,4},{4,5},{5,6},{6,7},{7,8},{8,9},{9,10},{10,1... | collective-permute-start | bytes 405512 | tf_op jit(solution)/shard_map/ppermute | solution.py:631
  149.5 13.2 %collective-permute-start.12 = (s16[264,256]{1,0:T(8,128)(2,1)S(1)}, s16[264,256]{1,0:T(8,128)(2,1)S(1)}, u32[]{:S(2)}, u32[]{:S(2)}) collective-permute-start(s16[264,256]{1,0:T(8,128)(2,1)S(1)} %get-tuple-element.39), channel_id=1, source_target_pairs={{0,2},{1,3},{2,4},{3,5},{4,6},{5,7},{6,8},{7,9},{8,10},{9,11},{10,... | collective-permute-start | bytes 405512 | tf_op jit(solution)/shard_map/ppermute | solution.py:631
  153.8 8.9 %collective-permute-start.13 = (s16[264,256]{1,0:T(8,128)(2,1)S(1)}, s16[264,256]{1,0:T(8,128)(2,1)S(1)}, u32[]{:S(2)}, u32[]{:S(2)}) collective-permute-start(s16[264,256]{1,0:T(8,128)(2,1)S(1)} %get-tuple-element.39), channel_id=1, source_target_pairs={{1,0},{2,1},{3,2},{4,3},{5,4},{6,5},{7,6},{8,7},{9,8},{10,9},{11,1... | collective-permute-start | bytes 405512 | tf_op jit(solution)/shard_map/ppermute | solution.py:631
  159.8 7.3 %collective-permute-start.14 = (s16[264,256]{1,0:T(8,128)(2,1)S(1)}, s16[264,256]{1,0:T(8,128)(2,1)S(1)}, u32[]{:S(2)}, u32[]{:S(2)}) collective-permute-start(s16[264,256]{1,0:T(8,128)(2,1)S(1)} %get-tuple-element.39), channel_id=1, source_target_pairs={{2,0},{3,1},{4,2},{5,3},{6,4},{7,5},{8,6},{9,7},{10,8},{11,9},{12,... | collective-permute-start | bytes 405512 | tf_op jit(solution)/shard_map/ppermute | solution.py:631

commit v8 on v7

--- a/solution.py
+++ b/solution.py
@@ -16,7 +16,7 @@
 ALPHA = math.log(2.0) / 64.0
 TOP = 32700.0
 CHUNK = 256
-PICK = 32
+PICK = 64
 PAD = 8
 
 
@@ -69,7 +69,7 @@
     return block.astype(jnp.int32).astype(jnp.int16)
 
 
-def widen_kernel(acq_ref, wide_ref, half_ref, sem):
+def widen_kernel(acq_ref, wide_ref, half_ref, sem, meanwhile):
     pieces = sem.shape[0]
     piece = half_ref.shape[0] // pieces
     copies = []
@@ -77,6 +77,7 @@
         span = pl.ds(k * piece, piece)
         copies.append(pltpu.make_async_copy(acq_ref.at[span, :], half_ref.at[span, :], sem.at[k]))
         copies[k].start()
+    meanwhile()
     for k in range(pieces):
         copies[k].wait()
 
@@ -93,53 +94,66 @@
 
 
 def first_gather_kernel(
-    counts_ref, acq_ref, lines_hbm, slots_hbm, out_ref, wide_ref, lines_ref, half_ref, sem, line_sem,
-    slots_ref, slot_sem, **sizes,
+    counts_ref, acq_ref, lines_hbm, slots_hbm, out_ref, wide_ref, places_ref,
+    lines_ref, half_ref, sem, line_sem, slots_ref, slot_sem, **sizes,
+):
+    fetch = pltpu.make_async_copy(lines_hbm, lines_ref, line_sem)
+
+    @pl.when(pl.program_id(0) == 0)
+    def _():
+        def slots_meanwhile():
+            to_places(slots_hbm, places_ref, slot_sem)
+            slots_of(places_ref, slots_ref, slot_sem, 0, **sizes).start()
+
+        fetch.start()
+        widen_kernel(acq_ref, wide_ref, half_ref, sem, slots_meanwhile)
+
+    gather_tile(
+        fetch, places_ref, slots_ref, slot_sem, counts_ref, lines_ref, out_ref, wide_ref, **sizes
+    )
+
+
+def next_gather_kernel(
+    counts_ref, wide_ref, lines_hbm, places_ref, out_ref, lines_ref, line_sem, slots_ref, slot_sem,
+    **sizes,
 ):
     fetch = pltpu.make_async_copy(lines_hbm, lines_ref, line_sem)
 
     @pl.when(pl.program_id(0) == 0)
     def _():
         fetch.start()
-        slots_of(slots_hbm, slots_ref, slot_sem, 0, **sizes).start()
-        widen_kernel(acq_ref, wide_ref, half_ref, sem)
-        fetch.wait()
-
-    gather_tile(slots_hbm, slots_ref, slot_sem, counts_ref, lines_ref, out_ref, wide_ref, **sizes)
-
-
-def next_gather_kernel(
-    counts_ref, wide_ref, lines_hbm, slots_hbm, out_ref, lines_ref, line_sem, slots_ref, slot_sem,
-    **sizes,
-):
-    fetch = pltpu.make_async_copy(lines_hbm, lines_ref, line_sem)
-
-    @pl.when(pl.program_id(0) == 0)
-    def _():
-        fetch.start()
-        slots_of(slots_hbm, slots_ref, slot_sem, 0, **sizes).start()
-        fetch.wait()
-
-    gather_tile(slots_hbm, slots_ref, slot_sem, counts_ref, lines_ref, out_ref, wide_ref, **sizes)
-
-
-def slots_of(slots_hbm, slots_ref, slot_sem, tile, *, first, cap):
+        slots_of(places_ref, slots_ref, slot_sem, 0, **sizes).start()
+
+    gather_tile(
+        fetch, places_ref, slots_ref, slot_sem, counts_ref, lines_ref, out_ref, wide_ref, **sizes
+    )
+
+
+def to_places(slots_hbm, places_ref, slot_sem):
+    fetch = pltpu.make_async_copy(slots_hbm, places_ref, slot_sem.at[0])
+    fetch.start()
+    fetch.wait()
+    slots = places_ref[...]
+    places_ref[...] = slots + (slots & ~7)
+
+
+def slots_of(places_ref, slots_ref, slot_sem, tile, *, first, cap):
     side = lax.rem(tile, 2)
     return pltpu.make_async_copy(
-        slots_hbm.at[first + tile], slots_ref.at[pl.ds(side * cap, cap)], slot_sem.at[side]
+        places_ref.at[first + tile], slots_ref.at[pl.ds(side * cap, cap)], slot_sem.at[side]
     )
 
 
 def gather_tile(
-    slots_hbm, slots_ref, slot_sem, counts_ref, lines_ref, out_ref, wide_ref, *, first, cap
+    fetch, places_ref, slots_ref, slot_sem, counts_ref, lines_ref, out_ref, wide_ref, *, first, cap
 ):
     step = pl.program_id(0)
 
     @pl.when(step + 1 < pl.num_programs(0))
     def _():
-        slots_of(slots_hbm, slots_ref, slot_sem, step + 1, first=first, cap=cap).start()
-
-    slots_of(slots_hbm, slots_ref, slot_sem, step, first=first, cap=cap).wait()
+        slots_of(places_ref, slots_ref, slot_sem, step + 1, first=first, cap=cap).start()
+
+    slots_of(places_ref, slots_ref, slot_sem, step, first=first, cap=cap).wait()
     count = counts_ref[first + step]
     start = lax.rem(step, 2) * cap
 
@@ -160,6 +174,10 @@
     picks = (count + PICK - 1) // PICK
     lax.fori_loop(0, picks, pick, 0)
     lax.fori_loop(picks, (count + CHUNK - 1) // CHUNK * (CHUNK // PICK), clear, 0)
+
+    @pl.when(step == 0)
+    def _():
+        fetch.wait()
 
     ids = lines_ref[pl.ds(first + step, 1), :]
     position = lax.broadcasted_iota(jnp.int32, ids.shape, 1)
@@ -182,15 +200,21 @@
     if first:
         body = next_gather_kernel
         source = pltpu.with_memory_space_constraint(source, pltpu.VMEM)
-        source_spec = whole
+        slots = pltpu.with_memory_space_constraint(slots, pltpu.VMEM)
+        source_spec, slots_spec = whole, whole
         out_specs, out_shape = rows_spec, rows_shape
         scratch = line_scratch + line_sem
     else:
         body = first_gather_kernel
         source = pltpu.with_memory_space_constraint(source, pltpu.HBM)
-        source_spec = pl.BlockSpec(memory_space=pltpu.HBM)
-        out_specs = [rows_spec, whole]
-        out_shape = [rows_shape, pltpu.VMEM((source.shape[0] * 2, 128), jnp.float32)]
+        slots = in_hbm(slots)
+        source_spec = slots_spec = pl.BlockSpec(memory_space=pltpu.HBM)
+        out_specs = [rows_spec, whole, whole]
+        out_shape = [
+            rows_shape,
+            pltpu.VMEM((source.shape[0] * 2, 128), jnp.float32),
+            pltpu.VMEM(slots.shape, jnp.int32),
+        ]
         scratch = (
             line_scratch
             + [pltpu.VMEM(source.shape, jnp.bfloat16), pltpu.SemaphoreType.DMA((8,))]
@@ -201,16 +225,19 @@
         grid_spec=pltpu.PrefetchScalarGridSpec(
             num_scalar_prefetch=1,
             grid=(tiles,),
-            in_specs=[source_spec] + [pl.BlockSpec(memory_space=pltpu.HBM)] * 2,
+            in_specs=[source_spec, pl.BlockSpec(memory_space=pltpu.HBM), slots_spec],
             out_specs=out_specs,
             scratch_shapes=scratch
-            + [pltpu.SMEM((2 * cap,), jnp.int32), pltpu.SemaphoreType.DMA((2,))],
+            + [
+                pltpu.SMEM((2 * cap,), jnp.int32),
+                pltpu.SemaphoreType.DMA((2,)),
+            ],
         ),
         out_shape=out_shape,
         compiler_params=params(14),
         cost_estimate=pl.CostEstimate(flops=0, transcendentals=0, bytes_accessed=40_000_000),
         name="gather_rows",
-    )(counts, source, in_hbm(lines), in_hbm(slots))
+    )(counts, source, in_hbm(lines), slots)
 
 
 def lines_kernel(
@@ -274,10 +301,9 @@
             spot = i if j == 0 else own + i
             code_ref[4, pl.ds(spot, 1), :] = target[i : i + 1].astype(jnp.float32)
 
-    acc_ref[...] = jnp.zeros(acc_ref.shape, jnp.float32)
     position = lax.broadcasted_iota(jnp.int32, (CHUNK, CHUNK), 0).astype(jnp.float32)
 
-    def add(start, width):
+    def add(start, width, first_group=False):
         rows = rows_ref[slot, pl.ds(pl.multiple_of(start * CHUNK, CHUNK), width * CHUNK), :]
         ids = [code_ref[4, pl.ds(start + i, 1), :] for i in range(width)]
         for m in range(acc_ref.shape[0] // CHUNK):
@@ -286,20 +312,22 @@
             ]
             hot = jnp.concatenate(hot, axis=1) if width > 1 else hot[0]
             span = pl.ds(m * CHUNK, CHUNK)
-            acc_ref[span, :] += jnp.dot(hot, rows, preferred_element_type=jnp.float32)
+            product = jnp.dot(hot, rows, preferred_element_type=jnp.float32)
+            acc_ref[span, :] = product if first_group else acc_ref[span, :] + product
 
     total = own + peer
+    head = lax.rem(total - 1, 4) + 1
+    for width in (1, 2, 3, 4):
+
+        @pl.when(head == width)
+        def _():
+            add(0, width, first_group=True)
 
     def four(i, carry):
-        add(i * 4, 4)
+        add(head + i * 4, 4)
         return carry
 
-    lax.fori_loop(0, total // 4, four, 0)
-    for width in (1, 2, 3):
-
-        @pl.when(total % 4 == width)
-        def _():
-            add(total // 4 * 4, width)
+    lax.fori_loop(0, (total - head) // 4, four, 0)
 
     outs = (a0_ref, a1_ref, a2_ref, a3_ref)
     for k in range(4):
@@ -586,13 +614,12 @@
     counts = send_counts[0]
     swap = [(i, i ^ 1) for i in range(cut_count)]
 
-    places = send_slots[0] + (send_slots[0] & ~7)
     rows, peer_rows = [], []
     for h in range(2):
-        source = wide if h else acquired
-        made = gather_rows(source, places, counts, send_lines[0], h * tile_half, tile_half)
+        source, slots = (wide, places) if h else (acquired, send_slots[0])
+        made = gather_rows(source, slots, counts, send_lines[0], h * tile_half, tile_half)
         if not h:
-            made, wide = made
+            made, wide, places = made
         rows.append(made)
         peer_rows.append(lax.ppermute(rows[h], "cuts", swap))
     cap = send_slots.shape[2]

time: 197 us -> 195 us (0.990)
  transfers between devices with their start and end apart: 17 -> 17, of which waited for: 8 -> 6; matrix products, arithmetic and copies ran while one was open for 1% -> 1% of each run, Pallas kernels for 25% -> 25%
where the time goes in v8:
time: 195 us; the launch traced here: 194 us
  Pallas kernels  66 us (34%)
  waiting for transfers between devices  53 us (27%)
  starting transfers between devices  44.3 us (23%)
  blocking collectives  25.2 us (13%)
  other arithmetic  2.7 us (1%)
    ppermute x9, waiting for transfers between devices, x_send(): lax.ppermute(block, 'cuts', [(i, (i + 2 * k) % cut_count) for i in range(...  37.4 us
    pallas_call x2, Pallas kernels, line_blocks(): pl.pallas_call(functools.partial(lines_kernel, first=first, cap=cap), gri...  31.6 us
    all_to_all x1, blocking collectives, local(): lax.all_to_all(outgoing, 'tile', split_axis=0, concat_axis=0, tiled=True)  25.2 us
    pallas_call x2, Pallas kernels, gather_rows(): pl.pallas_call(functools.partial(body, first=first, cap=cap), grid_spec=p...  19.6 us
    ppermute x4, starting transfers between devices, plane_send(): return lax.ppermute(coded, ('cuts', 'tile'), pairs)  15.6 us
    ppermute x9, starting transfers between devices, x_send(): lax.ppermute(block, 'cuts', [(i, (i + 2 * k) % cut_count) for i in range(...  11.8 us
    all_to_all x1, waiting for transfers between devices, local(): lax.all_to_all(a_sums, 'tile', split_axis=0, concat_axis=0, tiled=True)  10.6 us
    all_to_all x1, starting transfers between devices, local(): lax.all_to_all(b_blocks, 'tile', split_axis=0, concat_axis=0, tiled=True)  8.68 us
  transfers between devices with their start and end apart: 17, of which 6 were waited for; matrix products, arithmetic and copies ran while one was open for 1% of the time, Pallas kernels for 25%

profile of v8, /device:TPU:1, one launch (start us, length us, event | category | flops | bytes accessed | tf_op | source)
XLA Modules:
  0.0 193.8 jit_solution(17291744075819791911)
XLA Ops:
  0.6 0.0 copy-start.4
  0.6 0.6 copy-done.4
  1.3 12.1 %gather_rows.2 = (bf16[8,1296,256]{2,1,0:T(8,128)(2,1)}, f32[32768,128]{1,0:T(8,128)S(1)}, s32[16,1280]{1,0:T(8,128)S(1)}) custom-call(s32[16]{0:T(128)S(1)} %bitcast.11, bf16[16384,256]{1,0:T(8,128)(2,1)} %acq_ref.1, s32[16,1280]{1,0:T(8,128)} %bitcast.16, s32[16,1280]{1,0:T(8,128)} %bitcast.18), custom_call_target="tpu_custom_call" | custom-call | bytes 40000000 | tf_op jit(solution)/shard_map/gather_rows/pallas_call | solution.py:223
  13.4 1.9 collective-permute-start.1
  15.2 7.6 %gather_rows.3.own_hbm = bf16[8,1296,256]{2,1,0:T(8,128)(2,1)} custom-call(s32[16]{0:T(128)S(1)} %bitcast.12, f32[32768,128]{1,0:T(8,128)S(1)} %get-tuple-element.23.wide_ref, s32[16,1280]{1,0:T(8,128)} %bitcast.17, s32[16,1280]{1,0:T(8,128)S(1)} %get-tuple-element.24.places_ref), custom_call_target="tpu_custom_call" | custom-call | bytes 40000000 | tf_op jit(solution)/shard_map/gather_rows/pallas_call | solution.py:223
  22.8 0.1 collective-permute-start
  22.9 0.1 pad_add_fusion.place_ref
  23.0 1.0 collective-permute-done.1.peer_hbm
  24.0 1.0 fusion.7.peer_n
  25.0 15.8 %line_blocks.2 = (s16[1288,256]{1,0:T(8,128)(2,1)}, s16[1288,256]{1,0:T(8,128)(2,1)}, s16[1288,256]{1,0:T(8,128)(2,1)}, s16[1288,256]{1,0:T(8,128)(2,1)}, s16[16,392,256]{2,1,0:T(8,128)(2,1)}) custom-call(s32[16]{0:T(128)S(1)} %bitcast.13, s32[8]{0:T(128)S(1)} %fusion.7.peer_n, s32[2]{0:T(128)S(1)} %pad_add_fusion.place_ref, ...), custom_call_target="tpu_custom_call" | custom-call | flops 10737418240 | bytes 40000000 | tf_op jit(solution)/shard_map/line_blocks/pallas_call | solution.py:368
  40.8 1.2 collective-permute-start.5
  42.0 1.5 collective-permute-start.7
  43.5 1.0 fusion.6.peer_n
  44.5 15.8 %line_blocks.3 = (s16[1288,256]{1,0:T(8,128)(2,1)}, s16[1288,256]{1,0:T(8,128)(2,1)}, s16[1288,256]{1,0:T(8,128)(2,1)}, s16[1288,256]{1,0:T(8,128)(2,1)}, s16[16,392,256]{2,1,0:T(8,128)(2,1)}) custom-call(s32[16]{0:T(128)S(1)} %bitcast.14, s32[8]{0:T(128)S(1)} %fusion.6.peer_n, s32[2]{0:T(128)S(1)} %pad_add_fusion.place_ref, ...), custom_call_target="tpu_custom_call", output_to_operand_aliasing={{4}: (5, {})} | custom-call | flops 10737418240 | bytes 40000000 | tf_op jit(solution)/shard_map/line_blocks/pallas_call | solution.py:368
  60.3 0.0 collective-permute-done.5.p1
  60.4 0.6 slice_or_fusion.refs_0_
  61.0 8.7 %all-to-all-start.1 = ((s16[16,392,256]{2,1,0:T(8,128)(2,1)}), s16[16,392,256]{2,1,0:T(8,128)(2,1)}, u32[]{:S(2)}, u32[]{:S(2)}) async-start(s16[16,392,256]{2,1,0:T(8,128)(2,1)} %after.1), calls=%async_computation.1 | async-start | bytes 6422528 | tf_op jit(solution)/shard_map/all_to_all | solution.py:645
  69.7 0.7 collective-permute-start.6
  70.4 1.1 collective-permute-start.2
  71.5 1.2 collective-permute-start.3
  72.7 2.1 %collective-permute-start.4 = (s16[1288,256]{1,0:T(8,128)(2,1)}, s16[1288,256]{1,0:T(8,128)(2,1)S(1)}, u32[]{:S(2)}, u32[]{:S(2)}) collective-permute-start(s16[1288,256]{1,0:T(8,128)(2,1)} %get-tuple-element.30), channel_id=1, source_target_pairs={{0,96},{16,112},{32,0},{48,16},{64,32},{80,48},{96,64},{112,80},{1... | collective-permute-start | bytes 1978376 | tf_op jit(solution)/shard_map/ppermute | solution.py:633
  74.8 12.1 %collective-permute-done.6.p2 = s16[1288,256]{1,0:T(8,128)(2,1)S(1)} collective-permute-done((s16[1288,256]{1,0:T(8,128)(2,1)S(1)}, s16[1288,256]{1,0:T(8,128)(2,1)S(1)}, u32[]{:S(2)}, u32[]{:S(2)}) %collective-permute-start.6) | collective-permute-done | bytes 659488 | tf_op jit(solution)/shard_map/ppermute | solution.py:633
  86.9 2.9 %sum_x.2.alias_ref = s16[16,168,256]{2,1,0:T(8,128)(2,1)} custom-call(s16[1288,256]{1,0:T(8,128)(2,1)S(1)} %copy-done.1, s16[1288,256]{1,0:T(8,128)(2,1)S(1)} %collective-permute-done.5.p1, s16[1288,256]{1,0:T(8,128)(2,1)S(1)} %collective-permute-done.6.p2, s16[1288,256]{1,0:T(8,128)(2,1)S(1)} %collective-permute-done.7.p3, ...), custom_call_target="tpu_custom_call" | custom-call | tf_op jit(solution)/shard_map/sum_x/pallas_call | solution.py:429
  89.9 13.5 %collective-permute-done.2.p1 = s16[1288,256]{1,0:T(8,128)(2,1)S(1)} collective-permute-done((s16[1288,256]{1,0:T(8,128)(2,1)}, s16[1288,256]{1,0:T(8,128)(2,1)S(1)}, u32[]{:S(2)}, u32[]{:S(2)}) %collective-permute-start.2) | collective-permute-done | bytes 659488 | tf_op jit(solution)/shard_map/ppermute | solution.py:633
  103.4 11.7 %collective-permute-done.3.p2 = s16[1288,256]{1,0:T(8,128)(2,1)S(1)} collective-permute-done((s16[1288,256]{1,0:T(8,128)(2,1)}, s16[1288,256]{1,0:T(8,128)(2,1)S(1)}, u32[]{:S(2)}, u32[]{:S(2)}) %collective-permute-start.3) | collective-permute-done | bytes 659488 | tf_op jit(solution)/shard_map/ppermute | solution.py:633
  115.1 2.9 %sum_x.3 = s16[16,168,256]{2,1,0:T(8,128)(2,1)} custom-call(s16[1288,256]{1,0:T(8,128)(2,1)S(1)} %copy-done, s16[1288,256]{1,0:T(8,128)(2,1)S(1)} %collective-permute-done.2.p1, s16[1288,256]{1,0:T(8,128)(2,1)S(1)} %collective-permute-done.3.p2, s16[1288,256]{1,0:T(8,128)(2,1)S(1)} %collective-permute-done.4.p3, ...), custom_call_target="tpu_custom_call", output_to_operand_aliasing={{}: (4, {})} | custom-call | tf_op jit(solution)/shard_map/sum_x/pallas_call | solution.py:429
  118.0 0.0 copy-start.3
  118.1 0.0 copy-start.6
  118.1 0.0 all-to-all-done.1.in_hbm_ref
  118.1 6.3 %all-to-all-start = ((s16[16,168,256]{2,1,0:T(8,128)(2,1)}), s16[16,168,256]{2,1,0:T(8,128)(2,1)S(1)}, u32[]{:S(2)}, u32[]{:S(2)}) async-start(s16[16,168,256]{2,1,0:T(8,128)(2,1)} %sum_x.3), calls=%async_computation | async-start | bytes 2752512 | tf_op jit(solution)/shard_map/all_to_all | solution.py:649
  124.4 3.7 %sum_tile.1 = (s16[104,256]{1,0:T(8,128)(2,1)S(1)}, s16[104,256]{1,0:T(8,128)(2,1)S(1)}, s16[104,256]{1,0:T(8,128)(2,1)S(1)}, s16[104,256]{1,0:T(8,128)(2,1)S(1)}) custom-call(s16[16,392,256]{2,1,0:T(8,128)(2,1)} %all-to-all-done.1.in_hbm_ref), custom_call_target="tpu_custom_call" | custom-call | tf_op jit(solution)/shard_map/sum_tile/pallas_call | solution.py:472
  128.1 0.7 collective-permute-start.8
  128.7 3.2 %collective-permute-start.9 = (s16[104,256]{1,0:T(8,128)(2,1)S(1)}, s16[104,256]{1,0:T(8,128)(2,1)S(1)}, u32[]{:S(2)}, u32[]{:S(2)}) collective-permute-start(s16[104,256]{1,0:T(8,128)(2,1)S(1)} %get-tuple-element.38), channel_id=1, source_target_pairs={{0,64},{16,80},{32,96},{48,112},{64,0},{80,16},{96,32},{112,48},{1... | collective-permute-start | bytes 159752 | tf_op jit(solution)/shard_map/ppermute | solution.py:633
  132.0 0.0 collective-permute-start.10
  132.0 10.6 %all-to-all-done.a_ref = s16[16,168,256]{2,1,0:T(8,128)(2,1)S(1)} async-done(((s16[16,168,256]{2,1,0:T(8,128)(2,1)}), s16[16,168,256]{2,1,0:T(8,128)(2,1)S(1)}, u32[]{:S(2)}, u32[]{:S(2)}) %all-to-all-start) | async-done | bytes 1376288 | tf_op jit(solution)/shard_map/all_to_all | solution.py:649
  142.5 0.0 collective-permute-done.9.b2
  142.6 0.0 collective-permute-done.10.b3
  142.6 2.8 %own_plane.1 = (f32[256,256]{1,0:T(8,128)S(1)}, s16[264,256]{1,0:T(8,128)(2,1)S(1)}) custom-call(s16[16,168,256]{2,1,0:T(8,128)(2,1)S(1)} %all-to-all-done.a_ref, s16[104,256]{1,0:T(8,128)(2,1)S(1)} %get-tuple-element.36.b0, s16[104,256]{1,0:T(8,128)(2,1)S(1)} %collective-permute-done.8.b1, s16[104,256]{1,0:T(8,128)(2,1)S(1)} %collective-permute-done.9.b2, ...), custom_call_target="tpu_custom_call" | custom-call | tf_op jit(solution)/shard_map/own_plane/pallas_call | solution.py:523
  145.4 2.7 %collective-permute-start.11 = (s16[264,256]{1,0:T(8,128)(2,1)S(1)}, s16[264,256]{1,0:T(8,128)(2,1)S(1)}, u32[]{:S(2)}, u32[]{:S(2)}) collective-permute-start(s16[264,256]{1,0:T(8,128)(2,1)S(1)} %get-tuple-element.41), channel_id=1, source_target_pairs={{0,1},{1,2},{2,3},{3,4},{4,5},{5,6},{6,7},{7,8},{8,9},{9,10},{10,1... | collective-permute-start | bytes 405512 | tf_op jit(solution)/shard_map/ppermute | solution.py:658
  148.1 4.3 %collective-permute-start.12 = (s16[264,256]{1,0:T(8,128)(2,1)S(1)}, s16[264,256]{1,0:T(8,128)(2,1)S(1)}, u32[]{:S(2)}, u32[]{:S(2)}) collective-permute-start(s16[264,256]{1,0:T(8,128)(2,1)S(1)} %get-tuple-element.41), channel_id=1, source_target_pairs={{0,2},{1,3},{2,4},{3,5},{4,6},{5,7},{6,8},{7,9},{8,10},{9,11},{10,... | collective-permute-start | bytes 405512 | tf_op jit(solution)/shard_map/ppermute | solution.py:658
  152.4 5.6 %collective-permute-start.13 = (s16[264,256]{1,0:T(8,128)(2,1)S(1)}, s16[264,256]{1,0:T(8,128)(2,1)S(1)}, u32[]{:S(2)}, u32[]{:S(2)}) collective-permute-start(s16[264,256]{1,0:T(8,128)(2,1)S(1)} %get-tuple-element.41), channel_id=1, source_target_pairs={{1,0},{2,1},{3,2},{4,3},{5,4},{6,5},{7,6},{8,7},{9,8},{10,9},{11,1... | collective-permute-start | bytes 405512 | tf_op jit(solution)/shard_map/ppermute | solution.py:658
  157.9 3.1 %collective-permute-start.14 = (s16[264,256]{1,0:T(8,128)(2,1)S(1)}, s16[264,256]{1,0:T(8,128)(2,1)S(1)}, u32[]{:S(2)}, u32[]{:S(2)}) collective-permute-start(s16[264,256]{1,0:T(8,128)(2,1)S(1)} %get-tuple-element.41), channel_id=1, source_target_pairs={{2,0},{3,1},{4,2},{5,3},{6,4},{7,5},{8,6},{9,7},{10,8},{11,9},{12,... | collective-permute-start | bytes 405512 | tf_op jit(solution)/shard_map/ppermute | solution.py:658
  161.1 0.1 add_convert_fusion.edge_ref
  161.1 0.0 collective-permute-done.11.l1
  161.1 4.1 %collective-permute-done.14.r2 = s16[264,256]{1,0:T(8,128)(2,1)S(1)} collective-permute-done((s16[264,256]{1,0:T(8,128)(2,1)S(1)}, s16[264,256]{1,0:T(8,128)(2,1)S(1)}, u32[]{:S(2)}, u32[]{:S(2)}) %collective-permute-start.14) | collective-permute-done | bytes 135200 | tf_op jit(solution)/shard_map/ppermute | solution.py:658
  165.2 2.4 %smooth.1 = (bf16[256,256]{1,0:T(8,128)(2,1)}, bf16[16,128,256]{2,1,0:T(8,128)(2,1)S(1)}) custom-call(s32[2]{0:T(128)S(1)} %add_convert_fusion.edge_ref, s32[16]{0:T(128)S(1)} %bitcast.15, f32[256,256]{1,0:T(8,128)S(1)} %get-tuple-element.40.plane_ref, s16[264,256]{1,0:T(8,128)(2,1)S(1)} %collective-permute-done.11.l1, ...), custom_call_target="tpu_custom_call" | custom-call | tf_op jit(solution)/shard_map/smooth/pallas_call | solution.py:577
  167.6 25.2 %all_to_all.15 = bf16[16,128,256]{2,1,0:T(8,128)(2,1)S(1)} all-to-all(bf16[16,128,256]{2,1,0:T(8,128)(2,1)S(1)} %get-tuple-element.43), channel_id=1, replica_groups=mesh['cuts'=8,'tile'=16] {'tile'}, dimensions={0} | all-to-all | bytes 2097152 | tf_op jit(solution)/shard_map/all_to_all | solution.py:664
  192.9 1.0 copy.16
  (20 shorter events, 0.0 us)
Async XLA Ops:
  0.6 0.7 copy-start.4
  13.4 10.6 %collective-permute-start.1 = (bf16[8,1296,256]{2,1,0:T(8,128)(2,1)}, bf16[8,1296,256]{2,1,0:T(8,128)(2,1)}, u32[]{:S(2)}, u32[]{:S(2)}) collective-permute-start(bf16[8,1296,256]{2,1,0:T(8,128)(2,1)} %get-tuple-element.25.own_hbm), channel_id=1, source_target_pairs={{0,16},{16,0},{32,48},{48,32},{64,80},{80,64},{96,112},{112,96},{1... | collective-permute-start | bytes 15925256 | tf_op jit(solution)/shard_map/ppermute | solution.py:624
  15.2 9.7 %copy-start.5 = (s32[1,16]{1,0:T(1,128)S(1)}, s32[1,16]{1,0:T(1,128)}, u32[]{:S(2)}) copy-start(s32[1,16]{1,0:T(1,128)} %param.11) | copy-start | bytes 196
  22.8 20.7 %collective-permute-start = (bf16[8,1296,256]{2,1,0:T(8,128)(2,1)}, bf16[8,1296,256]{2,1,0:T(8,128)(2,1)}, u32[]{:S(2)}, u32[]{:S(2)}) collective-permute-start(bf16[8,1296,256]{2,1,0:T(8,128)(2,1)} %gather_rows.3.own_hbm), channel_id=1, source_target_pairs={{0,16},{16,0},{32,48},{48,32},{64,80},{80,64},{96,112},{112,96},{1... | collective-permute-start | bytes 15925256 | tf_op jit(solution)/shard_map/ppermute | solution.py:624
  40.8 19.5 %collective-permute-start.5 = (s16[1288,256]{1,0:T(8,128)(2,1)}, s16[1288,256]{1,0:T(8,128)(2,1)S(1)}, u32[]{:S(2)}, u32[]{:S(2)}) collective-permute-start(s16[1288,256]{1,0:T(8,128)(2,1)} %get-tuple-element.32), channel_id=1, source_target_pairs={{0,32},{16,48},{32,64},{48,80},{64,96},{80,112},{96,0},{112,16},{1... | collective-permute-start | bytes 1978376 | tf_op jit(solution)/shard_map/ppermute | solution.py:633
  42.0 18.3 %collective-permute-start.7 = (s16[1288,256]{1,0:T(8,128)(2,1)}, s16[1288,256]{1,0:T(8,128)(2,1)S(1)}, u32[]{:S(2)}, u32[]{:S(2)}) collective-permute-start(s16[1288,256]{1,0:T(8,128)(2,1)} %get-tuple-element.34), channel_id=1, source_target_pairs={{0,96},{16,112},{32,0},{48,16},{64,32},{80,48},{96,64},{112,80},{1... | collective-permute-start | bytes 1978376 | tf_op jit(solution)/shard_map/ppermute | solution.py:633
  61.0 8.7 %copy-start.7 = (s16[1288,256]{1,0:T(8,128)(2,1)S(1)}, s16[1288,256]{1,0:T(8,128)(2,1)}, u32[]{:S(2)}) copy-start(s16[1288,256]{1,0:T(8,128)(2,1)} %get-tuple-element.33) | copy-start | bytes 1978372
  61.0 26.0 %copy-start.1 = (s16[1288,256]{1,0:T(8,128)(2,1)S(1)}, s16[1288,256]{1,0:T(8,128)(2,1)}, u32[]{:S(2)}) copy-start(s16[1288,256]{1,0:T(8,128)(2,1)} %get-tuple-element.31.p0) | copy-start | bytes 1978372
  61.0 54.1 %copy-start = (s16[1288,256]{1,0:T(8,128)(2,1)S(1)}, s16[1288,256]{1,0:T(8,128)(2,1)}, u32[]{:S(2)}) copy-start(s16[1288,256]{1,0:T(8,128)(2,1)} %get-tuple-element.27.p0) | copy-start | bytes 1978372
  61.0 57.1 %all-to-all-start.1 = ((s16[16,392,256]{2,1,0:T(8,128)(2,1)}), s16[16,392,256]{2,1,0:T(8,128)(2,1)}, u32[]{:S(2)}, u32[]{:S(2)}) async-start(s16[16,392,256]{2,1,0:T(8,128)(2,1)} %after.1), calls=%async_computation.1 | async-start | bytes 6422528 | tf_op jit(solution)/shard_map/all_to_all | solution.py:645
  69.7 17.3 %collective-permute-start.6 = (s16[1288,256]{1,0:T(8,128)(2,1)S(1)}, s16[1288,256]{1,0:T(8,128)(2,1)S(1)}, u32[]{:S(2)}, u32[]{:S(2)}) collective-permute-start(s16[1288,256]{1,0:T(8,128)(2,1)S(1)} %copy-done.7), channel_id=1, source_target_pairs={{0,64},{16,80},{32,96},{48,112},{64,0},{80,16},{96,32},{112,48},{1... | collective-permute-start | bytes 1978376 | tf_op jit(solution)/shard_map/ppermute | solution.py:633
  70.4 33.0 %collective-permute-start.2 = (s16[1288,256]{1,0:T(8,128)(2,1)}, s16[1288,256]{1,0:T(8,128)(2,1)S(1)}, u32[]{:S(2)}, u32[]{:S(2)}) collective-permute-start(s16[1288,256]{1,0:T(8,128)(2,1)} %get-tuple-element.28), channel_id=1, source_target_pairs={{0,32},{16,48},{32,64},{48,80},{64,96},{80,112},{96,0},{112,16},{1... | collective-permute-start | bytes 1978376 | tf_op jit(solution)/shard_map/ppermute | solution.py:633
  71.5 43.6 %collective-permute-start.3 = (s16[1288,256]{1,0:T(8,128)(2,1)}, s16[1288,256]{1,0:T(8,128)(2,1)S(1)}, u32[]{:S(2)}, u32[]{:S(2)}) collective-permute-start(s16[1288,256]{1,0:T(8,128)(2,1)} %get-tuple-element.29), channel_id=1, source_target_pairs={{0,64},{16,80},{32,96},{48,112},{64,0},{80,16},{96,32},{112,48},{1... | collective-permute-start | bytes 1978376 | tf_op jit(solution)/shard_map/ppermute | solution.py:633
  72.7 42.4 %collective-permute-start.4 = (s16[1288,256]{1,0:T(8,128)(2,1)}, s16[1288,256]{1,0:T(8,128)(2,1)S(1)}, u32[]{:S(2)}, u32[]{:S(2)}) collective-permute-start(s16[1288,256]{1,0:T(8,128)(2,1)} %get-tuple-element.30), channel_id=1, source_target_pairs={{0,96},{16,112},{32,0},{48,16},{64,32},{80,48},{96,64},{112,80},{1... | collective-permute-start | bytes 1978376 | tf_op jit(solution)/shard_map/ppermute | solution.py:633
  115.1 27.5 %copy-start.2 = (bf16[256,1024]{1,0:T(8,128)(2,1)S(1)}, bf16[256,1024]{1,0:T(8,128)(2,1)}, u32[]{:S(2)}) copy-start(bf16[256,1024]{1,0:T(8,128)(2,1)} %stencil_ref.1) | copy-start | bytes 1572868
  118.0 47.2 %copy-start.3 = (s32[1,16,128]{2,1,0:T(8,128)S(1)}, s32[1,16,128]{2,1,0:T(8,128)}, u32[]{:S(2)}) copy-start(s32[1,16,128]{2,1,0:T(8,128)} %param.12) | copy-start | bytes 24580
  118.1 47.2 %copy-start.6 = (s32[1,16]{1,0:T(1,128)S(1)}, s32[1,16]{1,0:T(1,128)}, u32[]{:S(2)}) copy-start(s32[1,16]{1,0:T(1,128)} %param.13) | copy-start | bytes 196
  118.1 24.5 %all-to-all-start = ((s16[16,168,256]{2,1,0:T(8,128)(2,1)}), s16[16,168,256]{2,1,0:T(8,128)(2,1)S(1)}, u32[]{:S(2)}, u32[]{:S(2)}) async-start(s16[16,168,256]{2,1,0:T(8,128)(2,1)} %sum_x.3), calls=%async_computation | async-start | bytes 2752512 | tf_op jit(solution)/shard_map/all_to_all | solution.py:649
  128.1 14.5 %collective-permute-start.8 = (s16[104,256]{1,0:T(8,128)(2,1)S(1)}, s16[104,256]{1,0:T(8,128)(2,1)S(1)}, u32[]{:S(2)}, u32[]{:S(2)}) collective-permute-start(s16[104,256]{1,0:T(8,128)(2,1)S(1)} %get-tuple-element.37), channel_id=1, source_target_pairs={{0,32},{16,48},{32,64},{48,80},{64,96},{80,112},{96,0},{112,16},{1... | collective-permute-start | bytes 159752 | tf_op jit(solution)/shard_map/ppermute | solution.py:633
  128.7 13.8 %collective-permute-start.9 = (s16[104,256]{1,0:T(8,128)(2,1)S(1)}, s16[104,256]{1,0:T(8,128)(2,1)S(1)}, u32[]{:S(2)}, u32[]{:S(2)}) collective-permute-start(s16[104,256]{1,0:T(8,128)(2,1)S(1)} %get-tuple-element.38), channel_id=1, source_target_pairs={{0,64},{16,80},{32,96},{48,112},{64,0},{80,16},{96,32},{112,48},{1... | collective-permute-start | bytes 159752 | tf_op jit(solution)/shard_map/ppermute | solution.py:633
  132.0 10.6 %collective-permute-start.10 = (s16[104,256]{1,0:T(8,128)(2,1)S(1)}, s16[104,256]{1,0:T(8,128)(2,1)S(1)}, u32[]{:S(2)}, u32[]{:S(2)}) collective-permute-start(s16[104,256]{1,0:T(8,128)(2,1)S(1)} %get-tuple-element.39), channel_id=1, source_target_pairs={{0,96},{16,112},{32,0},{48,16},{64,32},{80,48},{96,64},{112,80},{1... | collective-permute-start | bytes 159752 | tf_op jit(solution)/shard_map/ppermute | solution.py:633
  145.4 15.7 %collective-permute-start.11 = (s16[264,256]{1,0:T(8,128)(2,1)S(1)}, s16[264,256]{1,0:T(8,128)(2,1)S(1)}, u32[]{:S(2)}, u32[]{:S(2)}) collective-permute-start(s16[264,256]{1,0:T(8,128)(2,1)S(1)} %get-tuple-element.41), channel_id=1, source_target_pairs={{0,1},{1,2},{2,3},{3,4},{4,5},{5,6},{6,7},{7,8},{8,9},{9,10},{10,1... | collective-permute-start | bytes 405512 | tf_op jit(solution)/shard_map/ppermute | solution.py:658
  148.1 13.1 %collective-permute-start.12 = (s16[264,256]{1,0:T(8,128)(2,1)S(1)}, s16[264,256]{1,0:T(8,128)(2,1)S(1)}, u32[]{:S(2)}, u32[]{:S(2)}) collective-permute-start(s16[264,256]{1,0:T(8,128)(2,1)S(1)} %get-tuple-element.41), channel_id=1, source_target_pairs={{0,2},{1,3},{2,4},{3,5},{4,6},{5,7},{6,8},{7,9},{8,10},{9,11},{10,... | collective-permute-start | bytes 405512 | tf_op jit(solution)/shard_map/ppermute | solution.py:658
  152.4 8.8 %collective-permute-start.13 = (s16[264,256]{1,0:T(8,128)(2,1)S(1)}, s16[264,256]{1,0:T(8,128)(2,1)S(1)}, u32[]{:S(2)}, u32[]{:S(2)}) collective-permute-start(s16[264,256]{1,0:T(8,128)(2,1)S(1)} %get-tuple-element.41), channel_id=1, source_target_pairs={{1,0},{2,1},{3,2},{4,3},{5,4},{6,5},{7,6},{8,7},{9,8},{10,9},{11,1... | collective-permute-start | bytes 405512 | tf_op jit(solution)/shard_map/ppermute | solution.py:658
  157.9 7.3 %collective-permute-start.14 = (s16[264,256]{1,0:T(8,128)(2,1)S(1)}, s16[264,256]{1,0:T(8,128)(2,1)S(1)}, u32[]{:S(2)}, u32[]{:S(2)}) collective-permute-start(s16[264,256]{1,0:T(8,128)(2,1)S(1)} %get-tuple-element.41), channel_id=1, source_target_pairs={{2,0},{3,1},{4,2},{5,3},{6,4},{7,5},{8,6},{9,7},{10,8},{11,9},{12,... | collective-permute-start | bytes 405512 | tf_op jit(solution)/shard_map/ppermute | solution.py:658

commit v9 on v8

--- a/solution.py
+++ b/solution.py
@@ -11,7 +11,7 @@
 NX = 256
 NY = 256
 TAPS = 4
-LA = 160
+LA = 144
 LB = NY - LA
 ALPHA = math.log(2.0) / 64.0
 TOP = 32700.0

time: 195 us -> 197 us (1.010)
  waiting for transfers between devices: 53 us -> 59.1 us
  Pallas kernels: 66 us -> 63.1 us
  blocking collectives: 25.2 us -> 22.8 us
    all_to_all x1, waiting for transfers between devices: 0.01 us -> 11.6 us  [local(): lax.all_to_all(b_blocks, 'tile', split_axis=0, concat_axis=0, tiled=True)]
    ppermute x9, waiting for transfers between devices: 37.4 us -> 33.2 us  [x_send(): lax.ppermute(block, 'cuts', [(i, (i + 2 * k) % cut_count) for i in range(...]
    all_to_all x1, blocking collectives: 25.2 us -> 22.8 us  [local(): lax.all_to_all(outgoing, 'tile', split_axis=0, concat_axis=0, tiled=True)]
    all_to_all x1, starting transfers between devices: 6.31 us -> 4.29 us  [local(): lax.all_to_all(a_sums, 'tile', split_axis=0, concat_axis=0, tiled=True)]
  transfers between devices with their start and end apart: 17 -> 17, of which waited for: 6 -> 8; matrix products, arithmetic and copies ran while one was open for 1% -> 1% of each run, Pallas kernels for 25% -> 24%
where the time goes in v9:
time: 197 us; the launch traced here: 195 us
  Pallas kernels  63.1 us (32%)
  waiting for transfers between devices  59.1 us (30%)
  starting transfers between devices  45 us (23%)
  blocking collectives  22.8 us (12%)
  other arithmetic  2.7 us (1%)
    ppermute x9, waiting for transfers between devices, x_send(): lax.ppermute(block, 'cuts', [(i, (i + 2 * k) % cut_count) for i in range(...  33.2 us
    pallas_call x2, Pallas kernels, line_blocks(): pl.pallas_call(functools.partial(lines_kernel, first=first, cap=cap), gri...  30 us
    all_to_all x1, blocking collectives, local(): lax.all_to_all(outgoing, 'tile', split_axis=0, concat_axis=0, tiled=True)  22.8 us
    pallas_call x2, Pallas kernels, gather_rows(): pl.pallas_call(functools.partial(body, first=first, cap=cap), grid_spec=p...  18.6 us
    ppermute x4, starting transfers between devices, plane_send(): return lax.ppermute(coded, ('cuts', 'tile'), pairs)  15.6 us
    ppermute x9, starting transfers between devices, x_send(): lax.ppermute(block, 'cuts', [(i, (i + 2 * k) % cut_count) for i in range(...  12.9 us
    all_to_all x1, waiting for transfers between devices, local(): lax.all_to_all(b_blocks, 'tile', split_axis=0, concat_axis=0, tiled=True)  11.6 us
    all_to_all x1, waiting for transfers between devices, local(): lax.all_to_all(a_sums, 'tile', split_axis=0, concat_axis=0, tiled=True)  9.86 us
  transfers between devices with their start and end apart: 17, of which 8 were waited for; matrix products, arithmetic and copies ran while one was open for 1% of the time, Pallas kernels for 24%

profile of v9, /device:TPU:1, one launch (start us, length us, event | category | flops | bytes accessed | tf_op | source)
XLA Modules:
  0.0 195.3 jit_solution(6165159982609404819)
XLA Ops:
  0.6 0.0 copy-start.4
  0.6 0.6 copy-done.4
  1.3 11.0 %gather_rows.2 = (bf16[8,1296,256]{2,1,0:T(8,128)(2,1)}, f32[32768,128]{1,0:T(8,128)S(1)}, s32[16,1280]{1,0:T(8,128)S(1)}) custom-call(s32[16]{0:T(128)S(1)} %bitcast.11, bf16[16384,256]{1,0:T(8,128)(2,1)} %acq_ref.1, s32[16,1280]{1,0:T(8,128)} %bitcast.16, s32[16,1280]{1,0:T(8,128)} %bitcast.18), custom_call_target="tpu_custom_call" | custom-call | bytes 40000000 | tf_op jit(solution)/shard_map/gather_rows/pallas_call | solution.py:223
  12.3 2.0 %collective-permute-start.1 = (bf16[8,1296,256]{2,1,0:T(8,128)(2,1)}, bf16[8,1296,256]{2,1,0:T(8,128)(2,1)}, u32[]{:S(2)}, u32[]{:S(2)}) collective-permute-start(bf16[8,1296,256]{2,1,0:T(8,128)(2,1)} %get-tuple-element.25.own_hbm), channel_id=1, source_target_pairs={{0,16},{16,0},{32,48},{48,32},{64,80},{80,64},{96,112},{112,96},{1... | collective-permute-start | bytes 15925256 | tf_op jit(solution)/shard_map/ppermute | solution.py:624
  14.3 7.6 %gather_rows.3.own_hbm = bf16[8,1296,256]{2,1,0:T(8,128)(2,1)} custom-call(s32[16]{0:T(128)S(1)} %bitcast.12, f32[32768,128]{1,0:T(8,128)S(1)} %get-tuple-element.23.wide_ref, s32[16,1280]{1,0:T(8,128)} %bitcast.17, s32[16,1280]{1,0:T(8,128)S(1)} %get-tuple-element.24.places_ref), custom_call_target="tpu_custom_call" | custom-call | bytes 40000000 | tf_op jit(solution)/shard_map/gather_rows/pallas_call | solution.py:223
  21.9 0.4 collective-permute-start
  22.3 0.1 pad_add_fusion.place_ref
  22.4 0.6 collective-permute-done.1.peer_hbm
  23.0 1.0 fusion.7.peer_n
  24.0 14.1 %line_blocks.2 = (s16[1160,256]{1,0:T(8,128)(2,1)}, s16[1160,256]{1,0:T(8,128)(2,1)}, s16[1160,256]{1,0:T(8,128)(2,1)}, s16[1160,256]{1,0:T(8,128)(2,1)}, s16[16,456,256]{2,1,0:T(8,128)(2,1)}) custom-call(s32[16]{0:T(128)S(1)} %bitcast.13, s32[8]{0:T(128)S(1)} %fusion.7.peer_n, s32[2]{0:T(128)S(1)} %pad_add_fusion.place_ref, ...), custom_call_target="tpu_custom_call" | custom-call | flops 10737418240 | bytes 40000000 | tf_op jit(solution)/shard_map/line_blocks/pallas_call | solution.py:368
  38.1 2.4 %collective-permute-start.5 = (s16[1160,256]{1,0:T(8,128)(2,1)}, s16[1160,256]{1,0:T(8,128)(2,1)S(1)}, u32[]{:S(2)}, u32[]{:S(2)}) collective-permute-start(s16[1160,256]{1,0:T(8,128)(2,1)} %get-tuple-element.32), channel_id=1, source_target_pairs={{0,32},{16,48},{32,64},{48,80},{64,96},{80,112},{96,0},{112,16},{1... | collective-permute-start | bytes 1781768 | tf_op jit(solution)/shard_map/ppermute | solution.py:633
  40.6 2.1 %collective-permute-start.7 = (s16[1160,256]{1,0:T(8,128)(2,1)}, s16[1160,256]{1,0:T(8,128)(2,1)S(1)}, u32[]{:S(2)}, u32[]{:S(2)}) collective-permute-start(s16[1160,256]{1,0:T(8,128)(2,1)} %get-tuple-element.34), channel_id=1, source_target_pairs={{0,96},{16,112},{32,0},{48,16},{64,32},{80,48},{96,64},{112,80},{1... | collective-permute-start | bytes 1781768 | tf_op jit(solution)/shard_map/ppermute | solution.py:633
  42.7 0.0 collective-permute-done.peer_hbm
  42.7 1.0 fusion.6.peer_n
  43.7 15.8 %line_blocks.3 = (s16[1160,256]{1,0:T(8,128)(2,1)}, s16[1160,256]{1,0:T(8,128)(2,1)}, s16[1160,256]{1,0:T(8,128)(2,1)}, s16[1160,256]{1,0:T(8,128)(2,1)}, s16[16,456,256]{2,1,0:T(8,128)(2,1)}) custom-call(s32[16]{0:T(128)S(1)} %bitcast.14, s32[8]{0:T(128)S(1)} %fusion.6.peer_n, s32[2]{0:T(128)S(1)} %pad_add_fusion.place_ref, ...), custom_call_target="tpu_custom_call", output_to_operand_aliasing={{4}: (5, {})} | custom-call | flops 10737418240 | bytes 40000000 | tf_op jit(solution)/shard_map/line_blocks/pallas_call | solution.py:368
  59.5 0.0 collective-permute-done.5.p1
  59.5 0.0 collective-permute-done.7.p3
  59.5 0.6 slice_or_fusion.refs_0_
  60.1 9.8 %all-to-all-start.1 = ((s16[16,456,256]{2,1,0:T(8,128)(2,1)}), s16[16,456,256]{2,1,0:T(8,128)(2,1)}, u32[]{:S(2)}, u32[]{:S(2)}) async-start(s16[16,456,256]{2,1,0:T(8,128)(2,1)} %after.1), calls=%async_computation.1 | async-start | bytes 7471104 | tf_op jit(solution)/shard_map/all_to_all | solution.py:645
  69.9 1.2 collective-permute-start.6
  71.1 0.0 collective-permute-start.2
  71.2 1.8 collective-permute-start.3
  73.0 2.1 %collective-permute-start.4 = (s16[1160,256]{1,0:T(8,128)(2,1)}, s16[1160,256]{1,0:T(8,128)(2,1)S(1)}, u32[]{:S(2)}, u32[]{:S(2)}) collective-permute-start(s16[1160,256]{1,0:T(8,128)(2,1)} %get-tuple-element.30), channel_id=1, source_target_pairs={{0,96},{16,112},{32,0},{48,16},{64,32},{80,48},{96,64},{112,80},{1... | collective-permute-start | bytes 1781768 | tf_op jit(solution)/shard_map/ppermute | solution.py:633
  75.1 10.6 %collective-permute-done.6.p2 = s16[1160,256]{1,0:T(8,128)(2,1)S(1)} collective-permute-done((s16[1160,256]{1,0:T(8,128)(2,1)S(1)}, s16[1160,256]{1,0:T(8,128)(2,1)S(1)}, u32[]{:S(2)}, u32[]{:S(2)}) %collective-permute-start.6) | collective-permute-done | bytes 593952 | tf_op jit(solution)/shard_map/ppermute | solution.py:633
  85.7 2.8 %sum_x.2.alias_ref = s16[16,152,256]{2,1,0:T(8,128)(2,1)} custom-call(s16[1160,256]{1,0:T(8,128)(2,1)S(1)} %copy-done, s16[1160,256]{1,0:T(8,128)(2,1)S(1)} %collective-permute-done.5.p1, s16[1160,256]{1,0:T(8,128)(2,1)S(1)} %collective-permute-done.6.p2, s16[1160,256]{1,0:T(8,128)(2,1)S(1)} %collective-permute-done.7.p3, ...), custom_call_target="tpu_custom_call" | custom-call | tf_op jit(solution)/shard_map/sum_x/pallas_call | solution.py:429
  88.4 12.6 %collective-permute-done.2.p1 = s16[1160,256]{1,0:T(8,128)(2,1)S(1)} collective-permute-done((s16[1160,256]{1,0:T(8,128)(2,1)}, s16[1160,256]{1,0:T(8,128)(2,1)S(1)}, u32[]{:S(2)}, u32[]{:S(2)}) %collective-permute-start.2) | collective-permute-done | bytes 593952 | tf_op jit(solution)/shard_map/ppermute | solution.py:633
  101.0 10.0 %collective-permute-done.3.p2 = s16[1160,256]{1,0:T(8,128)(2,1)S(1)} collective-permute-done((s16[1160,256]{1,0:T(8,128)(2,1)}, s16[1160,256]{1,0:T(8,128)(2,1)S(1)}, u32[]{:S(2)}, u32[]{:S(2)}) %collective-permute-start.3) | collective-permute-done | bytes 593952 | tf_op jit(solution)/shard_map/ppermute | solution.py:633
  111.0 2.8 %sum_x.3 = s16[16,152,256]{2,1,0:T(8,128)(2,1)} custom-call(s16[1160,256]{1,0:T(8,128)(2,1)S(1)} %copy-done.1, s16[1160,256]{1,0:T(8,128)(2,1)S(1)} %collective-permute-done.2.p1, s16[1160,256]{1,0:T(8,128)(2,1)S(1)} %collective-permute-done.3.p2, s16[1160,256]{1,0:T(8,128)(2,1)S(1)} %collective-permute-done.4.p3, ...), custom_call_target="tpu_custom_call", output_to_operand_aliasing={{}: (4, {})} | custom-call | tf_op jit(solution)/shard_map/sum_x/pallas_call | solution.py:429
  113.8 0.0 copy-start.3
  113.8 0.0 copy-start.6
  113.8 11.6 %all-to-all-done.1.in_hbm_ref = s16[16,456,256]{2,1,0:T(8,128)(2,1)} async-done(((s16[16,456,256]{2,1,0:T(8,128)(2,1)}), s16[16,456,256]{2,1,0:T(8,128)(2,1)}, u32[]{:S(2)}, u32[]{:S(2)}) %all-to-all-start.1) | async-done | bytes 3735584 | tf_op jit(solution)/shard_map/all_to_all | solution.py:645
  125.4 4.3 %all-to-all-start = ((s16[16,152,256]{2,1,0:T(8,128)(2,1)}), s16[16,152,256]{2,1,0:T(8,128)(2,1)S(1)}, u32[]{:S(2)}, u32[]{:S(2)}) async-start(s16[16,152,256]{2,1,0:T(8,128)(2,1)} %sum_x.3), calls=%async_computation | async-start | bytes 2490368 | tf_op jit(solution)/shard_map/all_to_all | solution.py:649
  129.7 3.9 %sum_tile.1 = (s16[120,256]{1,0:T(8,128)(2,1)S(1)}, s16[120,256]{1,0:T(8,128)(2,1)S(1)}, s16[120,256]{1,0:T(8,128)(2,1)S(1)}, s16[120,256]{1,0:T(8,128)(2,1)S(1)}) custom-call(s16[16,456,256]{2,1,0:T(8,128)(2,1)} %all-to-all-done.1.in_hbm_ref), custom_call_target="tpu_custom_call" | custom-call | tf_op jit(solution)/shard_map/sum_tile/pallas_call | solution.py:472
  133.6 0.1 collective-permute-start.8
  133.7 1.2 collective-permute-start.9
  134.8 2.0 %collective-permute-start.10 = (s16[120,256]{1,0:T(8,128)(2,1)S(1)}, s16[120,256]{1,0:T(8,128)(2,1)S(1)}, u32[]{:S(2)}, u32[]{:S(2)}) collective-permute-start(s16[120,256]{1,0:T(8,128)(2,1)S(1)} %get-tuple-element.39), channel_id=1, source_target_pairs={{0,96},{16,112},{32,0},{48,16},{64,32},{80,48},{96,64},{112,80},{1... | collective-permute-start | bytes 184328 | tf_op jit(solution)/shard_map/ppermute | solution.py:633
  136.8 9.9 %all-to-all-done.a_ref = s16[16,152,256]{2,1,0:T(8,128)(2,1)S(1)} async-done(((s16[16,152,256]{2,1,0:T(8,128)(2,1)}), s16[16,152,256]{2,1,0:T(8,128)(2,1)S(1)}, u32[]{:S(2)}, u32[]{:S(2)}) %all-to-all-start) | async-done | bytes 1245216 | tf_op jit(solution)/shard_map/all_to_all | solution.py:649
  146.7 2.8 %own_plane.1 = (f32[256,256]{1,0:T(8,128)S(1)}, s16[264,256]{1,0:T(8,128)(2,1)S(1)}) custom-call(s16[16,152,256]{2,1,0:T(8,128)(2,1)S(1)} %all-to-all-done.a_ref, s16[120,256]{1,0:T(8,128)(2,1)S(1)} %get-tuple-element.36.b0, s16[120,256]{1,0:T(8,128)(2,1)S(1)} %collective-permute-done.8.b1, s16[120,256]{1,0:T(8,128)(2,1)S(1)} %collective-permute-done.9.b2, ...), custom_call_target="tpu_custom_call" | custom-call | tf_op jit(solution)/shard_map/own_plane/pallas_call | solution.py:523
  149.5 2.6 %collective-permute-start.11 = (s16[264,256]{1,0:T(8,128)(2,1)S(1)}, s16[264,256]{1,0:T(8,128)(2,1)S(1)}, u32[]{:S(2)}, u32[]{:S(2)}) collective-permute-start(s16[264,256]{1,0:T(8,128)(2,1)S(1)} %get-tuple-element.41), channel_id=1, source_target_pairs={{0,1},{1,2},{2,3},{3,4},{4,5},{5,6},{6,7},{7,8},{8,9},{9,10},{10,1... | collective-permute-start | bytes 405512 | tf_op jit(solution)/shard_map/ppermute | solution.py:658
  152.1 4.2 %collective-permute-start.12 = (s16[264,256]{1,0:T(8,128)(2,1)S(1)}, s16[264,256]{1,0:T(8,128)(2,1)S(1)}, u32[]{:S(2)}, u32[]{:S(2)}) collective-permute-start(s16[264,256]{1,0:T(8,128)(2,1)S(1)} %get-tuple-element.41), channel_id=1, source_target_pairs={{0,2},{1,3},{2,4},{3,5},{4,6},{5,7},{6,8},{7,9},{8,10},{9,11},{10,... | collective-permute-start | bytes 405512 | tf_op jit(solution)/shard_map/ppermute | solution.py:658
  156.3 5.5 %collective-permute-start.13 = (s16[264,256]{1,0:T(8,128)(2,1)S(1)}, s16[264,256]{1,0:T(8,128)(2,1)S(1)}, u32[]{:S(2)}, u32[]{:S(2)}) collective-permute-start(s16[264,256]{1,0:T(8,128)(2,1)S(1)} %get-tuple-element.41), channel_id=1, source_target_pairs={{1,0},{2,1},{3,2},{4,3},{5,4},{6,5},{7,6},{8,7},{9,8},{10,9},{11,1... | collective-permute-start | bytes 405512 | tf_op jit(solution)/shard_map/ppermute | solution.py:658
  161.8 3.3 %collective-permute-start.14 = (s16[264,256]{1,0:T(8,128)(2,1)S(1)}, s16[264,256]{1,0:T(8,128)(2,1)S(1)}, u32[]{:S(2)}, u32[]{:S(2)}) collective-permute-start(s16[264,256]{1,0:T(8,128)(2,1)S(1)} %get-tuple-element.41), channel_id=1, source_target_pairs={{2,0},{3,1},{4,2},{5,3},{6,4},{7,5},{8,6},{9,7},{10,8},{11,9},{12,... | collective-permute-start | bytes 405512 | tf_op jit(solution)/shard_map/ppermute | solution.py:658
  165.1 0.1 add_convert_fusion.edge_ref
  165.2 1.4 collective-permute-done.13.r1
  166.7 2.4 %collective-permute-done.14.r2 = s16[264,256]{1,0:T(8,128)(2,1)S(1)} collective-permute-done((s16[264,256]{1,0:T(8,128)(2,1)S(1)}, s16[264,256]{1,0:T(8,128)(2,1)S(1)}, u32[]{:S(2)}, u32[]{:S(2)}) %collective-permute-start.14) | collective-permute-done | bytes 135200 | tf_op jit(solution)/shard_map/ppermute | solution.py:658
  169.1 2.4 %smooth.1 = (bf16[256,256]{1,0:T(8,128)(2,1)}, bf16[16,128,256]{2,1,0:T(8,128)(2,1)S(1)}) custom-call(s32[2]{0:T(128)S(1)} %add_convert_fusion.edge_ref, s32[16]{0:T(128)S(1)} %bitcast.15, f32[256,256]{1,0:T(8,128)S(1)} %get-tuple-element.40.plane_ref, s16[264,256]{1,0:T(8,128)(2,1)S(1)} %collective-permute-done.11.l1, ...), custom_call_target="tpu_custom_call" | custom-call | tf_op jit(solution)/shard_map/smooth/pallas_call | solution.py:577
  171.5 22.8 %all_to_all.15 = bf16[16,128,256]{2,1,0:T(8,128)(2,1)S(1)} all-to-all(bf16[16,128,256]{2,1,0:T(8,128)(2,1)S(1)} %get-tuple-element.43), channel_id=1, replica_groups=mesh['cuts'=8,'tile'=16] {'tile'}, dimensions={0} | all-to-all | bytes 2097152 | tf_op jit(solution)/shard_map/all_to_all | solution.py:664
  194.3 1.0 copy.16
  (20 shorter events, 0.0 us)
Async XLA Ops:
  0.6 0.7 copy-start.4
  12.3 10.7 %collective-permute-start.1 = (bf16[8,1296,256]{2,1,0:T(8,128)(2,1)}, bf16[8,1296,256]{2,1,0:T(8,128)(2,1)}, u32[]{:S(2)}, u32[]{:S(2)}) collective-permute-start(bf16[8,1296,256]{2,1,0:T(8,128)(2,1)} %get-tuple-element.25.own_hbm), channel_id=1, source_target_pairs={{0,16},{16,0},{32,48},{48,32},{64,80},{80,64},{96,112},{112,96},{1... | collective-permute-start | bytes 15925256 | tf_op jit(solution)/shard_map/ppermute | solution.py:624
  14.3 9.7 %copy-start.5 = (s32[1,16]{1,0:T(1,128)S(1)}, s32[1,16]{1,0:T(1,128)}, u32[]{:S(2)}) copy-start(s32[1,16]{1,0:T(1,128)} %param.11) | copy-start | bytes 196
  21.9 20.8 %collective-permute-start = (bf16[8,1296,256]{2,1,0:T(8,128)(2,1)}, bf16[8,1296,256]{2,1,0:T(8,128)(2,1)}, u32[]{:S(2)}, u32[]{:S(2)}) collective-permute-start(bf16[8,1296,256]{2,1,0:T(8,128)(2,1)} %gather_rows.3.own_hbm), channel_id=1, source_target_pairs={{0,16},{16,0},{32,48},{48,32},{64,80},{80,64},{96,112},{112,96},{1... | collective-permute-start | bytes 15925256 | tf_op jit(solution)/shard_map/ppermute | solution.py:624
  38.1 21.4 %collective-permute-start.5 = (s16[1160,256]{1,0:T(8,128)(2,1)}, s16[1160,256]{1,0:T(8,128)(2,1)S(1)}, u32[]{:S(2)}, u32[]{:S(2)}) collective-permute-start(s16[1160,256]{1,0:T(8,128)(2,1)} %get-tuple-element.32), channel_id=1, source_target_pairs={{0,32},{16,48},{32,64},{48,80},{64,96},{80,112},{96,0},{112,16},{1... | collective-permute-start | bytes 1781768 | tf_op jit(solution)/shard_map/ppermute | solution.py:633
  40.6 18.9 %collective-permute-start.7 = (s16[1160,256]{1,0:T(8,128)(2,1)}, s16[1160,256]{1,0:T(8,128)(2,1)S(1)}, u32[]{:S(2)}, u32[]{:S(2)}) collective-permute-start(s16[1160,256]{1,0:T(8,128)(2,1)} %get-tuple-element.34), channel_id=1, source_target_pairs={{0,96},{16,112},{32,0},{48,16},{64,32},{80,48},{96,64},{112,80},{1... | collective-permute-start | bytes 1781768 | tf_op jit(solution)/shard_map/ppermute | solution.py:633
  60.1 9.8 %copy-start.7 = (s16[1160,256]{1,0:T(8,128)(2,1)S(1)}, s16[1160,256]{1,0:T(8,128)(2,1)}, u32[]{:S(2)}) copy-start(s16[1160,256]{1,0:T(8,128)(2,1)} %get-tuple-element.33) | copy-start | bytes 1781764
  60.1 25.5 %copy-start = (s16[1160,256]{1,0:T(8,128)(2,1)S(1)}, s16[1160,256]{1,0:T(8,128)(2,1)}, u32[]{:S(2)}) copy-start(s16[1160,256]{1,0:T(8,128)(2,1)} %get-tuple-element.31.p0) | copy-start | bytes 1781764
  60.1 50.9 %copy-start.1 = (s16[1160,256]{1,0:T(8,128)(2,1)S(1)}, s16[1160,256]{1,0:T(8,128)(2,1)}, u32[]{:S(2)}) copy-start(s16[1160,256]{1,0:T(8,128)(2,1)} %get-tuple-element.27.p0) | copy-start | bytes 1781764
  60.1 65.3 %all-to-all-start.1 = ((s16[16,456,256]{2,1,0:T(8,128)(2,1)}), s16[16,456,256]{2,1,0:T(8,128)(2,1)}, u32[]{:S(2)}, u32[]{:S(2)}) async-start(s16[16,456,256]{2,1,0:T(8,128)(2,1)} %after.1), calls=%async_computation.1 | async-start | bytes 7471104 | tf_op jit(solution)/shard_map/all_to_all | solution.py:645
  69.9 15.7 %collective-permute-start.6 = (s16[1160,256]{1,0:T(8,128)(2,1)S(1)}, s16[1160,256]{1,0:T(8,128)(2,1)S(1)}, u32[]{:S(2)}, u32[]{:S(2)}) collective-permute-start(s16[1160,256]{1,0:T(8,128)(2,1)S(1)} %copy-done.7), channel_id=1, source_target_pairs={{0,64},{16,80},{32,96},{48,112},{64,0},{80,16},{96,32},{112,48},{1... | collective-permute-start | bytes 1781768 | tf_op jit(solution)/shard_map/ppermute | solution.py:633
  71.1 29.9 %collective-permute-start.2 = (s16[1160,256]{1,0:T(8,128)(2,1)}, s16[1160,256]{1,0:T(8,128)(2,1)S(1)}, u32[]{:S(2)}, u32[]{:S(2)}) collective-permute-start(s16[1160,256]{1,0:T(8,128)(2,1)} %get-tuple-element.28), channel_id=1, source_target_pairs={{0,32},{16,48},{32,64},{48,80},{64,96},{80,112},{96,0},{112,16},{1... | collective-permute-start | bytes 1781768 | tf_op jit(solution)/shard_map/ppermute | solution.py:633
  71.2 39.8 %collective-permute-start.3 = (s16[1160,256]{1,0:T(8,128)(2,1)}, s16[1160,256]{1,0:T(8,128)(2,1)S(1)}, u32[]{:S(2)}, u32[]{:S(2)}) collective-permute-start(s16[1160,256]{1,0:T(8,128)(2,1)} %get-tuple-element.29), channel_id=1, source_target_pairs={{0,64},{16,80},{32,96},{48,112},{64,0},{80,16},{96,32},{112,48},{1... | collective-permute-start | bytes 1781768 | tf_op jit(solution)/shard_map/ppermute | solution.py:633
  73.0 38.0 %collective-permute-start.4 = (s16[1160,256]{1,0:T(8,128)(2,1)}, s16[1160,256]{1,0:T(8,128)(2,1)S(1)}, u32[]{:S(2)}, u32[]{:S(2)}) collective-permute-start(s16[1160,256]{1,0:T(8,128)(2,1)} %get-tuple-element.30), channel_id=1, source_target_pairs={{0,96},{16,112},{32,0},{48,16},{64,32},{80,48},{96,64},{112,80},{1... | collective-permute-start | bytes 1781768 | tf_op jit(solution)/shard_map/ppermute | solution.py:633
  111.0 35.7 %copy-start.2 = (bf16[256,1024]{1,0:T(8,128)(2,1)S(1)}, bf16[256,1024]{1,0:T(8,128)(2,1)}, u32[]{:S(2)}) copy-start(bf16[256,1024]{1,0:T(8,128)(2,1)} %stencil_ref.1) | copy-start | bytes 1572868
  113.8 55.3 %copy-start.3 = (s32[1,16,128]{2,1,0:T(8,128)S(1)}, s32[1,16,128]{2,1,0:T(8,128)}, u32[]{:S(2)}) copy-start(s32[1,16,128]{2,1,0:T(8,128)} %param.12) | copy-start | bytes 24580
  113.8 55.3 %copy-start.6 = (s32[1,16]{1,0:T(1,128)S(1)}, s32[1,16]{1,0:T(1,128)}, u32[]{:S(2)}) copy-start(s32[1,16]{1,0:T(1,128)} %param.13) | copy-start | bytes 196
  125.4 21.3 %all-to-all-start = ((s16[16,152,256]{2,1,0:T(8,128)(2,1)}), s16[16,152,256]{2,1,0:T(8,128)(2,1)S(1)}, u32[]{:S(2)}, u32[]{:S(2)}) async-start(s16[16,152,256]{2,1,0:T(8,128)(2,1)} %sum_x.3), calls=%async_computation | async-start | bytes 2490368 | tf_op jit(solution)/shard_map/all_to_all | solution.py:649
  133.6 13.1 %collective-permute-start.8 = (s16[120,256]{1,0:T(8,128)(2,1)S(1)}, s16[120,256]{1,0:T(8,128)(2,1)S(1)}, u32[]{:S(2)}, u32[]{:S(2)}) collective-permute-start(s16[120,256]{1,0:T(8,128)(2,1)S(1)} %get-tuple-element.37), channel_id=1, source_target_pairs={{0,32},{16,48},{32,64},{48,80},{64,96},{80,112},{96,0},{112,16},{1... | collective-permute-start | bytes 184328 | tf_op jit(solution)/shard_map/ppermute | solution.py:633
  133.7 13.0 %collective-permute-start.9 = (s16[120,256]{1,0:T(8,128)(2,1)S(1)}, s16[120,256]{1,0:T(8,128)(2,1)S(1)}, u32[]{:S(2)}, u32[]{:S(2)}) collective-permute-start(s16[120,256]{1,0:T(8,128)(2,1)S(1)} %get-tuple-element.38), channel_id=1, source_target_pairs={{0,64},{16,80},{32,96},{48,112},{64,0},{80,16},{96,32},{112,48},{1... | collective-permute-start | bytes 184328 | tf_op jit(solution)/shard_map/ppermute | solution.py:633
  134.8 11.8 %collective-permute-start.10 = (s16[120,256]{1,0:T(8,128)(2,1)S(1)}, s16[120,256]{1,0:T(8,128)(2,1)S(1)}, u32[]{:S(2)}, u32[]{:S(2)}) collective-permute-start(s16[120,256]{1,0:T(8,128)(2,1)S(1)} %get-tuple-element.39), channel_id=1, source_target_pairs={{0,96},{16,112},{32,0},{48,16},{64,32},{80,48},{96,64},{112,80},{1... | collective-permute-start | bytes 184328 | tf_op jit(solution)/shard_map/ppermute | solution.py:633
  149.5 15.7 %collective-permute-start.11 = (s16[264,256]{1,0:T(8,128)(2,1)S(1)}, s16[264,256]{1,0:T(8,128)(2,1)S(1)}, u32[]{:S(2)}, u32[]{:S(2)}) collective-permute-start(s16[264,256]{1,0:T(8,128)(2,1)S(1)} %get-tuple-element.41), channel_id=1, source_target_pairs={{0,1},{1,2},{2,3},{3,4},{4,5},{5,6},{6,7},{7,8},{8,9},{9,10},{10,1... | collective-permute-start | bytes 405512 | tf_op jit(solution)/shard_map/ppermute | solution.py:658
  152.1 13.1 %collective-permute-start.12 = (s16[264,256]{1,0:T(8,128)(2,1)S(1)}, s16[264,256]{1,0:T(8,128)(2,1)S(1)}, u32[]{:S(2)}, u32[]{:S(2)}) collective-permute-start(s16[264,256]{1,0:T(8,128)(2,1)S(1)} %get-tuple-element.41), channel_id=1, source_target_pairs={{0,2},{1,3},{2,4},{3,5},{4,6},{5,7},{6,8},{7,9},{8,10},{9,11},{10,... | collective-permute-start | bytes 405512 | tf_op jit(solution)/shard_map/ppermute | solution.py:658
  156.3 10.4 %collective-permute-start.13 = (s16[264,256]{1,0:T(8,128)(2,1)S(1)}, s16[264,256]{1,0:T(8,128)(2,1)S(1)}, u32[]{:S(2)}, u32[]{:S(2)}) collective-permute-start(s16[264,256]{1,0:T(8,128)(2,1)S(1)} %get-tuple-element.41), channel_id=1, source_target_pairs={{1,0},{2,1},{3,2},{4,3},{5,4},{6,5},{7,6},{8,7},{9,8},{10,9},{11,1... | collective-permute-start | bytes 405512 | tf_op jit(solution)/shard_map/ppermute | solution.py:658
  161.8 7.3 %collective-permute-start.14 = (s16[264,256]{1,0:T(8,128)(2,1)S(1)}, s16[264,256]{1,0:T(8,128)(2,1)S(1)}, u32[]{:S(2)}, u32[]{:S(2)}) collective-permute-start(s16[264,256]{1,0:T(8,128)(2,1)S(1)} %get-tuple-element.41), channel_id=1, source_target_pairs={{2,0},{3,1},{4,2},{5,3},{6,4},{7,5},{8,6},{9,7},{10,8},{11,9},{12,... | collective-permute-start | bytes 405512 | tf_op jit(solution)/shard_map/ppermute | solution.py:658

commit v10 on v8

--- a/solution.py
+++ b/solution.py
@@ -400,15 +400,17 @@
     return row[:, 0:length]
 
 
-def sum_x_kernel(p0, p1, p2, p3, alias_ref, out_ref, sum_ref, sem, *, first):
+def sum_x_kernel(*refs, first, parts, early):
+    part_refs, early_ref = refs[:parts], refs[parts]
+    out_ref, sum_ref, sem = refs[parts + 1 + early :]
     tiles = sum_ref.shape[0]
 
     def copy_out(i):
         return pltpu.make_async_copy(sum_ref.at[i], out_ref.at[first + i], sem.at[i])
 
     for i in range(tiles):
-        total = jnp.zeros((LA, NX), jnp.float32)
-        for part in (p0, p1, p2, p3):
+        total = early_ref[i] if early else jnp.zeros((LA, NX), jnp.float32)
+        for part in part_refs:
             codes = code_row(part[pl.ds(tiles * LA, PAD), :], i, LA)
             total = total + decode(part[pl.ds(i * LA, LA), :], codes)
         values, code = encode(total)
@@ -419,16 +421,18 @@
         copy_out(i).wait()
 
 
-def sum_x(parts, old, first, tiles_all):
+def sum_x(parts, old, first, tiles_all, early=None):
     tiles = (parts[0].shape[0] - PAD) // LA
-    aliases = {}
+    args = list(parts) + ([] if early is None else [early])
+    aliases = {} if old is None else {len(args): 0}
     if old is None:
         old = jnp.zeros((16, NX), jnp.int16)
-    else:
-        aliases = {4: 0}
     return pl.pallas_call(
-        functools.partial(sum_x_kernel, first=first),
-        in_specs=[pl.BlockSpec(memory_space=pltpu.VMEM)] * 4 + [pl.BlockSpec(memory_space=pl.ANY)],
+        functools.partial(
+            sum_x_kernel, first=first, parts=len(parts), early=int(early is not None)
+        ),
+        in_specs=[pl.BlockSpec(memory_space=pltpu.VMEM)] * len(args)
+        + [pl.BlockSpec(memory_space=pl.ANY)],
         out_specs=pl.BlockSpec(memory_space=pltpu.HBM),
         out_shape=hbm((tiles_all, LA + PAD, NX), jnp.int16),
         scratch_shapes=[
@@ -438,7 +442,27 @@
         input_output_aliases=aliases,
         compiler_params=pltpu.CompilerParams(vmem_limit_bytes=12 * 1024 * 1024),
         name="sum_x",
-    )(*parts, old)
+    )(*args, old)
+
+
+def add_x_kernel(p0, p1, p2, out_ref):
+    tiles = out_ref.shape[0]
+    for i in range(tiles):
+        total = jnp.zeros((LA, NX), jnp.float32)
+        for part in (p0, p1, p2):
+            codes = code_row(part[pl.ds(tiles * LA, PAD), :], i, LA)
+            total = total + decode(part[pl.ds(i * LA, LA), :], codes)
+        out_ref[i] = total
+
+
+def add_x(parts):
+    tiles = (parts[0].shape[0] - PAD) // LA
+    return pl.pallas_call(
+        add_x_kernel,
+        out_shape=jax.ShapeDtypeStruct((tiles, LA, NX), jnp.float32),
+        compiler_params=pltpu.CompilerParams(vmem_limit_bytes=12 * 1024 * 1024),
+        name="add_x",
+    )(*parts)
 
 
 def sum_tile_kernel(in_hbm_ref, o0, o1, o2, o3, acc_ref, in_ref, sem):
@@ -643,9 +667,10 @@
     near = [a_parts[0][1][:16] | a_parts[0][3][:16]]
     b_blocks = after(b_blocks, near)
     b_arrived = lax.all_to_all(b_blocks, "tile", split_axis=0, concat_axis=0, tiled=True)
-    a_sums = None
-    for h in range(2):
-        a_sums = sum_x(a_parts[h], a_sums, h * tile_half, tile_count)
+    a_sums = sum_x(a_parts[0], None, 0, tile_count)
+    own_block, ahead, far, behind = a_parts[1]
+    early = add_x([own_block, ahead, behind])
+    a_sums = sum_x([far], a_sums, tile_half, tile_count, early)
     a_arrived = lax.all_to_all(a_sums, "tile", split_axis=0, concat_axis=0, tiled=True)
     b_sums = sum_tile(b_arrived)
     b_final = [b_sums[0]] + [x_send(b_sums[k], k) for k in (1, 2, 3)]
@@ -662,7 +687,7 @@
     edges = jnp.stack([spot > 0, spot < total - 1]).astype(jnp.int32)
     field, outgoing = smooth(edges, return_counts[0], plane, halos, return_slots[0])
     returned = lax.all_to_all(outgoing, "tile", split_axis=0, concat_axis=0, tiled=True)
-    return field[None], pltpu.with_memory_space_constraint(returned, pltpu.HBM)
+    return field[None], returned
 
 
 def solution(mesh):

time: 195 us -> 193 us (0.990)
  starting transfers between devices: 44.3 us -> 41.3 us
    pallas_call x2 -> x3, Pallas kernels: 5.87 us -> 5.48 us  [the longest x2 4.75 us: sum_x(): pl.pallas_call(functools.partial(sum_x_kernel, first=first, parts=len(par...]
  transfers between devices with their start and end apart: 17 -> 17, of which waited for: 6 -> 6; matrix products, arithmetic and copies ran while one was open for 1% -> 1% of each run, Pallas kernels for 25% -> 26%
where the time goes in v10:
time: 193 us; the launch traced here: 192 us
  Pallas kernels  67.5 us (35%)
  waiting for transfers between devices  53.1 us (28%)
  starting transfers between devices  41.3 us (21%)
  blocking collectives  25.1 us (13%)
  other arithmetic  2.7 us (1%)
    ppermute x9, waiting for transfers between devices, x_send(): lax.ppermute(block, 'cuts', [(i, (i + 2 * k) % cut_count) for i in range(...  37.2 us
    pallas_call x2, Pallas kernels, line_blocks(): pl.pallas_call(functools.partial(lines_kernel, first=first, cap=cap), gri...  32.2 us
    all_to_all x1, blocking collectives, local(): lax.all_to_all(outgoing, 'tile', split_axis=0, concat_axis=0, tiled=True)  25.1 us
    pallas_call x2, Pallas kernels, gather_rows(): pl.pallas_call(functools.partial(body, first=first, cap=cap), grid_spec=p...  20.9 us
    ppermute x4, starting transfers between devices, plane_send(): return lax.ppermute(coded, ('cuts', 'tile'), pairs)  15.6 us
    all_to_all x1, waiting for transfers between devices, local(): lax.all_to_all(a_sums, 'tile', split_axis=0, concat_axis=0, tiled=True)  11.5 us
    ppermute x9, starting transfers between devices, x_send(): lax.ppermute(block, 'cuts', [(i, (i + 2 * k) % cut_count) for i in range(...  10.3 us
    all_to_all x1, starting transfers between devices, local(): lax.all_to_all(b_blocks, 'tile', split_axis=0, concat_axis=0, tiled=True)  8.82 us
  transfers between devices with their start and end apart: 17, of which 6 were waited for; matrix products, arithmetic and copies ran while one was open for 1% of the time, Pallas kernels for 26%

profile of v10, /device:TPU:1, one launch (start us, length us, event | category | flops | bytes accessed | tf_op | source)
XLA Modules:
  0.0 192.2 jit_solution(9467160223146355591)
XLA Ops:
  0.6 0.0 copy-start.4
  0.6 0.6 copy-done.4
  1.3 12.3 %gather_rows.2 = (bf16[8,1296,256]{2,1,0:T(8,128)(2,1)}, f32[32768,128]{1,0:T(8,128)S(1)}, s32[16,1280]{1,0:T(8,128)S(1)}) custom-call(s32[16]{0:T(128)S(1)} %bitcast.11, bf16[16384,256]{1,0:T(8,128)(2,1)} %acq_ref.1, s32[16,1280]{1,0:T(8,128)} %bitcast.16, s32[16,1280]{1,0:T(8,128)} %bitcast.18), custom_call_target="tpu_custom_call" | custom-call | bytes 40000000 | tf_op jit(solution)/shard_map/gather_rows/pallas_call | solution.py:223
  13.6 0.5 collective-permute-start.1
  14.2 8.6 %gather_rows.3.own_hbm = bf16[8,1296,256]{2,1,0:T(8,128)(2,1)} custom-call(s32[16]{0:T(128)S(1)} %bitcast.12, f32[32768,128]{1,0:T(8,128)S(1)} %get-tuple-element.23.wide_ref, s32[16,1280]{1,0:T(8,128)} %bitcast.17, s32[16,1280]{1,0:T(8,128)S(1)} %get-tuple-element.24.places_ref), custom_call_target="tpu_custom_call" | custom-call | bytes 40000000 | tf_op jit(solution)/shard_map/gather_rows/pallas_call | solution.py:223
  22.7 0.1 collective-permute-start
  22.8 0.1 pad_add_fusion.place_ref
  22.9 1.0 fusion.7.peer_n
  23.9 15.7 %line_blocks.2 = (s16[1288,256]{1,0:T(8,128)(2,1)}, s16[1288,256]{1,0:T(8,128)(2,1)}, s16[1288,256]{1,0:T(8,128)(2,1)}, s16[1288,256]{1,0:T(8,128)(2,1)}, s16[16,392,256]{2,1,0:T(8,128)(2,1)}) custom-call(s32[16]{0:T(128)S(1)} %bitcast.13, s32[8]{0:T(128)S(1)} %fusion.7.peer_n, s32[2]{0:T(128)S(1)} %pad_add_fusion.place_ref, ...), custom_call_target="tpu_custom_call" | custom-call | flops 10737418240 | bytes 40000000 | tf_op jit(solution)/shard_map/line_blocks/pallas_call | solution.py:368
  39.6 0.8 collective-permute-start.5
  40.4 2.0 %collective-permute-start.7 = (s16[1288,256]{1,0:T(8,128)(2,1)}, s16[1288,256]{1,0:T(8,128)(2,1)S(1)}, u32[]{:S(2)}, u32[]{:S(2)}) collective-permute-start(s16[1288,256]{1,0:T(8,128)(2,1)} %get-tuple-element.34), channel_id=1, source_target_pairs={{0,96},{16,112},{32,0},{48,16},{64,32},{80,48},{96,64},{112,80},{1... | collective-permute-start | bytes 1978376 | tf_op jit(solution)/shard_map/ppermute | solution.py:657
  42.4 0.0 collective-permute-done.peer_hbm
  42.4 1.0 fusion.6.peer_n
  43.4 16.5 %line_blocks.3 = (s16[1288,256]{1,0:T(8,128)(2,1)}, s16[1288,256]{1,0:T(8,128)(2,1)}, s16[1288,256]{1,0:T(8,128)(2,1)}, s16[1288,256]{1,0:T(8,128)(2,1)}, s16[16,392,256]{2,1,0:T(8,128)(2,1)}) custom-call(s32[16]{0:T(128)S(1)} %bitcast.14, s32[8]{0:T(128)S(1)} %fusion.6.peer_n, s32[2]{0:T(128)S(1)} %pad_add_fusion.place_ref, ...), custom_call_target="tpu_custom_call", output_to_operand_aliasing={{4}: (5, {})} | custom-call | flops 10737418240 | bytes 40000000 | tf_op jit(solution)/shard_map/line_blocks/pallas_call | solution.py:368
  59.9 0.6 slice_or_fusion.refs_0_
  60.5 8.8 %all-to-all-start.1 = ((s16[16,392,256]{2,1,0:T(8,128)(2,1)}), s16[16,392,256]{2,1,0:T(8,128)(2,1)}, u32[]{:S(2)}, u32[]{:S(2)}) async-start(s16[16,392,256]{2,1,0:T(8,128)(2,1)} %after.1), calls=%async_computation.1 | async-start | bytes 6422528 | tf_op jit(solution)/shard_map/all_to_all | solution.py:669
  69.3 1.2 collective-permute-start.6
  70.5 1.3 collective-permute-start.3
  71.8 1.4 collective-permute-start.4
  73.2 0.7 collective-permute-start.2
  73.9 12.8 %collective-permute-done.6.refs_2_ = s16[1288,256]{1,0:T(8,128)(2,1)S(1)} collective-permute-done((s16[1288,256]{1,0:T(8,128)(2,1)}, s16[1288,256]{1,0:T(8,128)(2,1)S(1)}, u32[]{:S(2)}, u32[]{:S(2)}) %collective-permute-start.6) | collective-permute-done | bytes 659488 | tf_op jit(solution)/shard_map/ppermute | solution.py:657
  86.6 2.9 %sum_x.2.refs_2_ = s16[16,168,256]{2,1,0:T(8,128)(2,1)} custom-call(s16[1288,256]{1,0:T(8,128)(2,1)S(1)} %copy-done.1, s16[1288,256]{1,0:T(8,128)(2,1)S(1)} %collective-permute-done.5.refs_1_, s16[1288,256]{1,0:T(8,128)(2,1)S(1)} %collective-permute-done.6.refs_2_, s16[1288,256]{1,0:T(8,128)(2,1)S(1)} %collective-permute-done.7.refs_3_, ...), custom_call_target="tpu_custom_call" | custom-call | tf_op jit(solution)/shard_map/sum_x/pallas_call | solution.py:430
  89.5 13.9 %collective-permute-done.3.p1 = s16[1288,256]{1,0:T(8,128)(2,1)S(1)} collective-permute-done((s16[1288,256]{1,0:T(8,128)(2,1)}, s16[1288,256]{1,0:T(8,128)(2,1)S(1)}, u32[]{:S(2)}, u32[]{:S(2)}) %collective-permute-start.3) | collective-permute-done | bytes 659488 | tf_op jit(solution)/shard_map/ppermute | solution.py:657
  103.5 0.0 collective-permute-done.4.p2
  103.5 0.7 add_x.1.refs_1_
  104.2 0.0 copy-start.2
  104.2 0.0 copy-start.3
  104.2 0.0 copy-start.6
  104.3 10.5 %collective-permute-done.2.refs_0_ = s16[1288,256]{1,0:T(8,128)(2,1)S(1)} collective-permute-done((s16[1288,256]{1,0:T(8,128)(2,1)S(1)}, s16[1288,256]{1,0:T(8,128)(2,1)S(1)}, u32[]{:S(2)}, u32[]{:S(2)}) %collective-permute-start.2) | collective-permute-done | bytes 659488 | tf_op jit(solution)/shard_map/ppermute | solution.py:657
  114.8 1.8 sum_x.3
  116.6 0.3 all-to-all-done.1.in_hbm_ref
  116.9 6.0 %all-to-all-start = ((s16[16,168,256]{2,1,0:T(8,128)(2,1)}), s16[16,168,256]{2,1,0:T(8,128)(2,1)S(1)}, u32[]{:S(2)}, u32[]{:S(2)}) async-start(s16[16,168,256]{2,1,0:T(8,128)(2,1)} %sum_x.3), calls=%async_computation | async-start | bytes 2752512 | tf_op jit(solution)/shard_map/all_to_all | solution.py:674
  122.9 3.7 %sum_tile.1 = (s16[104,256]{1,0:T(8,128)(2,1)S(1)}, s16[104,256]{1,0:T(8,128)(2,1)S(1)}, s16[104,256]{1,0:T(8,128)(2,1)S(1)}, s16[104,256]{1,0:T(8,128)(2,1)S(1)}) custom-call(s16[16,392,256]{2,1,0:T(8,128)(2,1)} %all-to-all-done.1.in_hbm_ref), custom_call_target="tpu_custom_call" | custom-call | tf_op jit(solution)/shard_map/sum_tile/pallas_call | solution.py:496
  126.6 0.1 collective-permute-start.8
  126.7 2.9 %collective-permute-start.9 = (s16[104,256]{1,0:T(8,128)(2,1)S(1)}, s16[104,256]{1,0:T(8,128)(2,1)S(1)}, u32[]{:S(2)}, u32[]{:S(2)}) collective-permute-start(s16[104,256]{1,0:T(8,128)(2,1)S(1)} %get-tuple-element.38), channel_id=1, source_target_pairs={{0,64},{16,80},{32,96},{48,112},{64,0},{80,16},{96,32},{112,48},{1... | collective-permute-start | bytes 159752 | tf_op jit(solution)/shard_map/ppermute | solution.py:657
  129.6 0.0 collective-permute-start.10
  129.6 11.5 %all-to-all-done.a_ref = s16[16,168,256]{2,1,0:T(8,128)(2,1)S(1)} async-done(((s16[16,168,256]{2,1,0:T(8,128)(2,1)}), s16[16,168,256]{2,1,0:T(8,128)(2,1)S(1)}, u32[]{:S(2)}, u32[]{:S(2)}) %all-to-all-start) | async-done | bytes 1376288 | tf_op jit(solution)/shard_map/all_to_all | solution.py:674
  141.1 2.8 %own_plane.1 = (f32[256,256]{1,0:T(8,128)S(1)}, s16[264,256]{1,0:T(8,128)(2,1)S(1)}) custom-call(s16[16,168,256]{2,1,0:T(8,128)(2,1)S(1)} %all-to-all-done.a_ref, s16[104,256]{1,0:T(8,128)(2,1)S(1)} %get-tuple-element.36.b0, s16[104,256]{1,0:T(8,128)(2,1)S(1)} %collective-permute-done.8.b1, s16[104,256]{1,0:T(8,128)(2,1)S(1)} %collective-permute-done.9.b2, ...), custom_call_target="tpu_custom_call" | custom-call | tf_op jit(solution)/shard_map/own_plane/pallas_call | solution.py:547
  143.9 2.6 %collective-permute-start.11 = (s16[264,256]{1,0:T(8,128)(2,1)S(1)}, s16[264,256]{1,0:T(8,128)(2,1)S(1)}, u32[]{:S(2)}, u32[]{:S(2)}) collective-permute-start(s16[264,256]{1,0:T(8,128)(2,1)S(1)} %get-tuple-element.41), channel_id=1, source_target_pairs={{0,1},{1,2},{2,3},{3,4},{4,5},{5,6},{6,7},{7,8},{8,9},{9,10},{10,1... | collective-permute-start | bytes 405512 | tf_op jit(solution)/shard_map/ppermute | solution.py:683
  146.4 4.4 %collective-permute-start.12 = (s16[264,256]{1,0:T(8,128)(2,1)S(1)}, s16[264,256]{1,0:T(8,128)(2,1)S(1)}, u32[]{:S(2)}, u32[]{:S(2)}) collective-permute-start(s16[264,256]{1,0:T(8,128)(2,1)S(1)} %get-tuple-element.41), channel_id=1, source_target_pairs={{0,2},{1,3},{2,4},{3,5},{4,6},{5,7},{6,8},{7,9},{8,10},{9,11},{10,... | collective-permute-start | bytes 405512 | tf_op jit(solution)/shard_map/ppermute | solution.py:683
  150.9 5.4 %collective-permute-start.13 = (s16[264,256]{1,0:T(8,128)(2,1)S(1)}, s16[264,256]{1,0:T(8,128)(2,1)S(1)}, u32[]{:S(2)}, u32[]{:S(2)}) collective-permute-start(s16[264,256]{1,0:T(8,128)(2,1)S(1)} %get-tuple-element.41), channel_id=1, source_target_pairs={{1,0},{2,1},{3,2},{4,3},{5,4},{6,5},{7,6},{8,7},{9,8},{10,9},{11,1... | collective-permute-start | bytes 405512 | tf_op jit(solution)/shard_map/ppermute | solution.py:683
  156.3 3.2 %collective-permute-start.14 = (s16[264,256]{1,0:T(8,128)(2,1)S(1)}, s16[264,256]{1,0:T(8,128)(2,1)S(1)}, u32[]{:S(2)}, u32[]{:S(2)}) collective-permute-start(s16[264,256]{1,0:T(8,128)(2,1)S(1)} %get-tuple-element.41), channel_id=1, source_target_pairs={{2,0},{3,1},{4,2},{5,3},{6,4},{7,5},{8,6},{9,7},{10,8},{11,9},{12,... | collective-permute-start | bytes 405512 | tf_op jit(solution)/shard_map/ppermute | solution.py:683
  159.5 0.1 add_convert_fusion.edge_ref
  159.6 0.0 collective-permute-done.12.l2
  159.6 4.1 %collective-permute-done.14.r2 = s16[264,256]{1,0:T(8,128)(2,1)S(1)} collective-permute-done((s16[264,256]{1,0:T(8,128)(2,1)S(1)}, s16[264,256]{1,0:T(8,128)(2,1)S(1)}, u32[]{:S(2)}, u32[]{:S(2)}) %collective-permute-start.14) | collective-permute-done | bytes 135200 | tf_op jit(solution)/shard_map/ppermute | solution.py:683
  163.7 2.4 %smooth.1 = (bf16[256,256]{1,0:T(8,128)(2,1)}, bf16[16,128,256]{2,1,0:T(8,128)(2,1)S(1)}) custom-call(s32[2]{0:T(128)S(1)} %add_convert_fusion.edge_ref, s32[16]{0:T(128)S(1)} %bitcast.15, f32[256,256]{1,0:T(8,128)S(1)} %get-tuple-element.40.plane_ref, s16[264,256]{1,0:T(8,128)(2,1)S(1)} %collective-permute-done.11.l1, ...), custom_call_target="tpu_custom_call" | custom-call | tf_op jit(solution)/shard_map/smooth/pallas_call | solution.py:601
  166.2 25.1 %all_to_all.15 = bf16[16,128,256]{2,1,0:T(8,128)(2,1)S(1)} all-to-all(bf16[16,128,256]{2,1,0:T(8,128)(2,1)S(1)} %get-tuple-element.43), channel_id=1, replica_groups=mesh['cuts'=8,'tile'=16] {'tile'}, dimensions={0} | all-to-all | bytes 2097152 | tf_op jit(solution)/shard_map/all_to_all | solution.py:689
  191.3 1.0 copy.16
  (21 shorter events, 0.0 us)
Async XLA Ops:
  0.6 0.7 copy-start.4
  13.6 9.3 %collective-permute-start.1 = (bf16[8,1296,256]{2,1,0:T(8,128)(2,1)}, bf16[8,1296,256]{2,1,0:T(8,128)(2,1)}, u32[]{:S(2)}, u32[]{:S(2)}) collective-permute-start(bf16[8,1296,256]{2,1,0:T(8,128)(2,1)} %get-tuple-element.25.own_hbm), channel_id=1, source_target_pairs={{0,16},{16,0},{32,48},{48,32},{64,80},{80,64},{96,112},{112,96},{1... | collective-permute-start | bytes 15925256 | tf_op jit(solution)/shard_map/ppermute | solution.py:648
  14.2 9.8 %copy-start.5 = (s32[1,16]{1,0:T(1,128)S(1)}, s32[1,16]{1,0:T(1,128)}, u32[]{:S(2)}) copy-start(s32[1,16]{1,0:T(1,128)} %param.11) | copy-start | bytes 196
  22.7 19.7 %collective-permute-start = (bf16[8,1296,256]{2,1,0:T(8,128)(2,1)}, bf16[8,1296,256]{2,1,0:T(8,128)(2,1)}, u32[]{:S(2)}, u32[]{:S(2)}) collective-permute-start(bf16[8,1296,256]{2,1,0:T(8,128)(2,1)} %gather_rows.3.own_hbm), channel_id=1, source_target_pairs={{0,16},{16,0},{32,48},{48,32},{64,80},{80,64},{96,112},{112,96},{1... | collective-permute-start | bytes 15925256 | tf_op jit(solution)/shard_map/ppermute | solution.py:648
  39.6 20.3 %collective-permute-start.5 = (s16[1288,256]{1,0:T(8,128)(2,1)}, s16[1288,256]{1,0:T(8,128)(2,1)S(1)}, u32[]{:S(2)}, u32[]{:S(2)}) collective-permute-start(s16[1288,256]{1,0:T(8,128)(2,1)} %get-tuple-element.32), channel_id=1, source_target_pairs={{0,32},{16,48},{32,64},{48,80},{64,96},{80,112},{96,0},{112,16},{1... | collective-permute-start | bytes 1978376 | tf_op jit(solution)/shard_map/ppermute | solution.py:657
  40.4 19.5 %collective-permute-start.7 = (s16[1288,256]{1,0:T(8,128)(2,1)}, s16[1288,256]{1,0:T(8,128)(2,1)S(1)}, u32[]{:S(2)}, u32[]{:S(2)}) collective-permute-start(s16[1288,256]{1,0:T(8,128)(2,1)} %get-tuple-element.34), channel_id=1, source_target_pairs={{0,96},{16,112},{32,0},{48,16},{64,32},{80,48},{96,64},{112,80},{1... | collective-permute-start | bytes 1978376 | tf_op jit(solution)/shard_map/ppermute | solution.py:657
  60.5 12.7 %copy-start.7 = (s16[1288,256]{1,0:T(8,128)(2,1)S(1)}, s16[1288,256]{1,0:T(8,128)(2,1)}, u32[]{:S(2)}) copy-start(s16[1288,256]{1,0:T(8,128)(2,1)} %get-tuple-element.27) | copy-start | bytes 1978372
  60.5 26.1 %copy-start.1 = (s16[1288,256]{1,0:T(8,128)(2,1)S(1)}, s16[1288,256]{1,0:T(8,128)(2,1)}, u32[]{:S(2)}) copy-start(s16[1288,256]{1,0:T(8,128)(2,1)} %get-tuple-element.31.refs_0_) | copy-start | bytes 1978372
  60.5 43.0 %copy-start = (s16[1288,256]{1,0:T(8,128)(2,1)S(1)}, s16[1288,256]{1,0:T(8,128)(2,1)}, u32[]{:S(2)}) copy-start(s16[1288,256]{1,0:T(8,128)(2,1)} %get-tuple-element.28.p0) | copy-start | bytes 1978372
  60.5 56.4 %all-to-all-start.1 = ((s16[16,392,256]{2,1,0:T(8,128)(2,1)}), s16[16,392,256]{2,1,0:T(8,128)(2,1)}, u32[]{:S(2)}, u32[]{:S(2)}) async-start(s16[16,392,256]{2,1,0:T(8,128)(2,1)} %after.1), calls=%async_computation.1 | async-start | bytes 6422528 | tf_op jit(solution)/shard_map/all_to_all | solution.py:669
  69.3 17.3 %collective-permute-start.6 = (s16[1288,256]{1,0:T(8,128)(2,1)}, s16[1288,256]{1,0:T(8,128)(2,1)S(1)}, u32[]{:S(2)}, u32[]{:S(2)}) collective-permute-start(s16[1288,256]{1,0:T(8,128)(2,1)} %get-tuple-element.33), channel_id=1, source_target_pairs={{0,64},{16,80},{32,96},{48,112},{64,0},{80,16},{96,32},{112,48},{1... | collective-permute-start | bytes 1978376 | tf_op jit(solution)/shard_map/ppermute | solution.py:657
  70.5 33.0 %collective-permute-start.3 = (s16[1288,256]{1,0:T(8,128)(2,1)}, s16[1288,256]{1,0:T(8,128)(2,1)S(1)}, u32[]{:S(2)}, u32[]{:S(2)}) collective-permute-start(s16[1288,256]{1,0:T(8,128)(2,1)} %get-tuple-element.29), channel_id=1, source_target_pairs={{0,32},{16,48},{32,64},{48,80},{64,96},{80,112},{96,0},{112,16},{1... | collective-permute-start | bytes 1978376 | tf_op jit(solution)/shard_map/ppermute | solution.py:657
  71.8 31.7 %collective-permute-start.4 = (s16[1288,256]{1,0:T(8,128)(2,1)}, s16[1288,256]{1,0:T(8,128)(2,1)S(1)}, u32[]{:S(2)}, u32[]{:S(2)}) collective-permute-start(s16[1288,256]{1,0:T(8,128)(2,1)} %get-tuple-element.30), channel_id=1, source_target_pairs={{0,96},{16,112},{32,0},{48,16},{64,32},{80,48},{96,64},{112,80},{1... | collective-permute-start | bytes 1978376 | tf_op jit(solution)/shard_map/ppermute | solution.py:657
  73.2 41.6 %collective-permute-start.2 = (s16[1288,256]{1,0:T(8,128)(2,1)S(1)}, s16[1288,256]{1,0:T(8,128)(2,1)S(1)}, u32[]{:S(2)}, u32[]{:S(2)}) collective-permute-start(s16[1288,256]{1,0:T(8,128)(2,1)S(1)} %copy-done.7), channel_id=1, source_target_pairs={{0,64},{16,80},{32,96},{48,112},{64,0},{80,16},{96,32},{112,48},{1... | collective-permute-start | bytes 1978376 | tf_op jit(solution)/shard_map/ppermute | solution.py:657
  104.2 36.8 %copy-start.2 = (bf16[256,1024]{1,0:T(8,128)(2,1)S(1)}, bf16[256,1024]{1,0:T(8,128)(2,1)}, u32[]{:S(2)}) copy-start(bf16[256,1024]{1,0:T(8,128)(2,1)} %stencil_ref.1) | copy-start | bytes 1572868
  104.2 59.5 %copy-start.3 = (s32[1,16,128]{2,1,0:T(8,128)S(1)}, s32[1,16,128]{2,1,0:T(8,128)}, u32[]{:S(2)}) copy-start(s32[1,16,128]{2,1,0:T(8,128)} %param.12) | copy-start | bytes 24580
  104.2 59.5 %copy-start.6 = (s32[1,16]{1,0:T(1,128)S(1)}, s32[1,16]{1,0:T(1,128)}, u32[]{:S(2)}) copy-start(s32[1,16]{1,0:T(1,128)} %param.13) | copy-start | bytes 196
  116.9 24.1 %all-to-all-start = ((s16[16,168,256]{2,1,0:T(8,128)(2,1)}), s16[16,168,256]{2,1,0:T(8,128)(2,1)S(1)}, u32[]{:S(2)}, u32[]{:S(2)}) async-start(s16[16,168,256]{2,1,0:T(8,128)(2,1)} %sum_x.3), calls=%async_computation | async-start | bytes 2752512 | tf_op jit(solution)/shard_map/all_to_all | solution.py:674
  126.6 14.5 %collective-permute-start.8 = (s16[104,256]{1,0:T(8,128)(2,1)S(1)}, s16[104,256]{1,0:T(8,128)(2,1)S(1)}, u32[]{:S(2)}, u32[]{:S(2)}) collective-permute-start(s16[104,256]{1,0:T(8,128)(2,1)S(1)} %get-tuple-element.37), channel_id=1, source_target_pairs={{0,32},{16,48},{32,64},{48,80},{64,96},{80,112},{96,0},{112,16},{1... | collective-permute-start | bytes 159752 | tf_op jit(solution)/shard_map/ppermute | solution.py:657
  126.7 14.4 %collective-permute-start.9 = (s16[104,256]{1,0:T(8,128)(2,1)S(1)}, s16[104,256]{1,0:T(8,128)(2,1)S(1)}, u32[]{:S(2)}, u32[]{:S(2)}) collective-permute-start(s16[104,256]{1,0:T(8,128)(2,1)S(1)} %get-tuple-element.38), channel_id=1, source_target_pairs={{0,64},{16,80},{32,96},{48,112},{64,0},{80,16},{96,32},{112,48},{1... | collective-permute-start | bytes 159752 | tf_op jit(solution)/shard_map/ppermute | solution.py:657
  129.6 11.5 %collective-permute-start.10 = (s16[104,256]{1,0:T(8,128)(2,1)S(1)}, s16[104,256]{1,0:T(8,128)(2,1)S(1)}, u32[]{:S(2)}, u32[]{:S(2)}) collective-permute-start(s16[104,256]{1,0:T(8,128)(2,1)S(1)} %get-tuple-element.39), channel_id=1, source_target_pairs={{0,96},{16,112},{32,0},{48,16},{64,32},{80,48},{96,64},{112,80},{1... | collective-permute-start | bytes 159752 | tf_op jit(solution)/shard_map/ppermute | solution.py:657
  143.9 15.7 %collective-permute-start.11 = (s16[264,256]{1,0:T(8,128)(2,1)S(1)}, s16[264,256]{1,0:T(8,128)(2,1)S(1)}, u32[]{:S(2)}, u32[]{:S(2)}) collective-permute-start(s16[264,256]{1,0:T(8,128)(2,1)S(1)} %get-tuple-element.41), channel_id=1, source_target_pairs={{0,1},{1,2},{2,3},{3,4},{4,5},{5,6},{6,7},{7,8},{8,9},{9,10},{10,1... | collective-permute-start | bytes 405512 | tf_op jit(solution)/shard_map/ppermute | solution.py:683
  146.4 13.2 %collective-permute-start.12 = (s16[264,256]{1,0:T(8,128)(2,1)S(1)}, s16[264,256]{1,0:T(8,128)(2,1)S(1)}, u32[]{:S(2)}, u32[]{:S(2)}) collective-permute-start(s16[264,256]{1,0:T(8,128)(2,1)S(1)} %get-tuple-element.41), channel_id=1, source_target_pairs={{0,2},{1,3},{2,4},{3,5},{4,6},{5,7},{6,8},{7,9},{8,10},{9,11},{10,... | collective-permute-start | bytes 405512 | tf_op jit(solution)/shard_map/ppermute | solution.py:683
  150.9 8.8 %collective-permute-start.13 = (s16[264,256]{1,0:T(8,128)(2,1)S(1)}, s16[264,256]{1,0:T(8,128)(2,1)S(1)}, u32[]{:S(2)}, u32[]{:S(2)}) collective-permute-start(s16[264,256]{1,0:T(8,128)(2,1)S(1)} %get-tuple-element.41), channel_id=1, source_target_pairs={{1,0},{2,1},{3,2},{4,3},{5,4},{6,5},{7,6},{8,7},{9,8},{10,9},{11,1... | collective-permute-start | bytes 405512 | tf_op jit(solution)/shard_map/ppermute | solution.py:683
  156.3 7.5 %collective-permute-start.14 = (s16[264,256]{1,0:T(8,128)(2,1)S(1)}, s16[264,256]{1,0:T(8,128)(2,1)S(1)}, u32[]{:S(2)}, u32[]{:S(2)}) collective-permute-start(s16[264,256]{1,0:T(8,128)(2,1)S(1)} %get-tuple-element.41), channel_id=1, source_target_pairs={{2,0},{3,1},{4,2},{5,3},{6,4},{7,5},{8,6},{9,7},{10,8},{11,9},{12,... | collective-permute-start | bytes 405512 | tf_op jit(solution)/shard_map/ppermute | solution.py:683

commit v11 on v10

--- a/solution.py
+++ b/solution.py
@@ -556,7 +556,7 @@
     )(a, *bs, stencil)
 
 
-def smooth_kernel(edge_ref, counts_ref, plane_ref, l1, l2, r1, r2, reads_ref, out_ref, back_ref):
+def smooth_kernel(edge_ref, counts_ref, plane_ref, l2, r2, l1, r1, reads_ref, out_ref, back_ref):
     def halo(ref):
         table = ref[pl.ds(NY, PAD), :].astype(jnp.int32).astype(jnp.float32)
         parts = [
@@ -668,9 +668,9 @@
     b_blocks = after(b_blocks, near)
     b_arrived = lax.all_to_all(b_blocks, "tile", split_axis=0, concat_axis=0, tiled=True)
     a_sums = sum_x(a_parts[0], None, 0, tile_count)
-    own_block, ahead, far, behind = a_parts[1]
+    own_block, ahead, across, behind = a_parts[1]
     early = add_x([own_block, ahead, behind])
-    a_sums = sum_x([far], a_sums, tile_half, tile_count, early)
+    a_sums = sum_x([across], a_sums, tile_half, tile_count, early)
     a_arrived = lax.all_to_all(a_sums, "tile", split_axis=0, concat_axis=0, tiled=True)
     b_sums = sum_tile(b_arrived)
     b_final = [b_sums[0]] + [x_send(b_sums[k], k) for k in (1, 2, 3)]
@@ -682,7 +682,9 @@
         pairs = [(i, i + k) for i in range(total) if 0 <= i + k < total]
         return lax.ppermute(coded, ("cuts", "tile"), pairs)
 
-    halos = [plane_send(1), plane_send(2), plane_send(-1), plane_send(-2)]
+    far = [plane_send(2), plane_send(-2)]
+    near = [plane_send(1), plane_send(-1)]
+    halos = far + near
     spot = here * tile_count + lax.axis_index("tile")
     edges = jnp.stack([spot > 0, spot < total - 1]).astype(jnp.int32)
     field, outgoing = smooth(edges, return_counts[0], plane, halos, return_slots[0])

time: 193 us -> 194 us (level)
  starting transfers between devices: 41.3 us -> 47 us
  Pallas kernels: 67.5 us -> 64.4 us
  waiting for transfers between devices: 53.1 us -> 50.7 us
    ppermute x4, starting transfers between devices: 15.6 us -> 18.1 us  [plane_send(): return lax.ppermute(coded, ('cuts', 'tile'), pairs)]
    ppermute x4, waiting for transfers between devices: 4.12 us -> 1.88 us  [plane_send(): return lax.ppermute(coded, ('cuts', 'tile'), pairs)]
  transfers between devices with their start and end apart: 17 -> 17, of which waited for: 6 -> 7; matrix products, arithmetic and copies ran while one was open for 1% -> 1% of each run, Pallas kernels for 26% -> 25%
where the time goes in v11:
time: 194 us
  Pallas kernels  64.4 us (33%)
  waiting for transfers between devices  50.7 us (26%)
  starting transfers between devices  47 us (24%)
  blocking collectives  26.5 us (14%)
  other arithmetic  2.7 us (1%)
    ppermute x9, waiting for transfers between devices, x_send(): lax.ppermute(block, 'cuts', [(i, (i + 2 * k) % cut_count) for i in range(...  37 us
    pallas_call x2, Pallas kernels, line_blocks(): pl.pallas_call(functools.partial(lines_kernel, first=first, cap=cap), gri...  31.1 us
    all_to_all x1, blocking collectives, local(): lax.all_to_all(outgoing, 'tile', split_axis=0, concat_axis=0, tiled=True)  26.5 us
    pallas_call x2, Pallas kernels, gather_rows(): pl.pallas_call(functools.partial(body, first=first, cap=cap), grid_spec=p...  19 us
    ppermute x4, starting transfers between devices, plane_send(): return lax.ppermute(coded, ('cuts', 'tile'), pairs)  18.1 us
    all_to_all x1, waiting for transfers between devices, local(): lax.all_to_all(a_sums, 'tile', split_axis=0, concat_axis=0, tiled=True)  11.4 us
    ppermute x9, starting transfers between devices, x_send(): lax.ppermute(block, 'cuts', [(i, (i + 2 * k) % cut_count) for i in range(...  10.7 us
    all_to_all x1, starting transfers between devices, local(): lax.all_to_all(b_blocks, 'tile', split_axis=0, concat_axis=0, tiled=True)  9.64 us
  transfers between devices with their start and end apart: 17, of which 7 were waited for; matrix products, arithmetic and copies ran while one was open for 1% of the time, Pallas kernels for 25%

profile of v11, /device:TPU:1, one launch (start us, length us, event | category | flops | bytes accessed | tf_op | source)
XLA Modules:
  0.0 193.8 jit_solution(4313651134518105994)
XLA Ops:
  0.6 0.0 copy-start.4
  0.6 0.6 copy-done.4
  1.3 11.2 %gather_rows.2 = (bf16[8,1296,256]{2,1,0:T(8,128)(2,1)}, f32[32768,128]{1,0:T(8,128)S(1)}, s32[16,1280]{1,0:T(8,128)S(1)}) custom-call(s32[16]{0:T(128)S(1)} %bitcast.11, bf16[16384,256]{1,0:T(8,128)(2,1)} %acq_ref.1, s32[16,1280]{1,0:T(8,128)} %bitcast.16, s32[16,1280]{1,0:T(8,128)} %bitcast.18), custom_call_target="tpu_custom_call" | custom-call | bytes 40000000 | tf_op jit(solution)/shard_map/gather_rows/pallas_call | solution.py:223
  12.5 1.9 collective-permute-start.1
  14.4 7.8 %gather_rows.3.own_hbm = bf16[8,1296,256]{2,1,0:T(8,128)(2,1)} custom-call(s32[16]{0:T(128)S(1)} %bitcast.12, f32[32768,128]{1,0:T(8,128)S(1)} %get-tuple-element.23.wide_ref, s32[16,1280]{1,0:T(8,128)} %bitcast.17, s32[16,1280]{1,0:T(8,128)S(1)} %get-tuple-element.24.places_ref), custom_call_target="tpu_custom_call" | custom-call | bytes 40000000 | tf_op jit(solution)/shard_map/gather_rows/pallas_call | solution.py:223
  22.2 0.5 collective-permute-start
  22.7 0.1 pad_add_fusion.place_ref
  22.7 0.4 collective-permute-done.1.peer_hbm
  23.1 1.0 fusion.7.peer_n
  24.1 14.9 %line_blocks.2 = (s16[1288,256]{1,0:T(8,128)(2,1)}, s16[1288,256]{1,0:T(8,128)(2,1)}, s16[1288,256]{1,0:T(8,128)(2,1)}, s16[1288,256]{1,0:T(8,128)(2,1)}, s16[16,392,256]{2,1,0:T(8,128)(2,1)}) custom-call(s32[16]{0:T(128)S(1)} %bitcast.13, s32[8]{0:T(128)S(1)} %fusion.7.peer_n, s32[2]{0:T(128)S(1)} %pad_add_fusion.place_ref, ...), custom_call_target="tpu_custom_call" | custom-call | flops 10737418240 | bytes 40000000 | tf_op jit(solution)/shard_map/line_blocks/pallas_call | solution.py:368
  39.0 0.6 collective-permute-start.5
  39.7 2.7 %collective-permute-start.7 = (s16[1288,256]{1,0:T(8,128)(2,1)}, s16[1288,256]{1,0:T(8,128)(2,1)S(1)}, u32[]{:S(2)}, u32[]{:S(2)}) collective-permute-start(s16[1288,256]{1,0:T(8,128)(2,1)} %get-tuple-element.34), channel_id=1, source_target_pairs={{0,96},{16,112},{32,0},{48,16},{64,32},{80,48},{96,64},{112,80},{1... | collective-permute-start | bytes 1978376 | tf_op jit(solution)/shard_map/ppermute | solution.py:657
  42.4 1.0 fusion.6.peer_n
  43.4 16.2 %line_blocks.3 = (s16[1288,256]{1,0:T(8,128)(2,1)}, s16[1288,256]{1,0:T(8,128)(2,1)}, s16[1288,256]{1,0:T(8,128)(2,1)}, s16[1288,256]{1,0:T(8,128)(2,1)}, s16[16,392,256]{2,1,0:T(8,128)(2,1)}) custom-call(s32[16]{0:T(128)S(1)} %bitcast.14, s32[8]{0:T(128)S(1)} %fusion.6.peer_n, s32[2]{0:T(128)S(1)} %pad_add_fusion.place_ref, ...), custom_call_target="tpu_custom_call", output_to_operand_aliasing={{4}: (5, {})} | custom-call | flops 10737418240 | bytes 40000000 | tf_op jit(solution)/shard_map/line_blocks/pallas_call | solution.py:368
  59.6 0.6 slice_or_fusion.refs_0_
  60.2 9.6 %all-to-all-start.1 = ((s16[16,392,256]{2,1,0:T(8,128)(2,1)}), s16[16,392,256]{2,1,0:T(8,128)(2,1)}, u32[]{:S(2)}, u32[]{:S(2)}) async-start(s16[16,392,256]{2,1,0:T(8,128)(2,1)} %after.1), calls=%async_computation.1 | async-start | bytes 6422528 | tf_op jit(solution)/shard_map/all_to_all | solution.py:669
  69.8 0.8 collective-permute-start.6
  70.6 2.7 %collective-permute-start.4 = (s16[1288,256]{1,0:T(8,128)(2,1)}, s16[1288,256]{1,0:T(8,128)(2,1)S(1)}, u32[]{:S(2)}, u32[]{:S(2)}) collective-permute-start(s16[1288,256]{1,0:T(8,128)(2,1)} %get-tuple-element.30), channel_id=1, source_target_pairs={{0,96},{16,112},{32,0},{48,16},{64,32},{80,48},{96,64},{112,80},{1... | collective-permute-start | bytes 1978376 | tf_op jit(solution)/shard_map/ppermute | solution.py:657
  73.3 1.1 collective-permute-start.2
  74.3 12.5 %collective-permute-done.6.refs_2_ = s16[1288,256]{1,0:T(8,128)(2,1)S(1)} collective-permute-done((s16[1288,256]{1,0:T(8,128)(2,1)}, s16[1288,256]{1,0:T(8,128)(2,1)S(1)}, u32[]{:S(2)}, u32[]{:S(2)}) %collective-permute-start.6) | collective-permute-done | bytes 659488 | tf_op jit(solution)/shard_map/ppermute | solution.py:657
  86.9 2.9 %sum_x.2.refs_2_ = s16[16,168,256]{2,1,0:T(8,128)(2,1)} custom-call(s16[1288,256]{1,0:T(8,128)(2,1)S(1)} %copy-done.1, s16[1288,256]{1,0:T(8,128)(2,1)S(1)} %collective-permute-done.5.refs_1_, s16[1288,256]{1,0:T(8,128)(2,1)S(1)} %collective-permute-done.6.refs_2_, s16[1288,256]{1,0:T(8,128)(2,1)S(1)} %collective-permute-done.7.refs_3_, ...), custom_call_target="tpu_custom_call" | custom-call | tf_op jit(solution)/shard_map/sum_x/pallas_call | solution.py:430
  89.8 14.4 %collective-permute-done.3.p1 = s16[1288,256]{1,0:T(8,128)(2,1)S(1)} collective-permute-done((s16[1288,256]{1,0:T(8,128)(2,1)}, s16[1288,256]{1,0:T(8,128)(2,1)S(1)}, u32[]{:S(2)}, u32[]{:S(2)}) %collective-permute-start.3) | collective-permute-done | bytes 659488 | tf_op jit(solution)/shard_map/ppermute | solution.py:657
  104.2 0.0 collective-permute-done.4.p2
  104.2 0.7 add_x.1.refs_1_
  104.9 0.0 copy-start.2
  104.9 0.0 copy-start.3
  105.0 0.0 copy-start.6
  105.0 10.1 %collective-permute-done.2.refs_0_ = s16[1288,256]{1,0:T(8,128)(2,1)S(1)} collective-permute-done((s16[1288,256]{1,0:T(8,128)(2,1)S(1)}, s16[1288,256]{1,0:T(8,128)(2,1)S(1)}, u32[]{:S(2)}, u32[]{:S(2)}) %collective-permute-start.2) | collective-permute-done | bytes 659488 | tf_op jit(solution)/shard_map/ppermute | solution.py:657
  115.0 1.8 sum_x.3
  116.9 6.3 %all-to-all-start = ((s16[16,168,256]{2,1,0:T(8,128)(2,1)}), s16[16,168,256]{2,1,0:T(8,128)(2,1)S(1)}, u32[]{:S(2)}, u32[]{:S(2)}) async-start(s16[16,168,256]{2,1,0:T(8,128)(2,1)} %sum_x.3), calls=%async_computation | async-start | bytes 2752512 | tf_op jit(solution)/shard_map/all_to_all | solution.py:674
  123.2 3.7 %sum_tile.1 = (s16[104,256]{1,0:T(8,128)(2,1)S(1)}, s16[104,256]{1,0:T(8,128)(2,1)S(1)}, s16[104,256]{1,0:T(8,128)(2,1)S(1)}, s16[104,256]{1,0:T(8,128)(2,1)S(1)}) custom-call(s16[16,392,256]{2,1,0:T(8,128)(2,1)} %all-to-all-done.1.in_hbm_ref), custom_call_target="tpu_custom_call" | custom-call | tf_op jit(solution)/shard_map/sum_tile/pallas_call | solution.py:496
  126.8 0.1 collective-permute-start.8
  126.9 1.1 collective-permute-start.9
  128.0 1.6 collective-permute-start.10
  129.6 11.4 %all-to-all-done.a_ref = s16[16,168,256]{2,1,0:T(8,128)(2,1)S(1)} async-done(((s16[16,168,256]{2,1,0:T(8,128)(2,1)}), s16[16,168,256]{2,1,0:T(8,128)(2,1)S(1)}, u32[]{:S(2)}, u32[]{:S(2)}) %all-to-all-start) | async-done | bytes 1376288 | tf_op jit(solution)/shard_map/all_to_all | solution.py:674
  141.1 0.0 collective-permute-done.8.b1
  141.1 0.0 collective-permute-done.9.b2
  141.1 2.8 %own_plane.1 = (f32[256,256]{1,0:T(8,128)S(1)}, s16[264,256]{1,0:T(8,128)(2,1)S(1)}) custom-call(s16[16,168,256]{2,1,0:T(8,128)(2,1)S(1)} %all-to-all-done.a_ref, s16[104,256]{1,0:T(8,128)(2,1)S(1)} %get-tuple-element.36.b0, s16[104,256]{1,0:T(8,128)(2,1)S(1)} %collective-permute-done.8.b1, s16[104,256]{1,0:T(8,128)(2,1)S(1)} %collective-permute-done.9.b2, ...), custom_call_target="tpu_custom_call" | custom-call | tf_op jit(solution)/shard_map/own_plane/pallas_call | solution.py:547
  143.9 4.1 %collective-permute-start.11 = (s16[264,256]{1,0:T(8,128)(2,1)S(1)}, s16[264,256]{1,0:T(8,128)(2,1)S(1)}, u32[]{:S(2)}, u32[]{:S(2)}) collective-permute-start(s16[264,256]{1,0:T(8,128)(2,1)S(1)} %get-tuple-element.41), channel_id=1, source_target_pairs={{0,2},{1,3},{2,4},{3,5},{4,6},{5,7},{6,8},{7,9},{8,10},{9,11},{10,... | collective-permute-start | bytes 405512 | tf_op jit(solution)/shard_map/ppermute | solution.py:683
  148.0 5.1 %collective-permute-start.12 = (s16[264,256]{1,0:T(8,128)(2,1)S(1)}, s16[264,256]{1,0:T(8,128)(2,1)S(1)}, u32[]{:S(2)}, u32[]{:S(2)}) collective-permute-start(s16[264,256]{1,0:T(8,128)(2,1)S(1)} %get-tuple-element.41), channel_id=1, source_target_pairs={{2,0},{3,1},{4,2},{5,3},{6,4},{7,5},{8,6},{9,7},{10,8},{11,9},{12,... | collective-permute-start | bytes 405512 | tf_op jit(solution)/shard_map/ppermute | solution.py:683
  153.1 2.6 %collective-permute-start.13 = (s16[264,256]{1,0:T(8,128)(2,1)S(1)}, s16[264,256]{1,0:T(8,128)(2,1)S(1)}, u32[]{:S(2)}, u32[]{:S(2)}) collective-permute-start(s16[264,256]{1,0:T(8,128)(2,1)S(1)} %get-tuple-element.41), channel_id=1, source_target_pairs={{0,1},{1,2},{2,3},{3,4},{4,5},{5,6},{6,7},{7,8},{8,9},{9,10},{10,1... | collective-permute-start | bytes 405512 | tf_op jit(solution)/shard_map/ppermute | solution.py:683
  155.7 6.3 %collective-permute-start.14 = (s16[264,256]{1,0:T(8,128)(2,1)S(1)}, s16[264,256]{1,0:T(8,128)(2,1)S(1)}, u32[]{:S(2)}, u32[]{:S(2)}) collective-permute-start(s16[264,256]{1,0:T(8,128)(2,1)S(1)} %get-tuple-element.41), channel_id=1, source_target_pairs={{1,0},{2,1},{3,2},{4,3},{5,4},{6,5},{7,6},{8,7},{9,8},{10,9},{11,1... | collective-permute-start | bytes 405512 | tf_op jit(solution)/shard_map/ppermute | solution.py:683
  162.0 0.1 add_convert_fusion.edge_ref
  162.1 0.7 collective-permute-done.13.l1
  162.8 1.2 collective-permute-done.14.r1
  164.0 2.4 %smooth.1 = (bf16[256,256]{1,0:T(8,128)(2,1)}, bf16[16,128,256]{2,1,0:T(8,128)(2,1)S(1)}) custom-call(s32[2]{0:T(128)S(1)} %add_convert_fusion.edge_ref, s32[16]{0:T(128)S(1)} %bitcast.15, f32[256,256]{1,0:T(8,128)S(1)} %get-tuple-element.40.plane_ref, s16[264,256]{1,0:T(8,128)(2,1)S(1)} %collective-permute-done.11.l2, ...), custom_call_target="tpu_custom_call" | custom-call | tf_op jit(solution)/shard_map/smooth/pallas_call | solution.py:601
  166.4 26.5 %all_to_all.15 = bf16[16,128,256]{2,1,0:T(8,128)(2,1)S(1)} all-to-all(bf16[16,128,256]{2,1,0:T(8,128)(2,1)S(1)} %get-tuple-element.43), channel_id=1, replica_groups=mesh['cuts'=8,'tile'=16] {'tile'}, dimensions={0} | all-to-all | bytes 2097152 | tf_op jit(solution)/shard_map/all_to_all | solution.py:691
  192.9 1.0 copy.16
  (21 shorter events, 0.0 us)
Async XLA Ops:
  0.6 0.7 copy-start.4
  12.5 10.6 %collective-permute-start.1 = (bf16[8,1296,256]{2,1,0:T(8,128)(2,1)}, bf16[8,1296,256]{2,1,0:T(8,128)(2,1)}, u32[]{:S(2)}, u32[]{:S(2)}) collective-permute-start(bf16[8,1296,256]{2,1,0:T(8,128)(2,1)} %get-tuple-element.25.own_hbm), channel_id=1, source_target_pairs={{0,16},{16,0},{32,48},{48,32},{64,80},{80,64},{96,112},{112,96},{1... | collective-permute-start | bytes 15925256 | tf_op jit(solution)/shard_map/ppermute | solution.py:648
  14.4 9.7 %copy-start.5 = (s32[1,16]{1,0:T(1,128)S(1)}, s32[1,16]{1,0:T(1,128)}, u32[]{:S(2)}) copy-start(s32[1,16]{1,0:T(1,128)} %param.11) | copy-start | bytes 196
  22.2 20.2 %collective-permute-start = (bf16[8,1296,256]{2,1,0:T(8,128)(2,1)}, bf16[8,1296,256]{2,1,0:T(8,128)(2,1)}, u32[]{:S(2)}, u32[]{:S(2)}) collective-permute-start(bf16[8,1296,256]{2,1,0:T(8,128)(2,1)} %gather_rows.3.own_hbm), channel_id=1, source_target_pairs={{0,16},{16,0},{32,48},{48,32},{64,80},{80,64},{96,112},{112,96},{1... | collective-permute-start | bytes 15925256 | tf_op jit(solution)/shard_map/ppermute | solution.py:648
  39.0 20.5 %collective-permute-start.5 = (s16[1288,256]{1,0:T(8,128)(2,1)}, s16[1288,256]{1,0:T(8,128)(2,1)S(1)}, u32[]{:S(2)}, u32[]{:S(2)}) collective-permute-start(s16[1288,256]{1,0:T(8,128)(2,1)} %get-tuple-element.32), channel_id=1, source_target_pairs={{0,32},{16,48},{32,64},{48,80},{64,96},{80,112},{96,0},{112,16},{1... | collective-permute-start | bytes 1978376 | tf_op jit(solution)/shard_map/ppermute | solution.py:657
  39.7 19.9 %collective-permute-start.7 = (s16[1288,256]{1,0:T(8,128)(2,1)}, s16[1288,256]{1,0:T(8,128)(2,1)S(1)}, u32[]{:S(2)}, u32[]{:S(2)}) collective-permute-start(s16[1288,256]{1,0:T(8,128)(2,1)} %get-tuple-element.34), channel_id=1, source_target_pairs={{0,96},{16,112},{32,0},{48,16},{64,32},{80,48},{96,64},{112,80},{1... | collective-permute-start | bytes 1978376 | tf_op jit(solution)/shard_map/ppermute | solution.py:657
  60.2 13.1 %copy-start.7 = (s16[1288,256]{1,0:T(8,128)(2,1)S(1)}, s16[1288,256]{1,0:T(8,128)(2,1)}, u32[]{:S(2)}) copy-start(s16[1288,256]{1,0:T(8,128)(2,1)} %get-tuple-element.27) | copy-start | bytes 1978372
  60.2 26.7 %copy-start.1 = (s16[1288,256]{1,0:T(8,128)(2,1)S(1)}, s16[1288,256]{1,0:T(8,128)(2,1)}, u32[]{:S(2)}) copy-start(s16[1288,256]{1,0:T(8,128)(2,1)} %get-tuple-element.31.refs_0_) | copy-start | bytes 1978372
  60.2 44.0 %copy-start = (s16[1288,256]{1,0:T(8,128)(2,1)S(1)}, s16[1288,256]{1,0:T(8,128)(2,1)}, u32[]{:S(2)}) copy-start(s16[1288,256]{1,0:T(8,128)(2,1)} %get-tuple-element.28.p0) | copy-start | bytes 1978372
  60.2 56.7 %all-to-all-start.1 = ((s16[16,392,256]{2,1,0:T(8,128)(2,1)}), s16[16,392,256]{2,1,0:T(8,128)(2,1)}, u32[]{:S(2)}, u32[]{:S(2)}) async-start(s16[16,392,256]{2,1,0:T(8,128)(2,1)} %after.1), calls=%async_computation.1 | async-start | bytes 6422528 | tf_op jit(solution)/shard_map/all_to_all | solution.py:669
  69.8 17.0 %collective-permute-start.6 = (s16[1288,256]{1,0:T(8,128)(2,1)}, s16[1288,256]{1,0:T(8,128)(2,1)S(1)}, u32[]{:S(2)}, u32[]{:S(2)}) collective-permute-start(s16[1288,256]{1,0:T(8,128)(2,1)} %get-tuple-element.33), channel_id=1, source_target_pairs={{0,64},{16,80},{32,96},{48,112},{64,0},{80,16},{96,32},{112,48},{1... | collective-permute-start | bytes 1978376 | tf_op jit(solution)/shard_map/ppermute | solution.py:657
  70.6 33.6 %collective-permute-start.3 = (s16[1288,256]{1,0:T(8,128)(2,1)}, s16[1288,256]{1,0:T(8,128)(2,1)S(1)}, u32[]{:S(2)}, u32[]{:S(2)}) collective-permute-start(s16[1288,256]{1,0:T(8,128)(2,1)} %get-tuple-element.29), channel_id=1, source_target_pairs={{0,32},{16,48},{32,64},{48,80},{64,96},{80,112},{96,0},{112,16},{1... | collective-permute-start | bytes 1978376 | tf_op jit(solution)/shard_map/ppermute | solution.py:657
  70.6 33.6 %collective-permute-start.4 = (s16[1288,256]{1,0:T(8,128)(2,1)}, s16[1288,256]{1,0:T(8,128)(2,1)S(1)}, u32[]{:S(2)}, u32[]{:S(2)}) collective-permute-start(s16[1288,256]{1,0:T(8,128)(2,1)} %get-tuple-element.30), channel_id=1, source_target_pairs={{0,96},{16,112},{32,0},{48,16},{64,32},{80,48},{96,64},{112,80},{1... | collective-permute-start | bytes 1978376 | tf_op jit(solution)/shard_map/ppermute | solution.py:657
  73.3 41.7 %collective-permute-start.2 = (s16[1288,256]{1,0:T(8,128)(2,1)S(1)}, s16[1288,256]{1,0:T(8,128)(2,1)S(1)}, u32[]{:S(2)}, u32[]{:S(2)}) collective-permute-start(s16[1288,256]{1,0:T(8,128)(2,1)S(1)} %copy-done.7), channel_id=1, source_target_pairs={{0,64},{16,80},{32,96},{48,112},{64,0},{80,16},{96,32},{112,48},{1... | collective-permute-start | bytes 1978376 | tf_op jit(solution)/shard_map/ppermute | solution.py:657
  104.9 36.2 %copy-start.2 = (bf16[256,1024]{1,0:T(8,128)(2,1)S(1)}, bf16[256,1024]{1,0:T(8,128)(2,1)}, u32[]{:S(2)}) copy-start(bf16[256,1024]{1,0:T(8,128)(2,1)} %stencil_ref.1) | copy-start | bytes 1572868
  104.9 59.0 %copy-start.3 = (s32[1,16,128]{2,1,0:T(8,128)S(1)}, s32[1,16,128]{2,1,0:T(8,128)}, u32[]{:S(2)}) copy-start(s32[1,16,128]{2,1,0:T(8,128)} %param.12) | copy-start | bytes 24580
  105.0 59.0 %copy-start.6 = (s32[1,16]{1,0:T(1,128)S(1)}, s32[1,16]{1,0:T(1,128)}, u32[]{:S(2)}) copy-start(s32[1,16]{1,0:T(1,128)} %param.13) | copy-start | bytes 196
  116.9 24.2 %all-to-all-start = ((s16[16,168,256]{2,1,0:T(8,128)(2,1)}), s16[16,168,256]{2,1,0:T(8,128)(2,1)S(1)}, u32[]{:S(2)}, u32[]{:S(2)}) async-start(s16[16,168,256]{2,1,0:T(8,128)(2,1)} %sum_x.3), calls=%async_computation | async-start | bytes 2752512 | tf_op jit(solution)/shard_map/all_to_all | solution.py:674
  126.8 14.2 %collective-permute-start.8 = (s16[104,256]{1,0:T(8,128)(2,1)S(1)}, s16[104,256]{1,0:T(8,128)(2,1)S(1)}, u32[]{:S(2)}, u32[]{:S(2)}) collective-permute-start(s16[104,256]{1,0:T(8,128)(2,1)S(1)} %get-tuple-element.37), channel_id=1, source_target_pairs={{0,32},{16,48},{32,64},{48,80},{64,96},{80,112},{96,0},{112,16},{1... | collective-permute-start | bytes 159752 | tf_op jit(solution)/shard_map/ppermute | solution.py:657
  126.9 14.2 %collective-permute-start.9 = (s16[104,256]{1,0:T(8,128)(2,1)S(1)}, s16[104,256]{1,0:T(8,128)(2,1)S(1)}, u32[]{:S(2)}, u32[]{:S(2)}) collective-permute-start(s16[104,256]{1,0:T(8,128)(2,1)S(1)} %get-tuple-element.38), channel_id=1, source_target_pairs={{0,64},{16,80},{32,96},{48,112},{64,0},{80,16},{96,32},{112,48},{1... | collective-permute-start | bytes 159752 | tf_op jit(solution)/shard_map/ppermute | solution.py:657
  128.0 13.1 %collective-permute-start.10 = (s16[104,256]{1,0:T(8,128)(2,1)S(1)}, s16[104,256]{1,0:T(8,128)(2,1)S(1)}, u32[]{:S(2)}, u32[]{:S(2)}) collective-permute-start(s16[104,256]{1,0:T(8,128)(2,1)S(1)} %get-tuple-element.39), channel_id=1, source_target_pairs={{0,96},{16,112},{32,0},{48,16},{64,32},{80,48},{96,64},{112,80},{1... | collective-permute-start | bytes 159752 | tf_op jit(solution)/shard_map/ppermute | solution.py:657
  143.9 18.2 %collective-permute-start.11 = (s16[264,256]{1,0:T(8,128)(2,1)S(1)}, s16[264,256]{1,0:T(8,128)(2,1)S(1)}, u32[]{:S(2)}, u32[]{:S(2)}) collective-permute-start(s16[264,256]{1,0:T(8,128)(2,1)S(1)} %get-tuple-element.41), channel_id=1, source_target_pairs={{0,2},{1,3},{2,4},{3,5},{4,6},{5,7},{6,8},{7,9},{8,10},{9,11},{10,... | collective-permute-start | bytes 405512 | tf_op jit(solution)/shard_map/ppermute | solution.py:683
  148.0 14.1 %collective-permute-start.12 = (s16[264,256]{1,0:T(8,128)(2,1)S(1)}, s16[264,256]{1,0:T(8,128)(2,1)S(1)}, u32[]{:S(2)}, u32[]{:S(2)}) collective-permute-start(s16[264,256]{1,0:T(8,128)(2,1)S(1)} %get-tuple-element.41), channel_id=1, source_target_pairs={{2,0},{3,1},{4,2},{5,3},{6,4},{7,5},{8,6},{9,7},{10,8},{11,9},{12,... | collective-permute-start | bytes 405512 | tf_op jit(solution)/shard_map/ppermute | solution.py:683
  153.1 9.7 %collective-permute-start.13 = (s16[264,256]{1,0:T(8,128)(2,1)S(1)}, s16[264,256]{1,0:T(8,128)(2,1)S(1)}, u32[]{:S(2)}, u32[]{:S(2)}) collective-permute-start(s16[264,256]{1,0:T(8,128)(2,1)S(1)} %get-tuple-element.41), channel_id=1, source_target_pairs={{0,1},{1,2},{2,3},{3,4},{4,5},{5,6},{6,7},{7,8},{8,9},{9,10},{10,1... | collective-permute-start | bytes 405512 | tf_op jit(solution)/shard_map/ppermute | solution.py:683
  155.7 8.3 %collective-permute-start.14 = (s16[264,256]{1,0:T(8,128)(2,1)S(1)}, s16[264,256]{1,0:T(8,128)(2,1)S(1)}, u32[]{:S(2)}, u32[]{:S(2)}) collective-permute-start(s16[264,256]{1,0:T(8,128)(2,1)S(1)} %get-tuple-element.41), channel_id=1, source_target_pairs={{1,0},{2,1},{3,2},{4,3},{5,4},{6,5},{7,6},{8,7},{9,8},{10,9},{11,1... | collective-permute-start | bytes 405512 | tf_op jit(solution)/shard_map/ppermute | solution.py:683
